TPU v7x, 32 devices: a whole 2x2x4 slice. The times are simulated.
32 devices in a mesh: grp: 2 (over y), vec: 4 (over z), occ: 2 (over x), wlk: 2 (over core).
Axes of the slice: x: 2, y: 2, z: 4, core: 2. Of those that a mesh axis runs over, the one named last changes fastest.
Arguments:
- chol_half: bfloat16 [256, 256, 2048], P(('grp', 'vec'), 'occ'), parts along dimension 0, may hold values from -0.046875 to 0.046875
- theta: bfloat16 [8, 2048, 256], P(('grp', 'wlk'), 'vec', 'occ'), parts along dimension 0, may hold values from -6 to 6
Outputs:
- theta_grad: float32 [8, 2048, 256], P(('grp', 'wlk'), 'vec', 'occ'), parts along dimension 0
There are 2 independent parts, one for each index of `grp`. A program takes and returns all parts, laid end to end along the dimension named above; each array names one. Nothing has to cross between parts.
All inputs are finite; a program needn't handle non-finite values.
Results may differ from a plain program's by a relative error of at most 0.0042.
Values may be sent and summed in bfloat16 or wider, within the bound.
No kernel may reach another device: no remote copies, remote signals or barrier semaphores. Data moves between devices by JAX's collectives and lax.ppermute only.
A program may use at most 64 MiB of HBM per device.

v0:
```python
import functools

import jax
import jax.numpy as jnp
from jax import lax
from jax.experimental import pallas as pl
from jax.experimental.pallas import tpu as pltpu
from jax.sharding import PartitionSpec as P


AXES = ("grp", "vec", "occ", "wlk")
HALVES = 2
STREAMS = 4
BLOCK = 8
LARGE = pltpu.CompilerParams(vmem_limit_bytes=44 * 2**20)
SMALL = pltpu.CompilerParams(vmem_limit_bytes=24 * 2**20)


def general(chol_half, theta):
    widened = lax.all_gather(theta, "occ", axis=2, tiled=True)
    amplitude_sums = jnp.einsum(
        "gip,wpj->wgij",
        chol_half,
        lax.all_gather(widened, "vec", axis=1, tiled=True),
        preferred_element_type=jnp.float32,
    )
    amplitudes = amplitude_sums.astype(jnp.bfloat16)
    swapped = lax.all_to_all(amplitudes, "occ", split_axis=3, concat_axis=2, tiled=True)
    summed_rows = lax.psum_scatter(
        jnp.einsum("gap,wgba->pwb", chol_half, swapped, preferred_element_type=jnp.float32),
        "vec",
        scatter_dimension=0,
        tiled=True,
    )
    owned = lax.psum_scatter(summed_rows, "occ", scatter_dimension=2, tiled=True)
    return -jnp.transpose(owned, (1, 0, 2))


VMEM = pl.BlockSpec(memory_space=pltpu.VMEM)
SMEM = pl.BlockSpec(memory_space=pltpu.SMEM)


def peer(position, hop, shards, back=False):
    if shards & (shards - 1) == 0:
        return position ^ hop
    moved = position + (shards - hop if back else hop)
    return moved % shards if isinstance(moved, int) else lax.rem(moved, shards)


def hops_of(shards):
    return sorted(range(1, shards), key=lambda hop: (hop != shards // 2, -hop))


def groups_of(shards):
    hops = hops_of(shards) + [0]
    return [hops[: shards // 2], hops[shards // 2 :]]


def load_body(first, place, source, out, arrived):
    del place
    rows = out.shape[0] // STREAMS
    copies = [pltpu.make_async_copy(source.at[pl.ds(first + at * rows, rows)], out.at[pl.ds(at * rows, rows)], arrived.at[at]) for at in range(STREAMS)]
    for copy in copies:
        copy.start()
    for copy in copies:
        copy.wait()


def loaded(place, factors, first, count):
    return pl.pallas_call(
        functools.partial(load_body, first),
        in_specs=[SMEM, pl.BlockSpec(memory_space=pltpu.HBM)],
        out_specs=VMEM,
        out_shape=pltpu.VMEM((count, factors.shape[1]), factors.dtype),
        scratch_shapes=[pltpu.SemaphoreType.DMA((STREAMS,))],
        compiler_params=LARGE,
    )(place, factors)


def amplitude_body(shards, low, high, half, place, factors, *refs):
    pieces, own, far, rows = refs[:-3], refs[-3], refs[-2], refs[-1]
    owned, width = pieces[0].shape[0], own.shape[1]
    for step in range(shards):
        at = pl.multiple_of(peer(place[0], step, shards, True) * owned, owned)
        if len(pieces) == shards:
            rows[pl.ds(at, owned), :] = pieces[step][...]
        else:
            rows[pl.ds(at, owned), :width] = pieces[step][...]
            rows[pl.ds(at, owned), width:] = pieces[shards + step][...]
    part = width // HALVES
    for first in range(low, high, BLOCK):
        vectors = range(first, min(first + BLOCK, high))
        taken = jnp.concatenate([factors[g * width + half * part : g * width + (half + 1) * part, :] for g in vectors], axis=0)
        sums = jnp.dot(taken, rows[...], preferred_element_type=jnp.float32).astype(jnp.bfloat16)
        at = (first - low) * part
        own[at : at + sums.shape[0], :] = sums[:, :width]
        far[at : at + sums.shape[0], :] = sums[:, width:]


def amplitudes_of(place, factors, pieces, vectors, half, width, shards):
    orbitals = factors.shape[1]
    count = (vectors[1] - vectors[0]) * width // HALVES
    return pl.pallas_call(
        functools.partial(amplitude_body, shards, *vectors, half),
        in_specs=[SMEM] + [VMEM] * (1 + len(pieces)),
        out_specs=[VMEM] * 2,
        scratch_shapes=[pltpu.VMEM((orbitals, 2 * width), jnp.bfloat16)],
        out_shape=[jax.ShapeDtypeStruct((count, width), jnp.bfloat16)] * 2,
        compiler_params=SMALL,
        cost_estimate=pl.CostEstimate(flops=4 * count * orbitals * width, transcendentals=0, bytes_accessed=2 * count * orbitals),
    )(place, factors, *pieces)


def gradient_body(shards, parts, first, carried, groups, place, *refs):
    owns, fars, factors = refs[:parts], refs[parts : 2 * parts], refs[2 * parts]
    outs, sums = refs[2 * parts + 1 + carried : -1], refs[-1]
    width = owns[0].shape[1]
    part = width // HALVES
    slots = [(at, g) for at, own in enumerate(owns) for g in range(own.shape[0] // part)]
    for seen in range(0, len(slots), BLOCK):
        vectors = slots[seen : seen + BLOCK]
        wide = [jnp.concatenate([side[at][g * part : (g + 1) * part, :] for at, g in vectors], axis=1) for side in (owns, fars)]
        low = (first + seen) * width
        grown = jnp.dot(jnp.concatenate(wide, axis=0), factors[low : low + len(vectors) * width, :], preferred_element_type=jnp.float32)
        if seen == 0 and carried:
            sums[...] = refs[2 * parts + 1][...] + grown
        elif seen == 0:
            sums[...] = grown
        else:
            sums[...] += grown
    if len(outs) == 1:
        outs[0][...] = sums[...]
        return
    owned = sums.shape[1] // shards
    for hop in range(shards):
        low = pl.multiple_of(peer(place[0], hop, shards) * owned, owned)
        if groups is None:
            outs[hop][...] = sums[:, pl.ds(low, owned)].astype(outs[hop].dtype)
            continue
        outs[hop][...] = sums[:part, pl.ds(low, owned)].astype(outs[hop].dtype)
        for group, hops in enumerate(groups):
            if hop in hops:
                to = hops.index(hop) * owned
                outs[shards + group][:, to : to + owned] = sums[part:, pl.ds(low, owned)].astype(jnp.bfloat16)


def gradients_of(place, factors, owns, fars, shards, first=0, groups=None, carried=None, more=False):
    orbitals, width = factors.shape[1], owns[0].shape[1]
    part, owned = width // HALVES, orbitals // shards
    outs = [jax.ShapeDtypeStruct((2 * part, owned), jnp.bfloat16 if hop else jnp.float32) for hop in range(shards)]
    if more:
        outs = [jax.ShapeDtypeStruct((2 * part, orbitals), jnp.float32)]
    elif groups:
        outs = [jax.ShapeDtypeStruct((part, owned), jnp.float32)] * shards
        outs += [jax.ShapeDtypeStruct((part, owned * len(hops)), jnp.bfloat16) for hops in groups]
    count = sum(own.shape[0] for own in owns) * HALVES
    values = [place, *owns, *fars, factors] + ([] if carried is None else [carried])
    return pl.pallas_call(
        functools.partial(gradient_body, shards, len(owns), first, 0 if carried is None else 1, groups),
        in_specs=[SMEM] + [VMEM] * (len(values) - 1),
        out_specs=[VMEM] * len(outs),
        scratch_shapes=[pltpu.VMEM((2 * part, orbitals), jnp.float32)],
        out_shape=outs,
        compiler_params=SMALL,
        cost_estimate=pl.CostEstimate(flops=4 * count * orbitals * part, transcendentals=0, bytes_accessed=2 * count * orbitals),
    )(*values)


def split_body(each, *refs):
    inputs, outs = refs[: -(len(refs) // (each + 1)) - 1], refs[-(len(refs) // (each + 1)) - 1 :]
    for stage, own in enumerate(outs[:-1]):
        parts = inputs[stage * each : (stage + 1) * each]
        total = parts[0][...].astype(jnp.float32)
        for part in parts[1:]:
            total = total + part[...].astype(jnp.float32)
        half = own.shape[0]
        own[...] = total[:half]
        outs[-1][stage * half : (stage + 1) * half, :] = total[half:].astype(jnp.bfloat16)


def split_sums(stages):
    rows, columns = stages[0][0].shape
    outs = [jax.ShapeDtypeStruct((rows // 2, columns), jnp.float32)] * len(stages)
    outs += [jax.ShapeDtypeStruct((len(stages) * (rows // 2), columns), jnp.bfloat16)]
    flat = [part for stage in stages for part in stage]
    return pl.pallas_call(functools.partial(split_body, len(stages[0])), out_shape=outs, compiler_params=SMALL)(*flat)


def join_body(came, *refs):
    count = len(refs) // 2
    for at in range(count):
        own, out = refs[at], refs[count + at]
        columns = own.shape[1]
        out[...] = (own[...] + came[:, at * columns : (at + 1) * columns].astype(jnp.float32)).astype(out.dtype)


def join_sums(came, owns, kinds):
    outs = [jax.ShapeDtypeStruct(own.shape, kind) for own, kind in zip(owns, kinds)]
    return pl.pallas_call(join_body, out_shape=outs, compiler_params=SMALL)(came, *owns)


def total_body(plan, *refs):
    out = refs[-1]
    for walker, halves in enumerate(plan):
        rows = []
        for parts in halves:
            total = None
            for at, low, high in parts:
                value = refs[at][low:high, :].astype(jnp.float32)
                total = value if total is None else total + value
            rows.append(total)
        out[walker] = -jnp.concatenate(rows, axis=0).T


def totals_of(values, plan):
    part, owned = values[0].shape
    return pl.pallas_call(
        functools.partial(total_body, plan),
        out_shape=jax.ShapeDtypeStruct((len(plan), owned, part * HALVES), jnp.float32),
        compiler_params=SMALL,
    )(*values)


def parts_of(stage, stages, vectors):
    if stage == 0:
        return [0, vectors // 4, vectors]
    if stage == stages - 1:
        return [0, vectors - vectors // 4, vectors]
    return [0, vectors]


def paired(shape, chol_half, theta):
    return in_order(shape, chol_half, theta)


def in_order(shape, chol_half, theta):
    shards = shape["vec"]
    vectors, width, orbitals = chol_half.shape
    walkers = theta.shape[0]
    position = lax.axis_index("vec")
    place = position.reshape(1)
    whole = chol_half.reshape(vectors * width, orbitals)
    factors = loaded(place, whole, 0, vectors * width)

    def flat(grp, vec, occ, wlk):
        return ((grp * shape["vec"] + vec) * shape["occ"] + occ) * shape["wlk"] + wlk

    def moved(value, hop, across=False):
        pairs = [
            (flat(grp, vec, occ, wlk), flat(grp, peer(vec, hop, shards), 1 - occ if across else occ, wlk))
            for grp in range(shape["grp"])
            for vec in range(shards)
            for occ in range(shape["occ"])
            for wlk in range(shape["wlk"])
        ]
        return lax.ppermute(value, AXES, pairs)

    hops = range(1, shards)
    near = [theta[0]] + [moved(theta[0], hop) for hop in hops]
    across = moved(theta, 0, True)
    blocks = [near + [across[0]] + [moved(near[hop], 0, True) for hop in hops]]
    for walker in range(1, walkers):
        both = jnp.concatenate([theta[walker], across[walker]], axis=1)
        blocks.append([both] + [moved(both, hop) for hop in hops])

    stages = walkers * HALVES
    sides = []
    for stage in range(stages):
        owns, fars = [], []
        cuts = parts_of(stage, stages, vectors)
        for part in zip(cuts[:-1], cuts[1:]):
            own, far = amplitudes_of(place, factors, blocks[stage // HALVES], part, stage % HALVES, width, shards)
            owns.append(own)
            fars.append(moved(far, 0, True))
        sides.append((owns, fars))

    arrived = []
    for stage in range(stages - 1):
        got = gradients_of(place, factors, *sides[stage], shards)
        arrived.append([got[0]] + [moved(got[hop], hop) for hop in hops])
    part, values, plan = width // HALVES, [], []
    for some in (arrived[:-1], arrived[-1:]):
        *kept, crossing = split_sums(some)
        here = len(values)
        values += [*kept, moved(crossing, 0, True)]
        plan += [[(here + stage, 0, part), (here + len(kept), stage * part, (stage + 1) * part)] for stage in range(len(kept))]

    owns, fars = sides[-1]
    groups = groups_of(shards)
    (carried,) = gradients_of(place, factors, owns[:1], fars[:1], shards, more=True)
    got = gradients_of(place, factors, owns[1:], fars[1:], shards, parts_of(stages - 1, stages, vectors)[1], groups, carried)
    came = [moved(got[shards + at], 0, True) for at in range(len(groups))]
    ends = [None] * shards
    for at, group in enumerate(groups):
        joined = join_sums(came[at], [got[hop] for hop in group], [jnp.bfloat16 if hop else jnp.float32 for hop in group])
        for hop, value in zip(group, joined):
            ends[hop] = moved(value, hop) if hop else value
    plan.append([(len(values) + at, 0, part) for at in range(shards)])
    values += ends
    return totals_of(values, [plan[walker * HALVES : (walker + 1) * HALVES] for walker in range(walkers)])


def solution(mesh):
    placed = (P(("grp", "vec"), "occ", None), P(("grp", "wlk"), "vec", "occ"))
    pairs = mesh.shape["occ"] == 2
    return jax.shard_map(
        functools.partial(paired, dict(mesh.shape)) if pairs else general,
        mesh=mesh,
        in_specs=placed,
        out_specs=P(("grp", "wlk"), "vec", "occ"),
        check_vma=False,
    )
```

profile of v0, /device:TPU:0, one launch (start us, length us, event | category | flops | bytes accessed | tf_op | source)
XLA Modules:
  0.0 108.6 jit_solution(17043131300137990193)
XLA Ops:
  0.0 3.0 %collective-permute-start.3 = (bf16[2,512,128]{2,1,0:T(8,128)(2,1)}, bf16[2,512,128]{2,1,0:T(8,128)(2,1)S(1)}, u32[]{:S(2)}, u32[]{:S(2)}) collective-permute-start(bf16[2,512,128]{2,1,0:T(8,128)(2,1)} %param.3), channel_id=1, source_target_pairs={{0,2},{1,3},{2,0},{3,1},{4,6},{5,7},{6,4},{7,5},{8,10},{9,11},{10,... | collective-permute-start | bytes 786440 | tf_op jit(solution)/shard_map/ppermute | solution.py:256
  4.0 1.6 %collective-permute-start = (bf16[512,128]{1,0:T(8,128)(2,1)S(1)}, bf16[512,128]{1,0:T(8,128)(2,1)S(1)}, u32[]{:S(2)}, u32[]{:S(2)}) collective-permute-start(bf16[512,128]{1,0:T(8,128)(2,1)S(1)} %get-tuple-element.84.refs_0_), channel_id=1, source_target_pairs={{0,4},{1,5},{2,6},{3,7},{4,0},{5,1},{6,2},{7,3},{8,12},{9,13},{10,... | collective-permute-start | bytes 393224 | tf_op jit(solution)/shard_map/ppermute | solution.py:256
  5.6 2.6 %collective-permute-start.1 = (bf16[512,128]{1,0:T(8,128)(2,1)S(1)}, bf16[512,128]{1,0:T(8,128)(2,1)S(1)}, u32[]{:S(2)}, u32[]{:S(2)}) collective-permute-start(bf16[512,128]{1,0:T(8,128)(2,1)S(1)} %get-tuple-element.84.refs_0_), channel_id=1, source_target_pairs={{0,8},{1,9},{2,10},{3,11},{4,12},{5,13},{6,14},{7,15},{8,0},{9,1},... | collective-permute-start | bytes 393224 | tf_op jit(solution)/shard_map/ppermute | solution.py:256
  8.4 5.9 %shard_map.28.factors.refs_4_.refs_2_ = bf16[4096,2048]{1,0:T(8,128)(2,1)S(1)} custom-call(s32[1]{0:T(128)} %bitcast.place, bf16[4096,2048]{1,0:T(8,128)(2,1)} %bitcast.10), custom_call_target="tpu_custom_call" | custom-call | tf_op jit(solution)/shard_map/pallas_call | solution.py:70
  14.7 3.5 %collective-permute-done.1.refs_2_ = bf16[512,128]{1,0:T(8,128)(2,1)S(1)} collective-permute-done((bf16[512,128]{1,0:T(8,128)(2,1)S(1)}, bf16[512,128]{1,0:T(8,128)(2,1)S(1)}, u32[]{:S(2)}, u32[]{:S(2)}) %collective-permute-start.1) | collective-permute-done | bytes 131104 | tf_op jit(solution)/shard_map/ppermute | solution.py:256
  18.8 1.5 %collective-permute-start.6 = (bf16[512,128]{1,0:T(8,128)(2,1)S(1)}, bf16[512,128]{1,0:T(8,128)(2,1)S(1)}, u32[]{:S(2)}, u32[]{:S(2)}) collective-permute-start(bf16[512,128]{1,0:T(8,128)(2,1)S(1)} %collective-permute-done.2.refs_3_), channel_id=1, source_target_pairs={{0,2},{1,3},{2,0},{3,1},{4,6},{5,7},{6,4},{7,5},{8,10},{9,11},{10,... | collective-permute-start | bytes 393224 | tf_op jit(solution)/shard_map/ppermute | solution.py:256
  20.9 2.5 %collective-permute-start.18 = (bf16[512,256]{1,0:T(8,128)(2,1)S(1)}, bf16[512,256]{1,0:T(8,128)(2,1)S(1)}, u32[]{:S(2)}, u32[]{:S(2)}) collective-permute-start(bf16[512,256]{1,0:T(8,128)(2,1)S(1)} %pad_maximum_fusion.refs_0_), channel_id=1, source_target_pairs={{0,8},{1,9},{2,10},{3,11},{4,12},{5,13},{6,14},{7,15},{8,0},{9,1},... | collective-permute-start | bytes 786440 | tf_op jit(solution)/shard_map/ppermute | solution.py:256
  23.4 1.5 %collective-permute-start.19 = (bf16[512,256]{1,0:T(8,128)(2,1)S(1)}, bf16[512,256]{1,0:T(8,128)(2,1)S(1)}, u32[]{:S(2)}, u32[]{:S(2)}) collective-permute-start(bf16[512,256]{1,0:T(8,128)(2,1)S(1)} %pad_maximum_fusion.refs_0_), channel_id=1, source_target_pairs={{0,12},{1,13},{2,14},{3,15},{4,8},{5,9},{6,10},{7,11},{8,4},{9,5},... | collective-permute-start | bytes 786440 | tf_op jit(solution)/shard_map/ppermute | solution.py:256
  26.3 2.0 %shard_map.30 = (bf16[1536,128]{1,0:T(8,128)(2,1)S(1)}, bf16[1536,128]{1,0:T(8,128)(2,1)S(1)}) custom-call(s32[1]{0:T(128)} %bitcast.place, bf16[4096,2048]{1,0:T(8,128)(2,1)S(1)} %shard_map.28.factors.refs_4_.refs_2_, bf16[512,128]{1,0:T(8,128)(2,1)S(1)} %get-tuple-element.84.refs_0_, bf16[512,128]{1,0:T(8,128)(2,1)S(1)} %collective-permute-done.refs_1_, ...), custom_call_target="tpu_custom_call" | custom-call | flops 1610612736 | bytes 6291456 | tf_op jit(solution)/shard_map/pallas_call | solution.py:103
  28.3 1.6 %collective-permute-start.8 = (bf16[1536,128]{1,0:T(8,128)(2,1)S(1)}, bf16[1536,128]{1,0:T(8,128)(2,1)S(1)}, u32[]{:S(2)}, u32[]{:S(2)}) collective-permute-start(bf16[1536,128]{1,0:T(8,128)(2,1)S(1)} %get-tuple-element.47), channel_id=1, source_target_pairs={{0,2},{1,3},{2,0},{3,1},{4,6},{5,7},{6,4},{7,5},{8,10},{9,11},{10,... | collective-permute-start | bytes 1179656 | tf_op jit(solution)/shard_map/ppermute | solution.py:256
  29.9 2.5 %shard_map.32 = (bf16[2048,128]{1,0:T(8,128)(2,1)S(1)}, bf16[2048,128]{1,0:T(8,128)(2,1)S(1)}) custom-call(s32[1]{0:T(128)} %bitcast.place, bf16[4096,2048]{1,0:T(8,128)(2,1)S(1)} %shard_map.28.factors.refs_4_.refs_2_, bf16[512,128]{1,0:T(8,128)(2,1)S(1)} %get-tuple-element.84.refs_0_, bf16[512,128]{1,0:T(8,128)(2,1)S(1)} %collective-permute-done.refs_1_, ...), custom_call_target="tpu_custom_call" | custom-call | flops 2147483648 | bytes 8388608 | tf_op jit(solution)/shard_map/pallas_call | solution.py:103
  33.0 9.2 %collective-permute-done.18.refs_2_ = bf16[512,256]{1,0:T(8,128)(2,1)S(1)} collective-permute-done((bf16[512,256]{1,0:T(8,128)(2,1)S(1)}, bf16[512,256]{1,0:T(8,128)(2,1)S(1)}, u32[]{:S(2)}, u32[]{:S(2)}) %collective-permute-start.18) | collective-permute-done | bytes 262176 | tf_op jit(solution)/shard_map/ppermute | solution.py:256
  42.2 2.4 %shard_map.35 = (bf16[2048,128]{1,0:T(8,128)(2,1)S(1)}, bf16[2048,128]{1,0:T(8,128)(2,1)S(1)}) custom-call(s32[1]{0:T(128)} %bitcast.place, bf16[4096,2048]{1,0:T(8,128)(2,1)S(1)} %shard_map.28.factors.refs_4_.refs_2_, bf16[512,256]{1,0:T(8,128)(2,1)S(1)} %pad_maximum_fusion.refs_0_, bf16[512,256]{1,0:T(8,128)(2,1)S(1)} %collective-permute-done.17.refs_1_, ...), custom_call_target="tpu_custom_call" | custom-call | flops 2147483648 | bytes 8388608 | tf_op jit(solution)/shard_map/pallas_call | solution.py:103
  44.6 1.6 %collective-permute-start.20 = (bf16[2048,128]{1,0:T(8,128)(2,1)S(1)}, bf16[2048,128]{1,0:T(8,128)(2,1)S(1)}, u32[]{:S(2)}, u32[]{:S(2)}) collective-permute-start(bf16[2048,128]{1,0:T(8,128)(2,1)S(1)} %get-tuple-element.62), channel_id=1, source_target_pairs={{0,2},{1,3},{2,0},{3,1},{4,6},{5,7},{6,4},{7,5},{8,10},{9,11},{10,... | collective-permute-start | bytes 1572872 | tf_op jit(solution)/shard_map/ppermute | solution.py:256
  47.6 1.9 %shard_map.39 = (bf16[1536,128]{1,0:T(8,128)(2,1)S(1)}, bf16[1536,128]{1,0:T(8,128)(2,1)S(1)}) custom-call(s32[1]{0:T(128)} %bitcast.place, bf16[4096,2048]{1,0:T(8,128)(2,1)S(1)} %shard_map.28.factors.refs_4_.refs_2_, bf16[512,256]{1,0:T(8,128)(2,1)S(1)} %pad_maximum_fusion.refs_0_, bf16[512,256]{1,0:T(8,128)(2,1)S(1)} %collective-permute-done.17.refs_1_, ...), custom_call_target="tpu_custom_call" | custom-call | flops 1610612736 | bytes 6291456 | tf_op jit(solution)/shard_map/pallas_call | solution.py:103
  49.4 1.6 %collective-permute-start.26 = (bf16[1536,128]{1,0:T(8,128)(2,1)S(1)}, bf16[1536,128]{1,0:T(8,128)(2,1)S(1)}, u32[]{:S(2)}, u32[]{:S(2)}) collective-permute-start(bf16[1536,128]{1,0:T(8,128)(2,1)S(1)} %get-tuple-element.72), channel_id=1, source_target_pairs={{0,2},{1,3},{2,0},{3,1},{4,6},{5,7},{6,4},{7,5},{8,10},{9,11},{10,... | collective-permute-start | bytes 1179656 | tf_op jit(solution)/shard_map/ppermute | solution.py:256
  51.0 2.5 %shard_map.31 = (f32[128,512]{1,0:T(8,128)S(1)}, bf16[128,512]{1,0:T(8,128)(2,1)S(1)}, bf16[128,512]{1,0:T(8,128)(2,1)S(1)}, bf16[128,512]{1,0:T(8,128)(2,1)S(1)}) custom-call(s32[1]{0:T(128)} %bitcast.place, bf16[512,128]{1,0:T(8,128)(2,1)S(1)} %get-tuple-element.44.refs_0_, bf16[1536,128]{1,0:T(8,128)(2,1)S(1)} %get-tuple-element.45.refs_1_, ...), custom_call_target="tpu_custom_call" | custom-call | flops 2147483648 | bytes 16777216 | tf_op jit(solution)/shard_map/pallas_call | solution.py:158
  53.5 3.5 %collective-permute-start.9 = (bf16[128,512]{1,0:T(8,128)(2,1)S(1)}, bf16[128,512]{1,0:T(8,128)(2,1)S(1)}, u32[]{:S(2)}, u32[]{:S(2)}) collective-permute-start(bf16[128,512]{1,0:T(8,128)(2,1)S(1)} %get-tuple-element.49), channel_id=1, source_target_pairs={{0,4},{1,5},{2,6},{3,7},{4,0},{5,1},{6,2},{7,3},{8,12},{9,13},{10,... | collective-permute-start | bytes 393224 | tf_op jit(solution)/shard_map/ppermute | solution.py:256
  56.9 1.2 %collective-permute-start.10 = (bf16[128,512]{1,0:T(8,128)(2,1)S(1)}, bf16[128,512]{1,0:T(8,128)(2,1)S(1)}, u32[]{:S(2)}, u32[]{:S(2)}) collective-permute-start(bf16[128,512]{1,0:T(8,128)(2,1)S(1)} %get-tuple-element.50), channel_id=1, source_target_pairs={{0,8},{1,9},{2,10},{3,11},{4,12},{5,13},{6,14},{7,15},{8,0},{9,1},... | collective-permute-start | bytes 393224 | tf_op jit(solution)/shard_map/ppermute | solution.py:256
  58.2 2.7 %shard_map.33 = (f32[128,512]{1,0:T(8,128)S(1)}, bf16[128,512]{1,0:T(8,128)(2,1)S(1)}, bf16[128,512]{1,0:T(8,128)(2,1)S(1)}, bf16[128,512]{1,0:T(8,128)(2,1)S(1)}) custom-call(s32[1]{0:T(128)} %bitcast.place, bf16[2048,128]{1,0:T(8,128)(2,1)S(1)} %get-tuple-element.52.refs_0_, bf16[2048,128]{1,0:T(8,128)(2,1)S(1)} %collective-permute-done.12.refs_1_, ...), custom_call_target="tpu_custom_call" | custom-call | flops 2147483648 | bytes 16777216 | tf_op jit(solution)/shard_map/pallas_call | solution.py:158
  60.8 10.9 %collective-permute-done.26.refs_1_ = bf16[1536,128]{1,0:T(8,128)(2,1)S(1)} collective-permute-done((bf16[1536,128]{1,0:T(8,128)(2,1)S(1)}, bf16[1536,128]{1,0:T(8,128)(2,1)S(1)}, u32[]{:S(2)}, u32[]{:S(2)}) %collective-permute-start.26) | collective-permute-done | bytes 393248 | tf_op jit(solution)/shard_map/ppermute | solution.py:256
  71.7 3.3 %collective-permute-start.11 = (bf16[128,512]{1,0:T(8,128)(2,1)S(1)}, bf16[128,512]{1,0:T(8,128)(2,1)S(1)}, u32[]{:S(2)}, u32[]{:S(2)}) collective-permute-start(bf16[128,512]{1,0:T(8,128)(2,1)S(1)} %get-tuple-element.51), channel_id=1, source_target_pairs={{0,12},{1,13},{2,14},{3,15},{4,8},{5,9},{6,10},{7,11},{8,4},{9,5},... | collective-permute-start | bytes 393224 | tf_op jit(solution)/shard_map/ppermute | solution.py:256
  75.0 1.9 %shard_map.40.refs_3_ = f32[128,2048]{1,0:T(8,128)S(1)} custom-call(s32[1]{0:T(128)} %bitcast.place, bf16[1536,128]{1,0:T(8,128)(2,1)S(1)} %get-tuple-element.71.refs_0_, bf16[1536,128]{1,0:T(8,128)(2,1)S(1)} %collective-permute-done.26.refs_1_, bf16[4096,2048]{1,0:T(8,128)(2,1)S(1)} %shard_map.28.factors.refs_4_.refs_2_), custom_call_target="tpu_custom_call" | custom-call | flops 1610612736 | bytes 12582912 | tf_op jit(solution)/shard_map/pallas_call | solution.py:158
  78.9 3.3 %collective-permute-start.15 = (bf16[128,512]{1,0:T(8,128)(2,1)S(1)}, bf16[128,512]{1,0:T(8,128)(2,1)S(1)}, u32[]{:S(2)}, u32[]{:S(2)}) collective-permute-start(bf16[128,512]{1,0:T(8,128)(2,1)S(1)} %get-tuple-element.57), channel_id=1, source_target_pairs={{0,12},{1,13},{2,14},{3,15},{4,8},{5,9},{6,10},{7,11},{8,4},{9,5},... | collective-permute-start | bytes 393224 | tf_op jit(solution)/shard_map/ppermute | solution.py:256
  82.2 1.4 %collective-permute-start.27 = (bf16[64,1024]{1,0:T(8,128)(2,1)S(1)}, bf16[64,1024]{1,0:T(8,128)(2,1)S(1)}, u32[]{:S(2)}, u32[]{:S(2)}) collective-permute-start(bf16[64,1024]{1,0:T(8,128)(2,1)S(1)} %get-tuple-element.73), channel_id=1, source_target_pairs={{0,2},{1,3},{2,0},{3,1},{4,6},{5,7},{6,4},{7,5},{8,10},{9,11},{10,... | collective-permute-start | bytes 393224 | tf_op jit(solution)/shard_map/ppermute | solution.py:256
  84.2 2.5 %shard_map.36 = (f32[128,512]{1,0:T(8,128)S(1)}, bf16[128,512]{1,0:T(8,128)(2,1)S(1)}, bf16[128,512]{1,0:T(8,128)(2,1)S(1)}, bf16[128,512]{1,0:T(8,128)(2,1)S(1)}) custom-call(s32[1]{0:T(128)} %bitcast.place, bf16[2048,128]{1,0:T(8,128)(2,1)S(1)} %get-tuple-element.61.refs_0_, bf16[2048,128]{1,0:T(8,128)(2,1)S(1)} %collective-permute-done.20.refs_1_, ...), custom_call_target="tpu_custom_call" | custom-call | flops 2147483648 | bytes 16777216 | tf_op jit(solution)/shard_map/pallas_call | solution.py:158
  86.8 2.8 %collective-permute-done.14.refs_6_ = bf16[128,512]{1,0:T(8,128)(2,1)S(1)} collective-permute-done((bf16[128,512]{1,0:T(8,128)(2,1)S(1)}, bf16[128,512]{1,0:T(8,128)(2,1)S(1)}, u32[]{:S(2)}, u32[]{:S(2)}) %collective-permute-start.14) | collective-permute-done | bytes 131104 | tf_op jit(solution)/shard_map/ppermute | solution.py:256
  89.6 2.7 %collective-permute-start.23 = (bf16[128,512]{1,0:T(8,128)(2,1)S(1)}, bf16[128,512]{1,0:T(8,128)(2,1)S(1)}, u32[]{:S(2)}, u32[]{:S(2)}) collective-permute-start(bf16[128,512]{1,0:T(8,128)(2,1)S(1)} %get-tuple-element.66), channel_id=1, source_target_pairs={{0,12},{1,13},{2,14},{3,15},{4,8},{5,9},{6,10},{7,11},{8,4},{9,5},... | collective-permute-start | bytes 393224 | tf_op jit(solution)/shard_map/ppermute | solution.py:256
  92.5 1.3 %collective-permute-start.16 = (bf16[128,512]{1,0:T(8,128)(2,1)S(1)}, bf16[128,512]{1,0:T(8,128)(2,1)S(1)}, u32[]{:S(2)}, u32[]{:S(2)}) collective-permute-start(bf16[128,512]{1,0:T(8,128)(2,1)S(1)} %get-tuple-element.60), channel_id=1, source_target_pairs={{0,2},{1,3},{2,0},{3,1},{4,6},{5,7},{6,4},{7,5},{8,10},{9,11},{10,... | collective-permute-start | bytes 393224 | tf_op jit(solution)/shard_map/ppermute | solution.py:256
  93.8 6.7 %collective-permute-start.28 = (bf16[64,512]{1,0:T(8,128)(2,1)S(1)}, bf16[64,512]{1,0:T(8,128)(2,1)S(1)}, u32[]{:S(2)}, u32[]{:S(2)}) collective-permute-start(bf16[64,512]{1,0:T(8,128)(2,1)S(1)} %get-tuple-element.77), channel_id=1, source_target_pairs={{0,4},{1,5},{2,6},{3,7},{4,0},{5,1},{6,2},{7,3},{8,12},{9,13},{10,... | collective-permute-start | bytes 196616 | tf_op jit(solution)/shard_map/ppermute | solution.py:256
  101.4 1.6 %collective-permute-start.31 = (bf16[64,512]{1,0:T(8,128)(2,1)S(1)}, bf16[64,512]{1,0:T(8,128)(2,1)S(1)}, u32[]{:S(2)}, u32[]{:S(2)}) collective-permute-start(bf16[64,512]{1,0:T(8,128)(2,1)S(1)} %get-tuple-element.82), channel_id=1, source_target_pairs={{0,12},{1,13},{2,14},{3,15},{4,8},{5,9},{6,10},{7,11},{8,4},{9,5},... | collective-permute-start | bytes 196616 | tf_op jit(solution)/shard_map/ppermute | solution.py:256
  104.3 2.1 %collective-permute-done.30.refs_7_ = bf16[64,512]{1,0:T(8,128)(2,1)S(1)} collective-permute-done((bf16[64,512]{1,0:T(8,128)(2,1)S(1)}, bf16[64,512]{1,0:T(8,128)(2,1)S(1)}, u32[]{:S(2)}, u32[]{:S(2)}) %collective-permute-start.30) | collective-permute-done | bytes 65568 | tf_op jit(solution)/shard_map/ppermute | solution.py:256
  (52 shorter events, 13.4 us)
Async XLA Ops:
  0.0 20.3 %collective-permute-start.3 = (bf16[2,512,128]{2,1,0:T(8,128)(2,1)}, bf16[2,512,128]{2,1,0:T(8,128)(2,1)S(1)}, u32[]{:S(2)}, u32[]{:S(2)}) collective-permute-start(bf16[2,512,128]{2,1,0:T(8,128)(2,1)} %param.3), channel_id=1, source_target_pairs={{0,2},{1,3},{2,0},{3,1},{4,6},{5,7},{6,4},{7,5},{8,10},{9,11},{10,... | collective-permute-start | bytes 786440 | tf_op jit(solution)/shard_map/ppermute | solution.py:256
  4.0 10.4 %collective-permute-start = (bf16[512,128]{1,0:T(8,128)(2,1)S(1)}, bf16[512,128]{1,0:T(8,128)(2,1)S(1)}, u32[]{:S(2)}, u32[]{:S(2)}) collective-permute-start(bf16[512,128]{1,0:T(8,128)(2,1)S(1)} %get-tuple-element.84.refs_0_), channel_id=1, source_target_pairs={{0,4},{1,5},{2,6},{3,7},{4,0},{5,1},{6,2},{7,3},{8,12},{9,13},{10,... | collective-permute-start | bytes 393224 | tf_op jit(solution)/shard_map/ppermute | solution.py:256
  5.6 12.6 %collective-permute-start.1 = (bf16[512,128]{1,0:T(8,128)(2,1)S(1)}, bf16[512,128]{1,0:T(8,128)(2,1)S(1)}, u32[]{:S(2)}, u32[]{:S(2)}) collective-permute-start(bf16[512,128]{1,0:T(8,128)(2,1)S(1)} %get-tuple-element.84.refs_0_), channel_id=1, source_target_pairs={{0,8},{1,9},{2,10},{3,11},{4,12},{5,13},{6,14},{7,15},{8,0},{9,1},... | collective-permute-start | bytes 393224 | tf_op jit(solution)/shard_map/ppermute | solution.py:256
  8.2 10.6 %collective-permute-start.2 = (bf16[512,128]{1,0:T(8,128)(2,1)S(1)}, bf16[512,128]{1,0:T(8,128)(2,1)S(1)}, u32[]{:S(2)}, u32[]{:S(2)}) collective-permute-start(bf16[512,128]{1,0:T(8,128)(2,1)S(1)} %get-tuple-element.84.refs_0_), channel_id=1, source_target_pairs={{0,12},{1,13},{2,14},{3,15},{4,8},{5,9},{6,10},{7,11},{8,4},{9,5},... | collective-permute-start | bytes 393224 | tf_op jit(solution)/shard_map/ppermute | solution.py:256
  14.3 9.0 %collective-permute-start.4 = (bf16[512,128]{1,0:T(8,128)(2,1)S(1)}, bf16[512,128]{1,0:T(8,128)(2,1)S(1)}, u32[]{:S(2)}, u32[]{:S(2)}) collective-permute-start(bf16[512,128]{1,0:T(8,128)(2,1)S(1)} %collective-permute-done.refs_1_), channel_id=1, source_target_pairs={{0,2},{1,3},{2,0},{3,1},{4,6},{5,7},{6,4},{7,5},{8,10},{9,11},{10,... | collective-permute-start | bytes 393224 | tf_op jit(solution)/shard_map/ppermute | solution.py:256
  18.3 6.6 %collective-permute-start.5 = (bf16[512,128]{1,0:T(8,128)(2,1)S(1)}, bf16[512,128]{1,0:T(8,128)(2,1)S(1)}, u32[]{:S(2)}, u32[]{:S(2)}) collective-permute-start(bf16[512,128]{1,0:T(8,128)(2,1)S(1)} %collective-permute-done.1.refs_2_), channel_id=1, source_target_pairs={{0,2},{1,3},{2,0},{3,1},{4,6},{5,7},{6,4},{7,5},{8,10},{9,11},{10,... | collective-permute-start | bytes 393224 | tf_op jit(solution)/shard_map/ppermute | solution.py:256
  18.8 6.0 %collective-permute-start.6 = (bf16[512,128]{1,0:T(8,128)(2,1)S(1)}, bf16[512,128]{1,0:T(8,128)(2,1)S(1)}, u32[]{:S(2)}, u32[]{:S(2)}) collective-permute-start(bf16[512,128]{1,0:T(8,128)(2,1)S(1)} %collective-permute-done.2.refs_3_), channel_id=1, source_target_pairs={{0,2},{1,3},{2,0},{3,1},{4,6},{5,7},{6,4},{7,5},{8,10},{9,11},{10,... | collective-permute-start | bytes 393224 | tf_op jit(solution)/shard_map/ppermute | solution.py:256
  20.4 12.0 %collective-permute-start.17 = (bf16[512,256]{1,0:T(8,128)(2,1)S(1)}, bf16[512,256]{1,0:T(8,128)(2,1)S(1)}, u32[]{:S(2)}, u32[]{:S(2)}) collective-permute-start(bf16[512,256]{1,0:T(8,128)(2,1)S(1)} %pad_maximum_fusion.refs_0_), channel_id=1, source_target_pairs={{0,4},{1,5},{2,6},{3,7},{4,0},{5,1},{6,2},{7,3},{8,12},{9,13},{10,... | collective-permute-start | bytes 786440 | tf_op jit(solution)/shard_map/ppermute | solution.py:256
  20.9 21.3 %collective-permute-start.18 = (bf16[512,256]{1,0:T(8,128)(2,1)S(1)}, bf16[512,256]{1,0:T(8,128)(2,1)S(1)}, u32[]{:S(2)}, u32[]{:S(2)}) collective-permute-start(bf16[512,256]{1,0:T(8,128)(2,1)S(1)} %pad_maximum_fusion.refs_0_), channel_id=1, source_target_pairs={{0,8},{1,9},{2,10},{3,11},{4,12},{5,13},{6,14},{7,15},{8,0},{9,1},... | collective-permute-start | bytes 786440 | tf_op jit(solution)/shard_map/ppermute | solution.py:256
  23.4 18.9 %collective-permute-start.19 = (bf16[512,256]{1,0:T(8,128)(2,1)S(1)}, bf16[512,256]{1,0:T(8,128)(2,1)S(1)}, u32[]{:S(2)}, u32[]{:S(2)}) collective-permute-start(bf16[512,256]{1,0:T(8,128)(2,1)S(1)} %pad_maximum_fusion.refs_0_), channel_id=1, source_target_pairs={{0,12},{1,13},{2,14},{3,15},{4,8},{5,9},{6,10},{7,11},{8,4},{9,5},... | collective-permute-start | bytes 786440 | tf_op jit(solution)/shard_map/ppermute | solution.py:256
  25.7 23.7 %collective-permute-start.7 = (bf16[512,128]{1,0:T(8,128)(2,1)S(1)}, bf16[512,128]{1,0:T(8,128)(2,1)S(1)}, u32[]{:S(2)}, u32[]{:S(2)}) collective-permute-start(bf16[512,128]{1,0:T(8,128)(2,1)S(1)} %get-tuple-element.46), channel_id=1, source_target_pairs={{0,2},{1,3},{2,0},{3,1},{4,6},{5,7},{6,4},{7,5},{8,10},{9,11},{10,... | collective-permute-start | bytes 393224 | tf_op jit(solution)/shard_map/ppermute | solution.py:256
  28.3 22.7 %collective-permute-start.8 = (bf16[1536,128]{1,0:T(8,128)(2,1)S(1)}, bf16[1536,128]{1,0:T(8,128)(2,1)S(1)}, u32[]{:S(2)}, u32[]{:S(2)}) collective-permute-start(bf16[1536,128]{1,0:T(8,128)(2,1)S(1)} %get-tuple-element.47), channel_id=1, source_target_pairs={{0,2},{1,3},{2,0},{3,1},{4,6},{5,7},{6,4},{7,5},{8,10},{9,11},{10,... | collective-permute-start | bytes 1179656 | tf_op jit(solution)/shard_map/ppermute | solution.py:256
  32.4 24.6 %collective-permute-start.12 = (bf16[2048,128]{1,0:T(8,128)(2,1)S(1)}, bf16[2048,128]{1,0:T(8,128)(2,1)S(1)}, u32[]{:S(2)}, u32[]{:S(2)}) collective-permute-start(bf16[2048,128]{1,0:T(8,128)(2,1)S(1)} %get-tuple-element.53), channel_id=1, source_target_pairs={{0,2},{1,3},{2,0},{3,1},{4,6},{5,7},{6,4},{7,5},{8,10},{9,11},{10,... | collective-permute-start | bytes 1572872 | tf_op jit(solution)/shard_map/ppermute | solution.py:256
  44.6 39.0 %collective-permute-start.20 = (bf16[2048,128]{1,0:T(8,128)(2,1)S(1)}, bf16[2048,128]{1,0:T(8,128)(2,1)S(1)}, u32[]{:S(2)}, u32[]{:S(2)}) collective-permute-start(bf16[2048,128]{1,0:T(8,128)(2,1)S(1)} %get-tuple-element.62), channel_id=1, source_target_pairs={{0,2},{1,3},{2,0},{3,1},{4,6},{5,7},{6,4},{7,5},{8,10},{9,11},{10,... | collective-permute-start | bytes 1572872 | tf_op jit(solution)/shard_map/ppermute | solution.py:256
  47.0 29.9 %collective-permute-start.25 = (bf16[512,128]{1,0:T(8,128)(2,1)S(1)}, bf16[512,128]{1,0:T(8,128)(2,1)S(1)}, u32[]{:S(2)}, u32[]{:S(2)}) collective-permute-start(bf16[512,128]{1,0:T(8,128)(2,1)S(1)} %get-tuple-element.70), channel_id=1, source_target_pairs={{0,2},{1,3},{2,0},{3,1},{4,6},{5,7},{6,4},{7,5},{8,10},{9,11},{10,... | collective-permute-start | bytes 393224 | tf_op jit(solution)/shard_map/ppermute | solution.py:256
  49.4 22.3 %collective-permute-start.26 = (bf16[1536,128]{1,0:T(8,128)(2,1)S(1)}, bf16[1536,128]{1,0:T(8,128)(2,1)S(1)}, u32[]{:S(2)}, u32[]{:S(2)}) collective-permute-start(bf16[1536,128]{1,0:T(8,128)(2,1)S(1)} %get-tuple-element.72), channel_id=1, source_target_pairs={{0,2},{1,3},{2,0},{3,1},{4,6},{5,7},{6,4},{7,5},{8,10},{9,11},{10,... | collective-permute-start | bytes 1179656 | tf_op jit(solution)/shard_map/ppermute | solution.py:256
  53.5 24.3 %collective-permute-start.9 = (bf16[128,512]{1,0:T(8,128)(2,1)S(1)}, bf16[128,512]{1,0:T(8,128)(2,1)S(1)}, u32[]{:S(2)}, u32[]{:S(2)}) collective-permute-start(bf16[128,512]{1,0:T(8,128)(2,1)S(1)} %get-tuple-element.49), channel_id=1, source_target_pairs={{0,4},{1,5},{2,6},{3,7},{4,0},{5,1},{6,2},{7,3},{8,12},{9,13},{10,... | collective-permute-start | bytes 393224 | tf_op jit(solution)/shard_map/ppermute | solution.py:256
  56.9 22.0 %collective-permute-start.10 = (bf16[128,512]{1,0:T(8,128)(2,1)S(1)}, bf16[128,512]{1,0:T(8,128)(2,1)S(1)}, u32[]{:S(2)}, u32[]{:S(2)}) collective-permute-start(bf16[128,512]{1,0:T(8,128)(2,1)S(1)} %get-tuple-element.50), channel_id=1, source_target_pairs={{0,8},{1,9},{2,10},{3,11},{4,12},{5,13},{6,14},{7,15},{8,0},{9,1},... | collective-permute-start | bytes 393224 | tf_op jit(solution)/shard_map/ppermute | solution.py:256
  71.7 10.5 %collective-permute-start.11 = (bf16[128,512]{1,0:T(8,128)(2,1)S(1)}, bf16[128,512]{1,0:T(8,128)(2,1)S(1)}, u32[]{:S(2)}, u32[]{:S(2)}) collective-permute-start(bf16[128,512]{1,0:T(8,128)(2,1)S(1)} %get-tuple-element.51), channel_id=1, source_target_pairs={{0,12},{1,13},{2,14},{3,15},{4,8},{5,9},{6,10},{7,11},{8,4},{9,5},... | collective-permute-start | bytes 393224 | tf_op jit(solution)/shard_map/ppermute | solution.py:256
  76.9 9.9 %collective-permute-start.13 = (bf16[128,512]{1,0:T(8,128)(2,1)S(1)}, bf16[128,512]{1,0:T(8,128)(2,1)S(1)}, u32[]{:S(2)}, u32[]{:S(2)}) collective-permute-start(bf16[128,512]{1,0:T(8,128)(2,1)S(1)} %get-tuple-element.55), channel_id=1, source_target_pairs={{0,4},{1,5},{2,6},{3,7},{4,0},{5,1},{6,2},{7,3},{8,12},{9,13},{10,... | collective-permute-start | bytes 393224 | tf_op jit(solution)/shard_map/ppermute | solution.py:256
  77.8 11.9 %collective-permute-start.14 = (bf16[128,512]{1,0:T(8,128)(2,1)S(1)}, bf16[128,512]{1,0:T(8,128)(2,1)S(1)}, u32[]{:S(2)}, u32[]{:S(2)}) collective-permute-start(bf16[128,512]{1,0:T(8,128)(2,1)S(1)} %get-tuple-element.56), channel_id=1, source_target_pairs={{0,8},{1,9},{2,10},{3,11},{4,12},{5,13},{6,14},{7,15},{8,0},{9,1},... | collective-permute-start | bytes 393224 | tf_op jit(solution)/shard_map/ppermute | solution.py:256
  78.9 10.7 %collective-permute-start.15 = (bf16[128,512]{1,0:T(8,128)(2,1)S(1)}, bf16[128,512]{1,0:T(8,128)(2,1)S(1)}, u32[]{:S(2)}, u32[]{:S(2)}) collective-permute-start(bf16[128,512]{1,0:T(8,128)(2,1)S(1)} %get-tuple-element.57), channel_id=1, source_target_pairs={{0,12},{1,13},{2,14},{3,15},{4,8},{5,9},{6,10},{7,11},{8,4},{9,5},... | collective-permute-start | bytes 393224 | tf_op jit(solution)/shard_map/ppermute | solution.py:256
  82.2 10.2 %collective-permute-start.27 = (bf16[64,1024]{1,0:T(8,128)(2,1)S(1)}, bf16[64,1024]{1,0:T(8,128)(2,1)S(1)}, u32[]{:S(2)}, u32[]{:S(2)}) collective-permute-start(bf16[64,1024]{1,0:T(8,128)(2,1)S(1)} %get-tuple-element.73), channel_id=1, source_target_pairs={{0,2},{1,3},{2,0},{3,1},{4,6},{5,7},{6,4},{7,5},{8,10},{9,11},{10,... | collective-permute-start | bytes 393224 | tf_op jit(solution)/shard_map/ppermute | solution.py:256
  83.6 10.3 %collective-permute-start.29 = (bf16[64,1024]{1,0:T(8,128)(2,1)S(1)}, bf16[64,1024]{1,0:T(8,128)(2,1)S(1)}, u32[]{:S(2)}, u32[]{:S(2)}) collective-permute-start(bf16[64,1024]{1,0:T(8,128)(2,1)S(1)} %get-tuple-element.78), channel_id=1, source_target_pairs={{0,2},{1,3},{2,0},{3,1},{4,6},{5,7},{6,4},{7,5},{8,10},{9,11},{10,... | collective-permute-start | bytes 393224 | tf_op jit(solution)/shard_map/ppermute | solution.py:256
  86.7 13.9 %collective-permute-start.21 = (bf16[128,512]{1,0:T(8,128)(2,1)S(1)}, bf16[128,512]{1,0:T(8,128)(2,1)S(1)}, u32[]{:S(2)}, u32[]{:S(2)}) collective-permute-start(bf16[128,512]{1,0:T(8,128)(2,1)S(1)} %get-tuple-element.64), channel_id=1, source_target_pairs={{0,4},{1,5},{2,6},{3,7},{4,0},{5,1},{6,2},{7,3},{8,12},{9,13},{10,... | collective-permute-start | bytes 393224 | tf_op jit(solution)/shard_map/ppermute | solution.py:256
  89.6 11.8 %collective-permute-start.22 = (bf16[128,512]{1,0:T(8,128)(2,1)S(1)}, bf16[128,512]{1,0:T(8,128)(2,1)S(1)}, u32[]{:S(2)}, u32[]{:S(2)}) collective-permute-start(bf16[128,512]{1,0:T(8,128)(2,1)S(1)} %get-tuple-element.65), channel_id=1, source_target_pairs={{0,8},{1,9},{2,10},{3,11},{4,12},{5,13},{6,14},{7,15},{8,0},{9,1},... | collective-permute-start | bytes 393224 | tf_op jit(solution)/shard_map/ppermute | solution.py:256
  89.6 13.4 %collective-permute-start.23 = (bf16[128,512]{1,0:T(8,128)(2,1)S(1)}, bf16[128,512]{1,0:T(8,128)(2,1)S(1)}, u32[]{:S(2)}, u32[]{:S(2)}) collective-permute-start(bf16[128,512]{1,0:T(8,128)(2,1)S(1)} %get-tuple-element.66), channel_id=1, source_target_pairs={{0,12},{1,13},{2,14},{3,15},{4,8},{5,9},{6,10},{7,11},{8,4},{9,5},... | collective-permute-start | bytes 393224 | tf_op jit(solution)/shard_map/ppermute | solution.py:256
  92.5 11.8 %collective-permute-start.16 = (bf16[128,512]{1,0:T(8,128)(2,1)S(1)}, bf16[128,512]{1,0:T(8,128)(2,1)S(1)}, u32[]{:S(2)}, u32[]{:S(2)}) collective-permute-start(bf16[128,512]{1,0:T(8,128)(2,1)S(1)} %get-tuple-element.60), channel_id=1, source_target_pairs={{0,2},{1,3},{2,0},{3,1},{4,6},{5,7},{6,4},{7,5},{8,10},{9,11},{10,... | collective-permute-start | bytes 393224 | tf_op jit(solution)/shard_map/ppermute | solution.py:256
  93.8 10.4 %collective-permute-start.28 = (bf16[64,512]{1,0:T(8,128)(2,1)S(1)}, bf16[64,512]{1,0:T(8,128)(2,1)S(1)}, u32[]{:S(2)}, u32[]{:S(2)}) collective-permute-start(bf16[64,512]{1,0:T(8,128)(2,1)S(1)} %get-tuple-element.77), channel_id=1, source_target_pairs={{0,4},{1,5},{2,6},{3,7},{4,0},{5,1},{6,2},{7,3},{8,12},{9,13},{10,... | collective-permute-start | bytes 196616 | tf_op jit(solution)/shard_map/ppermute | solution.py:256
  100.6 5.8 %collective-permute-start.30 = (bf16[64,512]{1,0:T(8,128)(2,1)S(1)}, bf16[64,512]{1,0:T(8,128)(2,1)S(1)}, u32[]{:S(2)}, u32[]{:S(2)}) collective-permute-start(bf16[64,512]{1,0:T(8,128)(2,1)S(1)} %get-tuple-element.81), channel_id=1, source_target_pairs={{0,8},{1,9},{2,10},{3,11},{4,12},{5,13},{6,14},{7,15},{8,0},{9,1},... | collective-permute-start | bytes 196616 | tf_op jit(solution)/shard_map/ppermute | solution.py:256
  101.4 6.2 %collective-permute-start.31 = (bf16[64,512]{1,0:T(8,128)(2,1)S(1)}, bf16[64,512]{1,0:T(8,128)(2,1)S(1)}, u32[]{:S(2)}, u32[]{:S(2)}) collective-permute-start(bf16[64,512]{1,0:T(8,128)(2,1)S(1)} %get-tuple-element.82), channel_id=1, source_target_pairs={{0,12},{1,13},{2,14},{3,15},{4,8},{5,9},{6,10},{7,11},{8,4},{9,5},... | collective-permute-start | bytes 196616 | tf_op jit(solution)/shard_map/ppermute | solution.py:256
  103.1 4.5 %collective-permute-start.24 = (bf16[64,512]{1,0:T(8,128)(2,1)S(1)}, bf16[64,512]{1,0:T(8,128)(2,1)S(1)}, u32[]{:S(2)}, u32[]{:S(2)}) collective-permute-start(bf16[64,512]{1,0:T(8,128)(2,1)S(1)} %get-tuple-element.68), channel_id=1, source_target_pairs={{0,2},{1,3},{2,0},{3,1},{4,6},{5,7},{6,4},{7,5},{8,10},{9,11},{10,... | collective-permute-start | bytes 196616 | tf_op jit(solution)/shard_map/ppermute | solution.py:256
where the time goes:
time: 109 us
  starting transfers between devices  49.7 us (46%)
  waiting for transfers between devices  29.8 us (27%)
  Pallas kernels  27.8 us (26%)
    ppermute x32, starting transfers between devices, moved(): return lax.ppermute(value, AXES, pairs)  49.7 us
    ppermute x32, waiting for transfers between devices, moved(): return lax.ppermute(value, AXES, pairs)  29.8 us
    pallas_call x6, Pallas kernels, amplitudes_of(): pl.pallas_call(functools.partial(amplitude_body, shards, *vectors, half),...  10.4 us
    pallas_call x5, Pallas kernels, gradients_of(): pl.pallas_call(functools.partial(gradient_body, shards, len(owns), first,...  10.3 us
    pallas_call x1, Pallas kernels, loaded(): pl.pallas_call(functools.partial(load_body, first), in_specs=[SMEM, pl.Bl...  5.89 us
  transfers between devices with their start and end apart: 32, of which 6 were waited for; matrix products, arithmetic and copies ran while one was open for 1% of the time, Pallas kernels for 25%

commit v1 on v0

--- a/solution.py
+++ b/solution.py
@@ -47,37 +47,37 @@
     return moved % shards if isinstance(moved, int) else lax.rem(moved, shards)
 
 
-def hops_of(shards):
-    return sorted(range(1, shards), key=lambda hop: (hop != shards // 2, -hop))
-
-
 def groups_of(shards):
-    hops = hops_of(shards) + [0]
+    hops = list(range(shards - 1, -1, -1))
     return [hops[: shards // 2], hops[shards // 2 :]]
 
 
-def load_body(first, place, source, out, arrived):
+def load_body(half, place, source, out, arrived):
     del place
-    rows = out.shape[0] // STREAMS
-    copies = [pltpu.make_async_copy(source.at[pl.ds(first + at * rows, rows)], out.at[pl.ds(at * rows, rows)], arrived.at[at]) for at in range(STREAMS)]
+    vectors, part = out.shape[0] // STREAMS, out.shape[1]
+    copies = []
+    for at in range(STREAMS):
+        some = pl.ds(at * vectors, vectors)
+        copies.append(pltpu.make_async_copy(source.at[some, pl.ds(half * part, part)], out.at[some], arrived.at[at]))
     for copy in copies:
         copy.start()
     for copy in copies:
         copy.wait()
 
 
-def loaded(place, factors, first, count):
+def loaded(place, factors, half):
+    vectors, width, orbitals = factors.shape
     return pl.pallas_call(
-        functools.partial(load_body, first),
+        functools.partial(load_body, half),
         in_specs=[SMEM, pl.BlockSpec(memory_space=pltpu.HBM)],
         out_specs=VMEM,
-        out_shape=pltpu.VMEM((count, factors.shape[1]), factors.dtype),
+        out_shape=pltpu.VMEM((vectors, width // HALVES, orbitals), factors.dtype),
         scratch_shapes=[pltpu.SemaphoreType.DMA((STREAMS,))],
         compiler_params=LARGE,
     )(place, factors)
 
 
-def amplitude_body(shards, low, high, half, place, factors, *refs):
+def amplitude_body(shards, low, high, place, factors, *refs):
     pieces, own, far, rows = refs[:-3], refs[-3], refs[-2], refs[-1]
     owned, width = pieces[0].shape[0], own.shape[1]
     for step in range(shards):
@@ -87,21 +87,20 @@
         else:
             rows[pl.ds(at, owned), :width] = pieces[step][...]
             rows[pl.ds(at, owned), width:] = pieces[shards + step][...]
-    part = width // HALVES
+    part = factors.shape[1]
     for first in range(low, high, BLOCK):
-        vectors = range(first, min(first + BLOCK, high))
-        taken = jnp.concatenate([factors[g * width + half * part : g * width + (half + 1) * part, :] for g in vectors], axis=0)
+        taken = jnp.concatenate([factors[g] for g in range(first, min(first + BLOCK, high))], axis=0)
         sums = jnp.dot(taken, rows[...], preferred_element_type=jnp.float32).astype(jnp.bfloat16)
         at = (first - low) * part
         own[at : at + sums.shape[0], :] = sums[:, :width]
         far[at : at + sums.shape[0], :] = sums[:, width:]
 
 
-def amplitudes_of(place, factors, pieces, vectors, half, width, shards):
-    orbitals = factors.shape[1]
-    count = (vectors[1] - vectors[0]) * width // HALVES
+def amplitudes_of(place, factors, pieces, vectors, width, shards):
+    orbitals = factors.shape[2]
+    count = (vectors[1] - vectors[0]) * factors.shape[1]
     return pl.pallas_call(
-        functools.partial(amplitude_body, shards, *vectors, half),
+        functools.partial(amplitude_body, shards, *vectors),
         in_specs=[SMEM] + [VMEM] * (1 + len(pieces)),
         out_specs=[VMEM] * 2,
         scratch_shapes=[pltpu.VMEM((orbitals, 2 * width), jnp.bfloat16)],
@@ -112,18 +111,19 @@
 
 
 def gradient_body(shards, parts, first, carried, groups, place, *refs):
-    owns, fars, factors = refs[:parts], refs[parts : 2 * parts], refs[2 * parts]
-    outs, sums = refs[2 * parts + 1 + carried : -1], refs[-1]
+    owns, fars, factors = refs[:parts], refs[parts : 2 * parts], refs[2 * parts : 2 * parts + HALVES]
+    outs, sums = refs[2 * parts + HALVES + carried : -1], refs[-1]
     width = owns[0].shape[1]
     part = width // HALVES
     slots = [(at, g) for at, own in enumerate(owns) for g in range(own.shape[0] // part)]
     for seen in range(0, len(slots), BLOCK):
         vectors = slots[seen : seen + BLOCK]
         wide = [jnp.concatenate([side[at][g * part : (g + 1) * part, :] for at, g in vectors], axis=1) for side in (owns, fars)]
-        low = (first + seen) * width
-        grown = jnp.dot(jnp.concatenate(wide, axis=0), factors[low : low + len(vectors) * width, :], preferred_element_type=jnp.float32)
+        low = first + seen
+        rows = jnp.concatenate([loaded[g] for g in range(low, low + len(vectors)) for loaded in factors], axis=0)
+        grown = jnp.dot(jnp.concatenate(wide, axis=0), rows, preferred_element_type=jnp.float32)
         if seen == 0 and carried:
-            sums[...] = refs[2 * parts + 1][...] + grown
+            sums[...] = refs[2 * parts + HALVES][...] + grown
         elif seen == 0:
             sums[...] = grown
         else:
@@ -145,7 +145,7 @@
 
 
 def gradients_of(place, factors, owns, fars, shards, first=0, groups=None, carried=None, more=False):
-    orbitals, width = factors.shape[1], owns[0].shape[1]
+    orbitals, width = factors[0].shape[2], owns[0].shape[1]
     part, owned = width // HALVES, orbitals // shards
     outs = [jax.ShapeDtypeStruct((2 * part, owned), jnp.bfloat16 if hop else jnp.float32) for hop in range(shards)]
     if more:
@@ -154,7 +154,7 @@
         outs = [jax.ShapeDtypeStruct((part, owned), jnp.float32)] * shards
         outs += [jax.ShapeDtypeStruct((part, owned * len(hops)), jnp.bfloat16) for hops in groups]
     count = sum(own.shape[0] for own in owns) * HALVES
-    values = [place, *owns, *fars, factors] + ([] if carried is None else [carried])
+    values = [place, *owns, *fars, *factors] + ([] if carried is None else [carried])
     return pl.pallas_call(
         functools.partial(gradient_body, shards, len(owns), first, 0 if carried is None else 1, groups),
         in_specs=[SMEM] + [VMEM] * (len(values) - 1),
@@ -235,12 +235,13 @@
 
 def in_order(shape, chol_half, theta):
     shards = shape["vec"]
-    vectors, width, orbitals = chol_half.shape
+    vectors, width, _ = chol_half.shape
     walkers = theta.shape[0]
     position = lax.axis_index("vec")
     place = position.reshape(1)
-    whole = chol_half.reshape(vectors * width, orbitals)
-    factors = loaded(place, whole, 0, vectors * width)
+    factors = []
+    for half in range(HALVES):
+        factors.append(loaded(place, chol_half, half))
 
     def flat(grp, vec, occ, wlk):
         return ((grp * shape["vec"] + vec) * shape["occ"] + occ) * shape["wlk"] + wlk
@@ -269,7 +270,7 @@
         owns, fars = [], []
         cuts = parts_of(stage, stages, vectors)
         for part in zip(cuts[:-1], cuts[1:]):
-            own, far = amplitudes_of(place, factors, blocks[stage // HALVES], part, stage % HALVES, width, shards)
+            own, far = amplitudes_of(place, factors[stage % HALVES], blocks[stage // HALVES], part, width, shards)
             owns.append(own)
             fars.append(moved(far, 0, True))
         sides.append((owns, fars))

time: 109 us -> 110 us (level)
    pallas_call x7 -> x8, Pallas kernels: 16.3 us -> 17.5 us  [the longest x6 10.5 us: amplitudes_of(): pl.pallas_call(functools.partial(amplitude_body, shards, *vectors), in_sp...]
  transfers between devices with their start and end apart: 32 -> 32, of which waited for: 6 -> 7; matrix products, arithmetic and copies ran while one was open for 1% -> 1% of each run, Pallas kernels for 25% -> 25%
where the time goes in v1:
time: 110 us
  starting transfers between devices  50.6 us (46%)
  waiting for transfers between devices  28.9 us (26%)
  Pallas kernels  28.7 us (26%)
    ppermute x32, starting transfers between devices, moved(): return lax.ppermute(value, AXES, pairs)  50.6 us
    ppermute x32, waiting for transfers between devices, moved(): return lax.ppermute(value, AXES, pairs)  28.9 us
    pallas_call x6, Pallas kernels, amplitudes_of(): pl.pallas_call(functools.partial(amplitude_body, shards, *vectors), in_sp...  10.5 us
    pallas_call x5, Pallas kernels, gradients_of(): pl.pallas_call(functools.partial(gradient_body, shards, len(owns), first,...  9.97 us
    pallas_call x2, Pallas kernels, loaded(): pl.pallas_call(functools.partial(load_body, half), in_specs=[SMEM, pl.Blo...  7.01 us
  transfers between devices with their start and end apart: 32, of which 7 were waited for; matrix products, arithmetic and copies ran while one was open for 1% of the time, Pallas kernels for 25%

profile of v1, /device:TPU:0, one launch (start us, length us, event | category | flops | bytes accessed | tf_op | source)
XLA Modules:
  0.0 109.5 jit_solution(8879763077345867741)
XLA Ops:
  0.0 3.0 %collective-permute-start.3 = (bf16[2,512,128]{2,1,0:T(8,128)(2,1)}, bf16[2,512,128]{2,1,0:T(8,128)(2,1)S(1)}, u32[]{:S(2)}, u32[]{:S(2)}) collective-permute-start(bf16[2,512,128]{2,1,0:T(8,128)(2,1)} %param.3), channel_id=1, source_target_pairs={{0,2},{1,3},{2,0},{3,1},{4,6},{5,7},{6,4},{7,5},{8,10},{9,11},{10,... | collective-permute-start | bytes 786440 | tf_op jit(solution)/shard_map/ppermute | solution.py:257
  4.0 1.6 %collective-permute-start = (bf16[512,128]{1,0:T(8,128)(2,1)S(1)}, bf16[512,128]{1,0:T(8,128)(2,1)S(1)}, u32[]{:S(2)}, u32[]{:S(2)}) collective-permute-start(bf16[512,128]{1,0:T(8,128)(2,1)S(1)} %get-tuple-element.84.refs_0_), channel_id=1, source_target_pairs={{0,4},{1,5},{2,6},{3,7},{4,0},{5,1},{6,2},{7,3},{8,12},{9,13},{10,... | collective-permute-start | bytes 393224 | tf_op jit(solution)/shard_map/ppermute | solution.py:257
  5.6 2.6 %collective-permute-start.1 = (bf16[512,128]{1,0:T(8,128)(2,1)S(1)}, bf16[512,128]{1,0:T(8,128)(2,1)S(1)}, u32[]{:S(2)}, u32[]{:S(2)}) collective-permute-start(bf16[512,128]{1,0:T(8,128)(2,1)S(1)} %get-tuple-element.84.refs_0_), channel_id=1, source_target_pairs={{0,8},{1,9},{2,10},{3,11},{4,12},{5,13},{6,14},{7,15},{8,0},{9,1},... | collective-permute-start | bytes 393224 | tf_op jit(solution)/shard_map/ppermute | solution.py:257
  8.4 3.5 %shard_map.28.factors.refs_4_.refs_2_ = bf16[32,64,2048]{2,1,0:T(8,128)(2,1)S(1)} custom-call(s32[1]{0:T(128)} %bitcast.place, bf16[32,128,2048]{2,1,0:T(8,128)(2,1)} %source.3), custom_call_target="tpu_custom_call" | custom-call | tf_op jit(solution)/shard_map/pallas_call | solution.py:70
  11.9 3.5 %shard_map.31.refs_5_.factors.refs_3_ = bf16[32,64,2048]{2,1,0:T(8,128)(2,1)S(1)} custom-call(s32[1]{0:T(128)} %bitcast.place, bf16[32,128,2048]{2,1,0:T(8,128)(2,1)} %source.3), custom_call_target="tpu_custom_call" | custom-call | tf_op jit(solution)/shard_map/pallas_call | solution.py:70
  15.8 2.4 %collective-permute-done.1.refs_2_ = bf16[512,128]{1,0:T(8,128)(2,1)S(1)} collective-permute-done((bf16[512,128]{1,0:T(8,128)(2,1)S(1)}, bf16[512,128]{1,0:T(8,128)(2,1)S(1)}, u32[]{:S(2)}, u32[]{:S(2)}) %collective-permute-start.1) | collective-permute-done | bytes 131104 | tf_op jit(solution)/shard_map/ppermute | solution.py:257
  18.8 1.5 %collective-permute-start.6 = (bf16[512,128]{1,0:T(8,128)(2,1)S(1)}, bf16[512,128]{1,0:T(8,128)(2,1)S(1)}, u32[]{:S(2)}, u32[]{:S(2)}) collective-permute-start(bf16[512,128]{1,0:T(8,128)(2,1)S(1)} %collective-permute-done.2.refs_3_), channel_id=1, source_target_pairs={{0,2},{1,3},{2,0},{3,1},{4,6},{5,7},{6,4},{7,5},{8,10},{9,11},{10,... | collective-permute-start | bytes 393224 | tf_op jit(solution)/shard_map/ppermute | solution.py:257
  20.9 2.5 %collective-permute-start.18 = (bf16[512,256]{1,0:T(8,128)(2,1)S(1)}, bf16[512,256]{1,0:T(8,128)(2,1)S(1)}, u32[]{:S(2)}, u32[]{:S(2)}) collective-permute-start(bf16[512,256]{1,0:T(8,128)(2,1)S(1)} %pad_maximum_fusion.refs_0_), channel_id=1, source_target_pairs={{0,8},{1,9},{2,10},{3,11},{4,12},{5,13},{6,14},{7,15},{8,0},{9,1},... | collective-permute-start | bytes 786440 | tf_op jit(solution)/shard_map/ppermute | solution.py:257
  23.4 2.1 %collective-permute-start.19 = (bf16[512,256]{1,0:T(8,128)(2,1)S(1)}, bf16[512,256]{1,0:T(8,128)(2,1)S(1)}, u32[]{:S(2)}, u32[]{:S(2)}) collective-permute-start(bf16[512,256]{1,0:T(8,128)(2,1)S(1)} %pad_maximum_fusion.refs_0_), channel_id=1, source_target_pairs={{0,12},{1,13},{2,14},{3,15},{4,8},{5,9},{6,10},{7,11},{8,4},{9,5},... | collective-permute-start | bytes 786440 | tf_op jit(solution)/shard_map/ppermute | solution.py:257
  27.0 2.0 %shard_map.30 = (bf16[1536,128]{1,0:T(8,128)(2,1)S(1)}, bf16[1536,128]{1,0:T(8,128)(2,1)S(1)}) custom-call(s32[1]{0:T(128)} %bitcast.place, bf16[32,64,2048]{2,1,0:T(8,128)(2,1)S(1)} %shard_map.28.factors.refs_4_.refs_2_, bf16[512,128]{1,0:T(8,128)(2,1)S(1)} %get-tuple-element.84.refs_0_, bf16[512,128]{1,0:T(8,128)(2,1)S(1)} %collective-permute-done.refs_1_, ...), custom_call_target="tpu_custom_call" | custom-call | flops 1610612736 | bytes 6291456 | tf_op jit(solution)/shard_map/pallas_call | solution.py:102
  29.0 1.6 %collective-permute-start.8 = (bf16[1536,128]{1,0:T(8,128)(2,1)S(1)}, bf16[1536,128]{1,0:T(8,128)(2,1)S(1)}, u32[]{:S(2)}, u32[]{:S(2)}) collective-permute-start(bf16[1536,128]{1,0:T(8,128)(2,1)S(1)} %get-tuple-element.47), channel_id=1, source_target_pairs={{0,2},{1,3},{2,0},{3,1},{4,6},{5,7},{6,4},{7,5},{8,10},{9,11},{10,... | collective-permute-start | bytes 1179656 | tf_op jit(solution)/shard_map/ppermute | solution.py:257
  30.6 2.5 %shard_map.33 = (bf16[2048,128]{1,0:T(8,128)(2,1)S(1)}, bf16[2048,128]{1,0:T(8,128)(2,1)S(1)}) custom-call(s32[1]{0:T(128)} %bitcast.place, bf16[32,64,2048]{2,1,0:T(8,128)(2,1)S(1)} %shard_map.31.refs_5_.factors.refs_3_, bf16[512,128]{1,0:T(8,128)(2,1)S(1)} %get-tuple-element.84.refs_0_, bf16[512,128]{1,0:T(8,128)(2,1)S(1)} %collective-permute-done.refs_1_, ...), custom_call_target="tpu_custom_call" | custom-call | flops 2147483648 | bytes 8388608 | tf_op jit(solution)/shard_map/pallas_call | solution.py:102
  33.7 8.2 %collective-permute-done.18.refs_2_ = bf16[512,256]{1,0:T(8,128)(2,1)S(1)} collective-permute-done((bf16[512,256]{1,0:T(8,128)(2,1)S(1)}, bf16[512,256]{1,0:T(8,128)(2,1)S(1)}, u32[]{:S(2)}, u32[]{:S(2)}) %collective-permute-start.18) | collective-permute-done | bytes 262176 | tf_op jit(solution)/shard_map/ppermute | solution.py:257
  41.9 2.4 %shard_map.36 = (bf16[2048,128]{1,0:T(8,128)(2,1)S(1)}, bf16[2048,128]{1,0:T(8,128)(2,1)S(1)}) custom-call(s32[1]{0:T(128)} %bitcast.place, bf16[32,64,2048]{2,1,0:T(8,128)(2,1)S(1)} %shard_map.28.factors.refs_4_.refs_2_, bf16[512,256]{1,0:T(8,128)(2,1)S(1)} %pad_maximum_fusion.refs_0_, bf16[512,256]{1,0:T(8,128)(2,1)S(1)} %collective-permute-done.17.refs_1_, ...), custom_call_target="tpu_custom_call" | custom-call | flops 2147483648 | bytes 8388608 | tf_op jit(solution)/shard_map/pallas_call | solution.py:102
  44.4 1.6 %collective-permute-start.20 = (bf16[2048,128]{1,0:T(8,128)(2,1)S(1)}, bf16[2048,128]{1,0:T(8,128)(2,1)S(1)}, u32[]{:S(2)}, u32[]{:S(2)}) collective-permute-start(bf16[2048,128]{1,0:T(8,128)(2,1)S(1)} %get-tuple-element.62), channel_id=1, source_target_pairs={{0,2},{1,3},{2,0},{3,1},{4,6},{5,7},{6,4},{7,5},{8,10},{9,11},{10,... | collective-permute-start | bytes 1572872 | tf_op jit(solution)/shard_map/ppermute | solution.py:257
  47.3 1.9 %shard_map.40 = (bf16[1536,128]{1,0:T(8,128)(2,1)S(1)}, bf16[1536,128]{1,0:T(8,128)(2,1)S(1)}) custom-call(s32[1]{0:T(128)} %bitcast.place, bf16[32,64,2048]{2,1,0:T(8,128)(2,1)S(1)} %shard_map.31.refs_5_.factors.refs_3_, bf16[512,256]{1,0:T(8,128)(2,1)S(1)} %pad_maximum_fusion.refs_0_, bf16[512,256]{1,0:T(8,128)(2,1)S(1)} %collective-permute-done.17.refs_1_, ...), custom_call_target="tpu_custom_call" | custom-call | flops 1610612736 | bytes 6291456 | tf_op jit(solution)/shard_map/pallas_call | solution.py:102
  49.2 1.6 %collective-permute-start.26 = (bf16[1536,128]{1,0:T(8,128)(2,1)S(1)}, bf16[1536,128]{1,0:T(8,128)(2,1)S(1)}, u32[]{:S(2)}, u32[]{:S(2)}) collective-permute-start(bf16[1536,128]{1,0:T(8,128)(2,1)S(1)} %get-tuple-element.72), channel_id=1, source_target_pairs={{0,2},{1,3},{2,0},{3,1},{4,6},{5,7},{6,4},{7,5},{8,10},{9,11},{10,... | collective-permute-start | bytes 1179656 | tf_op jit(solution)/shard_map/ppermute | solution.py:257
  50.7 2.4 %shard_map.32 = (f32[128,512]{1,0:T(8,128)S(1)}, bf16[128,512]{1,0:T(8,128)(2,1)S(1)}, bf16[128,512]{1,0:T(8,128)(2,1)S(1)}, bf16[128,512]{1,0:T(8,128)(2,1)S(1)}) custom-call(s32[1]{0:T(128)} %bitcast.place, bf16[512,128]{1,0:T(8,128)(2,1)S(1)} %get-tuple-element.44.refs_0_, bf16[1536,128]{1,0:T(8,128)(2,1)S(1)} %get-tuple-element.45.refs_1_, ...), custom_call_target="tpu_custom_call" | custom-call | flops 2147483648 | bytes 16777216 | tf_op jit(solution)/shard_map/pallas_call | solution.py:158
  53.1 3.4 %collective-permute-start.9 = (bf16[128,512]{1,0:T(8,128)(2,1)S(1)}, bf16[128,512]{1,0:T(8,128)(2,1)S(1)}, u32[]{:S(2)}, u32[]{:S(2)}) collective-permute-start(bf16[128,512]{1,0:T(8,128)(2,1)S(1)} %get-tuple-element.49), channel_id=1, source_target_pairs={{0,4},{1,5},{2,6},{3,7},{4,0},{5,1},{6,2},{7,3},{8,12},{9,13},{10,... | collective-permute-start | bytes 393224 | tf_op jit(solution)/shard_map/ppermute | solution.py:257
  56.6 1.5 %collective-permute-start.10 = (bf16[128,512]{1,0:T(8,128)(2,1)S(1)}, bf16[128,512]{1,0:T(8,128)(2,1)S(1)}, u32[]{:S(2)}, u32[]{:S(2)}) collective-permute-start(bf16[128,512]{1,0:T(8,128)(2,1)S(1)} %get-tuple-element.50), channel_id=1, source_target_pairs={{0,8},{1,9},{2,10},{3,11},{4,12},{5,13},{6,14},{7,15},{8,0},{9,1},... | collective-permute-start | bytes 393224 | tf_op jit(solution)/shard_map/ppermute | solution.py:257
  58.1 2.6 %shard_map.34 = (f32[128,512]{1,0:T(8,128)S(1)}, bf16[128,512]{1,0:T(8,128)(2,1)S(1)}, bf16[128,512]{1,0:T(8,128)(2,1)S(1)}, bf16[128,512]{1,0:T(8,128)(2,1)S(1)}) custom-call(s32[1]{0:T(128)} %bitcast.place, bf16[2048,128]{1,0:T(8,128)(2,1)S(1)} %get-tuple-element.52.refs_0_, bf16[2048,128]{1,0:T(8,128)(2,1)S(1)} %collective-permute-done.12.refs_1_, ...), custom_call_target="tpu_custom_call" | custom-call | flops 2147483648 | bytes 16777216 | tf_op jit(solution)/shard_map/pallas_call | solution.py:158
  60.7 12.0 %collective-permute-done.26.refs_1_ = bf16[1536,128]{1,0:T(8,128)(2,1)S(1)} collective-permute-done((bf16[1536,128]{1,0:T(8,128)(2,1)S(1)}, bf16[1536,128]{1,0:T(8,128)(2,1)S(1)}, u32[]{:S(2)}, u32[]{:S(2)}) %collective-permute-start.26) | collective-permute-done | bytes 393248 | tf_op jit(solution)/shard_map/ppermute | solution.py:257
  72.7 3.4 %collective-permute-start.11 = (bf16[128,512]{1,0:T(8,128)(2,1)S(1)}, bf16[128,512]{1,0:T(8,128)(2,1)S(1)}, u32[]{:S(2)}, u32[]{:S(2)}) collective-permute-start(bf16[128,512]{1,0:T(8,128)(2,1)S(1)} %get-tuple-element.51), channel_id=1, source_target_pairs={{0,12},{1,13},{2,14},{3,15},{4,8},{5,9},{6,10},{7,11},{8,4},{9,5},... | collective-permute-start | bytes 393224 | tf_op jit(solution)/shard_map/ppermute | solution.py:257
  76.1 1.8 %shard_map.41.refs_4_ = f32[128,2048]{1,0:T(8,128)S(1)} custom-call(s32[1]{0:T(128)} %bitcast.place, bf16[1536,128]{1,0:T(8,128)(2,1)S(1)} %get-tuple-element.71.refs_0_, bf16[1536,128]{1,0:T(8,128)(2,1)S(1)} %collective-permute-done.26.refs_1_, bf16[32,64,2048]{2,1,0:T(8,128)(2,1)S(1)} %shard_map.28.factors.refs_4_.refs_2_, ...), custom_call_target="tpu_custom_call" | custom-call | flops 1610612736 | bytes 12582912 | tf_op jit(solution)/shard_map/pallas_call | solution.py:158
  79.9 3.4 %collective-permute-start.15 = (bf16[128,512]{1,0:T(8,128)(2,1)S(1)}, bf16[128,512]{1,0:T(8,128)(2,1)S(1)}, u32[]{:S(2)}, u32[]{:S(2)}) collective-permute-start(bf16[128,512]{1,0:T(8,128)(2,1)S(1)} %get-tuple-element.57), channel_id=1, source_target_pairs={{0,12},{1,13},{2,14},{3,15},{4,8},{5,9},{6,10},{7,11},{8,4},{9,5},... | collective-permute-start | bytes 393224 | tf_op jit(solution)/shard_map/ppermute | solution.py:257
  85.3 2.4 %shard_map.37 = (f32[128,512]{1,0:T(8,128)S(1)}, bf16[128,512]{1,0:T(8,128)(2,1)S(1)}, bf16[128,512]{1,0:T(8,128)(2,1)S(1)}, bf16[128,512]{1,0:T(8,128)(2,1)S(1)}) custom-call(s32[1]{0:T(128)} %bitcast.place, bf16[2048,128]{1,0:T(8,128)(2,1)S(1)} %get-tuple-element.61.refs_0_, bf16[2048,128]{1,0:T(8,128)(2,1)S(1)} %collective-permute-done.20.refs_1_, ...), custom_call_target="tpu_custom_call" | custom-call | flops 2147483648 | bytes 16777216 | tf_op jit(solution)/shard_map/pallas_call | solution.py:158
  87.8 2.5 %collective-permute-done.14.refs_6_ = bf16[128,512]{1,0:T(8,128)(2,1)S(1)} collective-permute-done((bf16[128,512]{1,0:T(8,128)(2,1)S(1)}, bf16[128,512]{1,0:T(8,128)(2,1)S(1)}, u32[]{:S(2)}, u32[]{:S(2)}) %collective-permute-start.14) | collective-permute-done | bytes 131104 | tf_op jit(solution)/shard_map/ppermute | solution.py:257
  90.3 2.9 %collective-permute-start.23 = (bf16[128,512]{1,0:T(8,128)(2,1)S(1)}, bf16[128,512]{1,0:T(8,128)(2,1)S(1)}, u32[]{:S(2)}, u32[]{:S(2)}) collective-permute-start(bf16[128,512]{1,0:T(8,128)(2,1)S(1)} %get-tuple-element.66), channel_id=1, source_target_pairs={{0,12},{1,13},{2,14},{3,15},{4,8},{5,9},{6,10},{7,11},{8,4},{9,5},... | collective-permute-start | bytes 393224 | tf_op jit(solution)/shard_map/ppermute | solution.py:257
  93.4 1.5 %collective-permute-start.16 = (bf16[128,512]{1,0:T(8,128)(2,1)S(1)}, bf16[128,512]{1,0:T(8,128)(2,1)S(1)}, u32[]{:S(2)}, u32[]{:S(2)}) collective-permute-start(bf16[128,512]{1,0:T(8,128)(2,1)S(1)} %get-tuple-element.60), channel_id=1, source_target_pairs={{0,2},{1,3},{2,0},{3,1},{4,6},{5,7},{6,4},{7,5},{8,10},{9,11},{10,... | collective-permute-start | bytes 393224 | tf_op jit(solution)/shard_map/ppermute | solution.py:257
  94.9 6.7 %collective-permute-start.28 = (bf16[64,512]{1,0:T(8,128)(2,1)S(1)}, bf16[64,512]{1,0:T(8,128)(2,1)S(1)}, u32[]{:S(2)}, u32[]{:S(2)}) collective-permute-start(bf16[64,512]{1,0:T(8,128)(2,1)S(1)} %get-tuple-element.77), channel_id=1, source_target_pairs={{0,4},{1,5},{2,6},{3,7},{4,0},{5,1},{6,2},{7,3},{8,12},{9,13},{10,... | collective-permute-start | bytes 196616 | tf_op jit(solution)/shard_map/ppermute | solution.py:257
  102.2 1.8 %collective-permute-start.31 = (bf16[64,512]{1,0:T(8,128)(2,1)S(1)}, bf16[64,512]{1,0:T(8,128)(2,1)S(1)}, u32[]{:S(2)}, u32[]{:S(2)}) collective-permute-start(bf16[64,512]{1,0:T(8,128)(2,1)S(1)} %get-tuple-element.82), channel_id=1, source_target_pairs={{0,12},{1,13},{2,14},{3,15},{4,8},{5,9},{6,10},{7,11},{8,4},{9,5},... | collective-permute-start | bytes 196616 | tf_op jit(solution)/shard_map/ppermute | solution.py:257
  104.9 2.3 %collective-permute-done.30.refs_7_ = bf16[64,512]{1,0:T(8,128)(2,1)S(1)} collective-permute-done((bf16[64,512]{1,0:T(8,128)(2,1)S(1)}, bf16[64,512]{1,0:T(8,128)(2,1)S(1)}, u32[]{:S(2)}, u32[]{:S(2)}) %collective-permute-start.30) | collective-permute-done | bytes 65568 | tf_op jit(solution)/shard_map/ppermute | solution.py:257
  (53 shorter events, 14.1 us)
Async XLA Ops:
  0.0 20.3 %collective-permute-start.3 = (bf16[2,512,128]{2,1,0:T(8,128)(2,1)}, bf16[2,512,128]{2,1,0:T(8,128)(2,1)S(1)}, u32[]{:S(2)}, u32[]{:S(2)}) collective-permute-start(bf16[2,512,128]{2,1,0:T(8,128)(2,1)} %param.3), channel_id=1, source_target_pairs={{0,2},{1,3},{2,0},{3,1},{4,6},{5,7},{6,4},{7,5},{8,10},{9,11},{10,... | collective-permute-start | bytes 786440 | tf_op jit(solution)/shard_map/ppermute | solution.py:257
  4.0 11.5 %collective-permute-start = (bf16[512,128]{1,0:T(8,128)(2,1)S(1)}, bf16[512,128]{1,0:T(8,128)(2,1)S(1)}, u32[]{:S(2)}, u32[]{:S(2)}) collective-permute-start(bf16[512,128]{1,0:T(8,128)(2,1)S(1)} %get-tuple-element.84.refs_0_), channel_id=1, source_target_pairs={{0,4},{1,5},{2,6},{3,7},{4,0},{5,1},{6,2},{7,3},{8,12},{9,13},{10,... | collective-permute-start | bytes 393224 | tf_op jit(solution)/shard_map/ppermute | solution.py:257
  5.6 12.6 %collective-permute-start.1 = (bf16[512,128]{1,0:T(8,128)(2,1)S(1)}, bf16[512,128]{1,0:T(8,128)(2,1)S(1)}, u32[]{:S(2)}, u32[]{:S(2)}) collective-permute-start(bf16[512,128]{1,0:T(8,128)(2,1)S(1)} %get-tuple-element.84.refs_0_), channel_id=1, source_target_pairs={{0,8},{1,9},{2,10},{3,11},{4,12},{5,13},{6,14},{7,15},{8,0},{9,1},... | collective-permute-start | bytes 393224 | tf_op jit(solution)/shard_map/ppermute | solution.py:257
  8.2 10.6 %collective-permute-start.2 = (bf16[512,128]{1,0:T(8,128)(2,1)S(1)}, bf16[512,128]{1,0:T(8,128)(2,1)S(1)}, u32[]{:S(2)}, u32[]{:S(2)}) collective-permute-start(bf16[512,128]{1,0:T(8,128)(2,1)S(1)} %get-tuple-element.84.refs_0_), channel_id=1, source_target_pairs={{0,12},{1,13},{2,14},{3,15},{4,8},{5,9},{6,10},{7,11},{8,4},{9,5},... | collective-permute-start | bytes 393224 | tf_op jit(solution)/shard_map/ppermute | solution.py:257
  15.5 7.9 %collective-permute-start.4 = (bf16[512,128]{1,0:T(8,128)(2,1)S(1)}, bf16[512,128]{1,0:T(8,128)(2,1)S(1)}, u32[]{:S(2)}, u32[]{:S(2)}) collective-permute-start(bf16[512,128]{1,0:T(8,128)(2,1)S(1)} %collective-permute-done.refs_1_), channel_id=1, source_target_pairs={{0,2},{1,3},{2,0},{3,1},{4,6},{5,7},{6,4},{7,5},{8,10},{9,11},{10,... | collective-permute-start | bytes 393224 | tf_op jit(solution)/shard_map/ppermute | solution.py:257
  18.3 7.2 %collective-permute-start.5 = (bf16[512,128]{1,0:T(8,128)(2,1)S(1)}, bf16[512,128]{1,0:T(8,128)(2,1)S(1)}, u32[]{:S(2)}, u32[]{:S(2)}) collective-permute-start(bf16[512,128]{1,0:T(8,128)(2,1)S(1)} %collective-permute-done.1.refs_2_), channel_id=1, source_target_pairs={{0,2},{1,3},{2,0},{3,1},{4,6},{5,7},{6,4},{7,5},{8,10},{9,11},{10,... | collective-permute-start | bytes 393224 | tf_op jit(solution)/shard_map/ppermute | solution.py:257
  18.8 6.7 %collective-permute-start.6 = (bf16[512,128]{1,0:T(8,128)(2,1)S(1)}, bf16[512,128]{1,0:T(8,128)(2,1)S(1)}, u32[]{:S(2)}, u32[]{:S(2)}) collective-permute-start(bf16[512,128]{1,0:T(8,128)(2,1)S(1)} %collective-permute-done.2.refs_3_), channel_id=1, source_target_pairs={{0,2},{1,3},{2,0},{3,1},{4,6},{5,7},{6,4},{7,5},{8,10},{9,11},{10,... | collective-permute-start | bytes 393224 | tf_op jit(solution)/shard_map/ppermute | solution.py:257
  20.4 12.7 %collective-permute-start.17 = (bf16[512,256]{1,0:T(8,128)(2,1)S(1)}, bf16[512,256]{1,0:T(8,128)(2,1)S(1)}, u32[]{:S(2)}, u32[]{:S(2)}) collective-permute-start(bf16[512,256]{1,0:T(8,128)(2,1)S(1)} %pad_maximum_fusion.refs_0_), channel_id=1, source_target_pairs={{0,4},{1,5},{2,6},{3,7},{4,0},{5,1},{6,2},{7,3},{8,12},{9,13},{10,... | collective-permute-start | bytes 786440 | tf_op jit(solution)/shard_map/ppermute | solution.py:257
  20.9 21.0 %collective-permute-start.18 = (bf16[512,256]{1,0:T(8,128)(2,1)S(1)}, bf16[512,256]{1,0:T(8,128)(2,1)S(1)}, u32[]{:S(2)}, u32[]{:S(2)}) collective-permute-start(bf16[512,256]{1,0:T(8,128)(2,1)S(1)} %pad_maximum_fusion.refs_0_), channel_id=1, source_target_pairs={{0,8},{1,9},{2,10},{3,11},{4,12},{5,13},{6,14},{7,15},{8,0},{9,1},... | collective-permute-start | bytes 786440 | tf_op jit(solution)/shard_map/ppermute | solution.py:257
  23.4 18.6 %collective-permute-start.19 = (bf16[512,256]{1,0:T(8,128)(2,1)S(1)}, bf16[512,256]{1,0:T(8,128)(2,1)S(1)}, u32[]{:S(2)}, u32[]{:S(2)}) collective-permute-start(bf16[512,256]{1,0:T(8,128)(2,1)S(1)} %pad_maximum_fusion.refs_0_), channel_id=1, source_target_pairs={{0,12},{1,13},{2,14},{3,15},{4,8},{5,9},{6,10},{7,11},{8,4},{9,5},... | collective-permute-start | bytes 786440 | tf_op jit(solution)/shard_map/ppermute | solution.py:257
  26.4 22.8 %collective-permute-start.7 = (bf16[512,128]{1,0:T(8,128)(2,1)S(1)}, bf16[512,128]{1,0:T(8,128)(2,1)S(1)}, u32[]{:S(2)}, u32[]{:S(2)}) collective-permute-start(bf16[512,128]{1,0:T(8,128)(2,1)S(1)} %get-tuple-element.46), channel_id=1, source_target_pairs={{0,2},{1,3},{2,0},{3,1},{4,6},{5,7},{6,4},{7,5},{8,10},{9,11},{10,... | collective-permute-start | bytes 393224 | tf_op jit(solution)/shard_map/ppermute | solution.py:257
  29.0 21.7 %collective-permute-start.8 = (bf16[1536,128]{1,0:T(8,128)(2,1)S(1)}, bf16[1536,128]{1,0:T(8,128)(2,1)S(1)}, u32[]{:S(2)}, u32[]{:S(2)}) collective-permute-start(bf16[1536,128]{1,0:T(8,128)(2,1)S(1)} %get-tuple-element.47), channel_id=1, source_target_pairs={{0,2},{1,3},{2,0},{3,1},{4,6},{5,7},{6,4},{7,5},{8,10},{9,11},{10,... | collective-permute-start | bytes 1179656 | tf_op jit(solution)/shard_map/ppermute | solution.py:257
  33.1 23.5 %collective-permute-start.12 = (bf16[2048,128]{1,0:T(8,128)(2,1)S(1)}, bf16[2048,128]{1,0:T(8,128)(2,1)S(1)}, u32[]{:S(2)}, u32[]{:S(2)}) collective-permute-start(bf16[2048,128]{1,0:T(8,128)(2,1)S(1)} %get-tuple-element.53), channel_id=1, source_target_pairs={{0,2},{1,3},{2,0},{3,1},{4,6},{5,7},{6,4},{7,5},{8,10},{9,11},{10,... | collective-permute-start | bytes 1572872 | tf_op jit(solution)/shard_map/ppermute | solution.py:257
  44.4 40.3 %collective-permute-start.20 = (bf16[2048,128]{1,0:T(8,128)(2,1)S(1)}, bf16[2048,128]{1,0:T(8,128)(2,1)S(1)}, u32[]{:S(2)}, u32[]{:S(2)}) collective-permute-start(bf16[2048,128]{1,0:T(8,128)(2,1)S(1)} %get-tuple-element.62), channel_id=1, source_target_pairs={{0,2},{1,3},{2,0},{3,1},{4,6},{5,7},{6,4},{7,5},{8,10},{9,11},{10,... | collective-permute-start | bytes 1572872 | tf_op jit(solution)/shard_map/ppermute | solution.py:257
  46.7 31.2 %collective-permute-start.25 = (bf16[512,128]{1,0:T(8,128)(2,1)S(1)}, bf16[512,128]{1,0:T(8,128)(2,1)S(1)}, u32[]{:S(2)}, u32[]{:S(2)}) collective-permute-start(bf16[512,128]{1,0:T(8,128)(2,1)S(1)} %get-tuple-element.70), channel_id=1, source_target_pairs={{0,2},{1,3},{2,0},{3,1},{4,6},{5,7},{6,4},{7,5},{8,10},{9,11},{10,... | collective-permute-start | bytes 393224 | tf_op jit(solution)/shard_map/ppermute | solution.py:257
  49.2 23.5 %collective-permute-start.26 = (bf16[1536,128]{1,0:T(8,128)(2,1)S(1)}, bf16[1536,128]{1,0:T(8,128)(2,1)S(1)}, u32[]{:S(2)}, u32[]{:S(2)}) collective-permute-start(bf16[1536,128]{1,0:T(8,128)(2,1)S(1)} %get-tuple-element.72), channel_id=1, source_target_pairs={{0,2},{1,3},{2,0},{3,1},{4,6},{5,7},{6,4},{7,5},{8,10},{9,11},{10,... | collective-permute-start | bytes 1179656 | tf_op jit(solution)/shard_map/ppermute | solution.py:257
  53.1 25.7 %collective-permute-start.9 = (bf16[128,512]{1,0:T(8,128)(2,1)S(1)}, bf16[128,512]{1,0:T(8,128)(2,1)S(1)}, u32[]{:S(2)}, u32[]{:S(2)}) collective-permute-start(bf16[128,512]{1,0:T(8,128)(2,1)S(1)} %get-tuple-element.49), channel_id=1, source_target_pairs={{0,4},{1,5},{2,6},{3,7},{4,0},{5,1},{6,2},{7,3},{8,12},{9,13},{10,... | collective-permute-start | bytes 393224 | tf_op jit(solution)/shard_map/ppermute | solution.py:257
  56.6 23.3 %collective-permute-start.10 = (bf16[128,512]{1,0:T(8,128)(2,1)S(1)}, bf16[128,512]{1,0:T(8,128)(2,1)S(1)}, u32[]{:S(2)}, u32[]{:S(2)}) collective-permute-start(bf16[128,512]{1,0:T(8,128)(2,1)S(1)} %get-tuple-element.50), channel_id=1, source_target_pairs={{0,8},{1,9},{2,10},{3,11},{4,12},{5,13},{6,14},{7,15},{8,0},{9,1},... | collective-permute-start | bytes 393224 | tf_op jit(solution)/shard_map/ppermute | solution.py:257
  72.7 10.5 %collective-permute-start.11 = (bf16[128,512]{1,0:T(8,128)(2,1)S(1)}, bf16[128,512]{1,0:T(8,128)(2,1)S(1)}, u32[]{:S(2)}, u32[]{:S(2)}) collective-permute-start(bf16[128,512]{1,0:T(8,128)(2,1)S(1)} %get-tuple-element.51), channel_id=1, source_target_pairs={{0,12},{1,13},{2,14},{3,15},{4,8},{5,9},{6,10},{7,11},{8,4},{9,5},... | collective-permute-start | bytes 393224 | tf_op jit(solution)/shard_map/ppermute | solution.py:257
  77.9 9.8 %collective-permute-start.13 = (bf16[128,512]{1,0:T(8,128)(2,1)S(1)}, bf16[128,512]{1,0:T(8,128)(2,1)S(1)}, u32[]{:S(2)}, u32[]{:S(2)}) collective-permute-start(bf16[128,512]{1,0:T(8,128)(2,1)S(1)} %get-tuple-element.55), channel_id=1, source_target_pairs={{0,4},{1,5},{2,6},{3,7},{4,0},{5,1},{6,2},{7,3},{8,12},{9,13},{10,... | collective-permute-start | bytes 393224 | tf_op jit(solution)/shard_map/ppermute | solution.py:257
  78.8 11.5 %collective-permute-start.14 = (bf16[128,512]{1,0:T(8,128)(2,1)S(1)}, bf16[128,512]{1,0:T(8,128)(2,1)S(1)}, u32[]{:S(2)}, u32[]{:S(2)}) collective-permute-start(bf16[128,512]{1,0:T(8,128)(2,1)S(1)} %get-tuple-element.56), channel_id=1, source_target_pairs={{0,8},{1,9},{2,10},{3,11},{4,12},{5,13},{6,14},{7,15},{8,0},{9,1},... | collective-permute-start | bytes 393224 | tf_op jit(solution)/shard_map/ppermute | solution.py:257
  79.9 10.5 %collective-permute-start.15 = (bf16[128,512]{1,0:T(8,128)(2,1)S(1)}, bf16[128,512]{1,0:T(8,128)(2,1)S(1)}, u32[]{:S(2)}, u32[]{:S(2)}) collective-permute-start(bf16[128,512]{1,0:T(8,128)(2,1)S(1)} %get-tuple-element.57), channel_id=1, source_target_pairs={{0,12},{1,13},{2,14},{3,15},{4,8},{5,9},{6,10},{7,11},{8,4},{9,5},... | collective-permute-start | bytes 393224 | tf_op jit(solution)/shard_map/ppermute | solution.py:257
  83.3 10.1 %collective-permute-start.27 = (bf16[64,1024]{1,0:T(8,128)(2,1)S(1)}, bf16[64,1024]{1,0:T(8,128)(2,1)S(1)}, u32[]{:S(2)}, u32[]{:S(2)}) collective-permute-start(bf16[64,1024]{1,0:T(8,128)(2,1)S(1)} %get-tuple-element.73), channel_id=1, source_target_pairs={{0,2},{1,3},{2,0},{3,1},{4,6},{5,7},{6,4},{7,5},{8,10},{9,11},{10,... | collective-permute-start | bytes 393224 | tf_op jit(solution)/shard_map/ppermute | solution.py:257
  84.6 10.2 %collective-permute-start.29 = (bf16[64,1024]{1,0:T(8,128)(2,1)S(1)}, bf16[64,1024]{1,0:T(8,128)(2,1)S(1)}, u32[]{:S(2)}, u32[]{:S(2)}) collective-permute-start(bf16[64,1024]{1,0:T(8,128)(2,1)S(1)} %get-tuple-element.78), channel_id=1, source_target_pairs={{0,2},{1,3},{2,0},{3,1},{4,6},{5,7},{6,4},{7,5},{8,10},{9,11},{10,... | collective-permute-start | bytes 393224 | tf_op jit(solution)/shard_map/ppermute | solution.py:257
  87.7 13.9 %collective-permute-start.21 = (bf16[128,512]{1,0:T(8,128)(2,1)S(1)}, bf16[128,512]{1,0:T(8,128)(2,1)S(1)}, u32[]{:S(2)}, u32[]{:S(2)}) collective-permute-start(bf16[128,512]{1,0:T(8,128)(2,1)S(1)} %get-tuple-element.64), channel_id=1, source_target_pairs={{0,4},{1,5},{2,6},{3,7},{4,0},{5,1},{6,2},{7,3},{8,12},{9,13},{10,... | collective-permute-start | bytes 393224 | tf_op jit(solution)/shard_map/ppermute | solution.py:257
  90.3 11.9 %collective-permute-start.22 = (bf16[128,512]{1,0:T(8,128)(2,1)S(1)}, bf16[128,512]{1,0:T(8,128)(2,1)S(1)}, u32[]{:S(2)}, u32[]{:S(2)}) collective-permute-start(bf16[128,512]{1,0:T(8,128)(2,1)S(1)} %get-tuple-element.65), channel_id=1, source_target_pairs={{0,8},{1,9},{2,10},{3,11},{4,12},{5,13},{6,14},{7,15},{8,0},{9,1},... | collective-permute-start | bytes 393224 | tf_op jit(solution)/shard_map/ppermute | solution.py:257
  90.3 13.8 %collective-permute-start.23 = (bf16[128,512]{1,0:T(8,128)(2,1)S(1)}, bf16[128,512]{1,0:T(8,128)(2,1)S(1)}, u32[]{:S(2)}, u32[]{:S(2)}) collective-permute-start(bf16[128,512]{1,0:T(8,128)(2,1)S(1)} %get-tuple-element.66), channel_id=1, source_target_pairs={{0,12},{1,13},{2,14},{3,15},{4,8},{5,9},{6,10},{7,11},{8,4},{9,5},... | collective-permute-start | bytes 393224 | tf_op jit(solution)/shard_map/ppermute | solution.py:257
  93.4 11.5 %collective-permute-start.16 = (bf16[128,512]{1,0:T(8,128)(2,1)S(1)}, bf16[128,512]{1,0:T(8,128)(2,1)S(1)}, u32[]{:S(2)}, u32[]{:S(2)}) collective-permute-start(bf16[128,512]{1,0:T(8,128)(2,1)S(1)} %get-tuple-element.60), channel_id=1, source_target_pairs={{0,2},{1,3},{2,0},{3,1},{4,6},{5,7},{6,4},{7,5},{8,10},{9,11},{10,... | collective-permute-start | bytes 393224 | tf_op jit(solution)/shard_map/ppermute | solution.py:257
  94.9 10.0 %collective-permute-start.28 = (bf16[64,512]{1,0:T(8,128)(2,1)S(1)}, bf16[64,512]{1,0:T(8,128)(2,1)S(1)}, u32[]{:S(2)}, u32[]{:S(2)}) collective-permute-start(bf16[64,512]{1,0:T(8,128)(2,1)S(1)} %get-tuple-element.77), channel_id=1, source_target_pairs={{0,4},{1,5},{2,6},{3,7},{4,0},{5,1},{6,2},{7,3},{8,12},{9,13},{10,... | collective-permute-start | bytes 196616 | tf_op jit(solution)/shard_map/ppermute | solution.py:257
  101.6 5.5 %collective-permute-start.30 = (bf16[64,512]{1,0:T(8,128)(2,1)S(1)}, bf16[64,512]{1,0:T(8,128)(2,1)S(1)}, u32[]{:S(2)}, u32[]{:S(2)}) collective-permute-start(bf16[64,512]{1,0:T(8,128)(2,1)S(1)} %get-tuple-element.81), channel_id=1, source_target_pairs={{0,8},{1,9},{2,10},{3,11},{4,12},{5,13},{6,14},{7,15},{8,0},{9,1},... | collective-permute-start | bytes 196616 | tf_op jit(solution)/shard_map/ppermute | solution.py:257
  102.2 6.2 %collective-permute-start.31 = (bf16[64,512]{1,0:T(8,128)(2,1)S(1)}, bf16[64,512]{1,0:T(8,128)(2,1)S(1)}, u32[]{:S(2)}, u32[]{:S(2)}) collective-permute-start(bf16[64,512]{1,0:T(8,128)(2,1)S(1)} %get-tuple-element.82), channel_id=1, source_target_pairs={{0,12},{1,13},{2,14},{3,15},{4,8},{5,9},{6,10},{7,11},{8,4},{9,5},... | collective-permute-start | bytes 196616 | tf_op jit(solution)/shard_map/ppermute | solution.py:257
  104.2 4.3 %collective-permute-start.24 = (bf16[64,512]{1,0:T(8,128)(2,1)S(1)}, bf16[64,512]{1,0:T(8,128)(2,1)S(1)}, u32[]{:S(2)}, u32[]{:S(2)}) collective-permute-start(bf16[64,512]{1,0:T(8,128)(2,1)S(1)} %get-tuple-element.68), channel_id=1, source_target_pairs={{0,2},{1,3},{2,0},{3,1},{4,6},{5,7},{6,4},{7,5},{8,10},{9,11},{10,... | collective-permute-start | bytes 196616 | tf_op jit(solution)/shard_map/ppermute | solution.py:257

commit v2 on v1

--- a/solution.py
+++ b/solution.py
@@ -47,11 +47,6 @@
     return moved % shards if isinstance(moved, int) else lax.rem(moved, shards)
 
 
-def groups_of(shards):
-    hops = list(range(shards - 1, -1, -1))
-    return [hops[: shards // 2], hops[shards // 2 :]]
-
-
 def load_body(half, place, source, out, arrived):
     del place
     vectors, part = out.shape[0] // STREAMS, out.shape[1]
@@ -110,7 +105,7 @@
     )(place, factors, *pieces)
 
 
-def gradient_body(shards, parts, first, carried, groups, place, *refs):
+def gradient_body(shards, parts, first, carried, crossing, place, *refs):
     owns, fars, factors = refs[:parts], refs[parts : 2 * parts], refs[2 * parts : 2 * parts + HALVES]
     outs, sums = refs[2 * parts + HALVES + carried : -1], refs[-1]
     width = owns[0].shape[1]
@@ -134,29 +129,25 @@
     owned = sums.shape[1] // shards
     for hop in range(shards):
         low = pl.multiple_of(peer(place[0], hop, shards) * owned, owned)
-        if groups is None:
+        if crossing:
+            outs[hop][...] = sums[:part, pl.ds(low, owned)]
+            outs[shards][:, hop * owned : (hop + 1) * owned] = sums[part:, pl.ds(low, owned)].astype(jnp.bfloat16)
+        else:
             outs[hop][...] = sums[:, pl.ds(low, owned)].astype(outs[hop].dtype)
-            continue
-        outs[hop][...] = sums[:part, pl.ds(low, owned)].astype(outs[hop].dtype)
-        for group, hops in enumerate(groups):
-            if hop in hops:
-                to = hops.index(hop) * owned
-                outs[shards + group][:, to : to + owned] = sums[part:, pl.ds(low, owned)].astype(jnp.bfloat16)
-
-
-def gradients_of(place, factors, owns, fars, shards, first=0, groups=None, carried=None, more=False):
+
+
+def gradients_of(place, factors, owns, fars, shards, first=0, crossing=False, carried=None, more=False):
     orbitals, width = factors[0].shape[2], owns[0].shape[1]
     part, owned = width // HALVES, orbitals // shards
     outs = [jax.ShapeDtypeStruct((2 * part, owned), jnp.bfloat16 if hop else jnp.float32) for hop in range(shards)]
     if more:
         outs = [jax.ShapeDtypeStruct((2 * part, orbitals), jnp.float32)]
-    elif groups:
-        outs = [jax.ShapeDtypeStruct((part, owned), jnp.float32)] * shards
-        outs += [jax.ShapeDtypeStruct((part, owned * len(hops)), jnp.bfloat16) for hops in groups]
+    elif crossing:
+        outs = [jax.ShapeDtypeStruct((part, owned), jnp.float32)] * shards + [jax.ShapeDtypeStruct((part, orbitals), jnp.bfloat16)]
     count = sum(own.shape[0] for own in owns) * HALVES
     values = [place, *owns, *fars, *factors] + ([] if carried is None else [carried])
     return pl.pallas_call(
-        functools.partial(gradient_body, shards, len(owns), first, 0 if carried is None else 1, groups),
+        functools.partial(gradient_body, shards, len(owns), first, 0 if carried is None else 1, crossing),
         in_specs=[SMEM] + [VMEM] * (len(values) - 1),
         out_specs=[VMEM] * len(outs),
         scratch_shapes=[pltpu.VMEM((2 * part, orbitals), jnp.float32)],
@@ -279,23 +270,17 @@
     for stage in range(stages - 1):
         got = gradients_of(place, factors, *sides[stage], shards)
         arrived.append([got[0]] + [moved(got[hop], hop) for hop in hops])
-    part, values, plan = width // HALVES, [], []
-    for some in (arrived[:-1], arrived[-1:]):
-        *kept, crossing = split_sums(some)
-        here = len(values)
-        values += [*kept, moved(crossing, 0, True)]
-        plan += [[(here + stage, 0, part), (here + len(kept), stage * part, (stage + 1) * part)] for stage in range(len(kept))]
+    *kept, crossing = split_sums(arrived)
+    part = width // HALVES
+    values = [*kept, moved(crossing, 0, True)]
+    plan = [[(stage, 0, part), (len(kept), stage * part, (stage + 1) * part)] for stage in range(len(kept))]
 
     owns, fars = sides[-1]
-    groups = groups_of(shards)
     (carried,) = gradients_of(place, factors, owns[:1], fars[:1], shards, more=True)
-    got = gradients_of(place, factors, owns[1:], fars[1:], shards, parts_of(stages - 1, stages, vectors)[1], groups, carried)
-    came = [moved(got[shards + at], 0, True) for at in range(len(groups))]
-    ends = [None] * shards
-    for at, group in enumerate(groups):
-        joined = join_sums(came[at], [got[hop] for hop in group], [jnp.bfloat16 if hop else jnp.float32 for hop in group])
-        for hop, value in zip(group, joined):
-            ends[hop] = moved(value, hop) if hop else value
+    *own, far = gradients_of(place, factors, owns[1:], fars[1:], shards, parts_of(stages - 1, stages, vectors)[1], True, carried)
+    came = moved(far, 0, True)
+    joined = join_sums(came, own, [jnp.bfloat16 if hop else jnp.float32 for hop in range(shards)])
+    ends = [moved(value, hop) if hop else value for hop, value in enumerate(joined)]
     plan.append([(len(values) + at, 0, part) for at in range(shards)])
     values += ends
     return totals_of(values, [plan[walker * HALVES : (walker + 1) * HALVES] for walker in range(walkers)])

time: 110 us -> 108 us (0.982)
  starting transfers between devices: 50.6 us -> 48.2 us
    ppermute x32 -> x30, starting transfers between devices: 50.6 us -> 48.2 us  [moved(): return lax.ppermute(value, AXES, pairs)]
    ppermute x32 -> x30, waiting for transfers between devices: 28.9 us -> 29.5 us  [moved(): return lax.ppermute(value, AXES, pairs)]
  transfers between devices with their start and end apart: 32 -> 30, of which waited for: 7 -> 7; matrix products, arithmetic and copies ran while one was open for 1% -> 1% of each run, Pallas kernels for 25% -> 26%
where the time goes in v2:
time: 108 us
  starting transfers between devices  48.2 us (45%)
  waiting for transfers between devices  29.5 us (27%)
  Pallas kernels  28.7 us (27%)
    ppermute x30, starting transfers between devices, moved(): return lax.ppermute(value, AXES, pairs)  48.2 us
    ppermute x30, waiting for transfers between devices, moved(): return lax.ppermute(value, AXES, pairs)  29.5 us
    pallas_call x6, Pallas kernels, amplitudes_of(): pl.pallas_call(functools.partial(amplitude_body, shards, *vectors), in_sp...  10.5 us
    pallas_call x5, Pallas kernels, gradients_of(): pl.pallas_call(functools.partial(gradient_body, shards, len(owns), first,...  9.98 us
    pallas_call x2, Pallas kernels, loaded(): pl.pallas_call(functools.partial(load_body, half), in_specs=[SMEM, pl.Blo...  7 us
  transfers between devices with their start and end apart: 30, of which 7 were waited for; matrix products, arithmetic and copies ran while one was open for 1% of the time, Pallas kernels for 26%

profile of v2, /device:TPU:0, one launch (start us, length us, event | category | flops | bytes accessed | tf_op | source)
XLA Modules:
  0.0 107.5 jit_solution(17243823362010206787)
XLA Ops:
  0.0 3.0 %collective-permute-start.3 = (bf16[2,512,128]{2,1,0:T(8,128)(2,1)}, bf16[2,512,128]{2,1,0:T(8,128)(2,1)S(1)}, u32[]{:S(2)}, u32[]{:S(2)}) collective-permute-start(bf16[2,512,128]{2,1,0:T(8,128)(2,1)} %param.3), channel_id=1, source_target_pairs={{0,2},{1,3},{2,0},{3,1},{4,6},{5,7},{6,4},{7,5},{8,10},{9,11},{10,... | collective-permute-start | bytes 786440 | tf_op jit(solution)/shard_map/ppermute | solution.py:248
  4.0 1.6 %collective-permute-start = (bf16[512,128]{1,0:T(8,128)(2,1)S(1)}, bf16[512,128]{1,0:T(8,128)(2,1)S(1)}, u32[]{:S(2)}, u32[]{:S(2)}) collective-permute-start(bf16[512,128]{1,0:T(8,128)(2,1)S(1)} %get-tuple-element.80.refs_0_), channel_id=1, source_target_pairs={{0,4},{1,5},{2,6},{3,7},{4,0},{5,1},{6,2},{7,3},{8,12},{9,13},{10,... | collective-permute-start | bytes 393224 | tf_op jit(solution)/shard_map/ppermute | solution.py:248
  5.6 2.6 %collective-permute-start.1 = (bf16[512,128]{1,0:T(8,128)(2,1)S(1)}, bf16[512,128]{1,0:T(8,128)(2,1)S(1)}, u32[]{:S(2)}, u32[]{:S(2)}) collective-permute-start(bf16[512,128]{1,0:T(8,128)(2,1)S(1)} %get-tuple-element.80.refs_0_), channel_id=1, source_target_pairs={{0,8},{1,9},{2,10},{3,11},{4,12},{5,13},{6,14},{7,15},{8,0},{9,1},... | collective-permute-start | bytes 393224 | tf_op jit(solution)/shard_map/ppermute | solution.py:248
  8.4 3.5 %shard_map.31.refs_5_.factors.refs_3_ = bf16[32,64,2048]{2,1,0:T(8,128)(2,1)S(1)} custom-call(s32[1]{0:T(128)} %bitcast.place, bf16[32,128,2048]{2,1,0:T(8,128)(2,1)} %source.3), custom_call_target="tpu_custom_call" | custom-call | tf_op jit(solution)/shard_map/pallas_call | solution.py:65
  11.9 3.5 %shard_map.28.factors.refs_4_.refs_2_ = bf16[32,64,2048]{2,1,0:T(8,128)(2,1)S(1)} custom-call(s32[1]{0:T(128)} %bitcast.place, bf16[32,128,2048]{2,1,0:T(8,128)(2,1)} %source.3), custom_call_target="tpu_custom_call" | custom-call | tf_op jit(solution)/shard_map/pallas_call | solution.py:65
  15.8 2.4 %collective-permute-done.1.refs_2_ = bf16[512,128]{1,0:T(8,128)(2,1)S(1)} collective-permute-done((bf16[512,128]{1,0:T(8,128)(2,1)S(1)}, bf16[512,128]{1,0:T(8,128)(2,1)S(1)}, u32[]{:S(2)}, u32[]{:S(2)}) %collective-permute-start.1) | collective-permute-done | bytes 131104 | tf_op jit(solution)/shard_map/ppermute | solution.py:248
  18.8 1.5 %collective-permute-start.6 = (bf16[512,128]{1,0:T(8,128)(2,1)S(1)}, bf16[512,128]{1,0:T(8,128)(2,1)S(1)}, u32[]{:S(2)}, u32[]{:S(2)}) collective-permute-start(bf16[512,128]{1,0:T(8,128)(2,1)S(1)} %collective-permute-done.2.refs_3_), channel_id=1, source_target_pairs={{0,2},{1,3},{2,0},{3,1},{4,6},{5,7},{6,4},{7,5},{8,10},{9,11},{10,... | collective-permute-start | bytes 393224 | tf_op jit(solution)/shard_map/ppermute | solution.py:248
  20.9 2.5 %collective-permute-start.17 = (bf16[512,256]{1,0:T(8,128)(2,1)S(1)}, bf16[512,256]{1,0:T(8,128)(2,1)S(1)}, u32[]{:S(2)}, u32[]{:S(2)}) collective-permute-start(bf16[512,256]{1,0:T(8,128)(2,1)S(1)} %pad_maximum_fusion.refs_0_), channel_id=1, source_target_pairs={{0,8},{1,9},{2,10},{3,11},{4,12},{5,13},{6,14},{7,15},{8,0},{9,1},... | collective-permute-start | bytes 786440 | tf_op jit(solution)/shard_map/ppermute | solution.py:248
  23.4 2.1 %collective-permute-start.18 = (bf16[512,256]{1,0:T(8,128)(2,1)S(1)}, bf16[512,256]{1,0:T(8,128)(2,1)S(1)}, u32[]{:S(2)}, u32[]{:S(2)}) collective-permute-start(bf16[512,256]{1,0:T(8,128)(2,1)S(1)} %pad_maximum_fusion.refs_0_), channel_id=1, source_target_pairs={{0,12},{1,13},{2,14},{3,15},{4,8},{5,9},{6,10},{7,11},{8,4},{9,5},... | collective-permute-start | bytes 786440 | tf_op jit(solution)/shard_map/ppermute | solution.py:248
  25.5 2.5 %shard_map.33 = (bf16[2048,128]{1,0:T(8,128)(2,1)S(1)}, bf16[2048,128]{1,0:T(8,128)(2,1)S(1)}) custom-call(s32[1]{0:T(128)} %bitcast.place, bf16[32,64,2048]{2,1,0:T(8,128)(2,1)S(1)} %shard_map.31.refs_5_.factors.refs_3_, bf16[512,128]{1,0:T(8,128)(2,1)S(1)} %get-tuple-element.80.refs_0_, bf16[512,128]{1,0:T(8,128)(2,1)S(1)} %collective-permute-done.refs_1_, ...), custom_call_target="tpu_custom_call" | custom-call | flops 2147483648 | bytes 8388608 | tf_op jit(solution)/shard_map/pallas_call | solution.py:97
  28.6 2.0 %shard_map.30 = (bf16[1536,128]{1,0:T(8,128)(2,1)S(1)}, bf16[1536,128]{1,0:T(8,128)(2,1)S(1)}) custom-call(s32[1]{0:T(128)} %bitcast.place, bf16[32,64,2048]{2,1,0:T(8,128)(2,1)S(1)} %shard_map.28.factors.refs_4_.refs_2_, bf16[512,128]{1,0:T(8,128)(2,1)S(1)} %get-tuple-element.80.refs_0_, bf16[512,128]{1,0:T(8,128)(2,1)S(1)} %collective-permute-done.refs_1_, ...), custom_call_target="tpu_custom_call" | custom-call | flops 1610612736 | bytes 6291456 | tf_op jit(solution)/shard_map/pallas_call | solution.py:97
  30.6 1.6 %collective-permute-start.8 = (bf16[1536,128]{1,0:T(8,128)(2,1)S(1)}, bf16[1536,128]{1,0:T(8,128)(2,1)S(1)}, u32[]{:S(2)}, u32[]{:S(2)}) collective-permute-start(bf16[1536,128]{1,0:T(8,128)(2,1)S(1)} %get-tuple-element.45), channel_id=1, source_target_pairs={{0,2},{1,3},{2,0},{3,1},{4,6},{5,7},{6,4},{7,5},{8,10},{9,11},{10,... | collective-permute-start | bytes 1179656 | tf_op jit(solution)/shard_map/ppermute | solution.py:248
  33.7 8.2 %collective-permute-done.17.refs_2_ = bf16[512,256]{1,0:T(8,128)(2,1)S(1)} collective-permute-done((bf16[512,256]{1,0:T(8,128)(2,1)S(1)}, bf16[512,256]{1,0:T(8,128)(2,1)S(1)}, u32[]{:S(2)}, u32[]{:S(2)}) %collective-permute-start.17) | collective-permute-done | bytes 262176 | tf_op jit(solution)/shard_map/ppermute | solution.py:248
  41.9 1.9 %shard_map.39 = (bf16[1536,128]{1,0:T(8,128)(2,1)S(1)}, bf16[1536,128]{1,0:T(8,128)(2,1)S(1)}) custom-call(s32[1]{0:T(128)} %bitcast.place, bf16[32,64,2048]{2,1,0:T(8,128)(2,1)S(1)} %shard_map.31.refs_5_.factors.refs_3_, bf16[512,256]{1,0:T(8,128)(2,1)S(1)} %pad_maximum_fusion.refs_0_, bf16[512,256]{1,0:T(8,128)(2,1)S(1)} %collective-permute-done.16.refs_1_, ...), custom_call_target="tpu_custom_call" | custom-call | flops 1610612736 | bytes 6291456 | tf_op jit(solution)/shard_map/pallas_call | solution.py:97
  43.8 1.6 %collective-permute-start.25 = (bf16[1536,128]{1,0:T(8,128)(2,1)S(1)}, bf16[1536,128]{1,0:T(8,128)(2,1)S(1)}, u32[]{:S(2)}, u32[]{:S(2)}) collective-permute-start(bf16[1536,128]{1,0:T(8,128)(2,1)S(1)} %get-tuple-element.69), channel_id=1, source_target_pairs={{0,2},{1,3},{2,0},{3,1},{4,6},{5,7},{6,4},{7,5},{8,10},{9,11},{10,... | collective-permute-start | bytes 1179656 | tf_op jit(solution)/shard_map/ppermute | solution.py:248
  46.8 2.4 %shard_map.35 = (bf16[2048,128]{1,0:T(8,128)(2,1)S(1)}, bf16[2048,128]{1,0:T(8,128)(2,1)S(1)}) custom-call(s32[1]{0:T(128)} %bitcast.place, bf16[32,64,2048]{2,1,0:T(8,128)(2,1)S(1)} %shard_map.28.factors.refs_4_.refs_2_, bf16[512,256]{1,0:T(8,128)(2,1)S(1)} %pad_maximum_fusion.refs_0_, bf16[512,256]{1,0:T(8,128)(2,1)S(1)} %collective-permute-done.16.refs_1_, ...), custom_call_target="tpu_custom_call" | custom-call | flops 2147483648 | bytes 8388608 | tf_op jit(solution)/shard_map/pallas_call | solution.py:97
  49.2 4.9 %collective-permute-done.7.refs_2_ = bf16[512,128]{1,0:T(8,128)(2,1)S(1)} collective-permute-done((bf16[512,128]{1,0:T(8,128)(2,1)S(1)}, bf16[512,128]{1,0:T(8,128)(2,1)S(1)}, u32[]{:S(2)}, u32[]{:S(2)}) %collective-permute-start.7) | collective-permute-done | bytes 131104 | tf_op jit(solution)/shard_map/ppermute | solution.py:248
  54.7 2.4 %shard_map.32 = (f32[128,512]{1,0:T(8,128)S(1)}, bf16[128,512]{1,0:T(8,128)(2,1)S(1)}, bf16[128,512]{1,0:T(8,128)(2,1)S(1)}, bf16[128,512]{1,0:T(8,128)(2,1)S(1)}) custom-call(s32[1]{0:T(128)} %bitcast.place, bf16[512,128]{1,0:T(8,128)(2,1)S(1)} %get-tuple-element.42.refs_0_, bf16[1536,128]{1,0:T(8,128)(2,1)S(1)} %get-tuple-element.43.refs_1_, ...), custom_call_target="tpu_custom_call" | custom-call | flops 2147483648 | bytes 16777216 | tf_op jit(solution)/shard_map/pallas_call | solution.py:149
  57.1 1.5 %collective-permute-start.10 = (bf16[128,512]{1,0:T(8,128)(2,1)S(1)}, bf16[128,512]{1,0:T(8,128)(2,1)S(1)}, u32[]{:S(2)}, u32[]{:S(2)}) collective-permute-start(bf16[128,512]{1,0:T(8,128)(2,1)S(1)} %get-tuple-element.48), channel_id=1, source_target_pairs={{0,8},{1,9},{2,10},{3,11},{4,12},{5,13},{6,14},{7,15},{8,0},{9,1},... | collective-permute-start | bytes 393224 | tf_op jit(solution)/shard_map/ppermute | solution.py:248
  58.6 2.0 %collective-permute-start.11 = (bf16[128,512]{1,0:T(8,128)(2,1)S(1)}, bf16[128,512]{1,0:T(8,128)(2,1)S(1)}, u32[]{:S(2)}, u32[]{:S(2)}) collective-permute-start(bf16[128,512]{1,0:T(8,128)(2,1)S(1)} %get-tuple-element.49), channel_id=1, source_target_pairs={{0,12},{1,13},{2,14},{3,15},{4,8},{5,9},{6,10},{7,11},{8,4},{9,5},... | collective-permute-start | bytes 393224 | tf_op jit(solution)/shard_map/ppermute | solution.py:248
  60.6 2.6 %shard_map.34 = (f32[128,512]{1,0:T(8,128)S(1)}, bf16[128,512]{1,0:T(8,128)(2,1)S(1)}, bf16[128,512]{1,0:T(8,128)(2,1)S(1)}, bf16[128,512]{1,0:T(8,128)(2,1)S(1)}) custom-call(s32[1]{0:T(128)} %bitcast.place, bf16[2048,128]{1,0:T(8,128)(2,1)S(1)} %get-tuple-element.50.refs_0_, bf16[2048,128]{1,0:T(8,128)(2,1)S(1)} %collective-permute-done.12.refs_1_, ...), custom_call_target="tpu_custom_call" | custom-call | flops 2147483648 | bytes 16777216 | tf_op jit(solution)/shard_map/pallas_call | solution.py:149
  63.7 1.8 %shard_map.40.refs_4_ = f32[128,2048]{1,0:T(8,128)S(1)} custom-call(s32[1]{0:T(128)} %bitcast.place, bf16[1536,128]{1,0:T(8,128)(2,1)S(1)} %get-tuple-element.68.refs_0_, bf16[1536,128]{1,0:T(8,128)(2,1)S(1)} %collective-permute-done.25.refs_1_, bf16[32,64,2048]{2,1,0:T(8,128)(2,1)S(1)} %shard_map.28.factors.refs_4_.refs_2_, ...), custom_call_target="tpu_custom_call" | custom-call | flops 1610612736 | bytes 12582912 | tf_op jit(solution)/shard_map/pallas_call | solution.py:149
  65.6 1.6 %collective-permute-start.13 = (bf16[128,512]{1,0:T(8,128)(2,1)S(1)}, bf16[128,512]{1,0:T(8,128)(2,1)S(1)}, u32[]{:S(2)}, u32[]{:S(2)}) collective-permute-start(bf16[128,512]{1,0:T(8,128)(2,1)S(1)} %get-tuple-element.53), channel_id=1, source_target_pairs={{0,4},{1,5},{2,6},{3,7},{4,0},{5,1},{6,2},{7,3},{8,12},{9,13},{10,... | collective-permute-start | bytes 393224 | tf_op jit(solution)/shard_map/ppermute | solution.py:248
  68.0 5.4 %collective-permute-done.19.refs_1_ = bf16[2048,128]{1,0:T(8,128)(2,1)S(1)} collective-permute-done((bf16[2048,128]{1,0:T(8,128)(2,1)S(1)}, bf16[2048,128]{1,0:T(8,128)(2,1)S(1)}, u32[]{:S(2)}, u32[]{:S(2)}) %collective-permute-start.19) | collective-permute-done | bytes 524320 | tf_op jit(solution)/shard_map/ppermute | solution.py:248
  73.4 2.3 %collective-permute-start.14 = (bf16[128,512]{1,0:T(8,128)(2,1)S(1)}, bf16[128,512]{1,0:T(8,128)(2,1)S(1)}, u32[]{:S(2)}, u32[]{:S(2)}) collective-permute-start(bf16[128,512]{1,0:T(8,128)(2,1)S(1)} %get-tuple-element.54), channel_id=1, source_target_pairs={{0,8},{1,9},{2,10},{3,11},{4,12},{5,13},{6,14},{7,15},{8,0},{9,1},... | collective-permute-start | bytes 393224 | tf_op jit(solution)/shard_map/ppermute | solution.py:248
  75.7 2.4 %shard_map.36 = (f32[128,512]{1,0:T(8,128)S(1)}, bf16[128,512]{1,0:T(8,128)(2,1)S(1)}, bf16[128,512]{1,0:T(8,128)(2,1)S(1)}, bf16[128,512]{1,0:T(8,128)(2,1)S(1)}) custom-call(s32[1]{0:T(128)} %bitcast.place, bf16[2048,128]{1,0:T(8,128)(2,1)S(1)} %get-tuple-element.56.refs_0_, bf16[2048,128]{1,0:T(8,128)(2,1)S(1)} %collective-permute-done.19.refs_1_, ...), custom_call_target="tpu_custom_call" | custom-call | flops 2147483648 | bytes 16777216 | tf_op jit(solution)/shard_map/pallas_call | solution.py:149
  80.5 2.6 %collective-permute-start.21 = (bf16[128,512]{1,0:T(8,128)(2,1)S(1)}, bf16[128,512]{1,0:T(8,128)(2,1)S(1)}, u32[]{:S(2)}, u32[]{:S(2)}) collective-permute-start(bf16[128,512]{1,0:T(8,128)(2,1)S(1)} %get-tuple-element.60), channel_id=1, source_target_pairs={{0,8},{1,9},{2,10},{3,11},{4,12},{5,13},{6,14},{7,15},{8,0},{9,1},... | collective-permute-start | bytes 393224 | tf_op jit(solution)/shard_map/ppermute | solution.py:248
  83.1 9.0 %collective-permute-start.22 = (bf16[128,512]{1,0:T(8,128)(2,1)S(1)}, bf16[128,512]{1,0:T(8,128)(2,1)S(1)}, u32[]{:S(2)}, u32[]{:S(2)}) collective-permute-start(bf16[128,512]{1,0:T(8,128)(2,1)S(1)} %get-tuple-element.61), channel_id=1, source_target_pairs={{0,12},{1,13},{2,14},{3,15},{4,8},{5,9},{6,10},{7,11},{8,4},{9,5},... | collective-permute-start | bytes 393224 | tf_op jit(solution)/shard_map/ppermute | solution.py:248
  92.1 3.4 %collective-permute-done.21.refs_10_ = bf16[128,512]{1,0:T(8,128)(2,1)S(1)} collective-permute-done((bf16[128,512]{1,0:T(8,128)(2,1)S(1)}, bf16[128,512]{1,0:T(8,128)(2,1)S(1)}, u32[]{:S(2)}, u32[]{:S(2)}) %collective-permute-start.21) | collective-permute-done | bytes 131104 | tf_op jit(solution)/shard_map/ppermute | solution.py:248
  96.5 2.6 %collective-permute-start.27 = (bf16[64,512]{1,0:T(8,128)(2,1)S(1)}, bf16[64,512]{1,0:T(8,128)(2,1)S(1)}, u32[]{:S(2)}, u32[]{:S(2)}) collective-permute-start(bf16[64,512]{1,0:T(8,128)(2,1)S(1)} %get-tuple-element.76), channel_id=1, source_target_pairs={{0,4},{1,5},{2,6},{3,7},{4,0},{5,1},{6,2},{7,3},{8,12},{9,13},{10,... | collective-permute-start | bytes 196616 | tf_op jit(solution)/shard_map/ppermute | solution.py:248
  99.1 1.3 %collective-permute-start.28 = (bf16[64,512]{1,0:T(8,128)(2,1)S(1)}, bf16[64,512]{1,0:T(8,128)(2,1)S(1)}, u32[]{:S(2)}, u32[]{:S(2)}) collective-permute-start(bf16[64,512]{1,0:T(8,128)(2,1)S(1)} %get-tuple-element.77), channel_id=1, source_target_pairs={{0,8},{1,9},{2,10},{3,11},{4,12},{5,13},{6,14},{7,15},{8,0},{9,1},... | collective-permute-start | bytes 196616 | tf_op jit(solution)/shard_map/ppermute | solution.py:248
  101.6 3.8 %collective-permute-done.28.refs_6_ = bf16[64,512]{1,0:T(8,128)(2,1)S(1)} collective-permute-done((bf16[64,512]{1,0:T(8,128)(2,1)S(1)}, bf16[64,512]{1,0:T(8,128)(2,1)S(1)}, u32[]{:S(2)}, u32[]{:S(2)}) %collective-permute-start.28) | collective-permute-done | bytes 65568 | tf_op jit(solution)/shard_map/ppermute | solution.py:248
  (47 shorter events, 14.9 us)
Async XLA Ops:
  0.0 20.3 %collective-permute-start.3 = (bf16[2,512,128]{2,1,0:T(8,128)(2,1)}, bf16[2,512,128]{2,1,0:T(8,128)(2,1)S(1)}, u32[]{:S(2)}, u32[]{:S(2)}) collective-permute-start(bf16[2,512,128]{2,1,0:T(8,128)(2,1)} %param.3), channel_id=1, source_target_pairs={{0,2},{1,3},{2,0},{3,1},{4,6},{5,7},{6,4},{7,5},{8,10},{9,11},{10,... | collective-permute-start | bytes 786440 | tf_op jit(solution)/shard_map/ppermute | solution.py:248
  4.0 11.5 %collective-permute-start = (bf16[512,128]{1,0:T(8,128)(2,1)S(1)}, bf16[512,128]{1,0:T(8,128)(2,1)S(1)}, u32[]{:S(2)}, u32[]{:S(2)}) collective-permute-start(bf16[512,128]{1,0:T(8,128)(2,1)S(1)} %get-tuple-element.80.refs_0_), channel_id=1, source_target_pairs={{0,4},{1,5},{2,6},{3,7},{4,0},{5,1},{6,2},{7,3},{8,12},{9,13},{10,... | collective-permute-start | bytes 393224 | tf_op jit(solution)/shard_map/ppermute | solution.py:248
  5.6 12.6 %collective-permute-start.1 = (bf16[512,128]{1,0:T(8,128)(2,1)S(1)}, bf16[512,128]{1,0:T(8,128)(2,1)S(1)}, u32[]{:S(2)}, u32[]{:S(2)}) collective-permute-start(bf16[512,128]{1,0:T(8,128)(2,1)S(1)} %get-tuple-element.80.refs_0_), channel_id=1, source_target_pairs={{0,8},{1,9},{2,10},{3,11},{4,12},{5,13},{6,14},{7,15},{8,0},{9,1},... | collective-permute-start | bytes 393224 | tf_op jit(solution)/shard_map/ppermute | solution.py:248
  8.2 10.6 %collective-permute-start.2 = (bf16[512,128]{1,0:T(8,128)(2,1)S(1)}, bf16[512,128]{1,0:T(8,128)(2,1)S(1)}, u32[]{:S(2)}, u32[]{:S(2)}) collective-permute-start(bf16[512,128]{1,0:T(8,128)(2,1)S(1)} %get-tuple-element.80.refs_0_), channel_id=1, source_target_pairs={{0,12},{1,13},{2,14},{3,15},{4,8},{5,9},{6,10},{7,11},{8,4},{9,5},... | collective-permute-start | bytes 393224 | tf_op jit(solution)/shard_map/ppermute | solution.py:248
  15.4 7.9 %collective-permute-start.4 = (bf16[512,128]{1,0:T(8,128)(2,1)S(1)}, bf16[512,128]{1,0:T(8,128)(2,1)S(1)}, u32[]{:S(2)}, u32[]{:S(2)}) collective-permute-start(bf16[512,128]{1,0:T(8,128)(2,1)S(1)} %collective-permute-done.refs_1_), channel_id=1, source_target_pairs={{0,2},{1,3},{2,0},{3,1},{4,6},{5,7},{6,4},{7,5},{8,10},{9,11},{10,... | collective-permute-start | bytes 393224 | tf_op jit(solution)/shard_map/ppermute | solution.py:248
  18.3 7.2 %collective-permute-start.5 = (bf16[512,128]{1,0:T(8,128)(2,1)S(1)}, bf16[512,128]{1,0:T(8,128)(2,1)S(1)}, u32[]{:S(2)}, u32[]{:S(2)}) collective-permute-start(bf16[512,128]{1,0:T(8,128)(2,1)S(1)} %collective-permute-done.1.refs_2_), channel_id=1, source_target_pairs={{0,2},{1,3},{2,0},{3,1},{4,6},{5,7},{6,4},{7,5},{8,10},{9,11},{10,... | collective-permute-start | bytes 393224 | tf_op jit(solution)/shard_map/ppermute | solution.py:248
  18.8 6.7 %collective-permute-start.6 = (bf16[512,128]{1,0:T(8,128)(2,1)S(1)}, bf16[512,128]{1,0:T(8,128)(2,1)S(1)}, u32[]{:S(2)}, u32[]{:S(2)}) collective-permute-start(bf16[512,128]{1,0:T(8,128)(2,1)S(1)} %collective-permute-done.2.refs_3_), channel_id=1, source_target_pairs={{0,2},{1,3},{2,0},{3,1},{4,6},{5,7},{6,4},{7,5},{8,10},{9,11},{10,... | collective-permute-start | bytes 393224 | tf_op jit(solution)/shard_map/ppermute | solution.py:248
  20.4 12.7 %collective-permute-start.16 = (bf16[512,256]{1,0:T(8,128)(2,1)S(1)}, bf16[512,256]{1,0:T(8,128)(2,1)S(1)}, u32[]{:S(2)}, u32[]{:S(2)}) collective-permute-start(bf16[512,256]{1,0:T(8,128)(2,1)S(1)} %pad_maximum_fusion.refs_0_), channel_id=1, source_target_pairs={{0,4},{1,5},{2,6},{3,7},{4,0},{5,1},{6,2},{7,3},{8,12},{9,13},{10,... | collective-permute-start | bytes 786440 | tf_op jit(solution)/shard_map/ppermute | solution.py:248
  20.9 21.0 %collective-permute-start.17 = (bf16[512,256]{1,0:T(8,128)(2,1)S(1)}, bf16[512,256]{1,0:T(8,128)(2,1)S(1)}, u32[]{:S(2)}, u32[]{:S(2)}) collective-permute-start(bf16[512,256]{1,0:T(8,128)(2,1)S(1)} %pad_maximum_fusion.refs_0_), channel_id=1, source_target_pairs={{0,8},{1,9},{2,10},{3,11},{4,12},{5,13},{6,14},{7,15},{8,0},{9,1},... | collective-permute-start | bytes 786440 | tf_op jit(solution)/shard_map/ppermute | solution.py:248
  23.4 18.6 %collective-permute-start.18 = (bf16[512,256]{1,0:T(8,128)(2,1)S(1)}, bf16[512,256]{1,0:T(8,128)(2,1)S(1)}, u32[]{:S(2)}, u32[]{:S(2)}) collective-permute-start(bf16[512,256]{1,0:T(8,128)(2,1)S(1)} %pad_maximum_fusion.refs_0_), channel_id=1, source_target_pairs={{0,12},{1,13},{2,14},{3,15},{4,8},{5,9},{6,10},{7,11},{8,4},{9,5},... | collective-permute-start | bytes 786440 | tf_op jit(solution)/shard_map/ppermute | solution.py:248
  28.0 30.5 %collective-permute-start.12 = (bf16[2048,128]{1,0:T(8,128)(2,1)S(1)}, bf16[2048,128]{1,0:T(8,128)(2,1)S(1)}, u32[]{:S(2)}, u32[]{:S(2)}) collective-permute-start(bf16[2048,128]{1,0:T(8,128)(2,1)S(1)} %get-tuple-element.51), channel_id=1, source_target_pairs={{0,2},{1,3},{2,0},{3,1},{4,6},{5,7},{6,4},{7,5},{8,10},{9,11},{10,... | collective-permute-start | bytes 1572872 | tf_op jit(solution)/shard_map/ppermute | solution.py:248
  30.6 24.0 %collective-permute-start.8 = (bf16[1536,128]{1,0:T(8,128)(2,1)S(1)}, bf16[1536,128]{1,0:T(8,128)(2,1)S(1)}, u32[]{:S(2)}, u32[]{:S(2)}) collective-permute-start(bf16[1536,128]{1,0:T(8,128)(2,1)S(1)} %get-tuple-element.45), channel_id=1, source_target_pairs={{0,2},{1,3},{2,0},{3,1},{4,6},{5,7},{6,4},{7,5},{8,10},{9,11},{10,... | collective-permute-start | bytes 1179656 | tf_op jit(solution)/shard_map/ppermute | solution.py:248
  33.1 21.0 %collective-permute-start.7 = (bf16[512,128]{1,0:T(8,128)(2,1)S(1)}, bf16[512,128]{1,0:T(8,128)(2,1)S(1)}, u32[]{:S(2)}, u32[]{:S(2)}) collective-permute-start(bf16[512,128]{1,0:T(8,128)(2,1)S(1)} %get-tuple-element.44), channel_id=1, source_target_pairs={{0,2},{1,3},{2,0},{3,1},{4,6},{5,7},{6,4},{7,5},{8,10},{9,11},{10,... | collective-permute-start | bytes 393224 | tf_op jit(solution)/shard_map/ppermute | solution.py:248
  43.8 19.4 %collective-permute-start.25 = (bf16[1536,128]{1,0:T(8,128)(2,1)S(1)}, bf16[1536,128]{1,0:T(8,128)(2,1)S(1)}, u32[]{:S(2)}, u32[]{:S(2)}) collective-permute-start(bf16[1536,128]{1,0:T(8,128)(2,1)S(1)} %get-tuple-element.69), channel_id=1, source_target_pairs={{0,2},{1,3},{2,0},{3,1},{4,6},{5,7},{6,4},{7,5},{8,10},{9,11},{10,... | collective-permute-start | bytes 1179656 | tf_op jit(solution)/shard_map/ppermute | solution.py:248
  46.2 19.4 %collective-permute-start.24 = (bf16[512,128]{1,0:T(8,128)(2,1)S(1)}, bf16[512,128]{1,0:T(8,128)(2,1)S(1)}, u32[]{:S(2)}, u32[]{:S(2)}) collective-permute-start(bf16[512,128]{1,0:T(8,128)(2,1)S(1)} %get-tuple-element.67), channel_id=1, source_target_pairs={{0,2},{1,3},{2,0},{3,1},{4,6},{5,7},{6,4},{7,5},{8,10},{9,11},{10,... | collective-permute-start | bytes 393224 | tf_op jit(solution)/shard_map/ppermute | solution.py:248
  54.1 19.2 %collective-permute-start.19 = (bf16[2048,128]{1,0:T(8,128)(2,1)S(1)}, bf16[2048,128]{1,0:T(8,128)(2,1)S(1)}, u32[]{:S(2)}, u32[]{:S(2)}) collective-permute-start(bf16[2048,128]{1,0:T(8,128)(2,1)S(1)} %get-tuple-element.57), channel_id=1, source_target_pairs={{0,2},{1,3},{2,0},{3,1},{4,6},{5,7},{6,4},{7,5},{8,10},{9,11},{10,... | collective-permute-start | bytes 1572872 | tf_op jit(solution)/shard_map/ppermute | solution.py:248
  57.1 21.0 %collective-permute-start.10 = (bf16[128,512]{1,0:T(8,128)(2,1)S(1)}, bf16[128,512]{1,0:T(8,128)(2,1)S(1)}, u32[]{:S(2)}, u32[]{:S(2)}) collective-permute-start(bf16[128,512]{1,0:T(8,128)(2,1)S(1)} %get-tuple-element.48), channel_id=1, source_target_pairs={{0,8},{1,9},{2,10},{3,11},{4,12},{5,13},{6,14},{7,15},{8,0},{9,1},... | collective-permute-start | bytes 393224 | tf_op jit(solution)/shard_map/ppermute | solution.py:248
  58.6 20.7 %collective-permute-start.11 = (bf16[128,512]{1,0:T(8,128)(2,1)S(1)}, bf16[128,512]{1,0:T(8,128)(2,1)S(1)}, u32[]{:S(2)}, u32[]{:S(2)}) collective-permute-start(bf16[128,512]{1,0:T(8,128)(2,1)S(1)} %get-tuple-element.49), channel_id=1, source_target_pairs={{0,12},{1,13},{2,14},{3,15},{4,8},{5,9},{6,10},{7,11},{8,4},{9,5},... | collective-permute-start | bytes 393224 | tf_op jit(solution)/shard_map/ppermute | solution.py:248
  63.2 16.7 %collective-permute-start.9 = (bf16[128,512]{1,0:T(8,128)(2,1)S(1)}, bf16[128,512]{1,0:T(8,128)(2,1)S(1)}, u32[]{:S(2)}, u32[]{:S(2)}) collective-permute-start(bf16[128,512]{1,0:T(8,128)(2,1)S(1)} %get-tuple-element.47), channel_id=1, source_target_pairs={{0,4},{1,5},{2,6},{3,7},{4,0},{5,1},{6,2},{7,3},{8,12},{9,13},{10,... | collective-permute-start | bytes 393224 | tf_op jit(solution)/shard_map/ppermute | solution.py:248
  65.6 14.9 %collective-permute-start.13 = (bf16[128,512]{1,0:T(8,128)(2,1)S(1)}, bf16[128,512]{1,0:T(8,128)(2,1)S(1)}, u32[]{:S(2)}, u32[]{:S(2)}) collective-permute-start(bf16[128,512]{1,0:T(8,128)(2,1)S(1)} %get-tuple-element.53), channel_id=1, source_target_pairs={{0,4},{1,5},{2,6},{3,7},{4,0},{5,1},{6,2},{7,3},{8,12},{9,13},{10,... | collective-permute-start | bytes 393224 | tf_op jit(solution)/shard_map/ppermute | solution.py:248
  73.4 9.7 %collective-permute-start.14 = (bf16[128,512]{1,0:T(8,128)(2,1)S(1)}, bf16[128,512]{1,0:T(8,128)(2,1)S(1)}, u32[]{:S(2)}, u32[]{:S(2)}) collective-permute-start(bf16[128,512]{1,0:T(8,128)(2,1)S(1)} %get-tuple-element.54), channel_id=1, source_target_pairs={{0,8},{1,9},{2,10},{3,11},{4,12},{5,13},{6,14},{7,15},{8,0},{9,1},... | collective-permute-start | bytes 393224 | tf_op jit(solution)/shard_map/ppermute | solution.py:248
  78.1 14.0 %collective-permute-start.15 = (bf16[128,512]{1,0:T(8,128)(2,1)S(1)}, bf16[128,512]{1,0:T(8,128)(2,1)S(1)}, u32[]{:S(2)}, u32[]{:S(2)}) collective-permute-start(bf16[128,512]{1,0:T(8,128)(2,1)S(1)} %get-tuple-element.55), channel_id=1, source_target_pairs={{0,12},{1,13},{2,14},{3,15},{4,8},{5,9},{6,10},{7,11},{8,4},{9,5},... | collective-permute-start | bytes 393224 | tf_op jit(solution)/shard_map/ppermute | solution.py:248
  79.3 17.1 %collective-permute-start.26 = (bf16[64,2048]{1,0:T(8,128)(2,1)S(1)}, bf16[64,2048]{1,0:T(8,128)(2,1)S(1)}, u32[]{:S(2)}, u32[]{:S(2)}) collective-permute-start(bf16[64,2048]{1,0:T(8,128)(2,1)S(1)} %get-tuple-element.70), channel_id=1, source_target_pairs={{0,2},{1,3},{2,0},{3,1},{4,6},{5,7},{6,4},{7,5},{8,10},{9,11},{10,... | collective-permute-start | bytes 786440 | tf_op jit(solution)/shard_map/ppermute | solution.py:248
  79.9 12.2 %collective-permute-start.20 = (bf16[128,512]{1,0:T(8,128)(2,1)S(1)}, bf16[128,512]{1,0:T(8,128)(2,1)S(1)}, u32[]{:S(2)}, u32[]{:S(2)}) collective-permute-start(bf16[128,512]{1,0:T(8,128)(2,1)S(1)} %get-tuple-element.59), channel_id=1, source_target_pairs={{0,4},{1,5},{2,6},{3,7},{4,0},{5,1},{6,2},{7,3},{8,12},{9,13},{10,... | collective-permute-start | bytes 393224 | tf_op jit(solution)/shard_map/ppermute | solution.py:248
  80.5 15.0 %collective-permute-start.21 = (bf16[128,512]{1,0:T(8,128)(2,1)S(1)}, bf16[128,512]{1,0:T(8,128)(2,1)S(1)}, u32[]{:S(2)}, u32[]{:S(2)}) collective-permute-start(bf16[128,512]{1,0:T(8,128)(2,1)S(1)} %get-tuple-element.60), channel_id=1, source_target_pairs={{0,8},{1,9},{2,10},{3,11},{4,12},{5,13},{6,14},{7,15},{8,0},{9,1},... | collective-permute-start | bytes 393224 | tf_op jit(solution)/shard_map/ppermute | solution.py:248
  83.1 12.4 %collective-permute-start.22 = (bf16[128,512]{1,0:T(8,128)(2,1)S(1)}, bf16[128,512]{1,0:T(8,128)(2,1)S(1)}, u32[]{:S(2)}, u32[]{:S(2)}) collective-permute-start(bf16[128,512]{1,0:T(8,128)(2,1)S(1)} %get-tuple-element.61), channel_id=1, source_target_pairs={{0,12},{1,13},{2,14},{3,15},{4,8},{5,9},{6,10},{7,11},{8,4},{9,5},... | collective-permute-start | bytes 393224 | tf_op jit(solution)/shard_map/ppermute | solution.py:248
  95.7 10.9 %collective-permute-start.23 = (bf16[192,512]{1,0:T(8,128)(2,1)S(1)}, bf16[192,512]{1,0:T(8,128)(2,1)S(1)}, u32[]{:S(2)}, u32[]{:S(2)}) collective-permute-start(bf16[192,512]{1,0:T(8,128)(2,1)S(1)} %get-tuple-element.65), channel_id=1, source_target_pairs={{0,2},{1,3},{2,0},{3,1},{4,6},{5,7},{6,4},{7,5},{8,10},{9,11},{10,... | collective-permute-start | bytes 589832 | tf_op jit(solution)/shard_map/ppermute | solution.py:248
  96.5 5.1 %collective-permute-start.27 = (bf16[64,512]{1,0:T(8,128)(2,1)S(1)}, bf16[64,512]{1,0:T(8,128)(2,1)S(1)}, u32[]{:S(2)}, u32[]{:S(2)}) collective-permute-start(bf16[64,512]{1,0:T(8,128)(2,1)S(1)} %get-tuple-element.76), channel_id=1, source_target_pairs={{0,4},{1,5},{2,6},{3,7},{4,0},{5,1},{6,2},{7,3},{8,12},{9,13},{10,... | collective-permute-start | bytes 196616 | tf_op jit(solution)/shard_map/ppermute | solution.py:248
  99.1 6.2 %collective-permute-start.28 = (bf16[64,512]{1,0:T(8,128)(2,1)S(1)}, bf16[64,512]{1,0:T(8,128)(2,1)S(1)}, u32[]{:S(2)}, u32[]{:S(2)}) collective-permute-start(bf16[64,512]{1,0:T(8,128)(2,1)S(1)} %get-tuple-element.77), channel_id=1, source_target_pairs={{0,8},{1,9},{2,10},{3,11},{4,12},{5,13},{6,14},{7,15},{8,0},{9,1},... | collective-permute-start | bytes 196616 | tf_op jit(solution)/shard_map/ppermute | solution.py:248
  100.4 6.2 %collective-permute-start.29 = (bf16[64,512]{1,0:T(8,128)(2,1)S(1)}, bf16[64,512]{1,0:T(8,128)(2,1)S(1)}, u32[]{:S(2)}, u32[]{:S(2)}) collective-permute-start(bf16[64,512]{1,0:T(8,128)(2,1)S(1)} %get-tuple-element.78), channel_id=1, source_target_pairs={{0,12},{1,13},{2,14},{3,15},{4,8},{5,9},{6,10},{7,11},{8,4},{9,5},... | collective-permute-start | bytes 196616 | tf_op jit(solution)/shard_map/ppermute | solution.py:248

commit v3 on v1

--- a/solution.py
+++ b/solution.py
@@ -49,7 +49,7 @@
 
 def groups_of(shards):
     hops = list(range(shards - 1, -1, -1))
-    return [hops[: shards // 2], hops[shards // 2 :]]
+    return [hops[:1], hops[1:]]
 
 
 def load_body(half, place, source, out, arrived):
@@ -279,12 +279,10 @@
     for stage in range(stages - 1):
         got = gradients_of(place, factors, *sides[stage], shards)
         arrived.append([got[0]] + [moved(got[hop], hop) for hop in hops])
-    part, values, plan = width // HALVES, [], []
-    for some in (arrived[:-1], arrived[-1:]):
-        *kept, crossing = split_sums(some)
-        here = len(values)
-        values += [*kept, moved(crossing, 0, True)]
-        plan += [[(here + stage, 0, part), (here + len(kept), stage * part, (stage + 1) * part)] for stage in range(len(kept))]
+    *kept, crossing = split_sums(arrived)
+    part = width // HALVES
+    values = [*kept, moved(crossing, 0, True)]
+    plan = [[(stage, 0, part), (len(kept), stage * part, (stage + 1) * part)] for stage in range(len(kept))]
 
     owns, fars = sides[-1]
     groups = groups_of(shards)

time: 110 us -> 117 us (1.064)
  waiting for transfers between devices: 28.9 us -> 44.5 us
  starting transfers between devices: 50.6 us -> 42.9 us
    ppermute x32 -> x31, waiting for transfers between devices: 28.9 us -> 44.5 us  [moved(): return lax.ppermute(value, AXES, pairs)]
    ppermute x32 -> x31, starting transfers between devices: 50.6 us -> 42.9 us  [moved(): return lax.ppermute(value, AXES, pairs)]
  transfers between devices with their start and end apart: 32 -> 31, of which waited for: 7 -> 11; matrix products, arithmetic and copies ran while one was open for 1% -> 1% of each run, Pallas kernels for 25% -> 24%
where the time goes in v3:
time: 117 us
  waiting for transfers between devices  44.5 us (38%)
  starting transfers between devices  42.9 us (37%)
  Pallas kernels  28.7 us (25%)
    ppermute x31, waiting for transfers between devices, moved(): return lax.ppermute(value, AXES, pairs)  44.5 us
    ppermute x31, starting transfers between devices, moved(): return lax.ppermute(value, AXES, pairs)  42.9 us
    pallas_call x6, Pallas kernels, amplitudes_of(): pl.pallas_call(functools.partial(amplitude_body, shards, *vectors), in_sp...  10.5 us
    pallas_call x5, Pallas kernels, gradients_of(): pl.pallas_call(functools.partial(gradient_body, shards, len(owns), first,...  9.98 us
    pallas_call x2, Pallas kernels, loaded(): pl.pallas_call(functools.partial(load_body, half), in_specs=[SMEM, pl.Blo...  7 us
  transfers between devices with their start and end apart: 31, of which 11 were waited for; matrix products, arithmetic and copies ran while one was open for 1% of the time, Pallas kernels for 24%

profile of v3, /device:TPU:0, one launch (start us, length us, event | category | flops | bytes accessed | tf_op | source)
XLA Modules:
  0.0 117.3 jit_solution(9824929470670191259)
XLA Ops:
  0.0 3.0 %collective-permute-start.3 = (bf16[2,512,128]{2,1,0:T(8,128)(2,1)}, bf16[2,512,128]{2,1,0:T(8,128)(2,1)S(1)}, u32[]{:S(2)}, u32[]{:S(2)}) collective-permute-start(bf16[2,512,128]{2,1,0:T(8,128)(2,1)} %param.3), channel_id=1, source_target_pairs={{0,2},{1,3},{2,0},{3,1},{4,6},{5,7},{6,4},{7,5},{8,10},{9,11},{10,... | collective-permute-start | bytes 786440 | tf_op jit(solution)/shard_map/ppermute | solution.py:257
  4.0 1.6 %collective-permute-start = (bf16[512,128]{1,0:T(8,128)(2,1)S(1)}, bf16[512,128]{1,0:T(8,128)(2,1)S(1)}, u32[]{:S(2)}, u32[]{:S(2)}) collective-permute-start(bf16[512,128]{1,0:T(8,128)(2,1)S(1)} %get-tuple-element.80.refs_0_), channel_id=1, source_target_pairs={{0,4},{1,5},{2,6},{3,7},{4,0},{5,1},{6,2},{7,3},{8,12},{9,13},{10,... | collective-permute-start | bytes 393224 | tf_op jit(solution)/shard_map/ppermute | solution.py:257
  5.6 2.6 %collective-permute-start.1 = (bf16[512,128]{1,0:T(8,128)(2,1)S(1)}, bf16[512,128]{1,0:T(8,128)(2,1)S(1)}, u32[]{:S(2)}, u32[]{:S(2)}) collective-permute-start(bf16[512,128]{1,0:T(8,128)(2,1)S(1)} %get-tuple-element.80.refs_0_), channel_id=1, source_target_pairs={{0,8},{1,9},{2,10},{3,11},{4,12},{5,13},{6,14},{7,15},{8,0},{9,1},... | collective-permute-start | bytes 393224 | tf_op jit(solution)/shard_map/ppermute | solution.py:257
  8.4 3.5 %shard_map.31.refs_5_.factors.refs_3_ = bf16[32,64,2048]{2,1,0:T(8,128)(2,1)S(1)} custom-call(s32[1]{0:T(128)} %bitcast.place, bf16[32,128,2048]{2,1,0:T(8,128)(2,1)} %source.3), custom_call_target="tpu_custom_call" | custom-call | tf_op jit(solution)/shard_map/pallas_call | solution.py:70
  11.9 3.5 %shard_map.28.factors.refs_4_.refs_2_ = bf16[32,64,2048]{2,1,0:T(8,128)(2,1)S(1)} custom-call(s32[1]{0:T(128)} %bitcast.place, bf16[32,128,2048]{2,1,0:T(8,128)(2,1)} %source.3), custom_call_target="tpu_custom_call" | custom-call | tf_op jit(solution)/shard_map/pallas_call | solution.py:70
  15.8 2.4 %collective-permute-done.1.refs_2_ = bf16[512,128]{1,0:T(8,128)(2,1)S(1)} collective-permute-done((bf16[512,128]{1,0:T(8,128)(2,1)S(1)}, bf16[512,128]{1,0:T(8,128)(2,1)S(1)}, u32[]{:S(2)}, u32[]{:S(2)}) %collective-permute-start.1) | collective-permute-done | bytes 131104 | tf_op jit(solution)/shard_map/ppermute | solution.py:257
  18.8 1.5 %collective-permute-start.6 = (bf16[512,128]{1,0:T(8,128)(2,1)S(1)}, bf16[512,128]{1,0:T(8,128)(2,1)S(1)}, u32[]{:S(2)}, u32[]{:S(2)}) collective-permute-start(bf16[512,128]{1,0:T(8,128)(2,1)S(1)} %collective-permute-done.2.refs_3_), channel_id=1, source_target_pairs={{0,2},{1,3},{2,0},{3,1},{4,6},{5,7},{6,4},{7,5},{8,10},{9,11},{10,... | collective-permute-start | bytes 393224 | tf_op jit(solution)/shard_map/ppermute | solution.py:257
  20.9 2.5 %collective-permute-start.17 = (bf16[512,256]{1,0:T(8,128)(2,1)S(1)}, bf16[512,256]{1,0:T(8,128)(2,1)S(1)}, u32[]{:S(2)}, u32[]{:S(2)}) collective-permute-start(bf16[512,256]{1,0:T(8,128)(2,1)S(1)} %pad_maximum_fusion.refs_0_), channel_id=1, source_target_pairs={{0,8},{1,9},{2,10},{3,11},{4,12},{5,13},{6,14},{7,15},{8,0},{9,1},... | collective-permute-start | bytes 786440 | tf_op jit(solution)/shard_map/ppermute | solution.py:257
  23.4 2.1 %collective-permute-start.18 = (bf16[512,256]{1,0:T(8,128)(2,1)S(1)}, bf16[512,256]{1,0:T(8,128)(2,1)S(1)}, u32[]{:S(2)}, u32[]{:S(2)}) collective-permute-start(bf16[512,256]{1,0:T(8,128)(2,1)S(1)} %pad_maximum_fusion.refs_0_), channel_id=1, source_target_pairs={{0,12},{1,13},{2,14},{3,15},{4,8},{5,9},{6,10},{7,11},{8,4},{9,5},... | collective-permute-start | bytes 786440 | tf_op jit(solution)/shard_map/ppermute | solution.py:257
  25.5 2.5 %shard_map.33 = (bf16[2048,128]{1,0:T(8,128)(2,1)S(1)}, bf16[2048,128]{1,0:T(8,128)(2,1)S(1)}) custom-call(s32[1]{0:T(128)} %bitcast.place, bf16[32,64,2048]{2,1,0:T(8,128)(2,1)S(1)} %shard_map.31.refs_5_.factors.refs_3_, bf16[512,128]{1,0:T(8,128)(2,1)S(1)} %get-tuple-element.80.refs_0_, bf16[512,128]{1,0:T(8,128)(2,1)S(1)} %collective-permute-done.refs_1_, ...), custom_call_target="tpu_custom_call" | custom-call | flops 2147483648 | bytes 8388608 | tf_op jit(solution)/shard_map/pallas_call | solution.py:102
  28.6 2.0 %shard_map.30 = (bf16[1536,128]{1,0:T(8,128)(2,1)S(1)}, bf16[1536,128]{1,0:T(8,128)(2,1)S(1)}) custom-call(s32[1]{0:T(128)} %bitcast.place, bf16[32,64,2048]{2,1,0:T(8,128)(2,1)S(1)} %shard_map.28.factors.refs_4_.refs_2_, bf16[512,128]{1,0:T(8,128)(2,1)S(1)} %get-tuple-element.80.refs_0_, bf16[512,128]{1,0:T(8,128)(2,1)S(1)} %collective-permute-done.refs_1_, ...), custom_call_target="tpu_custom_call" | custom-call | flops 1610612736 | bytes 6291456 | tf_op jit(solution)/shard_map/pallas_call | solution.py:102
  30.6 1.6 %collective-permute-start.8 = (bf16[1536,128]{1,0:T(8,128)(2,1)S(1)}, bf16[1536,128]{1,0:T(8,128)(2,1)S(1)}, u32[]{:S(2)}, u32[]{:S(2)}) collective-permute-start(bf16[1536,128]{1,0:T(8,128)(2,1)S(1)} %get-tuple-element.45), channel_id=1, source_target_pairs={{0,2},{1,3},{2,0},{3,1},{4,6},{5,7},{6,4},{7,5},{8,10},{9,11},{10,... | collective-permute-start | bytes 1179656 | tf_op jit(solution)/shard_map/ppermute | solution.py:257
  33.7 8.2 %collective-permute-done.17.refs_2_ = bf16[512,256]{1,0:T(8,128)(2,1)S(1)} collective-permute-done((bf16[512,256]{1,0:T(8,128)(2,1)S(1)}, bf16[512,256]{1,0:T(8,128)(2,1)S(1)}, u32[]{:S(2)}, u32[]{:S(2)}) %collective-permute-start.17) | collective-permute-done | bytes 262176 | tf_op jit(solution)/shard_map/ppermute | solution.py:257
  41.9 2.4 %shard_map.35 = (bf16[2048,128]{1,0:T(8,128)(2,1)S(1)}, bf16[2048,128]{1,0:T(8,128)(2,1)S(1)}) custom-call(s32[1]{0:T(128)} %bitcast.place, bf16[32,64,2048]{2,1,0:T(8,128)(2,1)S(1)} %shard_map.28.factors.refs_4_.refs_2_, bf16[512,256]{1,0:T(8,128)(2,1)S(1)} %pad_maximum_fusion.refs_0_, bf16[512,256]{1,0:T(8,128)(2,1)S(1)} %collective-permute-done.16.refs_1_, ...), custom_call_target="tpu_custom_call" | custom-call | flops 2147483648 | bytes 8388608 | tf_op jit(solution)/shard_map/pallas_call | solution.py:102
  44.4 1.6 %collective-permute-start.19 = (bf16[2048,128]{1,0:T(8,128)(2,1)S(1)}, bf16[2048,128]{1,0:T(8,128)(2,1)S(1)}, u32[]{:S(2)}, u32[]{:S(2)}) collective-permute-start(bf16[2048,128]{1,0:T(8,128)(2,1)S(1)} %get-tuple-element.57), channel_id=1, source_target_pairs={{0,2},{1,3},{2,0},{3,1},{4,6},{5,7},{6,4},{7,5},{8,10},{9,11},{10,... | collective-permute-start | bytes 1572872 | tf_op jit(solution)/shard_map/ppermute | solution.py:257
  45.9 1.9 %shard_map.39 = (bf16[1536,128]{1,0:T(8,128)(2,1)S(1)}, bf16[1536,128]{1,0:T(8,128)(2,1)S(1)}) custom-call(s32[1]{0:T(128)} %bitcast.place, bf16[32,64,2048]{2,1,0:T(8,128)(2,1)S(1)} %shard_map.31.refs_5_.factors.refs_3_, bf16[512,256]{1,0:T(8,128)(2,1)S(1)} %pad_maximum_fusion.refs_0_, bf16[512,256]{1,0:T(8,128)(2,1)S(1)} %collective-permute-done.16.refs_1_, ...), custom_call_target="tpu_custom_call" | custom-call | flops 1610612736 | bytes 6291456 | tf_op jit(solution)/shard_map/pallas_call | solution.py:102
  49.2 4.9 %collective-permute-done.7.refs_2_ = bf16[512,128]{1,0:T(8,128)(2,1)S(1)} collective-permute-done((bf16[512,128]{1,0:T(8,128)(2,1)S(1)}, bf16[512,128]{1,0:T(8,128)(2,1)S(1)}, u32[]{:S(2)}, u32[]{:S(2)}) %collective-permute-start.7) | collective-permute-done | bytes 131104 | tf_op jit(solution)/shard_map/ppermute | solution.py:257
  54.7 2.4 %shard_map.32 = (f32[128,512]{1,0:T(8,128)S(1)}, bf16[128,512]{1,0:T(8,128)(2,1)S(1)}, bf16[128,512]{1,0:T(8,128)(2,1)S(1)}, bf16[128,512]{1,0:T(8,128)(2,1)S(1)}) custom-call(s32[1]{0:T(128)} %bitcast.place, bf16[512,128]{1,0:T(8,128)(2,1)S(1)} %get-tuple-element.42.refs_0_, bf16[1536,128]{1,0:T(8,128)(2,1)S(1)} %get-tuple-element.43.refs_1_, ...), custom_call_target="tpu_custom_call" | custom-call | flops 2147483648 | bytes 16777216 | tf_op jit(solution)/shard_map/pallas_call | solution.py:158
  58.4 2.2 %collective-permute-start.11 = (bf16[128,512]{1,0:T(8,128)(2,1)S(1)}, bf16[128,512]{1,0:T(8,128)(2,1)S(1)}, u32[]{:S(2)}, u32[]{:S(2)}) collective-permute-start(bf16[128,512]{1,0:T(8,128)(2,1)S(1)} %get-tuple-element.49), channel_id=1, source_target_pairs={{0,12},{1,13},{2,14},{3,15},{4,8},{5,9},{6,10},{7,11},{8,4},{9,5},... | collective-permute-start | bytes 393224 | tf_op jit(solution)/shard_map/ppermute | solution.py:257
  60.6 2.6 %shard_map.34 = (f32[128,512]{1,0:T(8,128)S(1)}, bf16[128,512]{1,0:T(8,128)(2,1)S(1)}, bf16[128,512]{1,0:T(8,128)(2,1)S(1)}, bf16[128,512]{1,0:T(8,128)(2,1)S(1)}) custom-call(s32[1]{0:T(128)} %bitcast.place, bf16[2048,128]{1,0:T(8,128)(2,1)S(1)} %get-tuple-element.50.refs_0_, bf16[2048,128]{1,0:T(8,128)(2,1)S(1)} %collective-permute-done.12.refs_1_, ...), custom_call_target="tpu_custom_call" | custom-call | flops 2147483648 | bytes 16777216 | tf_op jit(solution)/shard_map/pallas_call | solution.py:158
  63.2 10.2 %collective-permute-done.24.refs_1_ = bf16[512,128]{1,0:T(8,128)(2,1)S(1)} collective-permute-done((bf16[512,128]{1,0:T(8,128)(2,1)S(1)}, bf16[512,128]{1,0:T(8,128)(2,1)S(1)}, u32[]{:S(2)}, u32[]{:S(2)}) %collective-permute-start.24) | collective-permute-done | bytes 131104 | tf_op jit(solution)/shard_map/ppermute | solution.py:257
  75.4 2.4 %shard_map.36 = (f32[128,512]{1,0:T(8,128)S(1)}, bf16[128,512]{1,0:T(8,128)(2,1)S(1)}, bf16[128,512]{1,0:T(8,128)(2,1)S(1)}, bf16[128,512]{1,0:T(8,128)(2,1)S(1)}) custom-call(s32[1]{0:T(128)} %bitcast.place, bf16[2048,128]{1,0:T(8,128)(2,1)S(1)} %get-tuple-element.56.refs_0_, bf16[2048,128]{1,0:T(8,128)(2,1)S(1)} %collective-permute-done.19.refs_1_, ...), custom_call_target="tpu_custom_call" | custom-call | flops 2147483648 | bytes 16777216 | tf_op jit(solution)/shard_map/pallas_call | solution.py:158
  77.8 2.4 %collective-permute-start.14 = (bf16[128,512]{1,0:T(8,128)(2,1)S(1)}, bf16[128,512]{1,0:T(8,128)(2,1)S(1)}, u32[]{:S(2)}, u32[]{:S(2)}) collective-permute-start(bf16[128,512]{1,0:T(8,128)(2,1)S(1)} %get-tuple-element.54), channel_id=1, source_target_pairs={{0,8},{1,9},{2,10},{3,11},{4,12},{5,13},{6,14},{7,15},{8,0},{9,1},... | collective-permute-start | bytes 393224 | tf_op jit(solution)/shard_map/ppermute | solution.py:257
  82.2 3.3 %collective-permute-start.21 = (bf16[128,512]{1,0:T(8,128)(2,1)S(1)}, bf16[128,512]{1,0:T(8,128)(2,1)S(1)}, u32[]{:S(2)}, u32[]{:S(2)}) collective-permute-start(bf16[128,512]{1,0:T(8,128)(2,1)S(1)} %get-tuple-element.60), channel_id=1, source_target_pairs={{0,8},{1,9},{2,10},{3,11},{4,12},{5,13},{6,14},{7,15},{8,0},{9,1},... | collective-permute-start | bytes 393224 | tf_op jit(solution)/shard_map/ppermute | solution.py:257
  85.5 2.2 %collective-permute-start.22 = (bf16[128,512]{1,0:T(8,128)(2,1)S(1)}, bf16[128,512]{1,0:T(8,128)(2,1)S(1)}, u32[]{:S(2)}, u32[]{:S(2)}) collective-permute-start(bf16[128,512]{1,0:T(8,128)(2,1)S(1)} %get-tuple-element.61), channel_id=1, source_target_pairs={{0,12},{1,13},{2,14},{3,15},{4,8},{5,9},{6,10},{7,11},{8,4},{9,5},... | collective-permute-start | bytes 393224 | tf_op jit(solution)/shard_map/ppermute | solution.py:257
  87.7 1.8 %shard_map.40.refs_4_ = f32[128,2048]{1,0:T(8,128)S(1)} custom-call(s32[1]{0:T(128)} %bitcast.place, bf16[1536,128]{1,0:T(8,128)(2,1)S(1)} %get-tuple-element.68.refs_0_, bf16[1536,128]{1,0:T(8,128)(2,1)S(1)} %collective-permute-done.25.refs_1_, bf16[32,64,2048]{2,1,0:T(8,128)(2,1)S(1)} %shard_map.28.factors.refs_4_.refs_2_, ...), custom_call_target="tpu_custom_call" | custom-call | flops 1610612736 | bytes 12582912 | tf_op jit(solution)/shard_map/pallas_call | solution.py:158
  91.4 7.9 %collective-permute-done.21.refs_10_ = bf16[128,512]{1,0:T(8,128)(2,1)S(1)} collective-permute-done((bf16[128,512]{1,0:T(8,128)(2,1)S(1)}, bf16[128,512]{1,0:T(8,128)(2,1)S(1)}, u32[]{:S(2)}, u32[]{:S(2)}) %collective-permute-start.21) | collective-permute-done | bytes 131104 | tf_op jit(solution)/shard_map/ppermute | solution.py:257
  101.6 4.3 %collective-permute-done.29.came = bf16[64,512]{1,0:T(8,128)(2,1)S(1)} collective-permute-done((bf16[64,512]{1,0:T(8,128)(2,1)S(1)}, bf16[64,512]{1,0:T(8,128)(2,1)S(1)}, u32[]{:S(2)}, u32[]{:S(2)}) %collective-permute-start.29) | collective-permute-done | bytes 65568 | tf_op jit(solution)/shard_map/ppermute | solution.py:257
  105.9 3.2 %collective-permute-start.30 = (bf16[64,512]{1,0:T(8,128)(2,1)S(1)}, bf16[64,512]{1,0:T(8,128)(2,1)S(1)}, u32[]{:S(2)}, u32[]{:S(2)}) collective-permute-start(bf16[64,512]{1,0:T(8,128)(2,1)S(1)} %shard_map.43), channel_id=1, source_target_pairs={{0,12},{1,13},{2,14},{3,15},{4,8},{5,9},{6,10},{7,11},{8,4},{9,5},... | collective-permute-start | bytes 196616 | tf_op jit(solution)/shard_map/ppermute | solution.py:257
  110.5 1.6 %collective-permute-done.30.refs_7_ = bf16[64,512]{1,0:T(8,128)(2,1)S(1)} collective-permute-done((bf16[64,512]{1,0:T(8,128)(2,1)S(1)}, bf16[64,512]{1,0:T(8,128)(2,1)S(1)}, u32[]{:S(2)}, u32[]{:S(2)}) %collective-permute-start.30) | collective-permute-done | bytes 65568 | tf_op jit(solution)/shard_map/ppermute | solution.py:257
  112.1 1.7 %collective-permute-done.27.refs_5_ = bf16[64,512]{1,0:T(8,128)(2,1)S(1)} collective-permute-done((bf16[64,512]{1,0:T(8,128)(2,1)S(1)}, bf16[64,512]{1,0:T(8,128)(2,1)S(1)}, u32[]{:S(2)}, u32[]{:S(2)}) %collective-permute-start.27) | collective-permute-done | bytes 65568 | tf_op jit(solution)/shard_map/ppermute | solution.py:257
  113.7 2.5 %collective-permute-done.28.refs_6_ = bf16[64,512]{1,0:T(8,128)(2,1)S(1)} collective-permute-done((bf16[64,512]{1,0:T(8,128)(2,1)S(1)}, bf16[64,512]{1,0:T(8,128)(2,1)S(1)}, u32[]{:S(2)}, u32[]{:S(2)}) %collective-permute-start.28) | collective-permute-done | bytes 65568 | tf_op jit(solution)/shard_map/ppermute | solution.py:257
  (50 shorter events, 18.7 us)
Async XLA Ops:
  0.0 20.3 %collective-permute-start.3 = (bf16[2,512,128]{2,1,0:T(8,128)(2,1)}, bf16[2,512,128]{2,1,0:T(8,128)(2,1)S(1)}, u32[]{:S(2)}, u32[]{:S(2)}) collective-permute-start(bf16[2,512,128]{2,1,0:T(8,128)(2,1)} %param.3), channel_id=1, source_target_pairs={{0,2},{1,3},{2,0},{3,1},{4,6},{5,7},{6,4},{7,5},{8,10},{9,11},{10,... | collective-permute-start | bytes 786440 | tf_op jit(solution)/shard_map/ppermute | solution.py:257
  4.0 11.5 %collective-permute-start = (bf16[512,128]{1,0:T(8,128)(2,1)S(1)}, bf16[512,128]{1,0:T(8,128)(2,1)S(1)}, u32[]{:S(2)}, u32[]{:S(2)}) collective-permute-start(bf16[512,128]{1,0:T(8,128)(2,1)S(1)} %get-tuple-element.80.refs_0_), channel_id=1, source_target_pairs={{0,4},{1,5},{2,6},{3,7},{4,0},{5,1},{6,2},{7,3},{8,12},{9,13},{10,... | collective-permute-start | bytes 393224 | tf_op jit(solution)/shard_map/ppermute | solution.py:257
  5.6 12.6 %collective-permute-start.1 = (bf16[512,128]{1,0:T(8,128)(2,1)S(1)}, bf16[512,128]{1,0:T(8,128)(2,1)S(1)}, u32[]{:S(2)}, u32[]{:S(2)}) collective-permute-start(bf16[512,128]{1,0:T(8,128)(2,1)S(1)} %get-tuple-element.80.refs_0_), channel_id=1, source_target_pairs={{0,8},{1,9},{2,10},{3,11},{4,12},{5,13},{6,14},{7,15},{8,0},{9,1},... | collective-permute-start | bytes 393224 | tf_op jit(solution)/shard_map/ppermute | solution.py:257
  8.2 10.6 %collective-permute-start.2 = (bf16[512,128]{1,0:T(8,128)(2,1)S(1)}, bf16[512,128]{1,0:T(8,128)(2,1)S(1)}, u32[]{:S(2)}, u32[]{:S(2)}) collective-permute-start(bf16[512,128]{1,0:T(8,128)(2,1)S(1)} %get-tuple-element.80.refs_0_), channel_id=1, source_target_pairs={{0,12},{1,13},{2,14},{3,15},{4,8},{5,9},{6,10},{7,11},{8,4},{9,5},... | collective-permute-start | bytes 393224 | tf_op jit(solution)/shard_map/ppermute | solution.py:257
  15.4 7.9 %collective-permute-start.4 = (bf16[512,128]{1,0:T(8,128)(2,1)S(1)}, bf16[512,128]{1,0:T(8,128)(2,1)S(1)}, u32[]{:S(2)}, u32[]{:S(2)}) collective-permute-start(bf16[512,128]{1,0:T(8,128)(2,1)S(1)} %collective-permute-done.refs_1_), channel_id=1, source_target_pairs={{0,2},{1,3},{2,0},{3,1},{4,6},{5,7},{6,4},{7,5},{8,10},{9,11},{10,... | collective-permute-start | bytes 393224 | tf_op jit(solution)/shard_map/ppermute | solution.py:257
  18.3 7.2 %collective-permute-start.5 = (bf16[512,128]{1,0:T(8,128)(2,1)S(1)}, bf16[512,128]{1,0:T(8,128)(2,1)S(1)}, u32[]{:S(2)}, u32[]{:S(2)}) collective-permute-start(bf16[512,128]{1,0:T(8,128)(2,1)S(1)} %collective-permute-done.1.refs_2_), channel_id=1, source_target_pairs={{0,2},{1,3},{2,0},{3,1},{4,6},{5,7},{6,4},{7,5},{8,10},{9,11},{10,... | collective-permute-start | bytes 393224 | tf_op jit(solution)/shard_map/ppermute | solution.py:257
  18.8 6.7 %collective-permute-start.6 = (bf16[512,128]{1,0:T(8,128)(2,1)S(1)}, bf16[512,128]{1,0:T(8,128)(2,1)S(1)}, u32[]{:S(2)}, u32[]{:S(2)}) collective-permute-start(bf16[512,128]{1,0:T(8,128)(2,1)S(1)} %collective-permute-done.2.refs_3_), channel_id=1, source_target_pairs={{0,2},{1,3},{2,0},{3,1},{4,6},{5,7},{6,4},{7,5},{8,10},{9,11},{10,... | collective-permute-start | bytes 393224 | tf_op jit(solution)/shard_map/ppermute | solution.py:257
  20.4 12.7 %collective-permute-start.16 = (bf16[512,256]{1,0:T(8,128)(2,1)S(1)}, bf16[512,256]{1,0:T(8,128)(2,1)S(1)}, u32[]{:S(2)}, u32[]{:S(2)}) collective-permute-start(bf16[512,256]{1,0:T(8,128)(2,1)S(1)} %pad_maximum_fusion.refs_0_), channel_id=1, source_target_pairs={{0,4},{1,5},{2,6},{3,7},{4,0},{5,1},{6,2},{7,3},{8,12},{9,13},{10,... | collective-permute-start | bytes 786440 | tf_op jit(solution)/shard_map/ppermute | solution.py:257
  20.9 21.0 %collective-permute-start.17 = (bf16[512,256]{1,0:T(8,128)(2,1)S(1)}, bf16[512,256]{1,0:T(8,128)(2,1)S(1)}, u32[]{:S(2)}, u32[]{:S(2)}) collective-permute-start(bf16[512,256]{1,0:T(8,128)(2,1)S(1)} %pad_maximum_fusion.refs_0_), channel_id=1, source_target_pairs={{0,8},{1,9},{2,10},{3,11},{4,12},{5,13},{6,14},{7,15},{8,0},{9,1},... | collective-permute-start | bytes 786440 | tf_op jit(solution)/shard_map/ppermute | solution.py:257
  23.4 18.6 %collective-permute-start.18 = (bf16[512,256]{1,0:T(8,128)(2,1)S(1)}, bf16[512,256]{1,0:T(8,128)(2,1)S(1)}, u32[]{:S(2)}, u32[]{:S(2)}) collective-permute-start(bf16[512,256]{1,0:T(8,128)(2,1)S(1)} %pad_maximum_fusion.refs_0_), channel_id=1, source_target_pairs={{0,12},{1,13},{2,14},{3,15},{4,8},{5,9},{6,10},{7,11},{8,4},{9,5},... | collective-permute-start | bytes 786440 | tf_op jit(solution)/shard_map/ppermute | solution.py:257
  28.0 30.4 %collective-permute-start.12 = (bf16[2048,128]{1,0:T(8,128)(2,1)S(1)}, bf16[2048,128]{1,0:T(8,128)(2,1)S(1)}, u32[]{:S(2)}, u32[]{:S(2)}) collective-permute-start(bf16[2048,128]{1,0:T(8,128)(2,1)S(1)} %get-tuple-element.51), channel_id=1, source_target_pairs={{0,2},{1,3},{2,0},{3,1},{4,6},{5,7},{6,4},{7,5},{8,10},{9,11},{10,... | collective-permute-start | bytes 1572872 | tf_op jit(solution)/shard_map/ppermute | solution.py:257
  30.6 24.0 %collective-permute-start.8 = (bf16[1536,128]{1,0:T(8,128)(2,1)S(1)}, bf16[1536,128]{1,0:T(8,128)(2,1)S(1)}, u32[]{:S(2)}, u32[]{:S(2)}) collective-permute-start(bf16[1536,128]{1,0:T(8,128)(2,1)S(1)} %get-tuple-element.45), channel_id=1, source_target_pairs={{0,2},{1,3},{2,0},{3,1},{4,6},{5,7},{6,4},{7,5},{8,10},{9,11},{10,... | collective-permute-start | bytes 1179656 | tf_op jit(solution)/shard_map/ppermute | solution.py:257
  33.1 21.0 %collective-permute-start.7 = (bf16[512,128]{1,0:T(8,128)(2,1)S(1)}, bf16[512,128]{1,0:T(8,128)(2,1)S(1)}, u32[]{:S(2)}, u32[]{:S(2)}) collective-permute-start(bf16[512,128]{1,0:T(8,128)(2,1)S(1)} %get-tuple-element.44), channel_id=1, source_target_pairs={{0,2},{1,3},{2,0},{3,1},{4,6},{5,7},{6,4},{7,5},{8,10},{9,11},{10,... | collective-permute-start | bytes 393224 | tf_op jit(solution)/shard_map/ppermute | solution.py:257
  44.4 29.9 %collective-permute-start.19 = (bf16[2048,128]{1,0:T(8,128)(2,1)S(1)}, bf16[2048,128]{1,0:T(8,128)(2,1)S(1)}, u32[]{:S(2)}, u32[]{:S(2)}) collective-permute-start(bf16[2048,128]{1,0:T(8,128)(2,1)S(1)} %get-tuple-element.57), channel_id=1, source_target_pairs={{0,2},{1,3},{2,0},{3,1},{4,6},{5,7},{6,4},{7,5},{8,10},{9,11},{10,... | collective-permute-start | bytes 1572872 | tf_op jit(solution)/shard_map/ppermute | solution.py:257
  47.8 37.8 %collective-permute-start.25 = (bf16[1536,128]{1,0:T(8,128)(2,1)S(1)}, bf16[1536,128]{1,0:T(8,128)(2,1)S(1)}, u32[]{:S(2)}, u32[]{:S(2)}) collective-permute-start(bf16[1536,128]{1,0:T(8,128)(2,1)S(1)} %get-tuple-element.69), channel_id=1, source_target_pairs={{0,2},{1,3},{2,0},{3,1},{4,6},{5,7},{6,4},{7,5},{8,10},{9,11},{10,... | collective-permute-start | bytes 1179656 | tf_op jit(solution)/shard_map/ppermute | solution.py:257
  54.1 19.2 %collective-permute-start.24 = (bf16[512,128]{1,0:T(8,128)(2,1)S(1)}, bf16[512,128]{1,0:T(8,128)(2,1)S(1)}, u32[]{:S(2)}, u32[]{:S(2)}) collective-permute-start(bf16[512,128]{1,0:T(8,128)(2,1)S(1)} %get-tuple-element.67), channel_id=1, source_target_pairs={{0,2},{1,3},{2,0},{3,1},{4,6},{5,7},{6,4},{7,5},{8,10},{9,11},{10,... | collective-permute-start | bytes 393224 | tf_op jit(solution)/shard_map/ppermute | solution.py:257
  57.1 20.7 %collective-permute-start.10 = (bf16[128,512]{1,0:T(8,128)(2,1)S(1)}, bf16[128,512]{1,0:T(8,128)(2,1)S(1)}, u32[]{:S(2)}, u32[]{:S(2)}) collective-permute-start(bf16[128,512]{1,0:T(8,128)(2,1)S(1)} %get-tuple-element.48), channel_id=1, source_target_pairs={{0,8},{1,9},{2,10},{3,11},{4,12},{5,13},{6,14},{7,15},{8,0},{9,1},... | collective-permute-start | bytes 393224 | tf_op jit(solution)/shard_map/ppermute | solution.py:257
  58.4 21.8 %collective-permute-start.11 = (bf16[128,512]{1,0:T(8,128)(2,1)S(1)}, bf16[128,512]{1,0:T(8,128)(2,1)S(1)}, u32[]{:S(2)}, u32[]{:S(2)}) collective-permute-start(bf16[128,512]{1,0:T(8,128)(2,1)S(1)} %get-tuple-element.49), channel_id=1, source_target_pairs={{0,12},{1,13},{2,14},{3,15},{4,8},{5,9},{6,10},{7,11},{8,4},{9,5},... | collective-permute-start | bytes 393224 | tf_op jit(solution)/shard_map/ppermute | solution.py:257
  73.4 8.1 %collective-permute-start.9 = (bf16[128,512]{1,0:T(8,128)(2,1)S(1)}, bf16[128,512]{1,0:T(8,128)(2,1)S(1)}, u32[]{:S(2)}, u32[]{:S(2)}) collective-permute-start(bf16[128,512]{1,0:T(8,128)(2,1)S(1)} %get-tuple-element.47), channel_id=1, source_target_pairs={{0,4},{1,5},{2,6},{3,7},{4,0},{5,1},{6,2},{7,3},{8,12},{9,13},{10,... | collective-permute-start | bytes 393224 | tf_op jit(solution)/shard_map/ppermute | solution.py:257
  74.3 7.9 %collective-permute-start.13 = (bf16[128,512]{1,0:T(8,128)(2,1)S(1)}, bf16[128,512]{1,0:T(8,128)(2,1)S(1)}, u32[]{:S(2)}, u32[]{:S(2)}) collective-permute-start(bf16[128,512]{1,0:T(8,128)(2,1)S(1)} %get-tuple-element.53), channel_id=1, source_target_pairs={{0,4},{1,5},{2,6},{3,7},{4,0},{5,1},{6,2},{7,3},{8,12},{9,13},{10,... | collective-permute-start | bytes 393224 | tf_op jit(solution)/shard_map/ppermute | solution.py:257
  77.8 12.9 %collective-permute-start.14 = (bf16[128,512]{1,0:T(8,128)(2,1)S(1)}, bf16[128,512]{1,0:T(8,128)(2,1)S(1)}, u32[]{:S(2)}, u32[]{:S(2)}) collective-permute-start(bf16[128,512]{1,0:T(8,128)(2,1)S(1)} %get-tuple-element.54), channel_id=1, source_target_pairs={{0,8},{1,9},{2,10},{3,11},{4,12},{5,13},{6,14},{7,15},{8,0},{9,1},... | collective-permute-start | bytes 393224 | tf_op jit(solution)/shard_map/ppermute | solution.py:257
  80.2 11.2 %collective-permute-start.15 = (bf16[128,512]{1,0:T(8,128)(2,1)S(1)}, bf16[128,512]{1,0:T(8,128)(2,1)S(1)}, u32[]{:S(2)}, u32[]{:S(2)}) collective-permute-start(bf16[128,512]{1,0:T(8,128)(2,1)S(1)} %get-tuple-element.55), channel_id=1, source_target_pairs={{0,12},{1,13},{2,14},{3,15},{4,8},{5,9},{6,10},{7,11},{8,4},{9,5},... | collective-permute-start | bytes 393224 | tf_op jit(solution)/shard_map/ppermute | solution.py:257
  81.4 9.9 %collective-permute-start.20 = (bf16[128,512]{1,0:T(8,128)(2,1)S(1)}, bf16[128,512]{1,0:T(8,128)(2,1)S(1)}, u32[]{:S(2)}, u32[]{:S(2)}) collective-permute-start(bf16[128,512]{1,0:T(8,128)(2,1)S(1)} %get-tuple-element.59), channel_id=1, source_target_pairs={{0,4},{1,5},{2,6},{3,7},{4,0},{5,1},{6,2},{7,3},{8,12},{9,13},{10,... | collective-permute-start | bytes 393224 | tf_op jit(solution)/shard_map/ppermute | solution.py:257
  82.2 17.1 %collective-permute-start.21 = (bf16[128,512]{1,0:T(8,128)(2,1)S(1)}, bf16[128,512]{1,0:T(8,128)(2,1)S(1)}, u32[]{:S(2)}, u32[]{:S(2)}) collective-permute-start(bf16[128,512]{1,0:T(8,128)(2,1)S(1)} %get-tuple-element.60), channel_id=1, source_target_pairs={{0,8},{1,9},{2,10},{3,11},{4,12},{5,13},{6,14},{7,15},{8,0},{9,1},... | collective-permute-start | bytes 393224 | tf_op jit(solution)/shard_map/ppermute | solution.py:257
  85.5 13.8 %collective-permute-start.22 = (bf16[128,512]{1,0:T(8,128)(2,1)S(1)}, bf16[128,512]{1,0:T(8,128)(2,1)S(1)}, u32[]{:S(2)}, u32[]{:S(2)}) collective-permute-start(bf16[128,512]{1,0:T(8,128)(2,1)S(1)} %get-tuple-element.61), channel_id=1, source_target_pairs={{0,12},{1,13},{2,14},{3,15},{4,8},{5,9},{6,10},{7,11},{8,4},{9,5},... | collective-permute-start | bytes 393224 | tf_op jit(solution)/shard_map/ppermute | solution.py:257
  90.7 18.4 %collective-permute-start.26 = (bf16[64,1536]{1,0:T(8,128)(2,1)S(1)}, bf16[64,1536]{1,0:T(8,128)(2,1)S(1)}, u32[]{:S(2)}, u32[]{:S(2)}) collective-permute-start(bf16[64,1536]{1,0:T(8,128)(2,1)S(1)} %get-tuple-element.70), channel_id=1, source_target_pairs={{0,2},{1,3},{2,0},{3,1},{4,6},{5,7},{6,4},{7,5},{8,10},{9,11},{10,... | collective-permute-start | bytes 589832 | tf_op jit(solution)/shard_map/ppermute | solution.py:257
  99.5 16.8 %collective-permute-start.23 = (bf16[192,512]{1,0:T(8,128)(2,1)S(1)}, bf16[192,512]{1,0:T(8,128)(2,1)S(1)}, u32[]{:S(2)}, u32[]{:S(2)}) collective-permute-start(bf16[192,512]{1,0:T(8,128)(2,1)S(1)} %get-tuple-element.65), channel_id=1, source_target_pairs={{0,2},{1,3},{2,0},{3,1},{4,6},{5,7},{6,4},{7,5},{8,10},{9,11},{10,... | collective-permute-start | bytes 589832 | tf_op jit(solution)/shard_map/ppermute | solution.py:257
  100.2 5.7 %collective-permute-start.29 = (bf16[64,512]{1,0:T(8,128)(2,1)S(1)}, bf16[64,512]{1,0:T(8,128)(2,1)S(1)}, u32[]{:S(2)}, u32[]{:S(2)}) collective-permute-start(bf16[64,512]{1,0:T(8,128)(2,1)S(1)} %get-tuple-element.77), channel_id=1, source_target_pairs={{0,2},{1,3},{2,0},{3,1},{4,6},{5,7},{6,4},{7,5},{8,10},{9,11},{10,... | collective-permute-start | bytes 196616 | tf_op jit(solution)/shard_map/ppermute | solution.py:257
  105.9 6.1 %collective-permute-start.30 = (bf16[64,512]{1,0:T(8,128)(2,1)S(1)}, bf16[64,512]{1,0:T(8,128)(2,1)S(1)}, u32[]{:S(2)}, u32[]{:S(2)}) collective-permute-start(bf16[64,512]{1,0:T(8,128)(2,1)S(1)} %shard_map.43), channel_id=1, source_target_pairs={{0,12},{1,13},{2,14},{3,15},{4,8},{5,9},{6,10},{7,11},{8,4},{9,5},... | collective-permute-start | bytes 196616 | tf_op jit(solution)/shard_map/ppermute | solution.py:257
  109.2 4.6 %collective-permute-start.27 = (bf16[64,512]{1,0:T(8,128)(2,1)S(1)}, bf16[64,512]{1,0:T(8,128)(2,1)S(1)}, u32[]{:S(2)}, u32[]{:S(2)}) collective-permute-start(bf16[64,512]{1,0:T(8,128)(2,1)S(1)} %get-tuple-element.75), channel_id=1, source_target_pairs={{0,4},{1,5},{2,6},{3,7},{4,0},{5,1},{6,2},{7,3},{8,12},{9,13},{10,... | collective-permute-start | bytes 196616 | tf_op jit(solution)/shard_map/ppermute | solution.py:257
  110.4 5.9 %collective-permute-start.28 = (bf16[64,512]{1,0:T(8,128)(2,1)S(1)}, bf16[64,512]{1,0:T(8,128)(2,1)S(1)}, u32[]{:S(2)}, u32[]{:S(2)}) collective-permute-start(bf16[64,512]{1,0:T(8,128)(2,1)S(1)} %get-tuple-element.76), channel_id=1, source_target_pairs={{0,8},{1,9},{2,10},{3,11},{4,12},{5,13},{6,14},{7,15},{8,0},{9,1},... | collective-permute-start | bytes 196616 | tf_op jit(solution)/shard_map/ppermute | solution.py:257

commit v4 on v3

--- a/solution.py
+++ b/solution.py
@@ -47,9 +47,13 @@
     return moved % shards if isinstance(moved, int) else lax.rem(moved, shards)
 
 
+def passed_on(shards):
+    return shards - 2 if shards > 2 and shards & (shards - 1) == 0 else None
+
+
 def groups_of(shards):
     hops = list(range(shards - 1, -1, -1))
-    return [hops[:1], hops[1:]]
+    return [hops[: shards // 2], hops[shards // 2 :]]
 
 
 def load_body(half, place, source, out, arrived):
@@ -110,53 +114,60 @@
     )(place, factors, *pieces)
 
 
-def gradient_body(shards, parts, first, carried, groups, place, *refs):
+def gradient_body(shards, parts, first, carried, group, place, *refs):
     owns, fars, factors = refs[:parts], refs[parts : 2 * parts], refs[2 * parts : 2 * parts + HALVES]
     outs, sums = refs[2 * parts + HALVES + carried : -1], refs[-1]
     width = owns[0].shape[1]
     part = width // HALVES
     slots = [(at, g) for at, own in enumerate(owns) for g in range(own.shape[0] // part)]
+    owned = factors[0].shape[2] // shards
+
+    def wide(vectors):
+        sides = [jnp.concatenate([side[at][g * part : (g + 1) * part, :] for at, g in vectors], axis=1) for side in (owns, fars)]
+        return jnp.concatenate(sides, axis=0)
+
+    def columns_of(hop):
+        return pl.ds(pl.multiple_of(peer(place[0], hop, shards) * owned, owned), owned)
+
+    if group is not None:
+        taken = wide(slots)
+        for at, hop in enumerate(group):
+            columns = columns_of(hop)
+            rows = jnp.concatenate([loaded[g, :, columns] for g in range(first, first + len(slots)) for loaded in factors], axis=0)
+            total = refs[2 * parts + HALVES][:, columns] + jnp.dot(taken, rows, preferred_element_type=jnp.float32)
+            outs[at][...] = total[:part]
+            outs[-1][:, at * owned : (at + 1) * owned] = total[part:].astype(jnp.bfloat16)
+        return
+
     for seen in range(0, len(slots), BLOCK):
         vectors = slots[seen : seen + BLOCK]
-        wide = [jnp.concatenate([side[at][g * part : (g + 1) * part, :] for at, g in vectors], axis=1) for side in (owns, fars)]
         low = first + seen
         rows = jnp.concatenate([loaded[g] for g in range(low, low + len(vectors)) for loaded in factors], axis=0)
-        grown = jnp.dot(jnp.concatenate(wide, axis=0), rows, preferred_element_type=jnp.float32)
-        if seen == 0 and carried:
-            sums[...] = refs[2 * parts + HALVES][...] + grown
-        elif seen == 0:
+        grown = jnp.dot(wide(vectors), rows, preferred_element_type=jnp.float32)
+        if seen == 0:
             sums[...] = grown
         else:
             sums[...] += grown
     if len(outs) == 1:
         outs[0][...] = sums[...]
         return
-    owned = sums.shape[1] // shards
     for hop in range(shards):
-        low = pl.multiple_of(peer(place[0], hop, shards) * owned, owned)
-        if groups is None:
-            outs[hop][...] = sums[:, pl.ds(low, owned)].astype(outs[hop].dtype)
-            continue
-        outs[hop][...] = sums[:part, pl.ds(low, owned)].astype(outs[hop].dtype)
-        for group, hops in enumerate(groups):
-            if hop in hops:
-                to = hops.index(hop) * owned
-                outs[shards + group][:, to : to + owned] = sums[part:, pl.ds(low, owned)].astype(jnp.bfloat16)
-
-
-def gradients_of(place, factors, owns, fars, shards, first=0, groups=None, carried=None, more=False):
+        outs[hop][...] = sums[:, columns_of(hop)].astype(outs[hop].dtype)
+
+
+def gradients_of(place, factors, owns, fars, shards, first=0, group=None, carried=None, more=False):
     orbitals, width = factors[0].shape[2], owns[0].shape[1]
     part, owned = width // HALVES, orbitals // shards
     outs = [jax.ShapeDtypeStruct((2 * part, owned), jnp.bfloat16 if hop else jnp.float32) for hop in range(shards)]
     if more:
         outs = [jax.ShapeDtypeStruct((2 * part, orbitals), jnp.float32)]
-    elif groups:
-        outs = [jax.ShapeDtypeStruct((part, owned), jnp.float32)] * shards
-        outs += [jax.ShapeDtypeStruct((part, owned * len(hops)), jnp.bfloat16) for hops in groups]
+    elif group:
+        outs = [jax.ShapeDtypeStruct((part, owned), jnp.float32)] * len(group)
+        outs += [jax.ShapeDtypeStruct((part, owned * len(group)), jnp.bfloat16)]
     count = sum(own.shape[0] for own in owns) * HALVES
     values = [place, *owns, *fars, *factors] + ([] if carried is None else [carried])
     return pl.pallas_call(
-        functools.partial(gradient_body, shards, len(owns), first, 0 if carried is None else 1, groups),
+        functools.partial(gradient_body, shards, len(owns), first, 0 if carried is None else 1, group),
         in_specs=[SMEM] + [VMEM] * (len(values) - 1),
         out_specs=[VMEM] * len(outs),
         scratch_shapes=[pltpu.VMEM((2 * part, orbitals), jnp.float32)],
@@ -202,20 +213,26 @@
 def total_body(plan, *refs):
     out = refs[-1]
     for walker, halves in enumerate(plan):
-        rows = []
-        for parts in halves:
-            total = None
-            for at, low, high in parts:
-                value = refs[at][low:high, :].astype(jnp.float32)
-                total = value if total is None else total + value
-            rows.append(total)
-        out[walker] = -jnp.concatenate(rows, axis=0).T
+
+        @pl.when(pl.program_id(0) == walker)
+        def add(halves=halves):
+            rows = []
+            for parts in halves:
+                total = None
+                for at, low, high in parts:
+                    value = refs[at][low:high, :].astype(jnp.float32)
+                    total = value if total is None else total + value
+                rows.append(total)
+            out[0] = -jnp.concatenate(rows, axis=0).T
 
 
 def totals_of(values, plan):
     part, owned = values[0].shape
     return pl.pallas_call(
         functools.partial(total_body, plan),
+        grid=(len(plan),),
+        in_specs=[VMEM] * len(values),
+        out_specs=pl.BlockSpec((1, owned, part * HALVES), lambda walker: (walker, 0, 0)),
         out_shape=jax.ShapeDtypeStruct((len(plan), owned, part * HALVES), jnp.float32),
         compiler_params=SMALL,
     )(*values)
@@ -262,7 +279,10 @@
     blocks = [near + [across[0]] + [moved(near[hop], 0, True) for hop in hops]]
     for walker in range(1, walkers):
         both = jnp.concatenate([theta[walker], across[walker]], axis=1)
-        blocks.append([both] + [moved(both, hop) for hop in hops])
+        pieces = {hop: moved(both, hop) for hop in hops if hop != passed_on(shards)}
+        if passed_on(shards):
+            pieces[passed_on(shards)] = moved(pieces[shards - 1], 1)
+        blocks.append([both] + [pieces[hop] for hop in hops])
 
     stages = walkers * HALVES
     sides = []
@@ -287,11 +307,12 @@
     owns, fars = sides[-1]
     groups = groups_of(shards)
     (carried,) = gradients_of(place, factors, owns[:1], fars[:1], shards, more=True)
-    got = gradients_of(place, factors, owns[1:], fars[1:], shards, parts_of(stages - 1, stages, vectors)[1], groups, carried)
-    came = [moved(got[shards + at], 0, True) for at in range(len(groups))]
+    cut = parts_of(stages - 1, stages, vectors)[1]
     ends = [None] * shards
-    for at, group in enumerate(groups):
-        joined = join_sums(came[at], [got[hop] for hop in group], [jnp.bfloat16 if hop else jnp.float32 for hop in group])
+    for group in groups:
+        *own, far = gradients_of(place, factors, owns[1:], fars[1:], shards, cut, group, carried)
+        came = moved(far, 0, True)
+        joined = join_sums(came, own, [jnp.bfloat16 if hop else jnp.float32 for hop in group])
         for hop, value in zip(group, joined):
             ends[hop] = moved(value, hop) if hop else value
     plan.append([(len(values) + at, 0, part) for at in range(shards)])

time: 117 us -> 122 us (1.043)
  waiting for transfers between devices: 44.5 us -> 48.3 us
    ppermute x31, waiting for transfers between devices: 44.5 us -> 48.3 us  [moved(): return lax.ppermute(value, AXES, pairs)]
    pallas_call x5 -> x6, Pallas kernels: 9.98 us -> 10.1 us  [gradients_of(): pl.pallas_call(functools.partial(gradient_body, shards, len(owns), first,...]
  transfers between devices with their start and end apart: 31 -> 31, of which waited for: 11 -> 10; matrix products, arithmetic and copies ran while one was open for 1% -> 1% of each run, Pallas kernels for 24% -> 23%
where the time goes in v4:
time: 122 us; the launch traced here: 121 us
  waiting for transfers between devices  48.3 us (40%)
  starting transfers between devices  43 us (35%)
  Pallas kernels  28.8 us (24%)
    ppermute x31, waiting for transfers between devices, moved(): return lax.ppermute(value, AXES, pairs)  48.3 us
    ppermute x31, starting transfers between devices, moved(): return lax.ppermute(value, AXES, pairs)  43 us
    pallas_call x6, Pallas kernels, amplitudes_of(): pl.pallas_call(functools.partial(amplitude_body, shards, *vectors), in_sp...  10.5 us
    pallas_call x6, Pallas kernels, gradients_of(): pl.pallas_call(functools.partial(gradient_body, shards, len(owns), first,...  10.1 us
    pallas_call x2, Pallas kernels, loaded(): pl.pallas_call(functools.partial(load_body, half), in_specs=[SMEM, pl.Blo...  7 us
  transfers between devices with their start and end apart: 31, of which 10 were waited for; matrix products, arithmetic and copies ran while one was open for 1% of the time, Pallas kernels for 23%

profile of v4, /device:TPU:0, one launch (start us, length us, event | category | flops | bytes accessed | tf_op | source)
XLA Modules:
  0.0 121.4 jit_solution(6469184017392577886)
XLA Ops:
  0.0 3.0 %collective-permute-start.3 = (bf16[2,512,128]{2,1,0:T(8,128)(2,1)}, bf16[2,512,128]{2,1,0:T(8,128)(2,1)S(1)}, u32[]{:S(2)}, u32[]{:S(2)}) collective-permute-start(bf16[2,512,128]{2,1,0:T(8,128)(2,1)} %param.3), channel_id=1, source_target_pairs={{0,2},{1,3},{2,0},{3,1},{4,6},{5,7},{6,4},{7,5},{8,10},{9,11},{10,... | collective-permute-start | bytes 786440 | tf_op jit(solution)/shard_map/ppermute | solution.py:274
  4.0 1.6 %collective-permute-start = (bf16[512,128]{1,0:T(8,128)(2,1)S(1)}, bf16[512,128]{1,0:T(8,128)(2,1)S(1)}, u32[]{:S(2)}, u32[]{:S(2)}) collective-permute-start(bf16[512,128]{1,0:T(8,128)(2,1)S(1)} %get-tuple-element.82.refs_0_), channel_id=1, source_target_pairs={{0,4},{1,5},{2,6},{3,7},{4,0},{5,1},{6,2},{7,3},{8,12},{9,13},{10,... | collective-permute-start | bytes 393224 | tf_op jit(solution)/shard_map/ppermute | solution.py:274
  5.6 3.9 %collective-permute-done.3 = bf16[2,512,128]{2,1,0:T(8,128)(2,1)S(1)} collective-permute-done((bf16[2,512,128]{2,1,0:T(8,128)(2,1)}, bf16[2,512,128]{2,1,0:T(8,128)(2,1)S(1)}, u32[]{:S(2)}, u32[]{:S(2)}) %collective-permute-start.3) | collective-permute-done | bytes 262176 | tf_op jit(solution)/shard_map/ppermute | solution.py:274
  9.5 3.9 %collective-permute-start.17 = (bf16[512,256]{1,0:T(8,128)(2,1)S(1)}, bf16[512,256]{1,0:T(8,128)(2,1)S(1)}, u32[]{:S(2)}, u32[]{:S(2)}) collective-permute-start(bf16[512,256]{1,0:T(8,128)(2,1)S(1)} %pad_maximum_fusion.refs_0_), channel_id=1, source_target_pairs={{0,12},{1,13},{2,14},{3,15},{4,8},{5,9},{6,10},{7,11},{8,4},{9,5},... | collective-permute-start | bytes 786440 | tf_op jit(solution)/shard_map/ppermute | solution.py:274
  13.5 1.9 %collective-permute-start.2 = (bf16[512,128]{1,0:T(8,128)(2,1)S(1)}, bf16[512,128]{1,0:T(8,128)(2,1)S(1)}, u32[]{:S(2)}, u32[]{:S(2)}) collective-permute-start(bf16[512,128]{1,0:T(8,128)(2,1)S(1)} %get-tuple-element.82.refs_0_), channel_id=1, source_target_pairs={{0,12},{1,13},{2,14},{3,15},{4,8},{5,9},{6,10},{7,11},{8,4},{9,5},... | collective-permute-start | bytes 393224 | tf_op jit(solution)/shard_map/ppermute | solution.py:274
  15.4 1.5 %collective-permute-start.4 = (bf16[512,128]{1,0:T(8,128)(2,1)S(1)}, bf16[512,128]{1,0:T(8,128)(2,1)S(1)}, u32[]{:S(2)}, u32[]{:S(2)}) collective-permute-start(bf16[512,128]{1,0:T(8,128)(2,1)S(1)} %collective-permute-done.refs_1_), channel_id=1, source_target_pairs={{0,2},{1,3},{2,0},{3,1},{4,6},{5,7},{6,4},{7,5},{8,10},{9,11},{10,... | collective-permute-start | bytes 393224 | tf_op jit(solution)/shard_map/ppermute | solution.py:274
  16.9 16.2 %collective-permute-done.1.refs_2_ = bf16[512,128]{1,0:T(8,128)(2,1)S(1)} collective-permute-done((bf16[512,128]{1,0:T(8,128)(2,1)S(1)}, bf16[512,128]{1,0:T(8,128)(2,1)S(1)}, u32[]{:S(2)}, u32[]{:S(2)}) %collective-permute-start.1) | collective-permute-done | bytes 131104 | tf_op jit(solution)/shard_map/ppermute | solution.py:274
  33.1 1.5 %collective-permute-start.5 = (bf16[512,128]{1,0:T(8,128)(2,1)S(1)}, bf16[512,128]{1,0:T(8,128)(2,1)S(1)}, u32[]{:S(2)}, u32[]{:S(2)}) collective-permute-start(bf16[512,128]{1,0:T(8,128)(2,1)S(1)} %collective-permute-done.1.refs_2_), channel_id=1, source_target_pairs={{0,2},{1,3},{2,0},{3,1},{4,6},{5,7},{6,4},{7,5},{8,10},{9,11},{10,... | collective-permute-start | bytes 393224 | tf_op jit(solution)/shard_map/ppermute | solution.py:274
  35.1 3.5 %shard_map.31.refs_5_.factors.refs_3_ = bf16[32,64,2048]{2,1,0:T(8,128)(2,1)S(1)} custom-call(s32[1]{0:T(128)} %bitcast.place, bf16[32,128,2048]{2,1,0:T(8,128)(2,1)} %source.3), custom_call_target="tpu_custom_call" | custom-call | tf_op jit(solution)/shard_map/pallas_call | solution.py:74
  38.6 3.5 %shard_map.28.factors.refs_4_.refs_2_ = bf16[32,64,2048]{2,1,0:T(8,128)(2,1)S(1)} custom-call(s32[1]{0:T(128)} %bitcast.place, bf16[32,128,2048]{2,1,0:T(8,128)(2,1)} %source.3), custom_call_target="tpu_custom_call" | custom-call | tf_op jit(solution)/shard_map/pallas_call | solution.py:74
  42.1 2.0 %collective-permute-start.16 = (bf16[512,256]{1,0:T(8,128)(2,1)S(1)}, bf16[512,256]{1,0:T(8,128)(2,1)S(1)}, u32[]{:S(2)}, u32[]{:S(2)}) collective-permute-start(bf16[512,256]{1,0:T(8,128)(2,1)S(1)} %pad_maximum_fusion.refs_0_), channel_id=1, source_target_pairs={{0,4},{1,5},{2,6},{3,7},{4,0},{5,1},{6,2},{7,3},{8,12},{9,13},{10,... | collective-permute-start | bytes 786440 | tf_op jit(solution)/shard_map/ppermute | solution.py:274
  44.2 2.0 %shard_map.30 = (bf16[1536,128]{1,0:T(8,128)(2,1)S(1)}, bf16[1536,128]{1,0:T(8,128)(2,1)S(1)}) custom-call(s32[1]{0:T(128)} %bitcast.place, bf16[32,64,2048]{2,1,0:T(8,128)(2,1)S(1)} %shard_map.28.factors.refs_4_.refs_2_, bf16[512,128]{1,0:T(8,128)(2,1)S(1)} %get-tuple-element.82.refs_0_, bf16[512,128]{1,0:T(8,128)(2,1)S(1)} %collective-permute-done.refs_1_, ...), custom_call_target="tpu_custom_call" | custom-call | flops 1610612736 | bytes 6291456 | tf_op jit(solution)/shard_map/pallas_call | solution.py:106
  46.2 1.6 %collective-permute-start.8 = (bf16[1536,128]{1,0:T(8,128)(2,1)S(1)}, bf16[1536,128]{1,0:T(8,128)(2,1)S(1)}, u32[]{:S(2)}, u32[]{:S(2)}) collective-permute-start(bf16[1536,128]{1,0:T(8,128)(2,1)S(1)} %get-tuple-element.46), channel_id=1, source_target_pairs={{0,2},{1,3},{2,0},{3,1},{4,6},{5,7},{6,4},{7,5},{8,10},{9,11},{10,... | collective-permute-start | bytes 1179656 | tf_op jit(solution)/shard_map/ppermute | solution.py:274
  47.8 2.5 %shard_map.33 = (bf16[2048,128]{1,0:T(8,128)(2,1)S(1)}, bf16[2048,128]{1,0:T(8,128)(2,1)S(1)}) custom-call(s32[1]{0:T(128)} %bitcast.place, bf16[32,64,2048]{2,1,0:T(8,128)(2,1)S(1)} %shard_map.31.refs_5_.factors.refs_3_, bf16[512,128]{1,0:T(8,128)(2,1)S(1)} %get-tuple-element.82.refs_0_, bf16[512,128]{1,0:T(8,128)(2,1)S(1)} %collective-permute-done.refs_1_, ...), custom_call_target="tpu_custom_call" | custom-call | flops 2147483648 | bytes 8388608 | tf_op jit(solution)/shard_map/pallas_call | solution.py:106
  51.8 1.6 %collective-permute-start.7 = (bf16[512,128]{1,0:T(8,128)(2,1)S(1)}, bf16[512,128]{1,0:T(8,128)(2,1)S(1)}, u32[]{:S(2)}, u32[]{:S(2)}) collective-permute-start(bf16[512,128]{1,0:T(8,128)(2,1)S(1)} %get-tuple-element.45), channel_id=1, source_target_pairs={{0,2},{1,3},{2,0},{3,1},{4,6},{5,7},{6,4},{7,5},{8,10},{9,11},{10,... | collective-permute-start | bytes 393224 | tf_op jit(solution)/shard_map/ppermute | solution.py:274
  53.4 1.7 %collective-permute-done.18.refs_2_ = bf16[512,256]{1,0:T(8,128)(2,1)S(1)} collective-permute-done((bf16[512,256]{1,0:T(8,128)(2,1)S(1)}, bf16[512,256]{1,0:T(8,128)(2,1)S(1)}, u32[]{:S(2)}, u32[]{:S(2)}) %collective-permute-start.18) | collective-permute-done | bytes 262176 | tf_op jit(solution)/shard_map/ppermute | solution.py:274
  55.0 2.4 %shard_map.35 = (bf16[2048,128]{1,0:T(8,128)(2,1)S(1)}, bf16[2048,128]{1,0:T(8,128)(2,1)S(1)}) custom-call(s32[1]{0:T(128)} %bitcast.place, bf16[32,64,2048]{2,1,0:T(8,128)(2,1)S(1)} %shard_map.28.factors.refs_4_.refs_2_, bf16[512,256]{1,0:T(8,128)(2,1)S(1)} %pad_maximum_fusion.refs_0_, bf16[512,256]{1,0:T(8,128)(2,1)S(1)} %collective-permute-done.16.refs_1_, ...), custom_call_target="tpu_custom_call" | custom-call | flops 2147483648 | bytes 8388608 | tf_op jit(solution)/shard_map/pallas_call | solution.py:106
  58.0 14.3 %collective-permute-done.7.refs_2_ = bf16[512,128]{1,0:T(8,128)(2,1)S(1)} collective-permute-done((bf16[512,128]{1,0:T(8,128)(2,1)S(1)}, bf16[512,128]{1,0:T(8,128)(2,1)S(1)}, u32[]{:S(2)}, u32[]{:S(2)}) %collective-permute-start.7) | collective-permute-done | bytes 131104 | tf_op jit(solution)/shard_map/ppermute | solution.py:274
  72.3 2.4 %shard_map.32 = (f32[128,512]{1,0:T(8,128)S(1)}, bf16[128,512]{1,0:T(8,128)(2,1)S(1)}, bf16[128,512]{1,0:T(8,128)(2,1)S(1)}, bf16[128,512]{1,0:T(8,128)(2,1)S(1)}) custom-call(s32[1]{0:T(128)} %bitcast.place, bf16[512,128]{1,0:T(8,128)(2,1)S(1)} %get-tuple-element.43.refs_0_, bf16[1536,128]{1,0:T(8,128)(2,1)S(1)} %get-tuple-element.44.refs_1_, ...), custom_call_target="tpu_custom_call" | custom-call | flops 2147483648 | bytes 16777216 | tf_op jit(solution)/shard_map/pallas_call | solution.py:169
  74.7 3.0 %collective-permute-start.10 = (bf16[128,512]{1,0:T(8,128)(2,1)S(1)}, bf16[128,512]{1,0:T(8,128)(2,1)S(1)}, u32[]{:S(2)}, u32[]{:S(2)}) collective-permute-start(bf16[128,512]{1,0:T(8,128)(2,1)S(1)} %get-tuple-element.49), channel_id=1, source_target_pairs={{0,8},{1,9},{2,10},{3,11},{4,12},{5,13},{6,14},{7,15},{8,0},{9,1},... | collective-permute-start | bytes 393224 | tf_op jit(solution)/shard_map/ppermute | solution.py:274
  79.8 1.9 %shard_map.39 = (bf16[1536,128]{1,0:T(8,128)(2,1)S(1)}, bf16[1536,128]{1,0:T(8,128)(2,1)S(1)}) custom-call(s32[1]{0:T(128)} %bitcast.place, bf16[32,64,2048]{2,1,0:T(8,128)(2,1)S(1)} %shard_map.31.refs_5_.factors.refs_3_, bf16[512,256]{1,0:T(8,128)(2,1)S(1)} %pad_maximum_fusion.refs_0_, bf16[512,256]{1,0:T(8,128)(2,1)S(1)} %collective-permute-done.16.refs_1_, ...), custom_call_target="tpu_custom_call" | custom-call | flops 1610612736 | bytes 6291456 | tf_op jit(solution)/shard_map/pallas_call | solution.py:106
  82.5 2.6 %shard_map.34 = (f32[128,512]{1,0:T(8,128)S(1)}, bf16[128,512]{1,0:T(8,128)(2,1)S(1)}, bf16[128,512]{1,0:T(8,128)(2,1)S(1)}, bf16[128,512]{1,0:T(8,128)(2,1)S(1)}) custom-call(s32[1]{0:T(128)} %bitcast.place, bf16[2048,128]{1,0:T(8,128)(2,1)S(1)} %get-tuple-element.51.refs_0_, bf16[2048,128]{1,0:T(8,128)(2,1)S(1)} %collective-permute-done.12.refs_1_, ...), custom_call_target="tpu_custom_call" | custom-call | flops 2147483648 | bytes 16777216 | tf_op jit(solution)/shard_map/pallas_call | solution.py:169
  86.5 2.0 %collective-permute-start.13 = (bf16[128,512]{1,0:T(8,128)(2,1)S(1)}, bf16[128,512]{1,0:T(8,128)(2,1)S(1)}, u32[]{:S(2)}, u32[]{:S(2)}) collective-permute-start(bf16[128,512]{1,0:T(8,128)(2,1)S(1)} %get-tuple-element.54), channel_id=1, source_target_pairs={{0,4},{1,5},{2,6},{3,7},{4,0},{5,1},{6,2},{7,3},{8,12},{9,13},{10,... | collective-permute-start | bytes 393224 | tf_op jit(solution)/shard_map/ppermute | solution.py:274
  88.5 2.4 %shard_map.36 = (f32[128,512]{1,0:T(8,128)S(1)}, bf16[128,512]{1,0:T(8,128)(2,1)S(1)}, bf16[128,512]{1,0:T(8,128)(2,1)S(1)}, bf16[128,512]{1,0:T(8,128)(2,1)S(1)}) custom-call(s32[1]{0:T(128)} %bitcast.place, bf16[2048,128]{1,0:T(8,128)(2,1)S(1)} %get-tuple-element.57.refs_0_, bf16[2048,128]{1,0:T(8,128)(2,1)S(1)} %collective-permute-done.19.refs_1_, ...), custom_call_target="tpu_custom_call" | custom-call | flops 2147483648 | bytes 16777216 | tf_op jit(solution)/shard_map/pallas_call | solution.py:169
  92.0 1.5 %collective-permute-start.15 = (bf16[128,512]{1,0:T(8,128)(2,1)S(1)}, bf16[128,512]{1,0:T(8,128)(2,1)S(1)}, u32[]{:S(2)}, u32[]{:S(2)}) collective-permute-start(bf16[128,512]{1,0:T(8,128)(2,1)S(1)} %get-tuple-element.56), channel_id=1, source_target_pairs={{0,12},{1,13},{2,14},{3,15},{4,8},{5,9},{6,10},{7,11},{8,4},{9,5},... | collective-permute-start | bytes 393224 | tf_op jit(solution)/shard_map/ppermute | solution.py:274
  96.4 1.5 %collective-permute-start.22 = (bf16[128,512]{1,0:T(8,128)(2,1)S(1)}, bf16[128,512]{1,0:T(8,128)(2,1)S(1)}, u32[]{:S(2)}, u32[]{:S(2)}) collective-permute-start(bf16[128,512]{1,0:T(8,128)(2,1)S(1)} %get-tuple-element.62), channel_id=1, source_target_pairs={{0,12},{1,13},{2,14},{3,15},{4,8},{5,9},{6,10},{7,11},{8,4},{9,5},... | collective-permute-start | bytes 393224 | tf_op jit(solution)/shard_map/ppermute | solution.py:274
  98.0 1.8 %shard_map.40.refs_4_ = f32[128,2048]{1,0:T(8,128)S(1)} custom-call(s32[1]{0:T(128)} %bitcast.place, bf16[1536,128]{1,0:T(8,128)(2,1)S(1)} %get-tuple-element.69.refs_0_, bf16[1536,128]{1,0:T(8,128)(2,1)S(1)} %collective-permute-done.25.refs_1_, bf16[32,64,2048]{2,1,0:T(8,128)(2,1)S(1)} %shard_map.28.factors.refs_4_.refs_2_, ...), custom_call_target="tpu_custom_call" | custom-call | flops 1610612736 | bytes 12582912 | tf_op jit(solution)/shard_map/pallas_call | solution.py:169
  100.2 5.1 %collective-permute-done.14.refs_6_ = bf16[128,512]{1,0:T(8,128)(2,1)S(1)} collective-permute-done((bf16[128,512]{1,0:T(8,128)(2,1)S(1)}, bf16[128,512]{1,0:T(8,128)(2,1)S(1)}, u32[]{:S(2)}, u32[]{:S(2)}) %collective-permute-start.14) | collective-permute-done | bytes 131104 | tf_op jit(solution)/shard_map/ppermute | solution.py:274
  106.3 1.6 %collective-permute-start.26 = (bf16[64,1024]{1,0:T(8,128)(2,1)S(1)}, bf16[64,1024]{1,0:T(8,128)(2,1)S(1)}, u32[]{:S(2)}, u32[]{:S(2)}) collective-permute-start(bf16[64,1024]{1,0:T(8,128)(2,1)S(1)} %get-tuple-element.71), channel_id=1, source_target_pairs={{0,2},{1,3},{2,0},{3,1},{4,6},{5,7},{6,4},{7,5},{8,10},{9,11},{10,... | collective-permute-start | bytes 393224 | tf_op jit(solution)/shard_map/ppermute | solution.py:274
  110.3 2.3 %collective-permute-start.29 = (bf16[64,512]{1,0:T(8,128)(2,1)S(1)}, bf16[64,512]{1,0:T(8,128)(2,1)S(1)}, u32[]{:S(2)}, u32[]{:S(2)}) collective-permute-start(bf16[64,512]{1,0:T(8,128)(2,1)S(1)} %get-tuple-element.79), channel_id=1, source_target_pairs={{0,8},{1,9},{2,10},{3,11},{4,12},{5,13},{6,14},{7,15},{8,0},{9,1},... | collective-permute-start | bytes 196616 | tf_op jit(solution)/shard_map/ppermute | solution.py:274
  112.6 3.4 %collective-permute-start.30 = (bf16[64,512]{1,0:T(8,128)(2,1)S(1)}, bf16[64,512]{1,0:T(8,128)(2,1)S(1)}, u32[]{:S(2)}, u32[]{:S(2)}) collective-permute-start(bf16[64,512]{1,0:T(8,128)(2,1)S(1)} %get-tuple-element.80), channel_id=1, source_target_pairs={{0,12},{1,13},{2,14},{3,15},{4,8},{5,9},{6,10},{7,11},{8,4},{9,5},... | collective-permute-start | bytes 196616 | tf_op jit(solution)/shard_map/ppermute | solution.py:274
  116.1 2.8 %collective-permute-done.30.refs_7_ = bf16[64,512]{1,0:T(8,128)(2,1)S(1)} collective-permute-done((bf16[64,512]{1,0:T(8,128)(2,1)S(1)}, bf16[64,512]{1,0:T(8,128)(2,1)S(1)}, u32[]{:S(2)}, u32[]{:S(2)}) %collective-permute-start.30) | collective-permute-done | bytes 65568 | tf_op jit(solution)/shard_map/ppermute | solution.py:274
  (51 shorter events, 18.4 us)
Async XLA Ops:
  0.0 9.5 %collective-permute-start.3 = (bf16[2,512,128]{2,1,0:T(8,128)(2,1)}, bf16[2,512,128]{2,1,0:T(8,128)(2,1)S(1)}, u32[]{:S(2)}, u32[]{:S(2)}) collective-permute-start(bf16[2,512,128]{2,1,0:T(8,128)(2,1)} %param.3), channel_id=1, source_target_pairs={{0,2},{1,3},{2,0},{3,1},{4,6},{5,7},{6,4},{7,5},{8,10},{9,11},{10,... | collective-permute-start | bytes 786440 | tf_op jit(solution)/shard_map/ppermute | solution.py:274
  4.0 11.4 %collective-permute-start = (bf16[512,128]{1,0:T(8,128)(2,1)S(1)}, bf16[512,128]{1,0:T(8,128)(2,1)S(1)}, u32[]{:S(2)}, u32[]{:S(2)}) collective-permute-start(bf16[512,128]{1,0:T(8,128)(2,1)S(1)} %get-tuple-element.82.refs_0_), channel_id=1, source_target_pairs={{0,4},{1,5},{2,6},{3,7},{4,0},{5,1},{6,2},{7,3},{8,12},{9,13},{10,... | collective-permute-start | bytes 393224 | tf_op jit(solution)/shard_map/ppermute | solution.py:274
  9.5 34.5 %collective-permute-start.17 = (bf16[512,256]{1,0:T(8,128)(2,1)S(1)}, bf16[512,256]{1,0:T(8,128)(2,1)S(1)}, u32[]{:S(2)}, u32[]{:S(2)}) collective-permute-start(bf16[512,256]{1,0:T(8,128)(2,1)S(1)} %pad_maximum_fusion.refs_0_), channel_id=1, source_target_pairs={{0,12},{1,13},{2,14},{3,15},{4,8},{5,9},{6,10},{7,11},{8,4},{9,5},... | collective-permute-start | bytes 786440 | tf_op jit(solution)/shard_map/ppermute | solution.py:274
  13.5 19.6 %collective-permute-start.1 = (bf16[512,128]{1,0:T(8,128)(2,1)S(1)}, bf16[512,128]{1,0:T(8,128)(2,1)S(1)}, u32[]{:S(2)}, u32[]{:S(2)}) collective-permute-start(bf16[512,128]{1,0:T(8,128)(2,1)S(1)} %get-tuple-element.82.refs_0_), channel_id=1, source_target_pairs={{0,8},{1,9},{2,10},{3,11},{4,12},{5,13},{6,14},{7,15},{8,0},{9,1},... | collective-permute-start | bytes 393224 | tf_op jit(solution)/shard_map/ppermute | solution.py:274
  13.5 21.1 %collective-permute-start.2 = (bf16[512,128]{1,0:T(8,128)(2,1)S(1)}, bf16[512,128]{1,0:T(8,128)(2,1)S(1)}, u32[]{:S(2)}, u32[]{:S(2)}) collective-permute-start(bf16[512,128]{1,0:T(8,128)(2,1)S(1)} %get-tuple-element.82.refs_0_), channel_id=1, source_target_pairs={{0,12},{1,13},{2,14},{3,15},{4,8},{5,9},{6,10},{7,11},{8,4},{9,5},... | collective-permute-start | bytes 393224 | tf_op jit(solution)/shard_map/ppermute | solution.py:274
  15.4 28.8 %collective-permute-start.4 = (bf16[512,128]{1,0:T(8,128)(2,1)S(1)}, bf16[512,128]{1,0:T(8,128)(2,1)S(1)}, u32[]{:S(2)}, u32[]{:S(2)}) collective-permute-start(bf16[512,128]{1,0:T(8,128)(2,1)S(1)} %collective-permute-done.refs_1_), channel_id=1, source_target_pairs={{0,2},{1,3},{2,0},{3,1},{4,6},{5,7},{6,4},{7,5},{8,10},{9,11},{10,... | collective-permute-start | bytes 393224 | tf_op jit(solution)/shard_map/ppermute | solution.py:274
  33.1 11.2 %collective-permute-start.5 = (bf16[512,128]{1,0:T(8,128)(2,1)S(1)}, bf16[512,128]{1,0:T(8,128)(2,1)S(1)}, u32[]{:S(2)}, u32[]{:S(2)}) collective-permute-start(bf16[512,128]{1,0:T(8,128)(2,1)S(1)} %collective-permute-done.1.refs_2_), channel_id=1, source_target_pairs={{0,2},{1,3},{2,0},{3,1},{4,6},{5,7},{6,4},{7,5},{8,10},{9,11},{10,... | collective-permute-start | bytes 393224 | tf_op jit(solution)/shard_map/ppermute | solution.py:274
  34.5 9.7 %collective-permute-start.6 = (bf16[512,128]{1,0:T(8,128)(2,1)S(1)}, bf16[512,128]{1,0:T(8,128)(2,1)S(1)}, u32[]{:S(2)}, u32[]{:S(2)}) collective-permute-start(bf16[512,128]{1,0:T(8,128)(2,1)S(1)} %collective-permute-done.2.refs_3_), channel_id=1, source_target_pairs={{0,2},{1,3},{2,0},{3,1},{4,6},{5,7},{6,4},{7,5},{8,10},{9,11},{10,... | collective-permute-start | bytes 393224 | tf_op jit(solution)/shard_map/ppermute | solution.py:274
  42.1 11.3 %collective-permute-start.16 = (bf16[512,256]{1,0:T(8,128)(2,1)S(1)}, bf16[512,256]{1,0:T(8,128)(2,1)S(1)}, u32[]{:S(2)}, u32[]{:S(2)}) collective-permute-start(bf16[512,256]{1,0:T(8,128)(2,1)S(1)} %pad_maximum_fusion.refs_0_), channel_id=1, source_target_pairs={{0,4},{1,5},{2,6},{3,7},{4,0},{5,1},{6,2},{7,3},{8,12},{9,13},{10,... | collective-permute-start | bytes 786440 | tf_op jit(solution)/shard_map/ppermute | solution.py:274
  44.1 11.0 %collective-permute-start.18 = (bf16[512,256]{1,0:T(8,128)(2,1)S(1)}, bf16[512,256]{1,0:T(8,128)(2,1)S(1)}, u32[]{:S(2)}, u32[]{:S(2)}) collective-permute-start(bf16[512,256]{1,0:T(8,128)(2,1)S(1)} %collective-permute-done.17.refs_3_), channel_id=1, source_target_pairs={{0,4},{1,5},{2,6},{3,7},{4,0},{5,1},{6,2},{7,3},{8,12},{9,13},{10,... | collective-permute-start | bytes 786440 | tf_op jit(solution)/shard_map/ppermute | solution.py:274
  46.2 26.1 %collective-permute-start.8 = (bf16[1536,128]{1,0:T(8,128)(2,1)S(1)}, bf16[1536,128]{1,0:T(8,128)(2,1)S(1)}, u32[]{:S(2)}, u32[]{:S(2)}) collective-permute-start(bf16[1536,128]{1,0:T(8,128)(2,1)S(1)} %get-tuple-element.46), channel_id=1, source_target_pairs={{0,2},{1,3},{2,0},{3,1},{4,6},{5,7},{6,4},{7,5},{8,10},{9,11},{10,... | collective-permute-start | bytes 1179656 | tf_op jit(solution)/shard_map/ppermute | solution.py:274
  50.3 31.4 %collective-permute-start.12 = (bf16[2048,128]{1,0:T(8,128)(2,1)S(1)}, bf16[2048,128]{1,0:T(8,128)(2,1)S(1)}, u32[]{:S(2)}, u32[]{:S(2)}) collective-permute-start(bf16[2048,128]{1,0:T(8,128)(2,1)S(1)} %get-tuple-element.52), channel_id=1, source_target_pairs={{0,2},{1,3},{2,0},{3,1},{4,6},{5,7},{6,4},{7,5},{8,10},{9,11},{10,... | collective-permute-start | bytes 1572872 | tf_op jit(solution)/shard_map/ppermute | solution.py:274
  51.8 20.5 %collective-permute-start.7 = (bf16[512,128]{1,0:T(8,128)(2,1)S(1)}, bf16[512,128]{1,0:T(8,128)(2,1)S(1)}, u32[]{:S(2)}, u32[]{:S(2)}) collective-permute-start(bf16[512,128]{1,0:T(8,128)(2,1)S(1)} %get-tuple-element.45), channel_id=1, source_target_pairs={{0,2},{1,3},{2,0},{3,1},{4,6},{5,7},{6,4},{7,5},{8,10},{9,11},{10,... | collective-permute-start | bytes 393224 | tf_op jit(solution)/shard_map/ppermute | solution.py:274
  57.4 29.1 %collective-permute-start.19 = (bf16[2048,128]{1,0:T(8,128)(2,1)S(1)}, bf16[2048,128]{1,0:T(8,128)(2,1)S(1)}, u32[]{:S(2)}, u32[]{:S(2)}) collective-permute-start(bf16[2048,128]{1,0:T(8,128)(2,1)S(1)} %get-tuple-element.58), channel_id=1, source_target_pairs={{0,2},{1,3},{2,0},{3,1},{4,6},{5,7},{6,4},{7,5},{8,10},{9,11},{10,... | collective-permute-start | bytes 1572872 | tf_op jit(solution)/shard_map/ppermute | solution.py:274
  74.7 10.4 %collective-permute-start.10 = (bf16[128,512]{1,0:T(8,128)(2,1)S(1)}, bf16[128,512]{1,0:T(8,128)(2,1)S(1)}, u32[]{:S(2)}, u32[]{:S(2)}) collective-permute-start(bf16[128,512]{1,0:T(8,128)(2,1)S(1)} %get-tuple-element.49), channel_id=1, source_target_pairs={{0,8},{1,9},{2,10},{3,11},{4,12},{5,13},{6,14},{7,15},{8,0},{9,1},... | collective-permute-start | bytes 393224 | tf_op jit(solution)/shard_map/ppermute | solution.py:274
  77.7 13.3 %collective-permute-start.11 = (bf16[128,512]{1,0:T(8,128)(2,1)S(1)}, bf16[128,512]{1,0:T(8,128)(2,1)S(1)}, u32[]{:S(2)}, u32[]{:S(2)}) collective-permute-start(bf16[128,512]{1,0:T(8,128)(2,1)S(1)} %get-tuple-element.50), channel_id=1, source_target_pairs={{0,12},{1,13},{2,14},{3,15},{4,8},{5,9},{6,10},{7,11},{8,4},{9,5},... | collective-permute-start | bytes 393224 | tf_op jit(solution)/shard_map/ppermute | solution.py:274
  79.0 13.0 %collective-permute-start.9 = (bf16[128,512]{1,0:T(8,128)(2,1)S(1)}, bf16[128,512]{1,0:T(8,128)(2,1)S(1)}, u32[]{:S(2)}, u32[]{:S(2)}) collective-permute-start(bf16[128,512]{1,0:T(8,128)(2,1)S(1)} %get-tuple-element.48), channel_id=1, source_target_pairs={{0,4},{1,5},{2,6},{3,7},{4,0},{5,1},{6,2},{7,3},{8,12},{9,13},{10,... | collective-permute-start | bytes 393224 | tf_op jit(solution)/shard_map/ppermute | solution.py:274
  81.7 14.7 %collective-permute-start.25 = (bf16[1536,128]{1,0:T(8,128)(2,1)S(1)}, bf16[1536,128]{1,0:T(8,128)(2,1)S(1)}, u32[]{:S(2)}, u32[]{:S(2)}) collective-permute-start(bf16[1536,128]{1,0:T(8,128)(2,1)S(1)} %get-tuple-element.70), channel_id=1, source_target_pairs={{0,2},{1,3},{2,0},{3,1},{4,6},{5,7},{6,4},{7,5},{8,10},{9,11},{10,... | collective-permute-start | bytes 1179656 | tf_op jit(solution)/shard_map/ppermute | solution.py:274
  85.1 8.4 %collective-permute-start.24 = (bf16[512,128]{1,0:T(8,128)(2,1)S(1)}, bf16[512,128]{1,0:T(8,128)(2,1)S(1)}, u32[]{:S(2)}, u32[]{:S(2)}) collective-permute-start(bf16[512,128]{1,0:T(8,128)(2,1)S(1)} %get-tuple-element.68), channel_id=1, source_target_pairs={{0,2},{1,3},{2,0},{3,1},{4,6},{5,7},{6,4},{7,5},{8,10},{9,11},{10,... | collective-permute-start | bytes 393224 | tf_op jit(solution)/shard_map/ppermute | solution.py:274
  86.5 8.9 %collective-permute-start.13 = (bf16[128,512]{1,0:T(8,128)(2,1)S(1)}, bf16[128,512]{1,0:T(8,128)(2,1)S(1)}, u32[]{:S(2)}, u32[]{:S(2)}) collective-permute-start(bf16[128,512]{1,0:T(8,128)(2,1)S(1)} %get-tuple-element.54), channel_id=1, source_target_pairs={{0,4},{1,5},{2,6},{3,7},{4,0},{5,1},{6,2},{7,3},{8,12},{9,13},{10,... | collective-permute-start | bytes 393224 | tf_op jit(solution)/shard_map/ppermute | solution.py:274
  90.9 14.4 %collective-permute-start.14 = (bf16[128,512]{1,0:T(8,128)(2,1)S(1)}, bf16[128,512]{1,0:T(8,128)(2,1)S(1)}, u32[]{:S(2)}, u32[]{:S(2)}) collective-permute-start(bf16[128,512]{1,0:T(8,128)(2,1)S(1)} %get-tuple-element.55), channel_id=1, source_target_pairs={{0,8},{1,9},{2,10},{3,11},{4,12},{5,13},{6,14},{7,15},{8,0},{9,1},... | collective-permute-start | bytes 393224 | tf_op jit(solution)/shard_map/ppermute | solution.py:274
  92.0 14.2 %collective-permute-start.15 = (bf16[128,512]{1,0:T(8,128)(2,1)S(1)}, bf16[128,512]{1,0:T(8,128)(2,1)S(1)}, u32[]{:S(2)}, u32[]{:S(2)}) collective-permute-start(bf16[128,512]{1,0:T(8,128)(2,1)S(1)} %get-tuple-element.56), channel_id=1, source_target_pairs={{0,12},{1,13},{2,14},{3,15},{4,8},{5,9},{6,10},{7,11},{8,4},{9,5},... | collective-permute-start | bytes 393224 | tf_op jit(solution)/shard_map/ppermute | solution.py:274
  93.6 14.3 %collective-permute-start.20 = (bf16[128,512]{1,0:T(8,128)(2,1)S(1)}, bf16[128,512]{1,0:T(8,128)(2,1)S(1)}, u32[]{:S(2)}, u32[]{:S(2)}) collective-permute-start(bf16[128,512]{1,0:T(8,128)(2,1)S(1)} %get-tuple-element.60), channel_id=1, source_target_pairs={{0,4},{1,5},{2,6},{3,7},{4,0},{5,1},{6,2},{7,3},{8,12},{9,13},{10,... | collective-permute-start | bytes 393224 | tf_op jit(solution)/shard_map/ppermute | solution.py:274
  95.4 13.8 %collective-permute-start.21 = (bf16[128,512]{1,0:T(8,128)(2,1)S(1)}, bf16[128,512]{1,0:T(8,128)(2,1)S(1)}, u32[]{:S(2)}, u32[]{:S(2)}) collective-permute-start(bf16[128,512]{1,0:T(8,128)(2,1)S(1)} %get-tuple-element.61), channel_id=1, source_target_pairs={{0,8},{1,9},{2,10},{3,11},{4,12},{5,13},{6,14},{7,15},{8,0},{9,1},... | collective-permute-start | bytes 393224 | tf_op jit(solution)/shard_map/ppermute | solution.py:274
  96.4 12.8 %collective-permute-start.22 = (bf16[128,512]{1,0:T(8,128)(2,1)S(1)}, bf16[128,512]{1,0:T(8,128)(2,1)S(1)}, u32[]{:S(2)}, u32[]{:S(2)}) collective-permute-start(bf16[128,512]{1,0:T(8,128)(2,1)S(1)} %get-tuple-element.62), channel_id=1, source_target_pairs={{0,12},{1,13},{2,14},{3,15},{4,8},{5,9},{6,10},{7,11},{8,4},{9,5},... | collective-permute-start | bytes 393224 | tf_op jit(solution)/shard_map/ppermute | solution.py:274
  105.3 5.0 %collective-permute-start.28 = (bf16[64,1024]{1,0:T(8,128)(2,1)S(1)}, bf16[64,1024]{1,0:T(8,128)(2,1)S(1)}, u32[]{:S(2)}, u32[]{:S(2)}) collective-permute-start(bf16[64,1024]{1,0:T(8,128)(2,1)S(1)} %get-tuple-element.76), channel_id=1, source_target_pairs={{0,2},{1,3},{2,0},{3,1},{4,6},{5,7},{6,4},{7,5},{8,10},{9,11},{10,... | collective-permute-start | bytes 393224 | tf_op jit(solution)/shard_map/ppermute | solution.py:274
  106.3 9.7 %collective-permute-start.26 = (bf16[64,1024]{1,0:T(8,128)(2,1)S(1)}, bf16[64,1024]{1,0:T(8,128)(2,1)S(1)}, u32[]{:S(2)}, u32[]{:S(2)}) collective-permute-start(bf16[64,1024]{1,0:T(8,128)(2,1)S(1)} %get-tuple-element.71), channel_id=1, source_target_pairs={{0,2},{1,3},{2,0},{3,1},{4,6},{5,7},{6,4},{7,5},{8,10},{9,11},{10,... | collective-permute-start | bytes 393224 | tf_op jit(solution)/shard_map/ppermute | solution.py:274
  109.4 11.0 %collective-permute-start.23 = (bf16[192,512]{1,0:T(8,128)(2,1)S(1)}, bf16[192,512]{1,0:T(8,128)(2,1)S(1)}, u32[]{:S(2)}, u32[]{:S(2)}) collective-permute-start(bf16[192,512]{1,0:T(8,128)(2,1)S(1)} %get-tuple-element.66), channel_id=1, source_target_pairs={{0,2},{1,3},{2,0},{3,1},{4,6},{5,7},{6,4},{7,5},{8,10},{9,11},{10,... | collective-permute-start | bytes 589832 | tf_op jit(solution)/shard_map/ppermute | solution.py:274
  110.3 5.8 %collective-permute-start.29 = (bf16[64,512]{1,0:T(8,128)(2,1)S(1)}, bf16[64,512]{1,0:T(8,128)(2,1)S(1)}, u32[]{:S(2)}, u32[]{:S(2)}) collective-permute-start(bf16[64,512]{1,0:T(8,128)(2,1)S(1)} %get-tuple-element.79), channel_id=1, source_target_pairs={{0,8},{1,9},{2,10},{3,11},{4,12},{5,13},{6,14},{7,15},{8,0},{9,1},... | collective-permute-start | bytes 196616 | tf_op jit(solution)/shard_map/ppermute | solution.py:274
  112.6 6.3 %collective-permute-start.30 = (bf16[64,512]{1,0:T(8,128)(2,1)S(1)}, bf16[64,512]{1,0:T(8,128)(2,1)S(1)}, u32[]{:S(2)}, u32[]{:S(2)}) collective-permute-start(bf16[64,512]{1,0:T(8,128)(2,1)S(1)} %get-tuple-element.80), channel_id=1, source_target_pairs={{0,12},{1,13},{2,14},{3,15},{4,8},{5,9},{6,10},{7,11},{8,4},{9,5},... | collective-permute-start | bytes 196616 | tf_op jit(solution)/shard_map/ppermute | solution.py:274
  116.0 4.3 %collective-permute-start.27 = (bf16[64,512]{1,0:T(8,128)(2,1)S(1)}, bf16[64,512]{1,0:T(8,128)(2,1)S(1)}, u32[]{:S(2)}, u32[]{:S(2)}) collective-permute-start(bf16[64,512]{1,0:T(8,128)(2,1)S(1)} %get-tuple-element.75), channel_id=1, source_target_pairs={{0,4},{1,5},{2,6},{3,7},{4,0},{5,1},{6,2},{7,3},{8,12},{9,13},{10,... | collective-permute-start | bytes 196616 | tf_op jit(solution)/shard_map/ppermute | solution.py:274

commit v5 on v4

--- a/solution.py
+++ b/solution.py
@@ -47,12 +47,16 @@
     return moved % shards if isinstance(moved, int) else lax.rem(moved, shards)
 
 
+def hops_of(shards):
+    return sorted(range(1, shards), key=lambda hop: (hop != shards - 1, hop))
+
+
 def passed_on(shards):
     return shards - 2 if shards > 2 and shards & (shards - 1) == 0 else None
 
 
 def groups_of(shards):
-    hops = list(range(shards - 1, -1, -1))
+    hops = hops_of(shards) + [0]
     return [hops[: shards // 2], hops[shards // 2 :]]
 
 
@@ -211,31 +215,30 @@
 
 
 def total_body(plan, *refs):
-    out = refs[-1]
-    for walker, halves in enumerate(plan):
-
-        @pl.when(pl.program_id(0) == walker)
-        def add(halves=halves):
-            rows = []
-            for parts in halves:
-                total = None
-                for at, low, high in parts:
-                    value = refs[at][low:high, :].astype(jnp.float32)
-                    total = value if total is None else total + value
-                rows.append(total)
-            out[0] = -jnp.concatenate(rows, axis=0).T
-
-
-def totals_of(values, plan):
+    rows = []
+    for parts in plan:
+        total = None
+        for at, low, high in parts:
+            value = refs[at][low:high, :].astype(jnp.float32)
+            total = value if total is None else total + value
+        rows.append(total)
+    refs[-1][0] = -jnp.concatenate(rows, axis=0).T
+
+
+def total_of(values, plan, walker, walkers, before):
     part, owned = values[0].shape
+    used = sorted({at for parts in plan for at, low, high in parts})
+    plan = [[(used.index(at), low, high) for at, low, high in parts] for parts in plan]
+    taken = [values[at] for at in used]
     return pl.pallas_call(
         functools.partial(total_body, plan),
-        grid=(len(plan),),
-        in_specs=[VMEM] * len(values),
-        out_specs=pl.BlockSpec((1, owned, part * HALVES), lambda walker: (walker, 0, 0)),
-        out_shape=jax.ShapeDtypeStruct((len(plan), owned, part * HALVES), jnp.float32),
+        grid=(1,),
+        in_specs=[VMEM] * len(taken) + ([] if before is None else [pl.BlockSpec(memory_space=pltpu.HBM)]),
+        out_specs=pl.BlockSpec((1, owned, part * HALVES), lambda i: (walker, 0, 0)),
+        out_shape=jax.ShapeDtypeStruct((walkers, owned, part * HALVES), jnp.float32),
+        input_output_aliases={} if before is None else {len(taken): 0},
         compiler_params=SMALL,
-    )(*values)
+    )(*taken, *([] if before is None else [before]))
 
 
 def parts_of(stage, stages, vectors):
@@ -299,10 +302,12 @@
     for stage in range(stages - 1):
         got = gradients_of(place, factors, *sides[stage], shards)
         arrived.append([got[0]] + [moved(got[hop], hop) for hop in hops])
-    *kept, crossing = split_sums(arrived)
-    part = width // HALVES
-    values = [*kept, moved(crossing, 0, True)]
-    plan = [[(stage, 0, part), (len(kept), stage * part, (stage + 1) * part)] for stage in range(len(kept))]
+    part, values, plan = width // HALVES, [], []
+    for some in (arrived[: stages - HALVES], arrived[stages - HALVES :]):
+        *kept, crossing = split_sums(some)
+        here = len(values)
+        values += [*kept, moved(crossing, 0, True)]
+        plan += [[(here + stage, 0, part), (here + len(kept), stage * part, (stage + 1) * part)] for stage in range(len(kept))]
 
     owns, fars = sides[-1]
     groups = groups_of(shards)
@@ -317,7 +322,10 @@
             ends[hop] = moved(value, hop) if hop else value
     plan.append([(len(values) + at, 0, part) for at in range(shards)])
     values += ends
-    return totals_of(values, [plan[walker * HALVES : (walker + 1) * HALVES] for walker in range(walkers)])
+    total = None
+    for walker in range(walkers):
+        total = total_of(values, plan[walker * HALVES : (walker + 1) * HALVES], walker, walkers, total)
+    return total
 
 
 def solution(mesh):

time: 122 us -> 117 us (0.959)
  waiting for transfers between devices: 48.3 us -> 39.5 us
  starting transfers between devices: 43 us -> 46.4 us
    ppermute x31 -> x32, waiting for transfers between devices: 48.3 us -> 39.5 us  [moved(): return lax.ppermute(value, AXES, pairs)]
    ppermute x31 -> x32, starting transfers between devices: 43 us -> 46.4 us  [moved(): return lax.ppermute(value, AXES, pairs)]
  transfers between devices with their start and end apart: 31 -> 32, of which waited for: 10 -> 11; matrix products, arithmetic and copies ran while one was open for 1% -> 1% of each run, Pallas kernels for 23% -> 25%
where the time goes in v5:
time: 117 us
  starting transfers between devices  46.4 us (40%)
  waiting for transfers between devices  39.5 us (34%)
  Pallas kernels  29.5 us (25%)
    ppermute x32, starting transfers between devices, moved(): return lax.ppermute(value, AXES, pairs)  46.4 us
    ppermute x32, waiting for transfers between devices, moved(): return lax.ppermute(value, AXES, pairs)  39.5 us
    pallas_call x6, Pallas kernels, amplitudes_of(): pl.pallas_call(functools.partial(amplitude_body, shards, *vectors), in_sp...  10.5 us
    pallas_call x6, Pallas kernels, gradients_of(): pl.pallas_call(functools.partial(gradient_body, shards, len(owns), first,...  10.1 us
    pallas_call x2, Pallas kernels, loaded(): pl.pallas_call(functools.partial(load_body, half), in_specs=[SMEM, pl.Blo...  7.01 us
  transfers between devices with their start and end apart: 32, of which 11 were waited for; matrix products, arithmetic and copies ran while one was open for 1% of the time, Pallas kernels for 25%

profile of v5, /device:TPU:0, one launch (start us, length us, event | category | flops | bytes accessed | tf_op | source)
XLA Modules:
  0.0 116.6 jit_solution(2436264681828435863)
XLA Ops:
  0.0 3.0 %collective-permute-start = (bf16[2,512,128]{2,1,0:T(8,128)(2,1)}, bf16[2,512,128]{2,1,0:T(8,128)(2,1)S(1)}, u32[]{:S(2)}, u32[]{:S(2)}) collective-permute-start(bf16[2,512,128]{2,1,0:T(8,128)(2,1)} %param.3), channel_id=1, source_target_pairs={{0,2},{1,3},{2,0},{3,1},{4,6},{5,7},{6,4},{7,5},{8,10},{9,11},{10,... | collective-permute-start | bytes 786440 | tf_op jit(solution)/shard_map/ppermute | solution.py:277
  4.0 1.6 %collective-permute-start.16 = (bf16[512,128]{1,0:T(8,128)(2,1)S(1)}, bf16[512,128]{1,0:T(8,128)(2,1)S(1)}, u32[]{:S(2)}, u32[]{:S(2)}) collective-permute-start(bf16[512,128]{1,0:T(8,128)(2,1)S(1)} %get-tuple-element.85.refs_0_), channel_id=1, source_target_pairs={{0,4},{1,5},{2,6},{3,7},{4,0},{5,1},{6,2},{7,3},{8,12},{9,13},{10,... | collective-permute-start | bytes 393224 | tf_op jit(solution)/shard_map/ppermute | solution.py:277
  5.6 2.6 %collective-permute-start.17 = (bf16[512,128]{1,0:T(8,128)(2,1)S(1)}, bf16[512,128]{1,0:T(8,128)(2,1)S(1)}, u32[]{:S(2)}, u32[]{:S(2)}) collective-permute-start(bf16[512,128]{1,0:T(8,128)(2,1)S(1)} %get-tuple-element.85.refs_0_), channel_id=1, source_target_pairs={{0,8},{1,9},{2,10},{3,11},{4,12},{5,13},{6,14},{7,15},{8,0},{9,1},... | collective-permute-start | bytes 393224 | tf_op jit(solution)/shard_map/ppermute | solution.py:277
  9.5 3.9 %collective-permute-start.2 = (bf16[512,256]{1,0:T(8,128)(2,1)S(1)}, bf16[512,256]{1,0:T(8,128)(2,1)S(1)}, u32[]{:S(2)}, u32[]{:S(2)}) collective-permute-start(bf16[512,256]{1,0:T(8,128)(2,1)S(1)} %pad_maximum_fusion.refs_0_), channel_id=1, source_target_pairs={{0,12},{1,13},{2,14},{3,15},{4,8},{5,9},{6,10},{7,11},{8,4},{9,5},... | collective-permute-start | bytes 786440 | tf_op jit(solution)/shard_map/ppermute | solution.py:277
  13.5 1.5 %collective-permute-start.19 = (bf16[512,128]{1,0:T(8,128)(2,1)S(1)}, bf16[512,128]{1,0:T(8,128)(2,1)S(1)}, u32[]{:S(2)}, u32[]{:S(2)}) collective-permute-start(bf16[512,128]{1,0:T(8,128)(2,1)S(1)} %collective-permute-done.16.refs_1_), channel_id=1, source_target_pairs={{0,2},{1,3},{2,0},{3,1},{4,6},{5,7},{6,4},{7,5},{8,10},{9,11},{10,... | collective-permute-start | bytes 393224 | tf_op jit(solution)/shard_map/ppermute | solution.py:277
  15.0 8.9 %collective-permute-done.17.refs_2_ = bf16[512,128]{1,0:T(8,128)(2,1)S(1)} collective-permute-done((bf16[512,128]{1,0:T(8,128)(2,1)S(1)}, bf16[512,128]{1,0:T(8,128)(2,1)S(1)}, u32[]{:S(2)}, u32[]{:S(2)}) %collective-permute-start.17) | collective-permute-done | bytes 131104 | tf_op jit(solution)/shard_map/ppermute | solution.py:277
  24.4 1.5 %collective-permute-start.21 = (bf16[512,128]{1,0:T(8,128)(2,1)S(1)}, bf16[512,128]{1,0:T(8,128)(2,1)S(1)}, u32[]{:S(2)}, u32[]{:S(2)}) collective-permute-start(bf16[512,128]{1,0:T(8,128)(2,1)S(1)} %collective-permute-done.18.refs_3_), channel_id=1, source_target_pairs={{0,2},{1,3},{2,0},{3,1},{4,6},{5,7},{6,4},{7,5},{8,10},{9,11},{10,... | collective-permute-start | bytes 393224 | tf_op jit(solution)/shard_map/ppermute | solution.py:277
  25.9 3.5 %shard_map.28.factors.refs_2_.refs_4_ = bf16[32,64,2048]{2,1,0:T(8,128)(2,1)S(1)} custom-call(s32[1]{0:T(128)} %bitcast.place, bf16[32,128,2048]{2,1,0:T(8,128)(2,1)} %source.3), custom_call_target="tpu_custom_call" | custom-call | tf_op jit(solution)/shard_map/pallas_call | solution.py:78
  29.4 3.5 %shard_map.30.refs_3_.factors.refs_5_ = bf16[32,64,2048]{2,1,0:T(8,128)(2,1)S(1)} custom-call(s32[1]{0:T(128)} %bitcast.place, bf16[32,128,2048]{2,1,0:T(8,128)(2,1)} %source.3), custom_call_target="tpu_custom_call" | custom-call | tf_op jit(solution)/shard_map/pallas_call | solution.py:78
  32.9 1.9 %collective-permute-start.1 = (bf16[512,256]{1,0:T(8,128)(2,1)S(1)}, bf16[512,256]{1,0:T(8,128)(2,1)S(1)}, u32[]{:S(2)}, u32[]{:S(2)}) collective-permute-start(bf16[512,256]{1,0:T(8,128)(2,1)S(1)} %pad_maximum_fusion.refs_0_), channel_id=1, source_target_pairs={{0,4},{1,5},{2,6},{3,7},{4,0},{5,1},{6,2},{7,3},{8,12},{9,13},{10,... | collective-permute-start | bytes 786440 | tf_op jit(solution)/shard_map/ppermute | solution.py:277
  35.8 1.6 %collective-permute-start.22 = (bf16[512,128]{1,0:T(8,128)(2,1)S(1)}, bf16[512,128]{1,0:T(8,128)(2,1)S(1)}, u32[]{:S(2)}, u32[]{:S(2)}) collective-permute-start(bf16[512,128]{1,0:T(8,128)(2,1)S(1)} %get-tuple-element.68), channel_id=1, source_target_pairs={{0,2},{1,3},{2,0},{3,1},{4,6},{5,7},{6,4},{7,5},{8,10},{9,11},{10,... | collective-permute-start | bytes 393224 | tf_op jit(solution)/shard_map/ppermute | solution.py:277
  37.4 2.0 %shard_map.41 = (bf16[1536,128]{1,0:T(8,128)(2,1)S(1)}, bf16[1536,128]{1,0:T(8,128)(2,1)S(1)}) custom-call(s32[1]{0:T(128)} %bitcast.place, bf16[32,64,2048]{2,1,0:T(8,128)(2,1)S(1)} %shard_map.28.factors.refs_2_.refs_4_, bf16[512,128]{1,0:T(8,128)(2,1)S(1)} %get-tuple-element.85.refs_0_, bf16[512,128]{1,0:T(8,128)(2,1)S(1)} %collective-permute-done.16.refs_1_, ...), custom_call_target="tpu_custom_call" | custom-call | flops 1610612736 | bytes 6291456 | tf_op jit(solution)/shard_map/pallas_call | solution.py:110
  40.1 2.5 %shard_map.43 = (bf16[2048,128]{1,0:T(8,128)(2,1)S(1)}, bf16[2048,128]{1,0:T(8,128)(2,1)S(1)}) custom-call(s32[1]{0:T(128)} %bitcast.place, bf16[32,64,2048]{2,1,0:T(8,128)(2,1)S(1)} %shard_map.30.refs_3_.factors.refs_5_, bf16[512,128]{1,0:T(8,128)(2,1)S(1)} %get-tuple-element.85.refs_0_, bf16[512,128]{1,0:T(8,128)(2,1)S(1)} %collective-permute-done.16.refs_1_, ...), custom_call_target="tpu_custom_call" | custom-call | flops 2147483648 | bytes 8388608 | tf_op jit(solution)/shard_map/pallas_call | solution.py:110
  44.5 2.4 %shard_map.29 = (bf16[2048,128]{1,0:T(8,128)(2,1)S(1)}, bf16[2048,128]{1,0:T(8,128)(2,1)S(1)}) custom-call(s32[1]{0:T(128)} %bitcast.place, bf16[32,64,2048]{2,1,0:T(8,128)(2,1)S(1)} %shard_map.28.factors.refs_2_.refs_4_, bf16[512,256]{1,0:T(8,128)(2,1)S(1)} %pad_maximum_fusion.refs_0_, bf16[512,256]{1,0:T(8,128)(2,1)S(1)} %collective-permute-done.1.refs_1_, ...), custom_call_target="tpu_custom_call" | custom-call | flops 2147483648 | bytes 8388608 | tf_op jit(solution)/shard_map/pallas_call | solution.py:110
  47.6 1.9 %shard_map.34 = (bf16[1536,128]{1,0:T(8,128)(2,1)S(1)}, bf16[1536,128]{1,0:T(8,128)(2,1)S(1)}) custom-call(s32[1]{0:T(128)} %bitcast.place, bf16[32,64,2048]{2,1,0:T(8,128)(2,1)S(1)} %shard_map.30.refs_3_.factors.refs_5_, bf16[512,256]{1,0:T(8,128)(2,1)S(1)} %pad_maximum_fusion.refs_0_, bf16[512,256]{1,0:T(8,128)(2,1)S(1)} %collective-permute-done.1.refs_1_, ...), custom_call_target="tpu_custom_call" | custom-call | flops 1610612736 | bytes 6291456 | tf_op jit(solution)/shard_map/pallas_call | solution.py:110
  49.5 1.5 %collective-permute-start.10 = (bf16[1536,128]{1,0:T(8,128)(2,1)S(1)}, bf16[1536,128]{1,0:T(8,128)(2,1)S(1)}, u32[]{:S(2)}, u32[]{:S(2)}) collective-permute-start(bf16[1536,128]{1,0:T(8,128)(2,1)S(1)} %get-tuple-element.55), channel_id=1, source_target_pairs={{0,2},{1,3},{2,0},{3,1},{4,6},{5,7},{6,4},{7,5},{8,10},{9,11},{10,... | collective-permute-start | bytes 1179656 | tf_op jit(solution)/shard_map/ppermute | solution.py:277
  51.4 2.4 %shard_map.42 = (f32[128,512]{1,0:T(8,128)S(1)}, bf16[128,512]{1,0:T(8,128)(2,1)S(1)}, bf16[128,512]{1,0:T(8,128)(2,1)S(1)}, bf16[128,512]{1,0:T(8,128)(2,1)S(1)}) custom-call(s32[1]{0:T(128)} %bitcast.place, bf16[512,128]{1,0:T(8,128)(2,1)S(1)} %get-tuple-element.66.refs_0_, bf16[1536,128]{1,0:T(8,128)(2,1)S(1)} %get-tuple-element.67.refs_1_, ...), custom_call_target="tpu_custom_call" | custom-call | flops 2147483648 | bytes 16777216 | tf_op jit(solution)/shard_map/pallas_call | solution.py:173
  53.8 2.1 %collective-permute-start.24 = (bf16[128,512]{1,0:T(8,128)(2,1)S(1)}, bf16[128,512]{1,0:T(8,128)(2,1)S(1)}, u32[]{:S(2)}, u32[]{:S(2)}) collective-permute-start(bf16[128,512]{1,0:T(8,128)(2,1)S(1)} %get-tuple-element.71), channel_id=1, source_target_pairs={{0,4},{1,5},{2,6},{3,7},{4,0},{5,1},{6,2},{7,3},{8,12},{9,13},{10,... | collective-permute-start | bytes 393224 | tf_op jit(solution)/shard_map/ppermute | solution.py:277
  57.7 5.0 %collective-permute-done.27.refs_1_ = bf16[2048,128]{1,0:T(8,128)(2,1)S(1)} collective-permute-done((bf16[2048,128]{1,0:T(8,128)(2,1)S(1)}, bf16[2048,128]{1,0:T(8,128)(2,1)S(1)}, u32[]{:S(2)}, u32[]{:S(2)}) %collective-permute-start.27) | collective-permute-done | bytes 524320 | tf_op jit(solution)/shard_map/ppermute | solution.py:277
  62.7 2.4 %collective-permute-start.26 = (bf16[128,512]{1,0:T(8,128)(2,1)S(1)}, bf16[128,512]{1,0:T(8,128)(2,1)S(1)}, u32[]{:S(2)}, u32[]{:S(2)}) collective-permute-start(bf16[128,512]{1,0:T(8,128)(2,1)S(1)} %get-tuple-element.73), channel_id=1, source_target_pairs={{0,12},{1,13},{2,14},{3,15},{4,8},{5,9},{6,10},{7,11},{8,4},{9,5},... | collective-permute-start | bytes 393224 | tf_op jit(solution)/shard_map/ppermute | solution.py:277
  65.0 2.6 %shard_map.44 = (f32[128,512]{1,0:T(8,128)S(1)}, bf16[128,512]{1,0:T(8,128)(2,1)S(1)}, bf16[128,512]{1,0:T(8,128)(2,1)S(1)}, bf16[128,512]{1,0:T(8,128)(2,1)S(1)}) custom-call(s32[1]{0:T(128)} %bitcast.place, bf16[2048,128]{1,0:T(8,128)(2,1)S(1)} %get-tuple-element.74.refs_0_, bf16[2048,128]{1,0:T(8,128)(2,1)S(1)} %collective-permute-done.27.refs_1_, ...), custom_call_target="tpu_custom_call" | custom-call | flops 2147483648 | bytes 16777216 | tf_op jit(solution)/shard_map/pallas_call | solution.py:173
  67.7 12.0 %collective-permute-done.10.refs_1_ = bf16[1536,128]{1,0:T(8,128)(2,1)S(1)} collective-permute-done((bf16[1536,128]{1,0:T(8,128)(2,1)S(1)}, bf16[1536,128]{1,0:T(8,128)(2,1)S(1)}, u32[]{:S(2)}, u32[]{:S(2)}) %collective-permute-start.10) | collective-permute-done | bytes 393248 | tf_op jit(solution)/shard_map/ppermute | solution.py:277
  80.3 1.8 %shard_map.35.refs_4_ = f32[128,2048]{1,0:T(8,128)S(1)} custom-call(s32[1]{0:T(128)} %bitcast.place, bf16[1536,128]{1,0:T(8,128)(2,1)S(1)} %get-tuple-element.54.refs_0_, bf16[1536,128]{1,0:T(8,128)(2,1)S(1)} %collective-permute-done.10.refs_1_, bf16[32,64,2048]{2,1,0:T(8,128)(2,1)S(1)} %shard_map.28.factors.refs_2_.refs_4_, ...), custom_call_target="tpu_custom_call" | custom-call | flops 1610612736 | bytes 12582912 | tf_op jit(solution)/shard_map/pallas_call | solution.py:173
  82.1 2.4 %collective-permute-done.9.refs_1_ = bf16[512,128]{1,0:T(8,128)(2,1)S(1)} collective-permute-done((bf16[512,128]{1,0:T(8,128)(2,1)S(1)}, bf16[512,128]{1,0:T(8,128)(2,1)S(1)}, u32[]{:S(2)}, u32[]{:S(2)}) %collective-permute-start.9) | collective-permute-done | bytes 131104 | tf_op jit(solution)/shard_map/ppermute | solution.py:277
  84.6 2.0 %collective-permute-start.28 = (bf16[128,512]{1,0:T(8,128)(2,1)S(1)}, bf16[128,512]{1,0:T(8,128)(2,1)S(1)}, u32[]{:S(2)}, u32[]{:S(2)}) collective-permute-start(bf16[128,512]{1,0:T(8,128)(2,1)S(1)} %get-tuple-element.77), channel_id=1, source_target_pairs={{0,4},{1,5},{2,6},{3,7},{4,0},{5,1},{6,2},{7,3},{8,12},{9,13},{10,... | collective-permute-start | bytes 393224 | tf_op jit(solution)/shard_map/ppermute | solution.py:277
  92.0 2.4 %shard_map.31 = (f32[128,512]{1,0:T(8,128)S(1)}, bf16[128,512]{1,0:T(8,128)(2,1)S(1)}, bf16[128,512]{1,0:T(8,128)(2,1)S(1)}, bf16[128,512]{1,0:T(8,128)(2,1)S(1)}) custom-call(s32[1]{0:T(128)} %bitcast.place, bf16[2048,128]{1,0:T(8,128)(2,1)S(1)} %get-tuple-element.44.refs_0_, bf16[2048,128]{1,0:T(8,128)(2,1)S(1)} %collective-permute-done.4.refs_1_, ...), custom_call_target="tpu_custom_call" | custom-call | flops 2147483648 | bytes 16777216 | tf_op jit(solution)/shard_map/pallas_call | solution.py:173
  95.6 3.9 %collective-permute-done.29.refs_6_ = bf16[128,512]{1,0:T(8,128)(2,1)S(1)} collective-permute-done((bf16[128,512]{1,0:T(8,128)(2,1)S(1)}, bf16[128,512]{1,0:T(8,128)(2,1)S(1)}, u32[]{:S(2)}, u32[]{:S(2)}) %collective-permute-start.29) | collective-permute-done | bytes 131104 | tf_op jit(solution)/shard_map/ppermute | solution.py:277
  99.5 2.0 %collective-permute-start.7 = (bf16[128,512]{1,0:T(8,128)(2,1)S(1)}, bf16[128,512]{1,0:T(8,128)(2,1)S(1)}, u32[]{:S(2)}, u32[]{:S(2)}) collective-permute-start(bf16[128,512]{1,0:T(8,128)(2,1)S(1)} %get-tuple-element.49), channel_id=1, source_target_pairs={{0,12},{1,13},{2,14},{3,15},{4,8},{5,9},{6,10},{7,11},{8,4},{9,5},... | collective-permute-start | bytes 393224 | tf_op jit(solution)/shard_map/ppermute | solution.py:277
  102.9 3.5 %collective-permute-start.13 = (bf16[64,512]{1,0:T(8,128)(2,1)S(1)}, bf16[64,512]{1,0:T(8,128)(2,1)S(1)}, u32[]{:S(2)}, u32[]{:S(2)}) collective-permute-start(bf16[64,512]{1,0:T(8,128)(2,1)S(1)} %get-tuple-element.63), channel_id=1, source_target_pairs={{0,4},{1,5},{2,6},{3,7},{4,0},{5,1},{6,2},{7,3},{8,12},{9,13},{10,... | collective-permute-start | bytes 196616 | tf_op jit(solution)/shard_map/ppermute | solution.py:277
  106.5 2.9 %collective-permute-done.6.refs_2_ = bf16[128,512]{1,0:T(8,128)(2,1)S(1)} collective-permute-done((bf16[128,512]{1,0:T(8,128)(2,1)S(1)}, bf16[128,512]{1,0:T(8,128)(2,1)S(1)}, u32[]{:S(2)}, u32[]{:S(2)}) %collective-permute-start.6) | collective-permute-done | bytes 131104 | tf_op jit(solution)/shard_map/ppermute | solution.py:277
  109.4 2.0 %collective-permute-start.15 = (bf16[64,512]{1,0:T(8,128)(2,1)S(1)}, bf16[64,512]{1,0:T(8,128)(2,1)S(1)}, u32[]{:S(2)}, u32[]{:S(2)}) collective-permute-start(bf16[64,512]{1,0:T(8,128)(2,1)S(1)} %get-tuple-element.65), channel_id=1, source_target_pairs={{0,12},{1,13},{2,14},{3,15},{4,8},{5,9},{6,10},{7,11},{8,4},{9,5},... | collective-permute-start | bytes 196616 | tf_op jit(solution)/shard_map/ppermute | solution.py:277
  113.5 2.0 %collective-permute-done.15.refs_5_ = bf16[64,512]{1,0:T(8,128)(2,1)S(1)} collective-permute-done((bf16[64,512]{1,0:T(8,128)(2,1)S(1)}, bf16[64,512]{1,0:T(8,128)(2,1)S(1)}, u32[]{:S(2)}, u32[]{:S(2)}) %collective-permute-start.15) | collective-permute-done | bytes 65568 | tf_op jit(solution)/shard_map/ppermute | solution.py:277
  (55 shorter events, 21.4 us)
Async XLA Ops:
  0.0 9.5 %collective-permute-start = (bf16[2,512,128]{2,1,0:T(8,128)(2,1)}, bf16[2,512,128]{2,1,0:T(8,128)(2,1)S(1)}, u32[]{:S(2)}, u32[]{:S(2)}) collective-permute-start(bf16[2,512,128]{2,1,0:T(8,128)(2,1)} %param.3), channel_id=1, source_target_pairs={{0,2},{1,3},{2,0},{3,1},{4,6},{5,7},{6,4},{7,5},{8,10},{9,11},{10,... | collective-permute-start | bytes 786440 | tf_op jit(solution)/shard_map/ppermute | solution.py:277
  4.0 9.5 %collective-permute-start.16 = (bf16[512,128]{1,0:T(8,128)(2,1)S(1)}, bf16[512,128]{1,0:T(8,128)(2,1)S(1)}, u32[]{:S(2)}, u32[]{:S(2)}) collective-permute-start(bf16[512,128]{1,0:T(8,128)(2,1)S(1)} %get-tuple-element.85.refs_0_), channel_id=1, source_target_pairs={{0,4},{1,5},{2,6},{3,7},{4,0},{5,1},{6,2},{7,3},{8,12},{9,13},{10,... | collective-permute-start | bytes 393224 | tf_op jit(solution)/shard_map/ppermute | solution.py:277
  5.6 18.3 %collective-permute-start.17 = (bf16[512,128]{1,0:T(8,128)(2,1)S(1)}, bf16[512,128]{1,0:T(8,128)(2,1)S(1)}, u32[]{:S(2)}, u32[]{:S(2)}) collective-permute-start(bf16[512,128]{1,0:T(8,128)(2,1)S(1)} %get-tuple-element.85.refs_0_), channel_id=1, source_target_pairs={{0,8},{1,9},{2,10},{3,11},{4,12},{5,13},{6,14},{7,15},{8,0},{9,1},... | collective-permute-start | bytes 393224 | tf_op jit(solution)/shard_map/ppermute | solution.py:277
  8.2 16.2 %collective-permute-start.18 = (bf16[512,128]{1,0:T(8,128)(2,1)S(1)}, bf16[512,128]{1,0:T(8,128)(2,1)S(1)}, u32[]{:S(2)}, u32[]{:S(2)}) collective-permute-start(bf16[512,128]{1,0:T(8,128)(2,1)S(1)} %get-tuple-element.85.refs_0_), channel_id=1, source_target_pairs={{0,12},{1,13},{2,14},{3,15},{4,8},{5,9},{6,10},{7,11},{8,4},{9,5},... | collective-permute-start | bytes 393224 | tf_op jit(solution)/shard_map/ppermute | solution.py:277
  9.5 27.8 %collective-permute-start.2 = (bf16[512,256]{1,0:T(8,128)(2,1)S(1)}, bf16[512,256]{1,0:T(8,128)(2,1)S(1)}, u32[]{:S(2)}, u32[]{:S(2)}) collective-permute-start(bf16[512,256]{1,0:T(8,128)(2,1)S(1)} %pad_maximum_fusion.refs_0_), channel_id=1, source_target_pairs={{0,12},{1,13},{2,14},{3,15},{4,8},{5,9},{6,10},{7,11},{8,4},{9,5},... | collective-permute-start | bytes 786440 | tf_op jit(solution)/shard_map/ppermute | solution.py:277
  13.5 21.4 %collective-permute-start.19 = (bf16[512,128]{1,0:T(8,128)(2,1)S(1)}, bf16[512,128]{1,0:T(8,128)(2,1)S(1)}, u32[]{:S(2)}, u32[]{:S(2)}) collective-permute-start(bf16[512,128]{1,0:T(8,128)(2,1)S(1)} %collective-permute-done.16.refs_1_), channel_id=1, source_target_pairs={{0,2},{1,3},{2,0},{3,1},{4,6},{5,7},{6,4},{7,5},{8,10},{9,11},{10,... | collective-permute-start | bytes 393224 | tf_op jit(solution)/shard_map/ppermute | solution.py:277
  23.9 11.0 %collective-permute-start.20 = (bf16[512,128]{1,0:T(8,128)(2,1)S(1)}, bf16[512,128]{1,0:T(8,128)(2,1)S(1)}, u32[]{:S(2)}, u32[]{:S(2)}) collective-permute-start(bf16[512,128]{1,0:T(8,128)(2,1)S(1)} %collective-permute-done.17.refs_2_), channel_id=1, source_target_pairs={{0,2},{1,3},{2,0},{3,1},{4,6},{5,7},{6,4},{7,5},{8,10},{9,11},{10,... | collective-permute-start | bytes 393224 | tf_op jit(solution)/shard_map/ppermute | solution.py:277
  24.4 10.5 %collective-permute-start.21 = (bf16[512,128]{1,0:T(8,128)(2,1)S(1)}, bf16[512,128]{1,0:T(8,128)(2,1)S(1)}, u32[]{:S(2)}, u32[]{:S(2)}) collective-permute-start(bf16[512,128]{1,0:T(8,128)(2,1)S(1)} %collective-permute-done.18.refs_3_), channel_id=1, source_target_pairs={{0,2},{1,3},{2,0},{3,1},{4,6},{5,7},{6,4},{7,5},{8,10},{9,11},{10,... | collective-permute-start | bytes 393224 | tf_op jit(solution)/shard_map/ppermute | solution.py:277
  32.9 11.1 %collective-permute-start.1 = (bf16[512,256]{1,0:T(8,128)(2,1)S(1)}, bf16[512,256]{1,0:T(8,128)(2,1)S(1)}, u32[]{:S(2)}, u32[]{:S(2)}) collective-permute-start(bf16[512,256]{1,0:T(8,128)(2,1)S(1)} %pad_maximum_fusion.refs_0_), channel_id=1, source_target_pairs={{0,4},{1,5},{2,6},{3,7},{4,0},{5,1},{6,2},{7,3},{8,12},{9,13},{10,... | collective-permute-start | bytes 786440 | tf_op jit(solution)/shard_map/ppermute | solution.py:277
  35.8 15.2 %collective-permute-start.22 = (bf16[512,128]{1,0:T(8,128)(2,1)S(1)}, bf16[512,128]{1,0:T(8,128)(2,1)S(1)}, u32[]{:S(2)}, u32[]{:S(2)}) collective-permute-start(bf16[512,128]{1,0:T(8,128)(2,1)S(1)} %get-tuple-element.68), channel_id=1, source_target_pairs={{0,2},{1,3},{2,0},{3,1},{4,6},{5,7},{6,4},{7,5},{8,10},{9,11},{10,... | collective-permute-start | bytes 393224 | tf_op jit(solution)/shard_map/ppermute | solution.py:277
  37.4 7.2 %collective-permute-start.3 = (bf16[512,256]{1,0:T(8,128)(2,1)S(1)}, bf16[512,256]{1,0:T(8,128)(2,1)S(1)}, u32[]{:S(2)}, u32[]{:S(2)}) collective-permute-start(bf16[512,256]{1,0:T(8,128)(2,1)S(1)} %collective-permute-done.2.refs_3_), channel_id=1, source_target_pairs={{0,4},{1,5},{2,6},{3,7},{4,0},{5,1},{6,2},{7,3},{8,12},{9,13},{10,... | collective-permute-start | bytes 786440 | tf_op jit(solution)/shard_map/ppermute | solution.py:277
  39.4 12.1 %collective-permute-start.23 = (bf16[1536,128]{1,0:T(8,128)(2,1)S(1)}, bf16[1536,128]{1,0:T(8,128)(2,1)S(1)}, u32[]{:S(2)}, u32[]{:S(2)}) collective-permute-start(bf16[1536,128]{1,0:T(8,128)(2,1)S(1)} %get-tuple-element.69), channel_id=1, source_target_pairs={{0,2},{1,3},{2,0},{3,1},{4,6},{5,7},{6,4},{7,5},{8,10},{9,11},{10,... | collective-permute-start | bytes 1179656 | tf_op jit(solution)/shard_map/ppermute | solution.py:277
  42.6 20.0 %collective-permute-start.27 = (bf16[2048,128]{1,0:T(8,128)(2,1)S(1)}, bf16[2048,128]{1,0:T(8,128)(2,1)S(1)}, u32[]{:S(2)}, u32[]{:S(2)}) collective-permute-start(bf16[2048,128]{1,0:T(8,128)(2,1)S(1)} %get-tuple-element.75), channel_id=1, source_target_pairs={{0,2},{1,3},{2,0},{3,1},{4,6},{5,7},{6,4},{7,5},{8,10},{9,11},{10,... | collective-permute-start | bytes 1572872 | tf_op jit(solution)/shard_map/ppermute | solution.py:277
  46.9 43.8 %collective-permute-start.4 = (bf16[2048,128]{1,0:T(8,128)(2,1)S(1)}, bf16[2048,128]{1,0:T(8,128)(2,1)S(1)}, u32[]{:S(2)}, u32[]{:S(2)}) collective-permute-start(bf16[2048,128]{1,0:T(8,128)(2,1)S(1)} %get-tuple-element.45), channel_id=1, source_target_pairs={{0,2},{1,3},{2,0},{3,1},{4,6},{5,7},{6,4},{7,5},{8,10},{9,11},{10,... | collective-permute-start | bytes 1572872 | tf_op jit(solution)/shard_map/ppermute | solution.py:277
  49.5 30.1 %collective-permute-start.10 = (bf16[1536,128]{1,0:T(8,128)(2,1)S(1)}, bf16[1536,128]{1,0:T(8,128)(2,1)S(1)}, u32[]{:S(2)}, u32[]{:S(2)}) collective-permute-start(bf16[1536,128]{1,0:T(8,128)(2,1)S(1)} %get-tuple-element.55), channel_id=1, source_target_pairs={{0,2},{1,3},{2,0},{3,1},{4,6},{5,7},{6,4},{7,5},{8,10},{9,11},{10,... | collective-permute-start | bytes 1179656 | tf_op jit(solution)/shard_map/ppermute | solution.py:277
  53.8 33.7 %collective-permute-start.24 = (bf16[128,512]{1,0:T(8,128)(2,1)S(1)}, bf16[128,512]{1,0:T(8,128)(2,1)S(1)}, u32[]{:S(2)}, u32[]{:S(2)}) collective-permute-start(bf16[128,512]{1,0:T(8,128)(2,1)S(1)} %get-tuple-element.71), channel_id=1, source_target_pairs={{0,4},{1,5},{2,6},{3,7},{4,0},{5,1},{6,2},{7,3},{8,12},{9,13},{10,... | collective-permute-start | bytes 393224 | tf_op jit(solution)/shard_map/ppermute | solution.py:277
  55.9 32.6 %collective-permute-start.25 = (bf16[128,512]{1,0:T(8,128)(2,1)S(1)}, bf16[128,512]{1,0:T(8,128)(2,1)S(1)}, u32[]{:S(2)}, u32[]{:S(2)}) collective-permute-start(bf16[128,512]{1,0:T(8,128)(2,1)S(1)} %get-tuple-element.72), channel_id=1, source_target_pairs={{0,8},{1,9},{2,10},{3,11},{4,12},{5,13},{6,14},{7,15},{8,0},{9,1},... | collective-permute-start | bytes 393224 | tf_op jit(solution)/shard_map/ppermute | solution.py:277
  62.7 27.3 %collective-permute-start.26 = (bf16[128,512]{1,0:T(8,128)(2,1)S(1)}, bf16[128,512]{1,0:T(8,128)(2,1)S(1)}, u32[]{:S(2)}, u32[]{:S(2)}) collective-permute-start(bf16[128,512]{1,0:T(8,128)(2,1)S(1)} %get-tuple-element.73), channel_id=1, source_target_pairs={{0,12},{1,13},{2,14},{3,15},{4,8},{5,9},{6,10},{7,11},{8,4},{9,5},... | collective-permute-start | bytes 393224 | tf_op jit(solution)/shard_map/ppermute | solution.py:277
  79.6 5.0 %collective-permute-start.9 = (bf16[512,128]{1,0:T(8,128)(2,1)S(1)}, bf16[512,128]{1,0:T(8,128)(2,1)S(1)}, u32[]{:S(2)}, u32[]{:S(2)}) collective-permute-start(bf16[512,128]{1,0:T(8,128)(2,1)S(1)} %get-tuple-element.53), channel_id=1, source_target_pairs={{0,2},{1,3},{2,0},{3,1},{4,6},{5,7},{6,4},{7,5},{8,10},{9,11},{10,... | collective-permute-start | bytes 393224 | tf_op jit(solution)/shard_map/ppermute | solution.py:277
  84.6 9.8 %collective-permute-start.28 = (bf16[128,512]{1,0:T(8,128)(2,1)S(1)}, bf16[128,512]{1,0:T(8,128)(2,1)S(1)}, u32[]{:S(2)}, u32[]{:S(2)}) collective-permute-start(bf16[128,512]{1,0:T(8,128)(2,1)S(1)} %get-tuple-element.77), channel_id=1, source_target_pairs={{0,4},{1,5},{2,6},{3,7},{4,0},{5,1},{6,2},{7,3},{8,12},{9,13},{10,... | collective-permute-start | bytes 393224 | tf_op jit(solution)/shard_map/ppermute | solution.py:277
  87.5 12.0 %collective-permute-start.29 = (bf16[128,512]{1,0:T(8,128)(2,1)S(1)}, bf16[128,512]{1,0:T(8,128)(2,1)S(1)}, u32[]{:S(2)}, u32[]{:S(2)}) collective-permute-start(bf16[128,512]{1,0:T(8,128)(2,1)S(1)} %get-tuple-element.78), channel_id=1, source_target_pairs={{0,8},{1,9},{2,10},{3,11},{4,12},{5,13},{6,14},{7,15},{8,0},{9,1},... | collective-permute-start | bytes 393224 | tf_op jit(solution)/shard_map/ppermute | solution.py:277
  88.5 11.0 %collective-permute-start.30 = (bf16[128,512]{1,0:T(8,128)(2,1)S(1)}, bf16[128,512]{1,0:T(8,128)(2,1)S(1)}, u32[]{:S(2)}, u32[]{:S(2)}) collective-permute-start(bf16[128,512]{1,0:T(8,128)(2,1)S(1)} %get-tuple-element.79), channel_id=1, source_target_pairs={{0,12},{1,13},{2,14},{3,15},{4,8},{5,9},{6,10},{7,11},{8,4},{9,5},... | collective-permute-start | bytes 393224 | tf_op jit(solution)/shard_map/ppermute | solution.py:277
  90.0 12.9 %collective-permute-start.11 = (bf16[64,1024]{1,0:T(8,128)(2,1)S(1)}, bf16[64,1024]{1,0:T(8,128)(2,1)S(1)}, u32[]{:S(2)}, u32[]{:S(2)}) collective-permute-start(bf16[64,1024]{1,0:T(8,128)(2,1)S(1)} %get-tuple-element.56), channel_id=1, source_target_pairs={{0,2},{1,3},{2,0},{3,1},{4,6},{5,7},{6,4},{7,5},{8,10},{9,11},{10,... | collective-permute-start | bytes 393224 | tf_op jit(solution)/shard_map/ppermute | solution.py:277
  90.7 10.9 %collective-permute-start.12 = (bf16[64,1024]{1,0:T(8,128)(2,1)S(1)}, bf16[64,1024]{1,0:T(8,128)(2,1)S(1)}, u32[]{:S(2)}, u32[]{:S(2)}) collective-permute-start(bf16[64,1024]{1,0:T(8,128)(2,1)S(1)} %get-tuple-element.60), channel_id=1, source_target_pairs={{0,2},{1,3},{2,0},{3,1},{4,6},{5,7},{6,4},{7,5},{8,10},{9,11},{10,... | collective-permute-start | bytes 393224 | tf_op jit(solution)/shard_map/ppermute | solution.py:277
  94.4 11.9 %collective-permute-start.5 = (bf16[128,512]{1,0:T(8,128)(2,1)S(1)}, bf16[128,512]{1,0:T(8,128)(2,1)S(1)}, u32[]{:S(2)}, u32[]{:S(2)}) collective-permute-start(bf16[128,512]{1,0:T(8,128)(2,1)S(1)} %get-tuple-element.47), channel_id=1, source_target_pairs={{0,4},{1,5},{2,6},{3,7},{4,0},{5,1},{6,2},{7,3},{8,12},{9,13},{10,... | collective-permute-start | bytes 393224 | tf_op jit(solution)/shard_map/ppermute | solution.py:277
  99.5 9.9 %collective-permute-start.6 = (bf16[128,512]{1,0:T(8,128)(2,1)S(1)}, bf16[128,512]{1,0:T(8,128)(2,1)S(1)}, u32[]{:S(2)}, u32[]{:S(2)}) collective-permute-start(bf16[128,512]{1,0:T(8,128)(2,1)S(1)} %get-tuple-element.48), channel_id=1, source_target_pairs={{0,8},{1,9},{2,10},{3,11},{4,12},{5,13},{6,14},{7,15},{8,0},{9,1},... | collective-permute-start | bytes 393224 | tf_op jit(solution)/shard_map/ppermute | solution.py:277
  99.5 11.9 %collective-permute-start.7 = (bf16[128,512]{1,0:T(8,128)(2,1)S(1)}, bf16[128,512]{1,0:T(8,128)(2,1)S(1)}, u32[]{:S(2)}, u32[]{:S(2)}) collective-permute-start(bf16[128,512]{1,0:T(8,128)(2,1)S(1)} %get-tuple-element.49), channel_id=1, source_target_pairs={{0,12},{1,13},{2,14},{3,15},{4,8},{5,9},{6,10},{7,11},{8,4},{9,5},... | collective-permute-start | bytes 393224 | tf_op jit(solution)/shard_map/ppermute | solution.py:277
  101.6 11.0 %collective-permute-start.31 = (bf16[128,512]{1,0:T(8,128)(2,1)S(1)}, bf16[128,512]{1,0:T(8,128)(2,1)S(1)}, u32[]{:S(2)}, u32[]{:S(2)}) collective-permute-start(bf16[128,512]{1,0:T(8,128)(2,1)S(1)} %get-tuple-element.82), channel_id=1, source_target_pairs={{0,2},{1,3},{2,0},{3,1},{4,6},{5,7},{6,4},{7,5},{8,10},{9,11},{10,... | collective-permute-start | bytes 393224 | tf_op jit(solution)/shard_map/ppermute | solution.py:277
  102.9 10.6 %collective-permute-start.13 = (bf16[64,512]{1,0:T(8,128)(2,1)S(1)}, bf16[64,512]{1,0:T(8,128)(2,1)S(1)}, u32[]{:S(2)}, u32[]{:S(2)}) collective-permute-start(bf16[64,512]{1,0:T(8,128)(2,1)S(1)} %get-tuple-element.63), channel_id=1, source_target_pairs={{0,4},{1,5},{2,6},{3,7},{4,0},{5,1},{6,2},{7,3},{8,12},{9,13},{10,... | collective-permute-start | bytes 196616 | tf_op jit(solution)/shard_map/ppermute | solution.py:277
  106.4 7.1 %collective-permute-start.14 = (bf16[64,512]{1,0:T(8,128)(2,1)S(1)}, bf16[64,512]{1,0:T(8,128)(2,1)S(1)}, u32[]{:S(2)}, u32[]{:S(2)}) collective-permute-start(bf16[64,512]{1,0:T(8,128)(2,1)S(1)} %get-tuple-element.64), channel_id=1, source_target_pairs={{0,8},{1,9},{2,10},{3,11},{4,12},{5,13},{6,14},{7,15},{8,0},{9,1},... | collective-permute-start | bytes 196616 | tf_op jit(solution)/shard_map/ppermute | solution.py:277
  109.4 6.1 %collective-permute-start.15 = (bf16[64,512]{1,0:T(8,128)(2,1)S(1)}, bf16[64,512]{1,0:T(8,128)(2,1)S(1)}, u32[]{:S(2)}, u32[]{:S(2)}) collective-permute-start(bf16[64,512]{1,0:T(8,128)(2,1)S(1)} %get-tuple-element.65), channel_id=1, source_target_pairs={{0,12},{1,13},{2,14},{3,15},{4,8},{5,9},{6,10},{7,11},{8,4},{9,5},... | collective-permute-start | bytes 196616 | tf_op jit(solution)/shard_map/ppermute | solution.py:277
  111.4 4.3 %collective-permute-start.8 = (bf16[64,512]{1,0:T(8,128)(2,1)S(1)}, bf16[64,512]{1,0:T(8,128)(2,1)S(1)}, u32[]{:S(2)}, u32[]{:S(2)}) collective-permute-start(bf16[64,512]{1,0:T(8,128)(2,1)S(1)} %get-tuple-element.51), channel_id=1, source_target_pairs={{0,2},{1,3},{2,0},{3,1},{4,6},{5,7},{6,4},{7,5},{8,10},{9,11},{10,... | collective-permute-start | bytes 196616 | tf_op jit(solution)/shard_map/ppermute | solution.py:277

commit v6 on v4

--- a/solution.py
+++ b/solution.py
@@ -51,11 +51,6 @@
     return shards - 2 if shards > 2 and shards & (shards - 1) == 0 else None
 
 
-def groups_of(shards):
-    hops = list(range(shards - 1, -1, -1))
-    return [hops[: shards // 2], hops[shards // 2 :]]
-
-
 def load_body(half, place, source, out, arrived):
     del place
     vectors, part = out.shape[0] // STREAMS, out.shape[1]
@@ -114,7 +109,7 @@
     )(place, factors, *pieces)
 
 
-def gradient_body(shards, parts, first, carried, group, place, *refs):
+def gradient_body(shards, parts, first, carried, apart, place, *refs):
     owns, fars, factors = refs[:parts], refs[parts : 2 * parts], refs[2 * parts : 2 * parts + HALVES]
     outs, sums = refs[2 * parts + HALVES + carried : -1], refs[-1]
     width = owns[0].shape[1]
@@ -129,22 +124,14 @@
     def columns_of(hop):
         return pl.ds(pl.multiple_of(peer(place[0], hop, shards) * owned, owned), owned)
 
-    if group is not None:
-        taken = wide(slots)
-        for at, hop in enumerate(group):
-            columns = columns_of(hop)
-            rows = jnp.concatenate([loaded[g, :, columns] for g in range(first, first + len(slots)) for loaded in factors], axis=0)
-            total = refs[2 * parts + HALVES][:, columns] + jnp.dot(taken, rows, preferred_element_type=jnp.float32)
-            outs[at][...] = total[:part]
-            outs[-1][:, at * owned : (at + 1) * owned] = total[part:].astype(jnp.bfloat16)
-        return
-
     for seen in range(0, len(slots), BLOCK):
         vectors = slots[seen : seen + BLOCK]
         low = first + seen
         rows = jnp.concatenate([loaded[g] for g in range(low, low + len(vectors)) for loaded in factors], axis=0)
         grown = jnp.dot(wide(vectors), rows, preferred_element_type=jnp.float32)
-        if seen == 0:
+        if seen == 0 and carried:
+            sums[...] = refs[2 * parts + HALVES][...] + grown
+        elif seen == 0:
             sums[...] = grown
         else:
             sums[...] += grown
@@ -152,22 +139,25 @@
         outs[0][...] = sums[...]
         return
     for hop in range(shards):
-        outs[hop][...] = sums[:, columns_of(hop)].astype(outs[hop].dtype)
-
-
-def gradients_of(place, factors, owns, fars, shards, first=0, group=None, carried=None, more=False):
+        if apart:
+            outs[hop][...] = sums[:part, columns_of(hop)].astype(outs[hop].dtype)
+            outs[shards + hop][...] = sums[part:, columns_of(hop)].astype(outs[shards + hop].dtype)
+        else:
+            outs[hop][...] = sums[:, columns_of(hop)].astype(outs[hop].dtype)
+
+
+def gradients_of(place, factors, owns, fars, shards, first=0, apart=False, carried=None, more=False):
     orbitals, width = factors[0].shape[2], owns[0].shape[1]
     part, owned = width // HALVES, orbitals // shards
     outs = [jax.ShapeDtypeStruct((2 * part, owned), jnp.bfloat16 if hop else jnp.float32) for hop in range(shards)]
     if more:
         outs = [jax.ShapeDtypeStruct((2 * part, orbitals), jnp.float32)]
-    elif group:
-        outs = [jax.ShapeDtypeStruct((part, owned), jnp.float32)] * len(group)
-        outs += [jax.ShapeDtypeStruct((part, owned * len(group)), jnp.bfloat16)]
+    elif apart:
+        outs = [jax.ShapeDtypeStruct((part, owned), jnp.bfloat16 if at else jnp.float32) for at in range(2 * shards)]
     count = sum(own.shape[0] for own in owns) * HALVES
     values = [place, *owns, *fars, *factors] + ([] if carried is None else [carried])
     return pl.pallas_call(
-        functools.partial(gradient_body, shards, len(owns), first, 0 if carried is None else 1, group),
+        functools.partial(gradient_body, shards, len(owns), first, 0 if carried is None else 1, apart),
         in_specs=[SMEM] + [VMEM] * (len(values) - 1),
         out_specs=[VMEM] * len(outs),
         scratch_shapes=[pltpu.VMEM((2 * part, orbitals), jnp.float32)],
@@ -197,19 +187,6 @@
     return pl.pallas_call(functools.partial(split_body, len(stages[0])), out_shape=outs, compiler_params=SMALL)(*flat)
 
 
-def join_body(came, *refs):
-    count = len(refs) // 2
-    for at in range(count):
-        own, out = refs[at], refs[count + at]
-        columns = own.shape[1]
-        out[...] = (own[...] + came[:, at * columns : (at + 1) * columns].astype(jnp.float32)).astype(out.dtype)
-
-
-def join_sums(came, owns, kinds):
-    outs = [jax.ShapeDtypeStruct(own.shape, kind) for own, kind in zip(owns, kinds)]
-    return pl.pallas_call(join_body, out_shape=outs, compiler_params=SMALL)(came, *owns)
-
-
 def total_body(plan, *refs):
     out = refs[-1]
     for walker, halves in enumerate(plan):
@@ -305,17 +282,11 @@
     plan = [[(stage, 0, part), (len(kept), stage * part, (stage + 1) * part)] for stage in range(len(kept))]
 
     owns, fars = sides[-1]
-    groups = groups_of(shards)
     (carried,) = gradients_of(place, factors, owns[:1], fars[:1], shards, more=True)
-    cut = parts_of(stages - 1, stages, vectors)[1]
-    ends = [None] * shards
-    for group in groups:
-        *own, far = gradients_of(place, factors, owns[1:], fars[1:], shards, cut, group, carried)
-        came = moved(far, 0, True)
-        joined = join_sums(came, own, [jnp.bfloat16 if hop else jnp.float32 for hop in group])
-        for hop, value in zip(group, joined):
-            ends[hop] = moved(value, hop) if hop else value
-    plan.append([(len(values) + at, 0, part) for at in range(shards)])
+    got = gradients_of(place, factors, owns[1:], fars[1:], shards, parts_of(stages - 1, stages, vectors)[1], True, carried)
+    ends = [got[0]] + [moved(got[hop], hop) for hop in hops]
+    ends += [moved(got[shards + hop], hop, True) for hop in range(shards)]
+    plan.append([(len(values) + at, 0, part) for at in range(len(ends))])
     values += ends
     return totals_of(values, [plan[walker * HALVES : (walker + 1) * HALVES] for walker in range(walkers)])
 

time: 122 us -> 116 us (0.951)
  waiting for transfers between devices: 48.3 us -> 35.6 us
  starting transfers between devices: 43 us -> 50.3 us
    ppermute x31 -> x33, waiting for transfers between devices: 48.3 us -> 35.6 us  [moved(): return lax.ppermute(value, AXES, pairs)]
    ppermute x31 -> x33, starting transfers between devices: 43 us -> 50.3 us  [moved(): return lax.ppermute(value, AXES, pairs)]
    pallas_call x6 -> x5, Pallas kernels: 10.1 us -> 9.98 us  [gradients_of(): pl.pallas_call(functools.partial(gradient_body, shards, len(owns), first,...]
  transfers between devices with their start and end apart: 31 -> 33, of which waited for: 10 -> 13; matrix products, arithmetic and copies ran while one was open for 1% -> 1% of each run, Pallas kernels for 23% -> 24%
where the time goes in v6:
time: 116 us
  starting transfers between devices  50.3 us (43%)
  waiting for transfers between devices  35.6 us (31%)
  Pallas kernels  28.6 us (25%)
    ppermute x33, starting transfers between devices, moved(): return lax.ppermute(value, AXES, pairs)  50.3 us
    ppermute x33, waiting for transfers between devices, moved(): return lax.ppermute(value, AXES, pairs)  35.6 us
    pallas_call x6, Pallas kernels, amplitudes_of(): pl.pallas_call(functools.partial(amplitude_body, shards, *vectors), in_sp...  10.5 us
    pallas_call x5, Pallas kernels, gradients_of(): pl.pallas_call(functools.partial(gradient_body, shards, len(owns), first,...  9.98 us
    pallas_call x2, Pallas kernels, loaded(): pl.pallas_call(functools.partial(load_body, half), in_specs=[SMEM, pl.Blo...  7.01 us
  transfers between devices with their start and end apart: 33, of which 13 were waited for; matrix products, arithmetic and copies ran while one was open for 1% of the time, Pallas kernels for 24%

profile of v6, /device:TPU:0, one launch (start us, length us, event | category | flops | bytes accessed | tf_op | source)
XLA Modules:
  0.0 115.8 jit_solution(2597643367238972206)
XLA Ops:
  0.0 3.0 %collective-permute-start.3 = (bf16[2,512,128]{2,1,0:T(8,128)(2,1)}, bf16[2,512,128]{2,1,0:T(8,128)(2,1)S(1)}, u32[]{:S(2)}, u32[]{:S(2)}) collective-permute-start(bf16[2,512,128]{2,1,0:T(8,128)(2,1)} %param.3), channel_id=1, source_target_pairs={{0,2},{1,3},{2,0},{3,1},{4,6},{5,7},{6,4},{7,5},{8,10},{9,11},{10,... | collective-permute-start | bytes 786440 | tf_op jit(solution)/shard_map/ppermute | solution.py:251
  4.0 1.6 %collective-permute-start = (bf16[512,128]{1,0:T(8,128)(2,1)S(1)}, bf16[512,128]{1,0:T(8,128)(2,1)S(1)}, u32[]{:S(2)}, u32[]{:S(2)}) collective-permute-start(bf16[512,128]{1,0:T(8,128)(2,1)S(1)} %get-tuple-element.78.refs_0_), channel_id=1, source_target_pairs={{0,4},{1,5},{2,6},{3,7},{4,0},{5,1},{6,2},{7,3},{8,12},{9,13},{10,... | collective-permute-start | bytes 393224 | tf_op jit(solution)/shard_map/ppermute | solution.py:251
  5.6 2.6 %collective-permute-start.1 = (bf16[512,128]{1,0:T(8,128)(2,1)S(1)}, bf16[512,128]{1,0:T(8,128)(2,1)S(1)}, u32[]{:S(2)}, u32[]{:S(2)}) collective-permute-start(bf16[512,128]{1,0:T(8,128)(2,1)S(1)} %get-tuple-element.78.refs_0_), channel_id=1, source_target_pairs={{0,8},{1,9},{2,10},{3,11},{4,12},{5,13},{6,14},{7,15},{8,0},{9,1},... | collective-permute-start | bytes 393224 | tf_op jit(solution)/shard_map/ppermute | solution.py:251
  9.5 3.9 %collective-permute-start.17 = (bf16[512,256]{1,0:T(8,128)(2,1)S(1)}, bf16[512,256]{1,0:T(8,128)(2,1)S(1)}, u32[]{:S(2)}, u32[]{:S(2)}) collective-permute-start(bf16[512,256]{1,0:T(8,128)(2,1)S(1)} %pad_maximum_fusion.refs_0_), channel_id=1, source_target_pairs={{0,12},{1,13},{2,14},{3,15},{4,8},{5,9},{6,10},{7,11},{8,4},{9,5},... | collective-permute-start | bytes 786440 | tf_op jit(solution)/shard_map/ppermute | solution.py:251
  15.0 8.9 %collective-permute-done.1.refs_2_ = bf16[512,128]{1,0:T(8,128)(2,1)S(1)} collective-permute-done((bf16[512,128]{1,0:T(8,128)(2,1)S(1)}, bf16[512,128]{1,0:T(8,128)(2,1)S(1)}, u32[]{:S(2)}, u32[]{:S(2)}) %collective-permute-start.1) | collective-permute-done | bytes 131104 | tf_op jit(solution)/shard_map/ppermute | solution.py:251
  25.9 3.5 %shard_map.28.factors.refs_4_.refs_2_ = bf16[32,64,2048]{2,1,0:T(8,128)(2,1)S(1)} custom-call(s32[1]{0:T(128)} %bitcast.place, bf16[32,128,2048]{2,1,0:T(8,128)(2,1)} %source.3), custom_call_target="tpu_custom_call" | custom-call | tf_op jit(solution)/shard_map/pallas_call | solution.py:69
  29.4 3.5 %shard_map.31.refs_5_.factors.refs_3_ = bf16[32,64,2048]{2,1,0:T(8,128)(2,1)S(1)} custom-call(s32[1]{0:T(128)} %bitcast.place, bf16[32,128,2048]{2,1,0:T(8,128)(2,1)} %source.3), custom_call_target="tpu_custom_call" | custom-call | tf_op jit(solution)/shard_map/pallas_call | solution.py:69
  32.9 1.9 %collective-permute-start.16 = (bf16[512,256]{1,0:T(8,128)(2,1)S(1)}, bf16[512,256]{1,0:T(8,128)(2,1)S(1)}, u32[]{:S(2)}, u32[]{:S(2)}) collective-permute-start(bf16[512,256]{1,0:T(8,128)(2,1)S(1)} %pad_maximum_fusion.refs_0_), channel_id=1, source_target_pairs={{0,4},{1,5},{2,6},{3,7},{4,0},{5,1},{6,2},{7,3},{8,12},{9,13},{10,... | collective-permute-start | bytes 786440 | tf_op jit(solution)/shard_map/ppermute | solution.py:251
  37.4 2.0 %shard_map.30 = (bf16[1536,128]{1,0:T(8,128)(2,1)S(1)}, bf16[1536,128]{1,0:T(8,128)(2,1)S(1)}) custom-call(s32[1]{0:T(128)} %bitcast.place, bf16[32,64,2048]{2,1,0:T(8,128)(2,1)S(1)} %shard_map.28.factors.refs_4_.refs_2_, bf16[512,128]{1,0:T(8,128)(2,1)S(1)} %get-tuple-element.78.refs_0_, bf16[512,128]{1,0:T(8,128)(2,1)S(1)} %collective-permute-done.refs_1_, ...), custom_call_target="tpu_custom_call" | custom-call | flops 1610612736 | bytes 6291456 | tf_op jit(solution)/shard_map/pallas_call | solution.py:101
  40.1 2.5 %shard_map.33 = (bf16[2048,128]{1,0:T(8,128)(2,1)S(1)}, bf16[2048,128]{1,0:T(8,128)(2,1)S(1)}) custom-call(s32[1]{0:T(128)} %bitcast.place, bf16[32,64,2048]{2,1,0:T(8,128)(2,1)S(1)} %shard_map.31.refs_5_.factors.refs_3_, bf16[512,128]{1,0:T(8,128)(2,1)S(1)} %get-tuple-element.78.refs_0_, bf16[512,128]{1,0:T(8,128)(2,1)S(1)} %collective-permute-done.refs_1_, ...), custom_call_target="tpu_custom_call" | custom-call | flops 2147483648 | bytes 8388608 | tf_op jit(solution)/shard_map/pallas_call | solution.py:101
  44.5 2.4 %shard_map.35 = (bf16[2048,128]{1,0:T(8,128)(2,1)S(1)}, bf16[2048,128]{1,0:T(8,128)(2,1)S(1)}) custom-call(s32[1]{0:T(128)} %bitcast.place, bf16[32,64,2048]{2,1,0:T(8,128)(2,1)S(1)} %shard_map.28.factors.refs_4_.refs_2_, bf16[512,256]{1,0:T(8,128)(2,1)S(1)} %pad_maximum_fusion.refs_0_, bf16[512,256]{1,0:T(8,128)(2,1)S(1)} %collective-permute-done.16.refs_1_, ...), custom_call_target="tpu_custom_call" | custom-call | flops 2147483648 | bytes 8388608 | tf_op jit(solution)/shard_map/pallas_call | solution.py:101
  47.6 3.8 %collective-permute-done.8.refs_3_ = bf16[1536,128]{1,0:T(8,128)(2,1)S(1)} collective-permute-done((bf16[1536,128]{1,0:T(8,128)(2,1)S(1)}, bf16[1536,128]{1,0:T(8,128)(2,1)S(1)}, u32[]{:S(2)}, u32[]{:S(2)}) %collective-permute-start.8) | collective-permute-done | bytes 393248 | tf_op jit(solution)/shard_map/ppermute | solution.py:251
  51.4 2.4 %shard_map.32 = (f32[128,512]{1,0:T(8,128)S(1)}, bf16[128,512]{1,0:T(8,128)(2,1)S(1)}, bf16[128,512]{1,0:T(8,128)(2,1)S(1)}, bf16[128,512]{1,0:T(8,128)(2,1)S(1)}) custom-call(s32[1]{0:T(128)} %bitcast.place, bf16[512,128]{1,0:T(8,128)(2,1)S(1)} %get-tuple-element.41.refs_0_, bf16[1536,128]{1,0:T(8,128)(2,1)S(1)} %get-tuple-element.42.refs_1_, ...), custom_call_target="tpu_custom_call" | custom-call | flops 2147483648 | bytes 16777216 | tf_op jit(solution)/shard_map/pallas_call | solution.py:159
  53.8 2.1 %collective-permute-start.9 = (bf16[128,512]{1,0:T(8,128)(2,1)S(1)}, bf16[128,512]{1,0:T(8,128)(2,1)S(1)}, u32[]{:S(2)}, u32[]{:S(2)}) collective-permute-start(bf16[128,512]{1,0:T(8,128)(2,1)S(1)} %get-tuple-element.46), channel_id=1, source_target_pairs={{0,4},{1,5},{2,6},{3,7},{4,0},{5,1},{6,2},{7,3},{8,12},{9,13},{10,... | collective-permute-start | bytes 393224 | tf_op jit(solution)/shard_map/ppermute | solution.py:251
  58.3 1.9 %shard_map.39 = (bf16[1536,128]{1,0:T(8,128)(2,1)S(1)}, bf16[1536,128]{1,0:T(8,128)(2,1)S(1)}) custom-call(s32[1]{0:T(128)} %bitcast.place, bf16[32,64,2048]{2,1,0:T(8,128)(2,1)S(1)} %shard_map.31.refs_5_.factors.refs_3_, bf16[512,256]{1,0:T(8,128)(2,1)S(1)} %pad_maximum_fusion.refs_0_, bf16[512,256]{1,0:T(8,128)(2,1)S(1)} %collective-permute-done.16.refs_1_, ...), custom_call_target="tpu_custom_call" | custom-call | flops 1610612736 | bytes 6291456 | tf_op jit(solution)/shard_map/pallas_call | solution.py:101
  60.2 2.5 %collective-permute-done.12.refs_1_ = bf16[2048,128]{1,0:T(8,128)(2,1)S(1)} collective-permute-done((bf16[2048,128]{1,0:T(8,128)(2,1)S(1)}, bf16[2048,128]{1,0:T(8,128)(2,1)S(1)}, u32[]{:S(2)}, u32[]{:S(2)}) %collective-permute-start.12) | collective-permute-done | bytes 524320 | tf_op jit(solution)/shard_map/ppermute | solution.py:251
  63.4 2.6 %shard_map.34 = (f32[128,512]{1,0:T(8,128)S(1)}, bf16[128,512]{1,0:T(8,128)(2,1)S(1)}, bf16[128,512]{1,0:T(8,128)(2,1)S(1)}, bf16[128,512]{1,0:T(8,128)(2,1)S(1)}) custom-call(s32[1]{0:T(128)} %bitcast.place, bf16[2048,128]{1,0:T(8,128)(2,1)S(1)} %get-tuple-element.49.refs_0_, bf16[2048,128]{1,0:T(8,128)(2,1)S(1)} %collective-permute-done.12.refs_1_, ...), custom_call_target="tpu_custom_call" | custom-call | flops 2147483648 | bytes 16777216 | tf_op jit(solution)/shard_map/pallas_call | solution.py:159
  66.0 1.9 %collective-permute-start.13 = (bf16[128,512]{1,0:T(8,128)(2,1)S(1)}, bf16[128,512]{1,0:T(8,128)(2,1)S(1)}, u32[]{:S(2)}, u32[]{:S(2)}) collective-permute-start(bf16[128,512]{1,0:T(8,128)(2,1)S(1)} %get-tuple-element.52), channel_id=1, source_target_pairs={{0,4},{1,5},{2,6},{3,7},{4,0},{5,1},{6,2},{7,3},{8,12},{9,13},{10,... | collective-permute-start | bytes 393224 | tf_op jit(solution)/shard_map/ppermute | solution.py:251
  67.9 6.0 %collective-permute-done.19.refs_1_ = bf16[2048,128]{1,0:T(8,128)(2,1)S(1)} collective-permute-done((bf16[2048,128]{1,0:T(8,128)(2,1)S(1)}, bf16[2048,128]{1,0:T(8,128)(2,1)S(1)}, u32[]{:S(2)}, u32[]{:S(2)}) %collective-permute-start.19) | collective-permute-done | bytes 524320 | tf_op jit(solution)/shard_map/ppermute | solution.py:251
  73.9 2.9 %collective-permute-start.14 = (bf16[128,512]{1,0:T(8,128)(2,1)S(1)}, bf16[128,512]{1,0:T(8,128)(2,1)S(1)}, u32[]{:S(2)}, u32[]{:S(2)}) collective-permute-start(bf16[128,512]{1,0:T(8,128)(2,1)S(1)} %get-tuple-element.53), channel_id=1, source_target_pairs={{0,8},{1,9},{2,10},{3,11},{4,12},{5,13},{6,14},{7,15},{8,0},{9,1},... | collective-permute-start | bytes 393224 | tf_op jit(solution)/shard_map/ppermute | solution.py:251
  76.8 2.4 %shard_map.36 = (f32[128,512]{1,0:T(8,128)S(1)}, bf16[128,512]{1,0:T(8,128)(2,1)S(1)}, bf16[128,512]{1,0:T(8,128)(2,1)S(1)}, bf16[128,512]{1,0:T(8,128)(2,1)S(1)}) custom-call(s32[1]{0:T(128)} %bitcast.place, bf16[2048,128]{1,0:T(8,128)(2,1)S(1)} %get-tuple-element.55.refs_0_, bf16[2048,128]{1,0:T(8,128)(2,1)S(1)} %collective-permute-done.19.refs_1_, ...), custom_call_target="tpu_custom_call" | custom-call | flops 2147483648 | bytes 16777216 | tf_op jit(solution)/shard_map/pallas_call | solution.py:159
  80.8 2.9 %collective-permute-start.21 = (bf16[128,512]{1,0:T(8,128)(2,1)S(1)}, bf16[128,512]{1,0:T(8,128)(2,1)S(1)}, u32[]{:S(2)}, u32[]{:S(2)}) collective-permute-start(bf16[128,512]{1,0:T(8,128)(2,1)S(1)} %get-tuple-element.59), channel_id=1, source_target_pairs={{0,8},{1,9},{2,10},{3,11},{4,12},{5,13},{6,14},{7,15},{8,0},{9,1},... | collective-permute-start | bytes 393224 | tf_op jit(solution)/shard_map/ppermute | solution.py:251
  83.7 3.1 %collective-permute-done.14.refs_6_ = bf16[128,512]{1,0:T(8,128)(2,1)S(1)} collective-permute-done((bf16[128,512]{1,0:T(8,128)(2,1)S(1)}, bf16[128,512]{1,0:T(8,128)(2,1)S(1)}, u32[]{:S(2)}, u32[]{:S(2)}) %collective-permute-start.14) | collective-permute-done | bytes 131104 | tf_op jit(solution)/shard_map/ppermute | solution.py:251
  86.8 2.0 %collective-permute-start.22 = (bf16[128,512]{1,0:T(8,128)(2,1)S(1)}, bf16[128,512]{1,0:T(8,128)(2,1)S(1)}, u32[]{:S(2)}, u32[]{:S(2)}) collective-permute-start(bf16[128,512]{1,0:T(8,128)(2,1)S(1)} %get-tuple-element.60), channel_id=1, source_target_pairs={{0,12},{1,13},{2,14},{3,15},{4,8},{5,9},{6,10},{7,11},{8,4},{9,5},... | collective-permute-start | bytes 393224 | tf_op jit(solution)/shard_map/ppermute | solution.py:251
  89.6 2.5 %collective-permute-start.24 = (bf16[512,128]{1,0:T(8,128)(2,1)S(1)}, bf16[512,128]{1,0:T(8,128)(2,1)S(1)}, u32[]{:S(2)}, u32[]{:S(2)}) collective-permute-start(bf16[512,128]{1,0:T(8,128)(2,1)S(1)} %get-tuple-element.66), channel_id=1, source_target_pairs={{0,2},{1,3},{2,0},{3,1},{4,6},{5,7},{6,4},{7,5},{8,10},{9,11},{10,... | collective-permute-start | bytes 393224 | tf_op jit(solution)/shard_map/ppermute | solution.py:251
  94.8 1.8 %shard_map.40.refs_4_ = f32[128,2048]{1,0:T(8,128)S(1)} custom-call(s32[1]{0:T(128)} %bitcast.place, bf16[1536,128]{1,0:T(8,128)(2,1)S(1)} %get-tuple-element.67.refs_0_, bf16[1536,128]{1,0:T(8,128)(2,1)S(1)} %collective-permute-done.25.refs_1_, bf16[32,64,2048]{2,1,0:T(8,128)(2,1)S(1)} %shard_map.28.factors.refs_4_.refs_2_, ...), custom_call_target="tpu_custom_call" | custom-call | flops 1610612736 | bytes 12582912 | tf_op jit(solution)/shard_map/pallas_call | solution.py:159
  97.4 2.0 %collective-permute-start.26 = (bf16[64,512]{1,0:T(8,128)(2,1)S(1)}, bf16[64,512]{1,0:T(8,128)(2,1)S(1)}, u32[]{:S(2)}, u32[]{:S(2)}) collective-permute-start(bf16[64,512]{1,0:T(8,128)(2,1)S(1)} %get-tuple-element.70), channel_id=1, source_target_pairs={{0,4},{1,5},{2,6},{3,7},{4,0},{5,1},{6,2},{7,3},{8,12},{9,13},{10,... | collective-permute-start | bytes 196616 | tf_op jit(solution)/shard_map/ppermute | solution.py:251
  99.4 2.1 %collective-permute-start.27 = (bf16[64,512]{1,0:T(8,128)(2,1)S(1)}, bf16[64,512]{1,0:T(8,128)(2,1)S(1)}, u32[]{:S(2)}, u32[]{:S(2)}) collective-permute-start(bf16[64,512]{1,0:T(8,128)(2,1)S(1)} %get-tuple-element.71), channel_id=1, source_target_pairs={{0,8},{1,9},{2,10},{3,11},{4,12},{5,13},{6,14},{7,15},{8,0},{9,1},... | collective-permute-start | bytes 196616 | tf_op jit(solution)/shard_map/ppermute | solution.py:251
  103.0 1.6 %collective-permute-start.30 = (bf16[64,512]{1,0:T(8,128)(2,1)S(1)}, bf16[64,512]{1,0:T(8,128)(2,1)S(1)}, u32[]{:S(2)}, u32[]{:S(2)}) collective-permute-start(bf16[64,512]{1,0:T(8,128)(2,1)S(1)} %get-tuple-element.74), channel_id=1, source_target_pairs={{0,6},{1,7},{2,4},{3,5},{4,2},{5,3},{6,0},{7,1},{8,14},{9,15},{10,... | collective-permute-start | bytes 196616 | tf_op jit(solution)/shard_map/ppermute | solution.py:251
  104.7 2.1 %collective-permute-done.27.refs_6_ = bf16[64,512]{1,0:T(8,128)(2,1)S(1)} collective-permute-done((bf16[64,512]{1,0:T(8,128)(2,1)S(1)}, bf16[64,512]{1,0:T(8,128)(2,1)S(1)}, u32[]{:S(2)}, u32[]{:S(2)}) %collective-permute-start.27) | collective-permute-done | bytes 65568 | tf_op jit(solution)/shard_map/ppermute | solution.py:251
  109.1 3.8 %collective-permute-done.31.refs_10_ = bf16[64,512]{1,0:T(8,128)(2,1)S(1)} collective-permute-done((bf16[64,512]{1,0:T(8,128)(2,1)S(1)}, bf16[64,512]{1,0:T(8,128)(2,1)S(1)}, u32[]{:S(2)}, u32[]{:S(2)}) %collective-permute-start.31) | collective-permute-done | bytes 65568 | tf_op jit(solution)/shard_map/ppermute | solution.py:251
  112.8 1.9 %collective-permute-done.32.refs_11_ = bf16[64,512]{1,0:T(8,128)(2,1)S(1)} collective-permute-done((bf16[64,512]{1,0:T(8,128)(2,1)S(1)}, bf16[64,512]{1,0:T(8,128)(2,1)S(1)}, u32[]{:S(2)}, u32[]{:S(2)}) %collective-permute-start.32) | collective-permute-done | bytes 65568 | tf_op jit(solution)/shard_map/ppermute | solution.py:251
  (52 shorter events, 25.3 us)
Async XLA Ops:
  0.0 9.5 %collective-permute-start.3 = (bf16[2,512,128]{2,1,0:T(8,128)(2,1)}, bf16[2,512,128]{2,1,0:T(8,128)(2,1)S(1)}, u32[]{:S(2)}, u32[]{:S(2)}) collective-permute-start(bf16[2,512,128]{2,1,0:T(8,128)(2,1)} %param.3), channel_id=1, source_target_pairs={{0,2},{1,3},{2,0},{3,1},{4,6},{5,7},{6,4},{7,5},{8,10},{9,11},{10,... | collective-permute-start | bytes 786440 | tf_op jit(solution)/shard_map/ppermute | solution.py:251
  4.0 9.5 %collective-permute-start = (bf16[512,128]{1,0:T(8,128)(2,1)S(1)}, bf16[512,128]{1,0:T(8,128)(2,1)S(1)}, u32[]{:S(2)}, u32[]{:S(2)}) collective-permute-start(bf16[512,128]{1,0:T(8,128)(2,1)S(1)} %get-tuple-element.78.refs_0_), channel_id=1, source_target_pairs={{0,4},{1,5},{2,6},{3,7},{4,0},{5,1},{6,2},{7,3},{8,12},{9,13},{10,... | collective-permute-start | bytes 393224 | tf_op jit(solution)/shard_map/ppermute | solution.py:251
  5.6 18.3 %collective-permute-start.1 = (bf16[512,128]{1,0:T(8,128)(2,1)S(1)}, bf16[512,128]{1,0:T(8,128)(2,1)S(1)}, u32[]{:S(2)}, u32[]{:S(2)}) collective-permute-start(bf16[512,128]{1,0:T(8,128)(2,1)S(1)} %get-tuple-element.78.refs_0_), channel_id=1, source_target_pairs={{0,8},{1,9},{2,10},{3,11},{4,12},{5,13},{6,14},{7,15},{8,0},{9,1},... | collective-permute-start | bytes 393224 | tf_op jit(solution)/shard_map/ppermute | solution.py:251
  8.2 16.2 %collective-permute-start.2 = (bf16[512,128]{1,0:T(8,128)(2,1)S(1)}, bf16[512,128]{1,0:T(8,128)(2,1)S(1)}, u32[]{:S(2)}, u32[]{:S(2)}) collective-permute-start(bf16[512,128]{1,0:T(8,128)(2,1)S(1)} %get-tuple-element.78.refs_0_), channel_id=1, source_target_pairs={{0,12},{1,13},{2,14},{3,15},{4,8},{5,9},{6,10},{7,11},{8,4},{9,5},... | collective-permute-start | bytes 393224 | tf_op jit(solution)/shard_map/ppermute | solution.py:251
  9.5 27.8 %collective-permute-start.17 = (bf16[512,256]{1,0:T(8,128)(2,1)S(1)}, bf16[512,256]{1,0:T(8,128)(2,1)S(1)}, u32[]{:S(2)}, u32[]{:S(2)}) collective-permute-start(bf16[512,256]{1,0:T(8,128)(2,1)S(1)} %pad_maximum_fusion.refs_0_), channel_id=1, source_target_pairs={{0,12},{1,13},{2,14},{3,15},{4,8},{5,9},{6,10},{7,11},{8,4},{9,5},... | collective-permute-start | bytes 786440 | tf_op jit(solution)/shard_map/ppermute | solution.py:251
  13.5 21.4 %collective-permute-start.4 = (bf16[512,128]{1,0:T(8,128)(2,1)S(1)}, bf16[512,128]{1,0:T(8,128)(2,1)S(1)}, u32[]{:S(2)}, u32[]{:S(2)}) collective-permute-start(bf16[512,128]{1,0:T(8,128)(2,1)S(1)} %collective-permute-done.refs_1_), channel_id=1, source_target_pairs={{0,2},{1,3},{2,0},{3,1},{4,6},{5,7},{6,4},{7,5},{8,10},{9,11},{10,... | collective-permute-start | bytes 393224 | tf_op jit(solution)/shard_map/ppermute | solution.py:251
  23.9 11.0 %collective-permute-start.5 = (bf16[512,128]{1,0:T(8,128)(2,1)S(1)}, bf16[512,128]{1,0:T(8,128)(2,1)S(1)}, u32[]{:S(2)}, u32[]{:S(2)}) collective-permute-start(bf16[512,128]{1,0:T(8,128)(2,1)S(1)} %collective-permute-done.1.refs_2_), channel_id=1, source_target_pairs={{0,2},{1,3},{2,0},{3,1},{4,6},{5,7},{6,4},{7,5},{8,10},{9,11},{10,... | collective-permute-start | bytes 393224 | tf_op jit(solution)/shard_map/ppermute | solution.py:251
  24.4 10.5 %collective-permute-start.6 = (bf16[512,128]{1,0:T(8,128)(2,1)S(1)}, bf16[512,128]{1,0:T(8,128)(2,1)S(1)}, u32[]{:S(2)}, u32[]{:S(2)}) collective-permute-start(bf16[512,128]{1,0:T(8,128)(2,1)S(1)} %collective-permute-done.2.refs_3_), channel_id=1, source_target_pairs={{0,2},{1,3},{2,0},{3,1},{4,6},{5,7},{6,4},{7,5},{8,10},{9,11},{10,... | collective-permute-start | bytes 393224 | tf_op jit(solution)/shard_map/ppermute | solution.py:251
  32.9 11.1 %collective-permute-start.16 = (bf16[512,256]{1,0:T(8,128)(2,1)S(1)}, bf16[512,256]{1,0:T(8,128)(2,1)S(1)}, u32[]{:S(2)}, u32[]{:S(2)}) collective-permute-start(bf16[512,256]{1,0:T(8,128)(2,1)S(1)} %pad_maximum_fusion.refs_0_), channel_id=1, source_target_pairs={{0,4},{1,5},{2,6},{3,7},{4,0},{5,1},{6,2},{7,3},{8,12},{9,13},{10,... | collective-permute-start | bytes 786440 | tf_op jit(solution)/shard_map/ppermute | solution.py:251
  35.8 11.8 %collective-permute-start.7 = (bf16[512,128]{1,0:T(8,128)(2,1)S(1)}, bf16[512,128]{1,0:T(8,128)(2,1)S(1)}, u32[]{:S(2)}, u32[]{:S(2)}) collective-permute-start(bf16[512,128]{1,0:T(8,128)(2,1)S(1)} %get-tuple-element.43), channel_id=1, source_target_pairs={{0,2},{1,3},{2,0},{3,1},{4,6},{5,7},{6,4},{7,5},{8,10},{9,11},{10,... | collective-permute-start | bytes 393224 | tf_op jit(solution)/shard_map/ppermute | solution.py:251
  37.4 7.2 %collective-permute-start.18 = (bf16[512,256]{1,0:T(8,128)(2,1)S(1)}, bf16[512,256]{1,0:T(8,128)(2,1)S(1)}, u32[]{:S(2)}, u32[]{:S(2)}) collective-permute-start(bf16[512,256]{1,0:T(8,128)(2,1)S(1)} %collective-permute-done.17.refs_3_), channel_id=1, source_target_pairs={{0,4},{1,5},{2,6},{3,7},{4,0},{5,1},{6,2},{7,3},{8,12},{9,13},{10,... | collective-permute-start | bytes 786440 | tf_op jit(solution)/shard_map/ppermute | solution.py:251
  39.4 12.1 %collective-permute-start.8 = (bf16[1536,128]{1,0:T(8,128)(2,1)S(1)}, bf16[1536,128]{1,0:T(8,128)(2,1)S(1)}, u32[]{:S(2)}, u32[]{:S(2)}) collective-permute-start(bf16[1536,128]{1,0:T(8,128)(2,1)S(1)} %get-tuple-element.44), channel_id=1, source_target_pairs={{0,2},{1,3},{2,0},{3,1},{4,6},{5,7},{6,4},{7,5},{8,10},{9,11},{10,... | collective-permute-start | bytes 1179656 | tf_op jit(solution)/shard_map/ppermute | solution.py:251
  42.6 20.0 %collective-permute-start.12 = (bf16[2048,128]{1,0:T(8,128)(2,1)S(1)}, bf16[2048,128]{1,0:T(8,128)(2,1)S(1)}, u32[]{:S(2)}, u32[]{:S(2)}) collective-permute-start(bf16[2048,128]{1,0:T(8,128)(2,1)S(1)} %get-tuple-element.50), channel_id=1, source_target_pairs={{0,2},{1,3},{2,0},{3,1},{4,6},{5,7},{6,4},{7,5},{8,10},{9,11},{10,... | collective-permute-start | bytes 1572872 | tf_op jit(solution)/shard_map/ppermute | solution.py:251
  46.9 27.0 %collective-permute-start.19 = (bf16[2048,128]{1,0:T(8,128)(2,1)S(1)}, bf16[2048,128]{1,0:T(8,128)(2,1)S(1)}, u32[]{:S(2)}, u32[]{:S(2)}) collective-permute-start(bf16[2048,128]{1,0:T(8,128)(2,1)S(1)} %get-tuple-element.56), channel_id=1, source_target_pairs={{0,2},{1,3},{2,0},{3,1},{4,6},{5,7},{6,4},{7,5},{8,10},{9,11},{10,... | collective-permute-start | bytes 1572872 | tf_op jit(solution)/shard_map/ppermute | solution.py:251
  53.8 12.2 %collective-permute-start.9 = (bf16[128,512]{1,0:T(8,128)(2,1)S(1)}, bf16[128,512]{1,0:T(8,128)(2,1)S(1)}, u32[]{:S(2)}, u32[]{:S(2)}) collective-permute-start(bf16[128,512]{1,0:T(8,128)(2,1)S(1)} %get-tuple-element.46), channel_id=1, source_target_pairs={{0,4},{1,5},{2,6},{3,7},{4,0},{5,1},{6,2},{7,3},{8,12},{9,13},{10,... | collective-permute-start | bytes 393224 | tf_op jit(solution)/shard_map/ppermute | solution.py:251
  55.9 23.3 %collective-permute-start.10 = (bf16[128,512]{1,0:T(8,128)(2,1)S(1)}, bf16[128,512]{1,0:T(8,128)(2,1)S(1)}, u32[]{:S(2)}, u32[]{:S(2)}) collective-permute-start(bf16[128,512]{1,0:T(8,128)(2,1)S(1)} %get-tuple-element.47), channel_id=1, source_target_pairs={{0,8},{1,9},{2,10},{3,11},{4,12},{5,13},{6,14},{7,15},{8,0},{9,1},... | collective-permute-start | bytes 393224 | tf_op jit(solution)/shard_map/ppermute | solution.py:251
  56.9 23.9 %collective-permute-start.11 = (bf16[128,512]{1,0:T(8,128)(2,1)S(1)}, bf16[128,512]{1,0:T(8,128)(2,1)S(1)}, u32[]{:S(2)}, u32[]{:S(2)}) collective-permute-start(bf16[128,512]{1,0:T(8,128)(2,1)S(1)} %get-tuple-element.48), channel_id=1, source_target_pairs={{0,12},{1,13},{2,14},{3,15},{4,8},{5,9},{6,10},{7,11},{8,4},{9,5},... | collective-permute-start | bytes 393224 | tf_op jit(solution)/shard_map/ppermute | solution.py:251
  62.7 32.1 %collective-permute-start.25 = (bf16[1536,128]{1,0:T(8,128)(2,1)S(1)}, bf16[1536,128]{1,0:T(8,128)(2,1)S(1)}, u32[]{:S(2)}, u32[]{:S(2)}) collective-permute-start(bf16[1536,128]{1,0:T(8,128)(2,1)S(1)} %get-tuple-element.68), channel_id=1, source_target_pairs={{0,2},{1,3},{2,0},{3,1},{4,6},{5,7},{6,4},{7,5},{8,10},{9,11},{10,... | collective-permute-start | bytes 1179656 | tf_op jit(solution)/shard_map/ppermute | solution.py:251
  66.0 14.7 %collective-permute-start.13 = (bf16[128,512]{1,0:T(8,128)(2,1)S(1)}, bf16[128,512]{1,0:T(8,128)(2,1)S(1)}, u32[]{:S(2)}, u32[]{:S(2)}) collective-permute-start(bf16[128,512]{1,0:T(8,128)(2,1)S(1)} %get-tuple-element.52), channel_id=1, source_target_pairs={{0,4},{1,5},{2,6},{3,7},{4,0},{5,1},{6,2},{7,3},{8,12},{9,13},{10,... | collective-permute-start | bytes 393224 | tf_op jit(solution)/shard_map/ppermute | solution.py:251
  73.9 12.9 %collective-permute-start.14 = (bf16[128,512]{1,0:T(8,128)(2,1)S(1)}, bf16[128,512]{1,0:T(8,128)(2,1)S(1)}, u32[]{:S(2)}, u32[]{:S(2)}) collective-permute-start(bf16[128,512]{1,0:T(8,128)(2,1)S(1)} %get-tuple-element.53), channel_id=1, source_target_pairs={{0,8},{1,9},{2,10},{3,11},{4,12},{5,13},{6,14},{7,15},{8,0},{9,1},... | collective-permute-start | bytes 393224 | tf_op jit(solution)/shard_map/ppermute | solution.py:251
  79.2 10.4 %collective-permute-start.15 = (bf16[128,512]{1,0:T(8,128)(2,1)S(1)}, bf16[128,512]{1,0:T(8,128)(2,1)S(1)}, u32[]{:S(2)}, u32[]{:S(2)}) collective-permute-start(bf16[128,512]{1,0:T(8,128)(2,1)S(1)} %get-tuple-element.54), channel_id=1, source_target_pairs={{0,12},{1,13},{2,14},{3,15},{4,8},{5,9},{6,10},{7,11},{8,4},{9,5},... | collective-permute-start | bytes 393224 | tf_op jit(solution)/shard_map/ppermute | solution.py:251
  80.7 11.4 %collective-permute-start.20 = (bf16[128,512]{1,0:T(8,128)(2,1)S(1)}, bf16[128,512]{1,0:T(8,128)(2,1)S(1)}, u32[]{:S(2)}, u32[]{:S(2)}) collective-permute-start(bf16[128,512]{1,0:T(8,128)(2,1)S(1)} %get-tuple-element.58), channel_id=1, source_target_pairs={{0,4},{1,5},{2,6},{3,7},{4,0},{5,1},{6,2},{7,3},{8,12},{9,13},{10,... | collective-permute-start | bytes 393224 | tf_op jit(solution)/shard_map/ppermute | solution.py:251
  80.8 11.5 %collective-permute-start.21 = (bf16[128,512]{1,0:T(8,128)(2,1)S(1)}, bf16[128,512]{1,0:T(8,128)(2,1)S(1)}, u32[]{:S(2)}, u32[]{:S(2)}) collective-permute-start(bf16[128,512]{1,0:T(8,128)(2,1)S(1)} %get-tuple-element.59), channel_id=1, source_target_pairs={{0,8},{1,9},{2,10},{3,11},{4,12},{5,13},{6,14},{7,15},{8,0},{9,1},... | collective-permute-start | bytes 393224 | tf_op jit(solution)/shard_map/ppermute | solution.py:251
  86.8 6.9 %collective-permute-start.22 = (bf16[128,512]{1,0:T(8,128)(2,1)S(1)}, bf16[128,512]{1,0:T(8,128)(2,1)S(1)}, u32[]{:S(2)}, u32[]{:S(2)}) collective-permute-start(bf16[128,512]{1,0:T(8,128)(2,1)S(1)} %get-tuple-element.60), channel_id=1, source_target_pairs={{0,12},{1,13},{2,14},{3,15},{4,8},{5,9},{6,10},{7,11},{8,4},{9,5},... | collective-permute-start | bytes 393224 | tf_op jit(solution)/shard_map/ppermute | solution.py:251
  89.6 7.0 %collective-permute-start.24 = (bf16[512,128]{1,0:T(8,128)(2,1)S(1)}, bf16[512,128]{1,0:T(8,128)(2,1)S(1)}, u32[]{:S(2)}, u32[]{:S(2)}) collective-permute-start(bf16[512,128]{1,0:T(8,128)(2,1)S(1)} %get-tuple-element.66), channel_id=1, source_target_pairs={{0,2},{1,3},{2,0},{3,1},{4,6},{5,7},{6,4},{7,5},{8,10},{9,11},{10,... | collective-permute-start | bytes 393224 | tf_op jit(solution)/shard_map/ppermute | solution.py:251
  93.9 20.9 %collective-permute-start.23 = (bf16[192,512]{1,0:T(8,128)(2,1)S(1)}, bf16[192,512]{1,0:T(8,128)(2,1)S(1)}, u32[]{:S(2)}, u32[]{:S(2)}) collective-permute-start(bf16[192,512]{1,0:T(8,128)(2,1)S(1)} %get-tuple-element.64), channel_id=1, source_target_pairs={{0,2},{1,3},{2,0},{3,1},{4,6},{5,7},{6,4},{7,5},{8,10},{9,11},{10,... | collective-permute-start | bytes 589832 | tf_op jit(solution)/shard_map/ppermute | solution.py:251
  99.4 7.3 %collective-permute-start.27 = (bf16[64,512]{1,0:T(8,128)(2,1)S(1)}, bf16[64,512]{1,0:T(8,128)(2,1)S(1)}, u32[]{:S(2)}, u32[]{:S(2)}) collective-permute-start(bf16[64,512]{1,0:T(8,128)(2,1)S(1)} %get-tuple-element.71), channel_id=1, source_target_pairs={{0,8},{1,9},{2,10},{3,11},{4,12},{5,13},{6,14},{7,15},{8,0},{9,1},... | collective-permute-start | bytes 196616 | tf_op jit(solution)/shard_map/ppermute | solution.py:251
  101.6 6.2 %collective-permute-start.28 = (bf16[64,512]{1,0:T(8,128)(2,1)S(1)}, bf16[64,512]{1,0:T(8,128)(2,1)S(1)}, u32[]{:S(2)}, u32[]{:S(2)}) collective-permute-start(bf16[64,512]{1,0:T(8,128)(2,1)S(1)} %get-tuple-element.72), channel_id=1, source_target_pairs={{0,12},{1,13},{2,14},{3,15},{4,8},{5,9},{6,10},{7,11},{8,4},{9,5},... | collective-permute-start | bytes 196616 | tf_op jit(solution)/shard_map/ppermute | solution.py:251
  101.9 7.2 %collective-permute-start.29 = (bf16[64,512]{1,0:T(8,128)(2,1)S(1)}, bf16[64,512]{1,0:T(8,128)(2,1)S(1)}, u32[]{:S(2)}, u32[]{:S(2)}) collective-permute-start(bf16[64,512]{1,0:T(8,128)(2,1)S(1)} %get-tuple-element.73), channel_id=1, source_target_pairs={{0,2},{1,3},{2,0},{3,1},{4,6},{5,7},{6,4},{7,5},{8,10},{9,11},{10,... | collective-permute-start | bytes 196616 | tf_op jit(solution)/shard_map/ppermute | solution.py:251
  103.0 6.0 %collective-permute-start.30 = (bf16[64,512]{1,0:T(8,128)(2,1)S(1)}, bf16[64,512]{1,0:T(8,128)(2,1)S(1)}, u32[]{:S(2)}, u32[]{:S(2)}) collective-permute-start(bf16[64,512]{1,0:T(8,128)(2,1)S(1)} %get-tuple-element.74), channel_id=1, source_target_pairs={{0,6},{1,7},{2,4},{3,5},{4,2},{5,3},{6,0},{7,1},{8,14},{9,15},{10,... | collective-permute-start | bytes 196616 | tf_op jit(solution)/shard_map/ppermute | solution.py:251
  106.8 6.1 %collective-permute-start.31 = (bf16[64,512]{1,0:T(8,128)(2,1)S(1)}, bf16[64,512]{1,0:T(8,128)(2,1)S(1)}, u32[]{:S(2)}, u32[]{:S(2)}) collective-permute-start(bf16[64,512]{1,0:T(8,128)(2,1)S(1)} %get-tuple-element.75), channel_id=1, source_target_pairs={{0,10},{1,11},{2,8},{3,9},{4,14},{5,15},{6,12},{7,13},{8,2},{9,3},... | collective-permute-start | bytes 196616 | tf_op jit(solution)/shard_map/ppermute | solution.py:251
  107.7 7.0 %collective-permute-start.32 = (bf16[64,512]{1,0:T(8,128)(2,1)S(1)}, bf16[64,512]{1,0:T(8,128)(2,1)S(1)}, u32[]{:S(2)}, u32[]{:S(2)}) collective-permute-start(bf16[64,512]{1,0:T(8,128)(2,1)S(1)} %get-tuple-element.76), channel_id=1, source_target_pairs={{0,14},{1,15},{2,12},{3,13},{4,10},{5,11},{6,8},{7,9},{8,6},{9,7},... | collective-permute-start | bytes 196616 | tf_op jit(solution)/shard_map/ppermute | solution.py:251
  (1 other events, 5.6 us)

commit v7 on v4

--- a/solution.py
+++ b/solution.py
@@ -58,10 +58,11 @@
 
 def load_body(half, place, source, out, arrived):
     del place
-    vectors, part = out.shape[0] // STREAMS, out.shape[1]
+    vectors, part = out.shape[:2]
+    cuts = [vectors * at // STREAMS for at in range(STREAMS + 1)]
     copies = []
-    for at in range(STREAMS):
-        some = pl.ds(at * vectors, vectors)
+    for at, (low, high) in enumerate(zip(cuts[:-1], cuts[1:])):
+        some = pl.ds(low, high - low)
         copies.append(pltpu.make_async_copy(source.at[some, pl.ds(half * part, part)], out.at[some], arrived.at[at]))
     for copy in copies:
         copy.start()

time: 122 us -> 122 us (level)
  no operation moved by 1% of the time
where the time goes in v7:
time: 122 us; the launch traced here: 121 us
  waiting for transfers between devices  48.3 us (40%)
  starting transfers between devices  43 us (35%)
  Pallas kernels  28.8 us (24%)
    ppermute x31, waiting for transfers between devices, moved(): return lax.ppermute(value, AXES, pairs)  48.3 us
    ppermute x31, starting transfers between devices, moved(): return lax.ppermute(value, AXES, pairs)  43 us
    pallas_call x6, Pallas kernels, amplitudes_of(): pl.pallas_call(functools.partial(amplitude_body, shards, *vectors), in_sp...  10.5 us
    pallas_call x6, Pallas kernels, gradients_of(): pl.pallas_call(functools.partial(gradient_body, shards, len(owns), first,...  10.1 us
    pallas_call x2, Pallas kernels, loaded(): pl.pallas_call(functools.partial(load_body, half), in_specs=[SMEM, pl.Blo...  7 us
  transfers between devices with their start and end apart: 31, of which 10 were waited for; matrix products, arithmetic and copies ran while one was open for 1% of the time, Pallas kernels for 23%

profile of v7, /device:TPU:0, one launch (start us, length us, event | category | flops | bytes accessed | tf_op | source)
XLA Modules:
  0.0 121.4 jit_solution(6469184017392577886)
XLA Ops:
  0.0 3.0 %collective-permute-start.3 = (bf16[2,512,128]{2,1,0:T(8,128)(2,1)}, bf16[2,512,128]{2,1,0:T(8,128)(2,1)S(1)}, u32[]{:S(2)}, u32[]{:S(2)}) collective-permute-start(bf16[2,512,128]{2,1,0:T(8,128)(2,1)} %param.3), channel_id=1, source_target_pairs={{0,2},{1,3},{2,0},{3,1},{4,6},{5,7},{6,4},{7,5},{8,10},{9,11},{10,... | collective-permute-start | bytes 786440 | tf_op jit(solution)/shard_map/ppermute | solution.py:275
  4.0 1.6 %collective-permute-start = (bf16[512,128]{1,0:T(8,128)(2,1)S(1)}, bf16[512,128]{1,0:T(8,128)(2,1)S(1)}, u32[]{:S(2)}, u32[]{:S(2)}) collective-permute-start(bf16[512,128]{1,0:T(8,128)(2,1)S(1)} %get-tuple-element.82.refs_0_), channel_id=1, source_target_pairs={{0,4},{1,5},{2,6},{3,7},{4,0},{5,1},{6,2},{7,3},{8,12},{9,13},{10,... | collective-permute-start | bytes 393224 | tf_op jit(solution)/shard_map/ppermute | solution.py:275
  5.6 3.9 %collective-permute-done.3 = bf16[2,512,128]{2,1,0:T(8,128)(2,1)S(1)} collective-permute-done((bf16[2,512,128]{2,1,0:T(8,128)(2,1)}, bf16[2,512,128]{2,1,0:T(8,128)(2,1)S(1)}, u32[]{:S(2)}, u32[]{:S(2)}) %collective-permute-start.3) | collective-permute-done | bytes 262176 | tf_op jit(solution)/shard_map/ppermute | solution.py:275
  9.5 3.9 %collective-permute-start.17 = (bf16[512,256]{1,0:T(8,128)(2,1)S(1)}, bf16[512,256]{1,0:T(8,128)(2,1)S(1)}, u32[]{:S(2)}, u32[]{:S(2)}) collective-permute-start(bf16[512,256]{1,0:T(8,128)(2,1)S(1)} %pad_maximum_fusion.refs_0_), channel_id=1, source_target_pairs={{0,12},{1,13},{2,14},{3,15},{4,8},{5,9},{6,10},{7,11},{8,4},{9,5},... | collective-permute-start | bytes 786440 | tf_op jit(solution)/shard_map/ppermute | solution.py:275
  13.5 1.9 %collective-permute-start.2 = (bf16[512,128]{1,0:T(8,128)(2,1)S(1)}, bf16[512,128]{1,0:T(8,128)(2,1)S(1)}, u32[]{:S(2)}, u32[]{:S(2)}) collective-permute-start(bf16[512,128]{1,0:T(8,128)(2,1)S(1)} %get-tuple-element.82.refs_0_), channel_id=1, source_target_pairs={{0,12},{1,13},{2,14},{3,15},{4,8},{5,9},{6,10},{7,11},{8,4},{9,5},... | collective-permute-start | bytes 393224 | tf_op jit(solution)/shard_map/ppermute | solution.py:275
  15.4 1.5 %collective-permute-start.4 = (bf16[512,128]{1,0:T(8,128)(2,1)S(1)}, bf16[512,128]{1,0:T(8,128)(2,1)S(1)}, u32[]{:S(2)}, u32[]{:S(2)}) collective-permute-start(bf16[512,128]{1,0:T(8,128)(2,1)S(1)} %collective-permute-done.refs_1_), channel_id=1, source_target_pairs={{0,2},{1,3},{2,0},{3,1},{4,6},{5,7},{6,4},{7,5},{8,10},{9,11},{10,... | collective-permute-start | bytes 393224 | tf_op jit(solution)/shard_map/ppermute | solution.py:275
  16.9 16.2 %collective-permute-done.1.refs_2_ = bf16[512,128]{1,0:T(8,128)(2,1)S(1)} collective-permute-done((bf16[512,128]{1,0:T(8,128)(2,1)S(1)}, bf16[512,128]{1,0:T(8,128)(2,1)S(1)}, u32[]{:S(2)}, u32[]{:S(2)}) %collective-permute-start.1) | collective-permute-done | bytes 131104 | tf_op jit(solution)/shard_map/ppermute | solution.py:275
  33.1 1.5 %collective-permute-start.5 = (bf16[512,128]{1,0:T(8,128)(2,1)S(1)}, bf16[512,128]{1,0:T(8,128)(2,1)S(1)}, u32[]{:S(2)}, u32[]{:S(2)}) collective-permute-start(bf16[512,128]{1,0:T(8,128)(2,1)S(1)} %collective-permute-done.1.refs_2_), channel_id=1, source_target_pairs={{0,2},{1,3},{2,0},{3,1},{4,6},{5,7},{6,4},{7,5},{8,10},{9,11},{10,... | collective-permute-start | bytes 393224 | tf_op jit(solution)/shard_map/ppermute | solution.py:275
  35.1 3.5 %shard_map.31.refs_5_.factors.refs_3_ = bf16[32,64,2048]{2,1,0:T(8,128)(2,1)S(1)} custom-call(s32[1]{0:T(128)} %bitcast.place, bf16[32,128,2048]{2,1,0:T(8,128)(2,1)} %source.3), custom_call_target="tpu_custom_call" | custom-call | tf_op jit(solution)/shard_map/pallas_call | solution.py:75
  38.6 3.5 %shard_map.28.factors.refs_4_.refs_2_ = bf16[32,64,2048]{2,1,0:T(8,128)(2,1)S(1)} custom-call(s32[1]{0:T(128)} %bitcast.place, bf16[32,128,2048]{2,1,0:T(8,128)(2,1)} %source.3), custom_call_target="tpu_custom_call" | custom-call | tf_op jit(solution)/shard_map/pallas_call | solution.py:75
  42.1 2.0 %collective-permute-start.16 = (bf16[512,256]{1,0:T(8,128)(2,1)S(1)}, bf16[512,256]{1,0:T(8,128)(2,1)S(1)}, u32[]{:S(2)}, u32[]{:S(2)}) collective-permute-start(bf16[512,256]{1,0:T(8,128)(2,1)S(1)} %pad_maximum_fusion.refs_0_), channel_id=1, source_target_pairs={{0,4},{1,5},{2,6},{3,7},{4,0},{5,1},{6,2},{7,3},{8,12},{9,13},{10,... | collective-permute-start | bytes 786440 | tf_op jit(solution)/shard_map/ppermute | solution.py:275
  44.2 2.0 %shard_map.30 = (bf16[1536,128]{1,0:T(8,128)(2,1)S(1)}, bf16[1536,128]{1,0:T(8,128)(2,1)S(1)}) custom-call(s32[1]{0:T(128)} %bitcast.place, bf16[32,64,2048]{2,1,0:T(8,128)(2,1)S(1)} %shard_map.28.factors.refs_4_.refs_2_, bf16[512,128]{1,0:T(8,128)(2,1)S(1)} %get-tuple-element.82.refs_0_, bf16[512,128]{1,0:T(8,128)(2,1)S(1)} %collective-permute-done.refs_1_, ...), custom_call_target="tpu_custom_call" | custom-call | flops 1610612736 | bytes 6291456 | tf_op jit(solution)/shard_map/pallas_call | solution.py:107
  46.2 1.6 %collective-permute-start.8 = (bf16[1536,128]{1,0:T(8,128)(2,1)S(1)}, bf16[1536,128]{1,0:T(8,128)(2,1)S(1)}, u32[]{:S(2)}, u32[]{:S(2)}) collective-permute-start(bf16[1536,128]{1,0:T(8,128)(2,1)S(1)} %get-tuple-element.46), channel_id=1, source_target_pairs={{0,2},{1,3},{2,0},{3,1},{4,6},{5,7},{6,4},{7,5},{8,10},{9,11},{10,... | collective-permute-start | bytes 1179656 | tf_op jit(solution)/shard_map/ppermute | solution.py:275
  47.8 2.5 %shard_map.33 = (bf16[2048,128]{1,0:T(8,128)(2,1)S(1)}, bf16[2048,128]{1,0:T(8,128)(2,1)S(1)}) custom-call(s32[1]{0:T(128)} %bitcast.place, bf16[32,64,2048]{2,1,0:T(8,128)(2,1)S(1)} %shard_map.31.refs_5_.factors.refs_3_, bf16[512,128]{1,0:T(8,128)(2,1)S(1)} %get-tuple-element.82.refs_0_, bf16[512,128]{1,0:T(8,128)(2,1)S(1)} %collective-permute-done.refs_1_, ...), custom_call_target="tpu_custom_call" | custom-call | flops 2147483648 | bytes 8388608 | tf_op jit(solution)/shard_map/pallas_call | solution.py:107
  51.8 1.6 %collective-permute-start.7 = (bf16[512,128]{1,0:T(8,128)(2,1)S(1)}, bf16[512,128]{1,0:T(8,128)(2,1)S(1)}, u32[]{:S(2)}, u32[]{:S(2)}) collective-permute-start(bf16[512,128]{1,0:T(8,128)(2,1)S(1)} %get-tuple-element.45), channel_id=1, source_target_pairs={{0,2},{1,3},{2,0},{3,1},{4,6},{5,7},{6,4},{7,5},{8,10},{9,11},{10,... | collective-permute-start | bytes 393224 | tf_op jit(solution)/shard_map/ppermute | solution.py:275
  53.4 1.7 %collective-permute-done.18.refs_2_ = bf16[512,256]{1,0:T(8,128)(2,1)S(1)} collective-permute-done((bf16[512,256]{1,0:T(8,128)(2,1)S(1)}, bf16[512,256]{1,0:T(8,128)(2,1)S(1)}, u32[]{:S(2)}, u32[]{:S(2)}) %collective-permute-start.18) | collective-permute-done | bytes 262176 | tf_op jit(solution)/shard_map/ppermute | solution.py:275
  55.0 2.4 %shard_map.35 = (bf16[2048,128]{1,0:T(8,128)(2,1)S(1)}, bf16[2048,128]{1,0:T(8,128)(2,1)S(1)}) custom-call(s32[1]{0:T(128)} %bitcast.place, bf16[32,64,2048]{2,1,0:T(8,128)(2,1)S(1)} %shard_map.28.factors.refs_4_.refs_2_, bf16[512,256]{1,0:T(8,128)(2,1)S(1)} %pad_maximum_fusion.refs_0_, bf16[512,256]{1,0:T(8,128)(2,1)S(1)} %collective-permute-done.16.refs_1_, ...), custom_call_target="tpu_custom_call" | custom-call | flops 2147483648 | bytes 8388608 | tf_op jit(solution)/shard_map/pallas_call | solution.py:107
  58.0 14.3 %collective-permute-done.7.refs_2_ = bf16[512,128]{1,0:T(8,128)(2,1)S(1)} collective-permute-done((bf16[512,128]{1,0:T(8,128)(2,1)S(1)}, bf16[512,128]{1,0:T(8,128)(2,1)S(1)}, u32[]{:S(2)}, u32[]{:S(2)}) %collective-permute-start.7) | collective-permute-done | bytes 131104 | tf_op jit(solution)/shard_map/ppermute | solution.py:275
  72.3 2.4 %shard_map.32 = (f32[128,512]{1,0:T(8,128)S(1)}, bf16[128,512]{1,0:T(8,128)(2,1)S(1)}, bf16[128,512]{1,0:T(8,128)(2,1)S(1)}, bf16[128,512]{1,0:T(8,128)(2,1)S(1)}) custom-call(s32[1]{0:T(128)} %bitcast.place, bf16[512,128]{1,0:T(8,128)(2,1)S(1)} %get-tuple-element.43.refs_0_, bf16[1536,128]{1,0:T(8,128)(2,1)S(1)} %get-tuple-element.44.refs_1_, ...), custom_call_target="tpu_custom_call" | custom-call | flops 2147483648 | bytes 16777216 | tf_op jit(solution)/shard_map/pallas_call | solution.py:170
  74.7 3.0 %collective-permute-start.10 = (bf16[128,512]{1,0:T(8,128)(2,1)S(1)}, bf16[128,512]{1,0:T(8,128)(2,1)S(1)}, u32[]{:S(2)}, u32[]{:S(2)}) collective-permute-start(bf16[128,512]{1,0:T(8,128)(2,1)S(1)} %get-tuple-element.49), channel_id=1, source_target_pairs={{0,8},{1,9},{2,10},{3,11},{4,12},{5,13},{6,14},{7,15},{8,0},{9,1},... | collective-permute-start | bytes 393224 | tf_op jit(solution)/shard_map/ppermute | solution.py:275
  79.8 1.9 %shard_map.39 = (bf16[1536,128]{1,0:T(8,128)(2,1)S(1)}, bf16[1536,128]{1,0:T(8,128)(2,1)S(1)}) custom-call(s32[1]{0:T(128)} %bitcast.place, bf16[32,64,2048]{2,1,0:T(8,128)(2,1)S(1)} %shard_map.31.refs_5_.factors.refs_3_, bf16[512,256]{1,0:T(8,128)(2,1)S(1)} %pad_maximum_fusion.refs_0_, bf16[512,256]{1,0:T(8,128)(2,1)S(1)} %collective-permute-done.16.refs_1_, ...), custom_call_target="tpu_custom_call" | custom-call | flops 1610612736 | bytes 6291456 | tf_op jit(solution)/shard_map/pallas_call | solution.py:107
  82.5 2.6 %shard_map.34 = (f32[128,512]{1,0:T(8,128)S(1)}, bf16[128,512]{1,0:T(8,128)(2,1)S(1)}, bf16[128,512]{1,0:T(8,128)(2,1)S(1)}, bf16[128,512]{1,0:T(8,128)(2,1)S(1)}) custom-call(s32[1]{0:T(128)} %bitcast.place, bf16[2048,128]{1,0:T(8,128)(2,1)S(1)} %get-tuple-element.51.refs_0_, bf16[2048,128]{1,0:T(8,128)(2,1)S(1)} %collective-permute-done.12.refs_1_, ...), custom_call_target="tpu_custom_call" | custom-call | flops 2147483648 | bytes 16777216 | tf_op jit(solution)/shard_map/pallas_call | solution.py:170
  86.5 2.0 %collective-permute-start.13 = (bf16[128,512]{1,0:T(8,128)(2,1)S(1)}, bf16[128,512]{1,0:T(8,128)(2,1)S(1)}, u32[]{:S(2)}, u32[]{:S(2)}) collective-permute-start(bf16[128,512]{1,0:T(8,128)(2,1)S(1)} %get-tuple-element.54), channel_id=1, source_target_pairs={{0,4},{1,5},{2,6},{3,7},{4,0},{5,1},{6,2},{7,3},{8,12},{9,13},{10,... | collective-permute-start | bytes 393224 | tf_op jit(solution)/shard_map/ppermute | solution.py:275
  88.5 2.4 %shard_map.36 = (f32[128,512]{1,0:T(8,128)S(1)}, bf16[128,512]{1,0:T(8,128)(2,1)S(1)}, bf16[128,512]{1,0:T(8,128)(2,1)S(1)}, bf16[128,512]{1,0:T(8,128)(2,1)S(1)}) custom-call(s32[1]{0:T(128)} %bitcast.place, bf16[2048,128]{1,0:T(8,128)(2,1)S(1)} %get-tuple-element.57.refs_0_, bf16[2048,128]{1,0:T(8,128)(2,1)S(1)} %collective-permute-done.19.refs_1_, ...), custom_call_target="tpu_custom_call" | custom-call | flops 2147483648 | bytes 16777216 | tf_op jit(solution)/shard_map/pallas_call | solution.py:170
  92.0 1.5 %collective-permute-start.15 = (bf16[128,512]{1,0:T(8,128)(2,1)S(1)}, bf16[128,512]{1,0:T(8,128)(2,1)S(1)}, u32[]{:S(2)}, u32[]{:S(2)}) collective-permute-start(bf16[128,512]{1,0:T(8,128)(2,1)S(1)} %get-tuple-element.56), channel_id=1, source_target_pairs={{0,12},{1,13},{2,14},{3,15},{4,8},{5,9},{6,10},{7,11},{8,4},{9,5},... | collective-permute-start | bytes 393224 | tf_op jit(solution)/shard_map/ppermute | solution.py:275
  96.4 1.5 %collective-permute-start.22 = (bf16[128,512]{1,0:T(8,128)(2,1)S(1)}, bf16[128,512]{1,0:T(8,128)(2,1)S(1)}, u32[]{:S(2)}, u32[]{:S(2)}) collective-permute-start(bf16[128,512]{1,0:T(8,128)(2,1)S(1)} %get-tuple-element.62), channel_id=1, source_target_pairs={{0,12},{1,13},{2,14},{3,15},{4,8},{5,9},{6,10},{7,11},{8,4},{9,5},... | collective-permute-start | bytes 393224 | tf_op jit(solution)/shard_map/ppermute | solution.py:275
  98.0 1.8 %shard_map.40.refs_4_ = f32[128,2048]{1,0:T(8,128)S(1)} custom-call(s32[1]{0:T(128)} %bitcast.place, bf16[1536,128]{1,0:T(8,128)(2,1)S(1)} %get-tuple-element.69.refs_0_, bf16[1536,128]{1,0:T(8,128)(2,1)S(1)} %collective-permute-done.25.refs_1_, bf16[32,64,2048]{2,1,0:T(8,128)(2,1)S(1)} %shard_map.28.factors.refs_4_.refs_2_, ...), custom_call_target="tpu_custom_call" | custom-call | flops 1610612736 | bytes 12582912 | tf_op jit(solution)/shard_map/pallas_call | solution.py:170
  100.2 5.1 %collective-permute-done.14.refs_6_ = bf16[128,512]{1,0:T(8,128)(2,1)S(1)} collective-permute-done((bf16[128,512]{1,0:T(8,128)(2,1)S(1)}, bf16[128,512]{1,0:T(8,128)(2,1)S(1)}, u32[]{:S(2)}, u32[]{:S(2)}) %collective-permute-start.14) | collective-permute-done | bytes 131104 | tf_op jit(solution)/shard_map/ppermute | solution.py:275
  106.3 1.6 %collective-permute-start.26 = (bf16[64,1024]{1,0:T(8,128)(2,1)S(1)}, bf16[64,1024]{1,0:T(8,128)(2,1)S(1)}, u32[]{:S(2)}, u32[]{:S(2)}) collective-permute-start(bf16[64,1024]{1,0:T(8,128)(2,1)S(1)} %get-tuple-element.71), channel_id=1, source_target_pairs={{0,2},{1,3},{2,0},{3,1},{4,6},{5,7},{6,4},{7,5},{8,10},{9,11},{10,... | collective-permute-start | bytes 393224 | tf_op jit(solution)/shard_map/ppermute | solution.py:275
  110.3 2.3 %collective-permute-start.29 = (bf16[64,512]{1,0:T(8,128)(2,1)S(1)}, bf16[64,512]{1,0:T(8,128)(2,1)S(1)}, u32[]{:S(2)}, u32[]{:S(2)}) collective-permute-start(bf16[64,512]{1,0:T(8,128)(2,1)S(1)} %get-tuple-element.79), channel_id=1, source_target_pairs={{0,8},{1,9},{2,10},{3,11},{4,12},{5,13},{6,14},{7,15},{8,0},{9,1},... | collective-permute-start | bytes 196616 | tf_op jit(solution)/shard_map/ppermute | solution.py:275
  112.6 3.4 %collective-permute-start.30 = (bf16[64,512]{1,0:T(8,128)(2,1)S(1)}, bf16[64,512]{1,0:T(8,128)(2,1)S(1)}, u32[]{:S(2)}, u32[]{:S(2)}) collective-permute-start(bf16[64,512]{1,0:T(8,128)(2,1)S(1)} %get-tuple-element.80), channel_id=1, source_target_pairs={{0,12},{1,13},{2,14},{3,15},{4,8},{5,9},{6,10},{7,11},{8,4},{9,5},... | collective-permute-start | bytes 196616 | tf_op jit(solution)/shard_map/ppermute | solution.py:275
  116.1 2.8 %collective-permute-done.30.refs_7_ = bf16[64,512]{1,0:T(8,128)(2,1)S(1)} collective-permute-done((bf16[64,512]{1,0:T(8,128)(2,1)S(1)}, bf16[64,512]{1,0:T(8,128)(2,1)S(1)}, u32[]{:S(2)}, u32[]{:S(2)}) %collective-permute-start.30) | collective-permute-done | bytes 65568 | tf_op jit(solution)/shard_map/ppermute | solution.py:275
  (51 shorter events, 18.4 us)
Async XLA Ops:
  0.0 9.5 %collective-permute-start.3 = (bf16[2,512,128]{2,1,0:T(8,128)(2,1)}, bf16[2,512,128]{2,1,0:T(8,128)(2,1)S(1)}, u32[]{:S(2)}, u32[]{:S(2)}) collective-permute-start(bf16[2,512,128]{2,1,0:T(8,128)(2,1)} %param.3), channel_id=1, source_target_pairs={{0,2},{1,3},{2,0},{3,1},{4,6},{5,7},{6,4},{7,5},{8,10},{9,11},{10,... | collective-permute-start | bytes 786440 | tf_op jit(solution)/shard_map/ppermute | solution.py:275
  4.0 11.4 %collective-permute-start = (bf16[512,128]{1,0:T(8,128)(2,1)S(1)}, bf16[512,128]{1,0:T(8,128)(2,1)S(1)}, u32[]{:S(2)}, u32[]{:S(2)}) collective-permute-start(bf16[512,128]{1,0:T(8,128)(2,1)S(1)} %get-tuple-element.82.refs_0_), channel_id=1, source_target_pairs={{0,4},{1,5},{2,6},{3,7},{4,0},{5,1},{6,2},{7,3},{8,12},{9,13},{10,... | collective-permute-start | bytes 393224 | tf_op jit(solution)/shard_map/ppermute | solution.py:275
  9.5 34.5 %collective-permute-start.17 = (bf16[512,256]{1,0:T(8,128)(2,1)S(1)}, bf16[512,256]{1,0:T(8,128)(2,1)S(1)}, u32[]{:S(2)}, u32[]{:S(2)}) collective-permute-start(bf16[512,256]{1,0:T(8,128)(2,1)S(1)} %pad_maximum_fusion.refs_0_), channel_id=1, source_target_pairs={{0,12},{1,13},{2,14},{3,15},{4,8},{5,9},{6,10},{7,11},{8,4},{9,5},... | collective-permute-start | bytes 786440 | tf_op jit(solution)/shard_map/ppermute | solution.py:275
  13.5 19.6 %collective-permute-start.1 = (bf16[512,128]{1,0:T(8,128)(2,1)S(1)}, bf16[512,128]{1,0:T(8,128)(2,1)S(1)}, u32[]{:S(2)}, u32[]{:S(2)}) collective-permute-start(bf16[512,128]{1,0:T(8,128)(2,1)S(1)} %get-tuple-element.82.refs_0_), channel_id=1, source_target_pairs={{0,8},{1,9},{2,10},{3,11},{4,12},{5,13},{6,14},{7,15},{8,0},{9,1},... | collective-permute-start | bytes 393224 | tf_op jit(solution)/shard_map/ppermute | solution.py:275
  13.5 21.1 %collective-permute-start.2 = (bf16[512,128]{1,0:T(8,128)(2,1)S(1)}, bf16[512,128]{1,0:T(8,128)(2,1)S(1)}, u32[]{:S(2)}, u32[]{:S(2)}) collective-permute-start(bf16[512,128]{1,0:T(8,128)(2,1)S(1)} %get-tuple-element.82.refs_0_), channel_id=1, source_target_pairs={{0,12},{1,13},{2,14},{3,15},{4,8},{5,9},{6,10},{7,11},{8,4},{9,5},... | collective-permute-start | bytes 393224 | tf_op jit(solution)/shard_map/ppermute | solution.py:275
  15.4 28.8 %collective-permute-start.4 = (bf16[512,128]{1,0:T(8,128)(2,1)S(1)}, bf16[512,128]{1,0:T(8,128)(2,1)S(1)}, u32[]{:S(2)}, u32[]{:S(2)}) collective-permute-start(bf16[512,128]{1,0:T(8,128)(2,1)S(1)} %collective-permute-done.refs_1_), channel_id=1, source_target_pairs={{0,2},{1,3},{2,0},{3,1},{4,6},{5,7},{6,4},{7,5},{8,10},{9,11},{10,... | collective-permute-start | bytes 393224 | tf_op jit(solution)/shard_map/ppermute | solution.py:275
  33.1 11.2 %collective-permute-start.5 = (bf16[512,128]{1,0:T(8,128)(2,1)S(1)}, bf16[512,128]{1,0:T(8,128)(2,1)S(1)}, u32[]{:S(2)}, u32[]{:S(2)}) collective-permute-start(bf16[512,128]{1,0:T(8,128)(2,1)S(1)} %collective-permute-done.1.refs_2_), channel_id=1, source_target_pairs={{0,2},{1,3},{2,0},{3,1},{4,6},{5,7},{6,4},{7,5},{8,10},{9,11},{10,... | collective-permute-start | bytes 393224 | tf_op jit(solution)/shard_map/ppermute | solution.py:275
  34.5 9.7 %collective-permute-start.6 = (bf16[512,128]{1,0:T(8,128)(2,1)S(1)}, bf16[512,128]{1,0:T(8,128)(2,1)S(1)}, u32[]{:S(2)}, u32[]{:S(2)}) collective-permute-start(bf16[512,128]{1,0:T(8,128)(2,1)S(1)} %collective-permute-done.2.refs_3_), channel_id=1, source_target_pairs={{0,2},{1,3},{2,0},{3,1},{4,6},{5,7},{6,4},{7,5},{8,10},{9,11},{10,... | collective-permute-start | bytes 393224 | tf_op jit(solution)/shard_map/ppermute | solution.py:275
  42.1 11.3 %collective-permute-start.16 = (bf16[512,256]{1,0:T(8,128)(2,1)S(1)}, bf16[512,256]{1,0:T(8,128)(2,1)S(1)}, u32[]{:S(2)}, u32[]{:S(2)}) collective-permute-start(bf16[512,256]{1,0:T(8,128)(2,1)S(1)} %pad_maximum_fusion.refs_0_), channel_id=1, source_target_pairs={{0,4},{1,5},{2,6},{3,7},{4,0},{5,1},{6,2},{7,3},{8,12},{9,13},{10,... | collective-permute-start | bytes 786440 | tf_op jit(solution)/shard_map/ppermute | solution.py:275
  44.1 11.0 %collective-permute-start.18 = (bf16[512,256]{1,0:T(8,128)(2,1)S(1)}, bf16[512,256]{1,0:T(8,128)(2,1)S(1)}, u32[]{:S(2)}, u32[]{:S(2)}) collective-permute-start(bf16[512,256]{1,0:T(8,128)(2,1)S(1)} %collective-permute-done.17.refs_3_), channel_id=1, source_target_pairs={{0,4},{1,5},{2,6},{3,7},{4,0},{5,1},{6,2},{7,3},{8,12},{9,13},{10,... | collective-permute-start | bytes 786440 | tf_op jit(solution)/shard_map/ppermute | solution.py:275
  46.2 26.1 %collective-permute-start.8 = (bf16[1536,128]{1,0:T(8,128)(2,1)S(1)}, bf16[1536,128]{1,0:T(8,128)(2,1)S(1)}, u32[]{:S(2)}, u32[]{:S(2)}) collective-permute-start(bf16[1536,128]{1,0:T(8,128)(2,1)S(1)} %get-tuple-element.46), channel_id=1, source_target_pairs={{0,2},{1,3},{2,0},{3,1},{4,6},{5,7},{6,4},{7,5},{8,10},{9,11},{10,... | collective-permute-start | bytes 1179656 | tf_op jit(solution)/shard_map/ppermute | solution.py:275
  50.3 31.4 %collective-permute-start.12 = (bf16[2048,128]{1,0:T(8,128)(2,1)S(1)}, bf16[2048,128]{1,0:T(8,128)(2,1)S(1)}, u32[]{:S(2)}, u32[]{:S(2)}) collective-permute-start(bf16[2048,128]{1,0:T(8,128)(2,1)S(1)} %get-tuple-element.52), channel_id=1, source_target_pairs={{0,2},{1,3},{2,0},{3,1},{4,6},{5,7},{6,4},{7,5},{8,10},{9,11},{10,... | collective-permute-start | bytes 1572872 | tf_op jit(solution)/shard_map/ppermute | solution.py:275
  51.8 20.5 %collective-permute-start.7 = (bf16[512,128]{1,0:T(8,128)(2,1)S(1)}, bf16[512,128]{1,0:T(8,128)(2,1)S(1)}, u32[]{:S(2)}, u32[]{:S(2)}) collective-permute-start(bf16[512,128]{1,0:T(8,128)(2,1)S(1)} %get-tuple-element.45), channel_id=1, source_target_pairs={{0,2},{1,3},{2,0},{3,1},{4,6},{5,7},{6,4},{7,5},{8,10},{9,11},{10,... | collective-permute-start | bytes 393224 | tf_op jit(solution)/shard_map/ppermute | solution.py:275
  57.4 29.1 %collective-permute-start.19 = (bf16[2048,128]{1,0:T(8,128)(2,1)S(1)}, bf16[2048,128]{1,0:T(8,128)(2,1)S(1)}, u32[]{:S(2)}, u32[]{:S(2)}) collective-permute-start(bf16[2048,128]{1,0:T(8,128)(2,1)S(1)} %get-tuple-element.58), channel_id=1, source_target_pairs={{0,2},{1,3},{2,0},{3,1},{4,6},{5,7},{6,4},{7,5},{8,10},{9,11},{10,... | collective-permute-start | bytes 1572872 | tf_op jit(solution)/shard_map/ppermute | solution.py:275
  74.7 10.4 %collective-permute-start.10 = (bf16[128,512]{1,0:T(8,128)(2,1)S(1)}, bf16[128,512]{1,0:T(8,128)(2,1)S(1)}, u32[]{:S(2)}, u32[]{:S(2)}) collective-permute-start(bf16[128,512]{1,0:T(8,128)(2,1)S(1)} %get-tuple-element.49), channel_id=1, source_target_pairs={{0,8},{1,9},{2,10},{3,11},{4,12},{5,13},{6,14},{7,15},{8,0},{9,1},... | collective-permute-start | bytes 393224 | tf_op jit(solution)/shard_map/ppermute | solution.py:275
  77.7 13.3 %collective-permute-start.11 = (bf16[128,512]{1,0:T(8,128)(2,1)S(1)}, bf16[128,512]{1,0:T(8,128)(2,1)S(1)}, u32[]{:S(2)}, u32[]{:S(2)}) collective-permute-start(bf16[128,512]{1,0:T(8,128)(2,1)S(1)} %get-tuple-element.50), channel_id=1, source_target_pairs={{0,12},{1,13},{2,14},{3,15},{4,8},{5,9},{6,10},{7,11},{8,4},{9,5},... | collective-permute-start | bytes 393224 | tf_op jit(solution)/shard_map/ppermute | solution.py:275
  79.0 13.0 %collective-permute-start.9 = (bf16[128,512]{1,0:T(8,128)(2,1)S(1)}, bf16[128,512]{1,0:T(8,128)(2,1)S(1)}, u32[]{:S(2)}, u32[]{:S(2)}) collective-permute-start(bf16[128,512]{1,0:T(8,128)(2,1)S(1)} %get-tuple-element.48), channel_id=1, source_target_pairs={{0,4},{1,5},{2,6},{3,7},{4,0},{5,1},{6,2},{7,3},{8,12},{9,13},{10,... | collective-permute-start | bytes 393224 | tf_op jit(solution)/shard_map/ppermute | solution.py:275
  81.7 14.7 %collective-permute-start.25 = (bf16[1536,128]{1,0:T(8,128)(2,1)S(1)}, bf16[1536,128]{1,0:T(8,128)(2,1)S(1)}, u32[]{:S(2)}, u32[]{:S(2)}) collective-permute-start(bf16[1536,128]{1,0:T(8,128)(2,1)S(1)} %get-tuple-element.70), channel_id=1, source_target_pairs={{0,2},{1,3},{2,0},{3,1},{4,6},{5,7},{6,4},{7,5},{8,10},{9,11},{10,... | collective-permute-start | bytes 1179656 | tf_op jit(solution)/shard_map/ppermute | solution.py:275
  85.1 8.4 %collective-permute-start.24 = (bf16[512,128]{1,0:T(8,128)(2,1)S(1)}, bf16[512,128]{1,0:T(8,128)(2,1)S(1)}, u32[]{:S(2)}, u32[]{:S(2)}) collective-permute-start(bf16[512,128]{1,0:T(8,128)(2,1)S(1)} %get-tuple-element.68), channel_id=1, source_target_pairs={{0,2},{1,3},{2,0},{3,1},{4,6},{5,7},{6,4},{7,5},{8,10},{9,11},{10,... | collective-permute-start | bytes 393224 | tf_op jit(solution)/shard_map/ppermute | solution.py:275
  86.5 8.9 %collective-permute-start.13 = (bf16[128,512]{1,0:T(8,128)(2,1)S(1)}, bf16[128,512]{1,0:T(8,128)(2,1)S(1)}, u32[]{:S(2)}, u32[]{:S(2)}) collective-permute-start(bf16[128,512]{1,0:T(8,128)(2,1)S(1)} %get-tuple-element.54), channel_id=1, source_target_pairs={{0,4},{1,5},{2,6},{3,7},{4,0},{5,1},{6,2},{7,3},{8,12},{9,13},{10,... | collective-permute-start | bytes 393224 | tf_op jit(solution)/shard_map/ppermute | solution.py:275
  90.9 14.4 %collective-permute-start.14 = (bf16[128,512]{1,0:T(8,128)(2,1)S(1)}, bf16[128,512]{1,0:T(8,128)(2,1)S(1)}, u32[]{:S(2)}, u32[]{:S(2)}) collective-permute-start(bf16[128,512]{1,0:T(8,128)(2,1)S(1)} %get-tuple-element.55), channel_id=1, source_target_pairs={{0,8},{1,9},{2,10},{3,11},{4,12},{5,13},{6,14},{7,15},{8,0},{9,1},... | collective-permute-start | bytes 393224 | tf_op jit(solution)/shard_map/ppermute | solution.py:275
  92.0 14.2 %collective-permute-start.15 = (bf16[128,512]{1,0:T(8,128)(2,1)S(1)}, bf16[128,512]{1,0:T(8,128)(2,1)S(1)}, u32[]{:S(2)}, u32[]{:S(2)}) collective-permute-start(bf16[128,512]{1,0:T(8,128)(2,1)S(1)} %get-tuple-element.56), channel_id=1, source_target_pairs={{0,12},{1,13},{2,14},{3,15},{4,8},{5,9},{6,10},{7,11},{8,4},{9,5},... | collective-permute-start | bytes 393224 | tf_op jit(solution)/shard_map/ppermute | solution.py:275
  93.6 14.3 %collective-permute-start.20 = (bf16[128,512]{1,0:T(8,128)(2,1)S(1)}, bf16[128,512]{1,0:T(8,128)(2,1)S(1)}, u32[]{:S(2)}, u32[]{:S(2)}) collective-permute-start(bf16[128,512]{1,0:T(8,128)(2,1)S(1)} %get-tuple-element.60), channel_id=1, source_target_pairs={{0,4},{1,5},{2,6},{3,7},{4,0},{5,1},{6,2},{7,3},{8,12},{9,13},{10,... | collective-permute-start | bytes 393224 | tf_op jit(solution)/shard_map/ppermute | solution.py:275
  95.4 13.8 %collective-permute-start.21 = (bf16[128,512]{1,0:T(8,128)(2,1)S(1)}, bf16[128,512]{1,0:T(8,128)(2,1)S(1)}, u32[]{:S(2)}, u32[]{:S(2)}) collective-permute-start(bf16[128,512]{1,0:T(8,128)(2,1)S(1)} %get-tuple-element.61), channel_id=1, source_target_pairs={{0,8},{1,9},{2,10},{3,11},{4,12},{5,13},{6,14},{7,15},{8,0},{9,1},... | collective-permute-start | bytes 393224 | tf_op jit(solution)/shard_map/ppermute | solution.py:275
  96.4 12.8 %collective-permute-start.22 = (bf16[128,512]{1,0:T(8,128)(2,1)S(1)}, bf16[128,512]{1,0:T(8,128)(2,1)S(1)}, u32[]{:S(2)}, u32[]{:S(2)}) collective-permute-start(bf16[128,512]{1,0:T(8,128)(2,1)S(1)} %get-tuple-element.62), channel_id=1, source_target_pairs={{0,12},{1,13},{2,14},{3,15},{4,8},{5,9},{6,10},{7,11},{8,4},{9,5},... | collective-permute-start | bytes 393224 | tf_op jit(solution)/shard_map/ppermute | solution.py:275
  105.3 5.0 %collective-permute-start.28 = (bf16[64,1024]{1,0:T(8,128)(2,1)S(1)}, bf16[64,1024]{1,0:T(8,128)(2,1)S(1)}, u32[]{:S(2)}, u32[]{:S(2)}) collective-permute-start(bf16[64,1024]{1,0:T(8,128)(2,1)S(1)} %get-tuple-element.76), channel_id=1, source_target_pairs={{0,2},{1,3},{2,0},{3,1},{4,6},{5,7},{6,4},{7,5},{8,10},{9,11},{10,... | collective-permute-start | bytes 393224 | tf_op jit(solution)/shard_map/ppermute | solution.py:275
  106.3 9.7 %collective-permute-start.26 = (bf16[64,1024]{1,0:T(8,128)(2,1)S(1)}, bf16[64,1024]{1,0:T(8,128)(2,1)S(1)}, u32[]{:S(2)}, u32[]{:S(2)}) collective-permute-start(bf16[64,1024]{1,0:T(8,128)(2,1)S(1)} %get-tuple-element.71), channel_id=1, source_target_pairs={{0,2},{1,3},{2,0},{3,1},{4,6},{5,7},{6,4},{7,5},{8,10},{9,11},{10,... | collective-permute-start | bytes 393224 | tf_op jit(solution)/shard_map/ppermute | solution.py:275
  109.4 11.0 %collective-permute-start.23 = (bf16[192,512]{1,0:T(8,128)(2,1)S(1)}, bf16[192,512]{1,0:T(8,128)(2,1)S(1)}, u32[]{:S(2)}, u32[]{:S(2)}) collective-permute-start(bf16[192,512]{1,0:T(8,128)(2,1)S(1)} %get-tuple-element.66), channel_id=1, source_target_pairs={{0,2},{1,3},{2,0},{3,1},{4,6},{5,7},{6,4},{7,5},{8,10},{9,11},{10,... | collective-permute-start | bytes 589832 | tf_op jit(solution)/shard_map/ppermute | solution.py:275
  110.3 5.8 %collective-permute-start.29 = (bf16[64,512]{1,0:T(8,128)(2,1)S(1)}, bf16[64,512]{1,0:T(8,128)(2,1)S(1)}, u32[]{:S(2)}, u32[]{:S(2)}) collective-permute-start(bf16[64,512]{1,0:T(8,128)(2,1)S(1)} %get-tuple-element.79), channel_id=1, source_target_pairs={{0,8},{1,9},{2,10},{3,11},{4,12},{5,13},{6,14},{7,15},{8,0},{9,1},... | collective-permute-start | bytes 196616 | tf_op jit(solution)/shard_map/ppermute | solution.py:275
  112.6 6.3 %collective-permute-start.30 = (bf16[64,512]{1,0:T(8,128)(2,1)S(1)}, bf16[64,512]{1,0:T(8,128)(2,1)S(1)}, u32[]{:S(2)}, u32[]{:S(2)}) collective-permute-start(bf16[64,512]{1,0:T(8,128)(2,1)S(1)} %get-tuple-element.80), channel_id=1, source_target_pairs={{0,12},{1,13},{2,14},{3,15},{4,8},{5,9},{6,10},{7,11},{8,4},{9,5},... | collective-permute-start | bytes 196616 | tf_op jit(solution)/shard_map/ppermute | solution.py:275
  116.0 4.3 %collective-permute-start.27 = (bf16[64,512]{1,0:T(8,128)(2,1)S(1)}, bf16[64,512]{1,0:T(8,128)(2,1)S(1)}, u32[]{:S(2)}, u32[]{:S(2)}) collective-permute-start(bf16[64,512]{1,0:T(8,128)(2,1)S(1)} %get-tuple-element.75), channel_id=1, source_target_pairs={{0,4},{1,5},{2,6},{3,7},{4,0},{5,1},{6,2},{7,3},{8,12},{9,13},{10,... | collective-permute-start | bytes 196616 | tf_op jit(solution)/shard_map/ppermute | solution.py:275

commit v8 on v7

--- a/solution.py
+++ b/solution.py
@@ -47,6 +47,10 @@
     return moved % shards if isinstance(moved, int) else lax.rem(moved, shards)
 
 
+def hops_of(shards):
+    return sorted(range(1, shards), key=lambda hop: (hop != shards - 1, hop))
+
+
 def passed_on(shards):
     return shards - 2 if shards > 2 and shards & (shards - 1) == 0 else None
 
@@ -54,6 +58,15 @@
 def groups_of(shards):
     hops = list(range(shards - 1, -1, -1))
     return [hops[: shards // 2], hops[shards // 2 :]]
+
+
+def by_neighbour(shards):
+    return 1 if shards > 2 else None
+
+
+def rows_of(hop, shards, owned):
+    cut = owned // 2 if shards > 2 and hop == hops_of(shards)[-1] else owned
+    return [(low, low + cut) for low in range(0, owned, cut)]
 
 
 def load_body(half, place, source, out, arrived):
@@ -82,16 +95,12 @@
     )(place, factors)
 
 
-def amplitude_body(shards, low, high, place, factors, *refs):
+def amplitude_body(shards, layout, low, high, place, factors, *refs):
     pieces, own, far, rows = refs[:-3], refs[-3], refs[-2], refs[-1]
-    owned, width = pieces[0].shape[0], own.shape[1]
-    for step in range(shards):
-        at = pl.multiple_of(peer(place[0], step, shards, True) * owned, owned)
-        if len(pieces) == shards:
-            rows[pl.ds(at, owned), :] = pieces[step][...]
-        else:
-            rows[pl.ds(at, owned), :width] = pieces[step][...]
-            rows[pl.ds(at, owned), width:] = pieces[shards + step][...]
+    owned, width = rows.shape[0] // shards, own.shape[1]
+    for piece, (hop, row, column) in zip(pieces, layout):
+        at = pl.multiple_of(peer(place[0], hop, shards, True) * owned + row, piece.shape[0])
+        rows[pl.ds(at, piece.shape[0]), column : column + piece.shape[1]] = piece[...]
     part = factors.shape[1]
     for first in range(low, high, BLOCK):
         taken = jnp.concatenate([factors[g] for g in range(first, min(first + BLOCK, high))], axis=0)
@@ -102,10 +111,11 @@
 
 
 def amplitudes_of(place, factors, pieces, vectors, width, shards):
+    pieces, layout = [piece[0] for piece in pieces], tuple(piece[1:] for piece in pieces)
     orbitals = factors.shape[2]
     count = (vectors[1] - vectors[0]) * factors.shape[1]
     return pl.pallas_call(
-        functools.partial(amplitude_body, shards, *vectors),
+        functools.partial(amplitude_body, shards, layout, *vectors),
         in_specs=[SMEM] + [VMEM] * (1 + len(pieces)),
         out_specs=[VMEM] * 2,
         scratch_shapes=[pltpu.VMEM((orbitals, 2 * width), jnp.bfloat16)],
@@ -275,15 +285,23 @@
         return lax.ppermute(value, AXES, pairs)
 
     hops = range(1, shards)
-    near = [theta[0]] + [moved(theta[0], hop) for hop in hops]
     across = moved(theta, 0, True)
-    blocks = [near + [across[0]] + [moved(near[hop], 0, True) for hop in hops]]
+    block = [(theta[0], 0, 0, 0), (across[0], 0, 0, width)]
+    for hop in hops:
+        for low, high in rows_of(hop, shards, theta.shape[1]):
+            came = moved(theta[0, low:high], hop)
+            block.append((came, hop, low, 0))
+            if hop != by_neighbour(shards):
+                block.append((moved(came, 0, True), hop, low, width))
+    if by_neighbour(shards):
+        block.append((moved(across[0], by_neighbour(shards)), by_neighbour(shards), 0, width))
+    blocks = [block]
     for walker in range(1, walkers):
         both = jnp.concatenate([theta[walker], across[walker]], axis=1)
         pieces = {hop: moved(both, hop) for hop in hops if hop != passed_on(shards)}
         if passed_on(shards):
             pieces[passed_on(shards)] = moved(pieces[shards - 1], 1)
-        blocks.append([both] + [pieces[hop] for hop in hops])
+        blocks.append([(both, 0, 0, 0)] + [(pieces[hop], hop, 0, 0) for hop in hops])
 
     stages = walkers * HALVES
     sides = []

time: 122 us -> 128 us (1.049)
  starting transfers between devices: 43 us -> 46 us
  waiting for transfers between devices: 48.3 us -> 50.9 us
    ppermute x31 -> x33, starting transfers between devices: 43 us -> 46 us  [moved(): return lax.ppermute(value, AXES, pairs)]
    ppermute x31 -> x33, waiting for transfers between devices: 48.3 us -> 50.9 us  [moved(): return lax.ppermute(value, AXES, pairs)]
  transfers between devices with their start and end apart: 31 -> 33, of which waited for: 10 -> 12; matrix products, arithmetic and copies ran while one was open for 1% -> 2% of each run, Pallas kernels for 23% -> 22%
where the time goes in v8:
time: 128 us
  waiting for transfers between devices  50.9 us (40%)
  starting transfers between devices  46 us (36%)
  Pallas kernels  28.8 us (22%)
  local copies, waits for them, and re-layouts  1.89 us (1%)
    ppermute x33, waiting for transfers between devices, moved(): return lax.ppermute(value, AXES, pairs)  50.9 us
    ppermute x33, starting transfers between devices, moved(): return lax.ppermute(value, AXES, pairs)  46 us
    pallas_call x6, Pallas kernels, amplitudes_of(): pl.pallas_call(functools.partial(amplitude_body, shards, layout, *vectors...  10.5 us
    pallas_call x6, Pallas kernels, gradients_of(): pl.pallas_call(functools.partial(gradient_body, shards, len(owns), first,...  10.1 us
    pallas_call x2, Pallas kernels, loaded(): pl.pallas_call(functools.partial(load_body, half), in_specs=[SMEM, pl.Blo...  7 us
  transfers between devices with their start and end apart: 33, of which 12 were waited for; matrix products, arithmetic and copies ran while one was open for 2% of the time, Pallas kernels for 22%

profile of v8, /device:TPU:0, one launch (start us, length us, event | category | flops | bytes accessed | tf_op | source)
XLA Modules:
  0.0 127.7 jit_solution(891051774693443231)
XLA Ops:
  0.0 3.0 %collective-permute-start = (bf16[2,512,128]{2,1,0:T(8,128)(2,1)}, bf16[2,512,128]{2,1,0:T(8,128)(2,1)S(1)}, u32[]{:S(2)}, u32[]{:S(2)}) collective-permute-start(bf16[2,512,128]{2,1,0:T(8,128)(2,1)} %param.3), channel_id=1, source_target_pairs={{0,2},{1,3},{2,0},{3,1},{4,6},{5,7},{6,4},{7,5},{8,10},{9,11},{10,... | collective-permute-start | bytes 786440 | tf_op jit(solution)/shard_map/ppermute | solution.py:285
  4.0 3.7 %collective-permute-start.6 = (bf16[512,128]{1,0:T(8,128)(2,1)S(1)}, bf16[512,128]{1,0:T(8,128)(2,1)S(1)}, u32[]{:S(2)}, u32[]{:S(2)}) collective-permute-start(bf16[512,128]{1,0:T(8,128)(2,1)S(1)} %get-tuple-element.82.refs_0_), channel_id=1, source_target_pairs={{0,12},{1,13},{2,14},{3,15},{4,8},{5,9},{6,10},{7,11},{8,4},{9,5},... | collective-permute-start | bytes 393224 | tf_op jit(solution)/shard_map/ppermute | solution.py:285
  7.6 1.8 %collective-permute-done = bf16[2,512,128]{2,1,0:T(8,128)(2,1)S(1)} collective-permute-done((bf16[2,512,128]{2,1,0:T(8,128)(2,1)}, bf16[2,512,128]{2,1,0:T(8,128)(2,1)S(1)}, u32[]{:S(2)}, u32[]{:S(2)}) %collective-permute-start) | collective-permute-done | bytes 262176 | tf_op jit(solution)/shard_map/ppermute | solution.py:285
  9.5 3.9 %collective-permute-start.19 = (bf16[512,256]{1,0:T(8,128)(2,1)S(1)}, bf16[512,256]{1,0:T(8,128)(2,1)S(1)}, u32[]{:S(2)}, u32[]{:S(2)}) collective-permute-start(bf16[512,256]{1,0:T(8,128)(2,1)S(1)} %pad_maximum_fusion.refs_0_), channel_id=1, source_target_pairs={{0,12},{1,13},{2,14},{3,15},{4,8},{5,9},{6,10},{7,11},{8,4},{9,5},... | collective-permute-start | bytes 786440 | tf_op jit(solution)/shard_map/ppermute | solution.py:285
  14.4 2.9 %collective-permute-start.4 = (bf16[256,128]{1,0:T(8,128)(2,1)S(1)}, bf16[256,128]{1,0:T(8,128)(2,1)S(1)}, u32[]{:S(2)}, u32[]{:S(2)}) collective-permute-start(bf16[256,128]{1,0:T(8,128)(2,1)S(1)} %get-tuple-element.85), channel_id=1, source_target_pairs={{0,8},{1,9},{2,10},{3,11},{4,12},{5,13},{6,14},{7,15},{8,0},{9,1},... | collective-permute-start | bytes 196616 | tf_op jit(solution)/shard_map/ppermute | solution.py:285
  17.3 1.5 %collective-permute-start.7 = (bf16[512,128]{1,0:T(8,128)(2,1)S(1)}, bf16[512,128]{1,0:T(8,128)(2,1)S(1)}, u32[]{:S(2)}, u32[]{:S(2)}) collective-permute-start(bf16[512,128]{1,0:T(8,128)(2,1)S(1)} %collective-permute-done.6.refs_7_), channel_id=1, source_target_pairs={{0,2},{1,3},{2,0},{3,1},{4,6},{5,7},{6,4},{7,5},{8,10},{9,11},{10,... | collective-permute-start | bytes 393224 | tf_op jit(solution)/shard_map/ppermute | solution.py:285
  18.8 10.1 %collective-permute-done.2.refs_3_ = bf16[256,128]{1,0:T(8,128)(2,1)S(1)} collective-permute-done((bf16[256,128]{1,0:T(8,128)(2,1)S(1)}, bf16[256,128]{1,0:T(8,128)(2,1)S(1)}, u32[]{:S(2)}, u32[]{:S(2)}) %collective-permute-start.2) | collective-permute-done | bytes 65568 | tf_op jit(solution)/shard_map/ppermute | solution.py:285
  31.7 3.5 %shard_map.31.refs_5_.factors.refs_3_ = bf16[32,64,2048]{2,1,0:T(8,128)(2,1)S(1)} custom-call(s32[1]{0:T(128)} %bitcast.place, bf16[32,128,2048]{2,1,0:T(8,128)(2,1)} %source.3), custom_call_target="tpu_custom_call" | custom-call | tf_op jit(solution)/shard_map/pallas_call | solution.py:88
  35.2 3.5 %shard_map.28.factors.refs_4_.refs_2_ = bf16[32,64,2048]{2,1,0:T(8,128)(2,1)S(1)} custom-call(s32[1]{0:T(128)} %bitcast.place, bf16[32,128,2048]{2,1,0:T(8,128)(2,1)} %source.3), custom_call_target="tpu_custom_call" | custom-call | tf_op jit(solution)/shard_map/pallas_call | solution.py:88
  38.7 1.4 %collective-permute-start.18 = (bf16[512,256]{1,0:T(8,128)(2,1)S(1)}, bf16[512,256]{1,0:T(8,128)(2,1)S(1)}, u32[]{:S(2)}, u32[]{:S(2)}) collective-permute-start(bf16[512,256]{1,0:T(8,128)(2,1)S(1)} %pad_maximum_fusion.refs_0_), channel_id=1, source_target_pairs={{0,4},{1,5},{2,6},{3,7},{4,0},{5,1},{6,2},{7,3},{8,12},{9,13},{10,... | collective-permute-start | bytes 786440 | tf_op jit(solution)/shard_map/ppermute | solution.py:285
  40.8 2.5 %shard_map.33 = (bf16[2048,128]{1,0:T(8,128)(2,1)S(1)}, bf16[2048,128]{1,0:T(8,128)(2,1)S(1)}) custom-call(s32[1]{0:T(128)} %bitcast.place, bf16[32,64,2048]{2,1,0:T(8,128)(2,1)S(1)} %shard_map.31.refs_5_.factors.refs_3_, bf16[512,128]{1,0:T(8,128)(2,1)S(1)} %get-tuple-element.82.refs_0_, bf16[512,128]{1,0:T(8,128)(2,1)S(1)} %get-tuple-element.84.refs_1_, ...), custom_call_target="tpu_custom_call" | custom-call | flops 2147483648 | bytes 8388608 | tf_op jit(solution)/shard_map/pallas_call | solution.py:117
  44.6 2.0 %shard_map.30 = (bf16[1536,128]{1,0:T(8,128)(2,1)S(1)}, bf16[1536,128]{1,0:T(8,128)(2,1)S(1)}) custom-call(s32[1]{0:T(128)} %bitcast.place, bf16[32,64,2048]{2,1,0:T(8,128)(2,1)S(1)} %shard_map.28.factors.refs_4_.refs_2_, bf16[512,128]{1,0:T(8,128)(2,1)S(1)} %get-tuple-element.82.refs_0_, bf16[512,128]{1,0:T(8,128)(2,1)S(1)} %get-tuple-element.84.refs_1_, ...), custom_call_target="tpu_custom_call" | custom-call | flops 1610612736 | bytes 6291456 | tf_op jit(solution)/shard_map/pallas_call | solution.py:117
  49.6 1.6 %collective-permute-done.20.refs_2_ = bf16[512,256]{1,0:T(8,128)(2,1)S(1)} collective-permute-done((bf16[512,256]{1,0:T(8,128)(2,1)S(1)}, bf16[512,256]{1,0:T(8,128)(2,1)S(1)}, u32[]{:S(2)}, u32[]{:S(2)}) %collective-permute-start.20) | collective-permute-done | bytes 262176 | tf_op jit(solution)/shard_map/ppermute | solution.py:285
  51.2 2.4 %shard_map.35 = (bf16[2048,128]{1,0:T(8,128)(2,1)S(1)}, bf16[2048,128]{1,0:T(8,128)(2,1)S(1)}) custom-call(s32[1]{0:T(128)} %bitcast.place, bf16[32,64,2048]{2,1,0:T(8,128)(2,1)S(1)} %shard_map.28.factors.refs_4_.refs_2_, bf16[512,256]{1,0:T(8,128)(2,1)S(1)} %pad_maximum_fusion.refs_0_, bf16[512,256]{1,0:T(8,128)(2,1)S(1)} %collective-permute-done.18.refs_1_, ...), custom_call_target="tpu_custom_call" | custom-call | flops 2147483648 | bytes 8388608 | tf_op jit(solution)/shard_map/pallas_call | solution.py:117
  54.8 1.9 %shard_map.39 = (bf16[1536,128]{1,0:T(8,128)(2,1)S(1)}, bf16[1536,128]{1,0:T(8,128)(2,1)S(1)}) custom-call(s32[1]{0:T(128)} %bitcast.place, bf16[32,64,2048]{2,1,0:T(8,128)(2,1)S(1)} %shard_map.31.refs_5_.factors.refs_3_, bf16[512,256]{1,0:T(8,128)(2,1)S(1)} %pad_maximum_fusion.refs_0_, bf16[512,256]{1,0:T(8,128)(2,1)S(1)} %collective-permute-done.18.refs_1_, ...), custom_call_target="tpu_custom_call" | custom-call | flops 1610612736 | bytes 6291456 | tf_op jit(solution)/shard_map/pallas_call | solution.py:117
  58.4 11.0 %collective-permute-done.9.refs_2_ = bf16[512,128]{1,0:T(8,128)(2,1)S(1)} collective-permute-done((bf16[512,128]{1,0:T(8,128)(2,1)S(1)}, bf16[512,128]{1,0:T(8,128)(2,1)S(1)}, u32[]{:S(2)}, u32[]{:S(2)}) %collective-permute-start.9) | collective-permute-done | bytes 131104 | tf_op jit(solution)/shard_map/ppermute | solution.py:285
  70.6 2.4 %shard_map.32 = (f32[128,512]{1,0:T(8,128)S(1)}, bf16[128,512]{1,0:T(8,128)(2,1)S(1)}, bf16[128,512]{1,0:T(8,128)(2,1)S(1)}, bf16[128,512]{1,0:T(8,128)(2,1)S(1)}) custom-call(s32[1]{0:T(128)} %bitcast.place, bf16[512,128]{1,0:T(8,128)(2,1)S(1)} %get-tuple-element.43.refs_0_, bf16[1536,128]{1,0:T(8,128)(2,1)S(1)} %get-tuple-element.44.refs_1_, ...), custom_call_target="tpu_custom_call" | custom-call | flops 2147483648 | bytes 16777216 | tf_op jit(solution)/shard_map/pallas_call | solution.py:180
  74.4 1.8 %collective-permute-start.12 = (bf16[128,512]{1,0:T(8,128)(2,1)S(1)}, bf16[128,512]{1,0:T(8,128)(2,1)S(1)}, u32[]{:S(2)}, u32[]{:S(2)}) collective-permute-start(bf16[128,512]{1,0:T(8,128)(2,1)S(1)} %get-tuple-element.49), channel_id=1, source_target_pairs={{0,8},{1,9},{2,10},{3,11},{4,12},{5,13},{6,14},{7,15},{8,0},{9,1},... | collective-permute-start | bytes 393224 | tf_op jit(solution)/shard_map/ppermute | solution.py:285
  76.2 2.6 %shard_map.34 = (f32[128,512]{1,0:T(8,128)S(1)}, bf16[128,512]{1,0:T(8,128)(2,1)S(1)}, bf16[128,512]{1,0:T(8,128)(2,1)S(1)}, bf16[128,512]{1,0:T(8,128)(2,1)S(1)}) custom-call(s32[1]{0:T(128)} %bitcast.place, bf16[2048,128]{1,0:T(8,128)(2,1)S(1)} %get-tuple-element.51.refs_0_, bf16[2048,128]{1,0:T(8,128)(2,1)S(1)} %collective-permute-done.14.refs_1_, ...), custom_call_target="tpu_custom_call" | custom-call | flops 2147483648 | bytes 16777216 | tf_op jit(solution)/shard_map/pallas_call | solution.py:180
  78.8 10.1 %collective-permute-done.26.refs_1_ = bf16[512,128]{1,0:T(8,128)(2,1)S(1)} collective-permute-done((bf16[512,128]{1,0:T(8,128)(2,1)S(1)}, bf16[512,128]{1,0:T(8,128)(2,1)S(1)}, u32[]{:S(2)}, u32[]{:S(2)}) %collective-permute-start.26) | collective-permute-done | bytes 131104 | tf_op jit(solution)/shard_map/ppermute | solution.py:285
  89.0 1.7 %collective-permute-start.13 = (bf16[128,512]{1,0:T(8,128)(2,1)S(1)}, bf16[128,512]{1,0:T(8,128)(2,1)S(1)}, u32[]{:S(2)}, u32[]{:S(2)}) collective-permute-start(bf16[128,512]{1,0:T(8,128)(2,1)S(1)} %get-tuple-element.50), channel_id=1, source_target_pairs={{0,12},{1,13},{2,14},{3,15},{4,8},{5,9},{6,10},{7,11},{8,4},{9,5},... | collective-permute-start | bytes 393224 | tf_op jit(solution)/shard_map/ppermute | solution.py:285
  90.7 2.4 %shard_map.36 = (f32[128,512]{1,0:T(8,128)S(1)}, bf16[128,512]{1,0:T(8,128)(2,1)S(1)}, bf16[128,512]{1,0:T(8,128)(2,1)S(1)}, bf16[128,512]{1,0:T(8,128)(2,1)S(1)}) custom-call(s32[1]{0:T(128)} %bitcast.place, bf16[2048,128]{1,0:T(8,128)(2,1)S(1)} %get-tuple-element.57.refs_0_, bf16[2048,128]{1,0:T(8,128)(2,1)S(1)} %collective-permute-done.21.refs_1_, ...), custom_call_target="tpu_custom_call" | custom-call | flops 2147483648 | bytes 16777216 | tf_op jit(solution)/shard_map/pallas_call | solution.py:180
  93.1 2.7 %collective-permute-start.16 = (bf16[128,512]{1,0:T(8,128)(2,1)S(1)}, bf16[128,512]{1,0:T(8,128)(2,1)S(1)}, u32[]{:S(2)}, u32[]{:S(2)}) collective-permute-start(bf16[128,512]{1,0:T(8,128)(2,1)S(1)} %get-tuple-element.55), channel_id=1, source_target_pairs={{0,8},{1,9},{2,10},{3,11},{4,12},{5,13},{6,14},{7,15},{8,0},{9,1},... | collective-permute-start | bytes 393224 | tf_op jit(solution)/shard_map/ppermute | solution.py:285
  95.8 1.7 %collective-permute-start.17 = (bf16[128,512]{1,0:T(8,128)(2,1)S(1)}, bf16[128,512]{1,0:T(8,128)(2,1)S(1)}, u32[]{:S(2)}, u32[]{:S(2)}) collective-permute-start(bf16[128,512]{1,0:T(8,128)(2,1)S(1)} %get-tuple-element.56), channel_id=1, source_target_pairs={{0,12},{1,13},{2,14},{3,15},{4,8},{5,9},{6,10},{7,11},{8,4},{9,5},... | collective-permute-start | bytes 393224 | tf_op jit(solution)/shard_map/ppermute | solution.py:285
  98.0 3.3 %collective-permute-done.15.refs_5_ = bf16[128,512]{1,0:T(8,128)(2,1)S(1)} collective-permute-done((bf16[128,512]{1,0:T(8,128)(2,1)S(1)}, bf16[128,512]{1,0:T(8,128)(2,1)S(1)}, u32[]{:S(2)}, u32[]{:S(2)}) %collective-permute-start.15) | collective-permute-done | bytes 131104 | tf_op jit(solution)/shard_map/ppermute | solution.py:285
  101.4 1.6 %collective-permute-start.24 = (bf16[128,512]{1,0:T(8,128)(2,1)S(1)}, bf16[128,512]{1,0:T(8,128)(2,1)S(1)}, u32[]{:S(2)}, u32[]{:S(2)}) collective-permute-start(bf16[128,512]{1,0:T(8,128)(2,1)S(1)} %get-tuple-element.62), channel_id=1, source_target_pairs={{0,12},{1,13},{2,14},{3,15},{4,8},{5,9},{6,10},{7,11},{8,4},{9,5},... | collective-permute-start | bytes 393224 | tf_op jit(solution)/shard_map/ppermute | solution.py:285
  103.0 1.8 %shard_map.40.refs_4_ = f32[128,2048]{1,0:T(8,128)S(1)} custom-call(s32[1]{0:T(128)} %bitcast.place, bf16[1536,128]{1,0:T(8,128)(2,1)S(1)} %get-tuple-element.69.refs_0_, bf16[1536,128]{1,0:T(8,128)(2,1)S(1)} %collective-permute-done.27.refs_1_, bf16[32,64,2048]{2,1,0:T(8,128)(2,1)S(1)} %shard_map.28.factors.refs_4_.refs_2_, ...), custom_call_target="tpu_custom_call" | custom-call | flops 1610612736 | bytes 12582912 | tf_op jit(solution)/shard_map/pallas_call | solution.py:180
  108.6 6.7 %collective-permute-done.23.refs_10_ = bf16[128,512]{1,0:T(8,128)(2,1)S(1)} collective-permute-done((bf16[128,512]{1,0:T(8,128)(2,1)S(1)}, bf16[128,512]{1,0:T(8,128)(2,1)S(1)}, u32[]{:S(2)}, u32[]{:S(2)}) %collective-permute-start.23) | collective-permute-done | bytes 131104 | tf_op jit(solution)/shard_map/ppermute | solution.py:285
  116.7 3.3 %collective-permute-start.31 = (bf16[64,512]{1,0:T(8,128)(2,1)S(1)}, bf16[64,512]{1,0:T(8,128)(2,1)S(1)}, u32[]{:S(2)}, u32[]{:S(2)}) collective-permute-start(bf16[64,512]{1,0:T(8,128)(2,1)S(1)} %get-tuple-element.79), channel_id=1, source_target_pairs={{0,8},{1,9},{2,10},{3,11},{4,12},{5,13},{6,14},{7,15},{8,0},{9,1},... | collective-permute-start | bytes 196616 | tf_op jit(solution)/shard_map/ppermute | solution.py:285
  120.0 2.1 %collective-permute-start.32 = (bf16[64,512]{1,0:T(8,128)(2,1)S(1)}, bf16[64,512]{1,0:T(8,128)(2,1)S(1)}, u32[]{:S(2)}, u32[]{:S(2)}) collective-permute-start(bf16[64,512]{1,0:T(8,128)(2,1)S(1)} %get-tuple-element.80), channel_id=1, source_target_pairs={{0,12},{1,13},{2,14},{3,15},{4,8},{5,9},{6,10},{7,11},{8,4},{9,5},... | collective-permute-start | bytes 196616 | tf_op jit(solution)/shard_map/ppermute | solution.py:285
  122.2 2.3 %collective-permute-done.31.refs_6_ = bf16[64,512]{1,0:T(8,128)(2,1)S(1)} collective-permute-done((bf16[64,512]{1,0:T(8,128)(2,1)S(1)}, bf16[64,512]{1,0:T(8,128)(2,1)S(1)}, u32[]{:S(2)}, u32[]{:S(2)}) %collective-permute-start.31) | collective-permute-done | bytes 65568 | tf_op jit(solution)/shard_map/ppermute | solution.py:285
  124.5 1.6 %collective-permute-done.32.refs_7_ = bf16[64,512]{1,0:T(8,128)(2,1)S(1)} collective-permute-done((bf16[64,512]{1,0:T(8,128)(2,1)S(1)}, bf16[64,512]{1,0:T(8,128)(2,1)S(1)}, u32[]{:S(2)}, u32[]{:S(2)}) %collective-permute-start.32) | collective-permute-done | bytes 65568 | tf_op jit(solution)/shard_map/ppermute | solution.py:285
  (56 shorter events, 22.6 us)
Async XLA Ops:
  0.0 9.5 %collective-permute-start = (bf16[2,512,128]{2,1,0:T(8,128)(2,1)}, bf16[2,512,128]{2,1,0:T(8,128)(2,1)S(1)}, u32[]{:S(2)}, u32[]{:S(2)}) collective-permute-start(bf16[2,512,128]{2,1,0:T(8,128)(2,1)} %param.3), channel_id=1, source_target_pairs={{0,2},{1,3},{2,0},{3,1},{4,6},{5,7},{6,4},{7,5},{8,10},{9,11},{10,... | collective-permute-start | bytes 786440 | tf_op jit(solution)/shard_map/ppermute | solution.py:285
  4.0 13.4 %collective-permute-start.6 = (bf16[512,128]{1,0:T(8,128)(2,1)S(1)}, bf16[512,128]{1,0:T(8,128)(2,1)S(1)}, u32[]{:S(2)}, u32[]{:S(2)}) collective-permute-start(bf16[512,128]{1,0:T(8,128)(2,1)S(1)} %get-tuple-element.82.refs_0_), channel_id=1, source_target_pairs={{0,12},{1,13},{2,14},{3,15},{4,8},{5,9},{6,10},{7,11},{8,4},{9,5},... | collective-permute-start | bytes 393224 | tf_op jit(solution)/shard_map/ppermute | solution.py:285
  7.6 23.2 %collective-permute-start.1 = (bf16[512,128]{1,0:T(8,128)(2,1)S(1)}, bf16[512,128]{1,0:T(8,128)(2,1)S(1)}, u32[]{:S(2)}, u32[]{:S(2)}) collective-permute-start(bf16[512,128]{1,0:T(8,128)(2,1)S(1)} %get-tuple-element.82.refs_0_), channel_id=1, source_target_pairs={{0,4},{1,5},{2,6},{3,7},{4,0},{5,1},{6,2},{7,3},{8,12},{9,13},{10,... | collective-permute-start | bytes 393224 | tf_op jit(solution)/shard_map/ppermute | solution.py:285
  9.5 30.6 %collective-permute-start.19 = (bf16[512,256]{1,0:T(8,128)(2,1)S(1)}, bf16[512,256]{1,0:T(8,128)(2,1)S(1)}, u32[]{:S(2)}, u32[]{:S(2)}) collective-permute-start(bf16[512,256]{1,0:T(8,128)(2,1)S(1)} %pad_maximum_fusion.refs_0_), channel_id=1, source_target_pairs={{0,12},{1,13},{2,14},{3,15},{4,8},{5,9},{6,10},{7,11},{8,4},{9,5},... | collective-permute-start | bytes 786440 | tf_op jit(solution)/shard_map/ppermute | solution.py:285
  14.3 14.6 %collective-permute-start.2 = (bf16[256,128]{1,0:T(8,128)(2,1)S(1)}, bf16[256,128]{1,0:T(8,128)(2,1)S(1)}, u32[]{:S(2)}, u32[]{:S(2)}) collective-permute-start(bf16[256,128]{1,0:T(8,128)(2,1)S(1)} %get-tuple-element.86), channel_id=1, source_target_pairs={{0,8},{1,9},{2,10},{3,11},{4,12},{5,13},{6,14},{7,15},{8,0},{9,1},... | collective-permute-start | bytes 196616 | tf_op jit(solution)/shard_map/ppermute | solution.py:285
  14.4 15.2 %collective-permute-start.4 = (bf16[256,128]{1,0:T(8,128)(2,1)S(1)}, bf16[256,128]{1,0:T(8,128)(2,1)S(1)}, u32[]{:S(2)}, u32[]{:S(2)}) collective-permute-start(bf16[256,128]{1,0:T(8,128)(2,1)S(1)} %get-tuple-element.85), channel_id=1, source_target_pairs={{0,8},{1,9},{2,10},{3,11},{4,12},{5,13},{6,14},{7,15},{8,0},{9,1},... | collective-permute-start | bytes 196616 | tf_op jit(solution)/shard_map/ppermute | solution.py:285
  17.3 23.5 %collective-permute-start.7 = (bf16[512,128]{1,0:T(8,128)(2,1)S(1)}, bf16[512,128]{1,0:T(8,128)(2,1)S(1)}, u32[]{:S(2)}, u32[]{:S(2)}) collective-permute-start(bf16[512,128]{1,0:T(8,128)(2,1)S(1)} %collective-permute-done.6.refs_7_), channel_id=1, source_target_pairs={{0,2},{1,3},{2,0},{3,1},{4,6},{5,7},{6,4},{7,5},{8,10},{9,11},{10,... | collective-permute-start | bytes 393224 | tf_op jit(solution)/shard_map/ppermute | solution.py:285
  29.0 11.9 %collective-permute-start.8 = (bf16[512,128]{1,0:T(8,128)(2,1)S(1)}, bf16[512,128]{1,0:T(8,128)(2,1)S(1)}, u32[]{:S(2)}, u32[]{:S(2)}) collective-permute-start(bf16[512,128]{1,0:T(8,128)(2,1)S(1)} %get-tuple-element.84.refs_1_), channel_id=1, source_target_pairs={{0,4},{1,5},{2,6},{3,7},{4,0},{5,1},{6,2},{7,3},{8,12},{9,13},{10,... | collective-permute-start | bytes 393224 | tf_op jit(solution)/shard_map/ppermute | solution.py:285
  29.7 9.1 %collective-permute-start.3 = (bf16[256,128]{1,0:T(8,128)(2,1)S(1)}, bf16[256,128]{1,0:T(8,128)(2,1)S(1)}, u32[]{:S(2)}, u32[]{:S(2)}) collective-permute-start(bf16[256,128]{1,0:T(8,128)(2,1)S(1)} %collective-permute-done.2.refs_3_), channel_id=1, source_target_pairs={{0,2},{1,3},{2,0},{3,1},{4,6},{5,7},{6,4},{7,5},{8,10},{9,11},{10,... | collective-permute-start | bytes 196616 | tf_op jit(solution)/shard_map/ppermute | solution.py:285
  30.8 10.0 %collective-permute-start.5 = (bf16[256,128]{1,0:T(8,128)(2,1)S(1)}, bf16[256,128]{1,0:T(8,128)(2,1)S(1)}, u32[]{:S(2)}, u32[]{:S(2)}) collective-permute-start(bf16[256,128]{1,0:T(8,128)(2,1)S(1)} %collective-permute-done.4.refs_5_), channel_id=1, source_target_pairs={{0,2},{1,3},{2,0},{3,1},{4,6},{5,7},{6,4},{7,5},{8,10},{9,11},{10,... | collective-permute-start | bytes 196616 | tf_op jit(solution)/shard_map/ppermute | solution.py:285
  38.7 10.9 %collective-permute-start.18 = (bf16[512,256]{1,0:T(8,128)(2,1)S(1)}, bf16[512,256]{1,0:T(8,128)(2,1)S(1)}, u32[]{:S(2)}, u32[]{:S(2)}) collective-permute-start(bf16[512,256]{1,0:T(8,128)(2,1)S(1)} %pad_maximum_fusion.refs_0_), channel_id=1, source_target_pairs={{0,4},{1,5},{2,6},{3,7},{4,0},{5,1},{6,2},{7,3},{8,12},{9,13},{10,... | collective-permute-start | bytes 786440 | tf_op jit(solution)/shard_map/ppermute | solution.py:285
  40.1 11.1 %collective-permute-start.20 = (bf16[512,256]{1,0:T(8,128)(2,1)S(1)}, bf16[512,256]{1,0:T(8,128)(2,1)S(1)}, u32[]{:S(2)}, u32[]{:S(2)}) collective-permute-start(bf16[512,256]{1,0:T(8,128)(2,1)S(1)} %collective-permute-done.19.refs_3_), channel_id=1, source_target_pairs={{0,4},{1,5},{2,6},{3,7},{4,0},{5,1},{6,2},{7,3},{8,12},{9,13},{10,... | collective-permute-start | bytes 786440 | tf_op jit(solution)/shard_map/ppermute | solution.py:285
  43.4 31.0 %collective-permute-start.14 = (bf16[2048,128]{1,0:T(8,128)(2,1)S(1)}, bf16[2048,128]{1,0:T(8,128)(2,1)S(1)}, u32[]{:S(2)}, u32[]{:S(2)}) collective-permute-start(bf16[2048,128]{1,0:T(8,128)(2,1)S(1)} %get-tuple-element.52), channel_id=1, source_target_pairs={{0,2},{1,3},{2,0},{3,1},{4,6},{5,7},{6,4},{7,5},{8,10},{9,11},{10,... | collective-permute-start | bytes 1572872 | tf_op jit(solution)/shard_map/ppermute | solution.py:285
  46.5 24.0 %collective-permute-start.10 = (bf16[1536,128]{1,0:T(8,128)(2,1)S(1)}, bf16[1536,128]{1,0:T(8,128)(2,1)S(1)}, u32[]{:S(2)}, u32[]{:S(2)}) collective-permute-start(bf16[1536,128]{1,0:T(8,128)(2,1)S(1)} %get-tuple-element.46), channel_id=1, source_target_pairs={{0,2},{1,3},{2,0},{3,1},{4,6},{5,7},{6,4},{7,5},{8,10},{9,11},{10,... | collective-permute-start | bytes 1179656 | tf_op jit(solution)/shard_map/ppermute | solution.py:285
  48.4 21.0 %collective-permute-start.9 = (bf16[512,128]{1,0:T(8,128)(2,1)S(1)}, bf16[512,128]{1,0:T(8,128)(2,1)S(1)}, u32[]{:S(2)}, u32[]{:S(2)}) collective-permute-start(bf16[512,128]{1,0:T(8,128)(2,1)S(1)} %get-tuple-element.45), channel_id=1, source_target_pairs={{0,2},{1,3},{2,0},{3,1},{4,6},{5,7},{6,4},{7,5},{8,10},{9,11},{10,... | collective-permute-start | bytes 393224 | tf_op jit(solution)/shard_map/ppermute | solution.py:285
  53.6 37.1 %collective-permute-start.21 = (bf16[2048,128]{1,0:T(8,128)(2,1)S(1)}, bf16[2048,128]{1,0:T(8,128)(2,1)S(1)}, u32[]{:S(2)}, u32[]{:S(2)}) collective-permute-start(bf16[2048,128]{1,0:T(8,128)(2,1)S(1)} %get-tuple-element.58), channel_id=1, source_target_pairs={{0,2},{1,3},{2,0},{3,1},{4,6},{5,7},{6,4},{7,5},{8,10},{9,11},{10,... | collective-permute-start | bytes 1572872 | tf_op jit(solution)/shard_map/ppermute | solution.py:285
  56.7 44.6 %collective-permute-start.27 = (bf16[1536,128]{1,0:T(8,128)(2,1)S(1)}, bf16[1536,128]{1,0:T(8,128)(2,1)S(1)}, u32[]{:S(2)}, u32[]{:S(2)}) collective-permute-start(bf16[1536,128]{1,0:T(8,128)(2,1)S(1)} %get-tuple-element.70), channel_id=1, source_target_pairs={{0,2},{1,3},{2,0},{3,1},{4,6},{5,7},{6,4},{7,5},{8,10},{9,11},{10,... | collective-permute-start | bytes 1179656 | tf_op jit(solution)/shard_map/ppermute | solution.py:285
  69.5 19.5 %collective-permute-start.26 = (bf16[512,128]{1,0:T(8,128)(2,1)S(1)}, bf16[512,128]{1,0:T(8,128)(2,1)S(1)}, u32[]{:S(2)}, u32[]{:S(2)}) collective-permute-start(bf16[512,128]{1,0:T(8,128)(2,1)S(1)} %get-tuple-element.68), channel_id=1, source_target_pairs={{0,2},{1,3},{2,0},{3,1},{4,6},{5,7},{6,4},{7,5},{8,10},{9,11},{10,... | collective-permute-start | bytes 393224 | tf_op jit(solution)/shard_map/ppermute | solution.py:285
  73.0 20.1 %collective-permute-start.11 = (bf16[128,512]{1,0:T(8,128)(2,1)S(1)}, bf16[128,512]{1,0:T(8,128)(2,1)S(1)}, u32[]{:S(2)}, u32[]{:S(2)}) collective-permute-start(bf16[128,512]{1,0:T(8,128)(2,1)S(1)} %get-tuple-element.48), channel_id=1, source_target_pairs={{0,4},{1,5},{2,6},{3,7},{4,0},{5,1},{6,2},{7,3},{8,12},{9,13},{10,... | collective-permute-start | bytes 393224 | tf_op jit(solution)/shard_map/ppermute | solution.py:285
  74.4 21.5 %collective-permute-start.12 = (bf16[128,512]{1,0:T(8,128)(2,1)S(1)}, bf16[128,512]{1,0:T(8,128)(2,1)S(1)}, u32[]{:S(2)}, u32[]{:S(2)}) collective-permute-start(bf16[128,512]{1,0:T(8,128)(2,1)S(1)} %get-tuple-element.49), channel_id=1, source_target_pairs={{0,8},{1,9},{2,10},{3,11},{4,12},{5,13},{6,14},{7,15},{8,0},{9,1},... | collective-permute-start | bytes 393224 | tf_op jit(solution)/shard_map/ppermute | solution.py:285
  89.0 8.6 %collective-permute-start.13 = (bf16[128,512]{1,0:T(8,128)(2,1)S(1)}, bf16[128,512]{1,0:T(8,128)(2,1)S(1)}, u32[]{:S(2)}, u32[]{:S(2)}) collective-permute-start(bf16[128,512]{1,0:T(8,128)(2,1)S(1)} %get-tuple-element.50), channel_id=1, source_target_pairs={{0,12},{1,13},{2,14},{3,15},{4,8},{5,9},{6,10},{7,11},{8,4},{9,5},... | collective-permute-start | bytes 393224 | tf_op jit(solution)/shard_map/ppermute | solution.py:285
  90.7 10.6 %collective-permute-start.15 = (bf16[128,512]{1,0:T(8,128)(2,1)S(1)}, bf16[128,512]{1,0:T(8,128)(2,1)S(1)}, u32[]{:S(2)}, u32[]{:S(2)}) collective-permute-start(bf16[128,512]{1,0:T(8,128)(2,1)S(1)} %get-tuple-element.54), channel_id=1, source_target_pairs={{0,4},{1,5},{2,6},{3,7},{4,0},{5,1},{6,2},{7,3},{8,12},{9,13},{10,... | collective-permute-start | bytes 393224 | tf_op jit(solution)/shard_map/ppermute | solution.py:285
  93.1 12.9 %collective-permute-start.16 = (bf16[128,512]{1,0:T(8,128)(2,1)S(1)}, bf16[128,512]{1,0:T(8,128)(2,1)S(1)}, u32[]{:S(2)}, u32[]{:S(2)}) collective-permute-start(bf16[128,512]{1,0:T(8,128)(2,1)S(1)} %get-tuple-element.55), channel_id=1, source_target_pairs={{0,8},{1,9},{2,10},{3,11},{4,12},{5,13},{6,14},{7,15},{8,0},{9,1},... | collective-permute-start | bytes 393224 | tf_op jit(solution)/shard_map/ppermute | solution.py:285
  95.8 11.6 %collective-permute-start.17 = (bf16[128,512]{1,0:T(8,128)(2,1)S(1)}, bf16[128,512]{1,0:T(8,128)(2,1)S(1)}, u32[]{:S(2)}, u32[]{:S(2)}) collective-permute-start(bf16[128,512]{1,0:T(8,128)(2,1)S(1)} %get-tuple-element.56), channel_id=1, source_target_pairs={{0,12},{1,13},{2,14},{3,15},{4,8},{5,9},{6,10},{7,11},{8,4},{9,5},... | collective-permute-start | bytes 393224 | tf_op jit(solution)/shard_map/ppermute | solution.py:285
  97.6 11.0 %collective-permute-start.22 = (bf16[128,512]{1,0:T(8,128)(2,1)S(1)}, bf16[128,512]{1,0:T(8,128)(2,1)S(1)}, u32[]{:S(2)}, u32[]{:S(2)}) collective-permute-start(bf16[128,512]{1,0:T(8,128)(2,1)S(1)} %get-tuple-element.60), channel_id=1, source_target_pairs={{0,4},{1,5},{2,6},{3,7},{4,0},{5,1},{6,2},{7,3},{8,12},{9,13},{10,... | collective-permute-start | bytes 393224 | tf_op jit(solution)/shard_map/ppermute | solution.py:285
  101.3 14.0 %collective-permute-start.23 = (bf16[128,512]{1,0:T(8,128)(2,1)S(1)}, bf16[128,512]{1,0:T(8,128)(2,1)S(1)}, u32[]{:S(2)}, u32[]{:S(2)}) collective-permute-start(bf16[128,512]{1,0:T(8,128)(2,1)S(1)} %get-tuple-element.61), channel_id=1, source_target_pairs={{0,8},{1,9},{2,10},{3,11},{4,12},{5,13},{6,14},{7,15},{8,0},{9,1},... | collective-permute-start | bytes 393224 | tf_op jit(solution)/shard_map/ppermute | solution.py:285
  101.4 14.0 %collective-permute-start.24 = (bf16[128,512]{1,0:T(8,128)(2,1)S(1)}, bf16[128,512]{1,0:T(8,128)(2,1)S(1)}, u32[]{:S(2)}, u32[]{:S(2)}) collective-permute-start(bf16[128,512]{1,0:T(8,128)(2,1)S(1)} %get-tuple-element.62), channel_id=1, source_target_pairs={{0,12},{1,13},{2,14},{3,15},{4,8},{5,9},{6,10},{7,11},{8,4},{9,5},... | collective-permute-start | bytes 393224 | tf_op jit(solution)/shard_map/ppermute | solution.py:285
  106.1 10.6 %collective-permute-start.30 = (bf16[64,1024]{1,0:T(8,128)(2,1)S(1)}, bf16[64,1024]{1,0:T(8,128)(2,1)S(1)}, u32[]{:S(2)}, u32[]{:S(2)}) collective-permute-start(bf16[64,1024]{1,0:T(8,128)(2,1)S(1)} %get-tuple-element.76), channel_id=1, source_target_pairs={{0,2},{1,3},{2,0},{3,1},{4,6},{5,7},{6,4},{7,5},{8,10},{9,11},{10,... | collective-permute-start | bytes 393224 | tf_op jit(solution)/shard_map/ppermute | solution.py:285
  107.5 14.6 %collective-permute-start.28 = (bf16[64,1024]{1,0:T(8,128)(2,1)S(1)}, bf16[64,1024]{1,0:T(8,128)(2,1)S(1)}, u32[]{:S(2)}, u32[]{:S(2)}) collective-permute-start(bf16[64,1024]{1,0:T(8,128)(2,1)S(1)} %get-tuple-element.71), channel_id=1, source_target_pairs={{0,2},{1,3},{2,0},{3,1},{4,6},{5,7},{6,4},{7,5},{8,10},{9,11},{10,... | collective-permute-start | bytes 393224 | tf_op jit(solution)/shard_map/ppermute | solution.py:285
  115.5 11.2 %collective-permute-start.25 = (bf16[192,512]{1,0:T(8,128)(2,1)S(1)}, bf16[192,512]{1,0:T(8,128)(2,1)S(1)}, u32[]{:S(2)}, u32[]{:S(2)}) collective-permute-start(bf16[192,512]{1,0:T(8,128)(2,1)S(1)} %get-tuple-element.66), channel_id=1, source_target_pairs={{0,2},{1,3},{2,0},{3,1},{4,6},{5,7},{6,4},{7,5},{8,10},{9,11},{10,... | collective-permute-start | bytes 589832 | tf_op jit(solution)/shard_map/ppermute | solution.py:285
  116.7 7.8 %collective-permute-start.31 = (bf16[64,512]{1,0:T(8,128)(2,1)S(1)}, bf16[64,512]{1,0:T(8,128)(2,1)S(1)}, u32[]{:S(2)}, u32[]{:S(2)}) collective-permute-start(bf16[64,512]{1,0:T(8,128)(2,1)S(1)} %get-tuple-element.79), channel_id=1, source_target_pairs={{0,8},{1,9},{2,10},{3,11},{4,12},{5,13},{6,14},{7,15},{8,0},{9,1},... | collective-permute-start | bytes 196616 | tf_op jit(solution)/shard_map/ppermute | solution.py:285
  120.0 6.1 %collective-permute-start.32 = (bf16[64,512]{1,0:T(8,128)(2,1)S(1)}, bf16[64,512]{1,0:T(8,128)(2,1)S(1)}, u32[]{:S(2)}, u32[]{:S(2)}) collective-permute-start(bf16[64,512]{1,0:T(8,128)(2,1)S(1)} %get-tuple-element.80), channel_id=1, source_target_pairs={{0,12},{1,13},{2,14},{3,15},{4,8},{5,9},{6,10},{7,11},{8,4},{9,5},... | collective-permute-start | bytes 196616 | tf_op jit(solution)/shard_map/ppermute | solution.py:285
  (1 other events, 4.6 us)
